TPU v7x, 32 devices: a whole 2x2x4 slice. The times are simulated.
32 devices in a mesh: dp: 8 (over y, x, core), tensor: 4 (over z).
Axes of the slice: x: 2, y: 2, z: 4, core: 2. Of those that a mesh axis runs over, the one named last changes fastest.
Arguments:
- hidden_in: bfloat16 [32, 512, 768], P('dp'), may hold values from -6 to 6
- out_grad: bfloat16 [32, 512, 768], P('dp'), may hold values from -3 to 3
- segment_ids: int32 [32, 512], P('dp'), may hold values from 0 to 7, never falling along the last dimension, each value on 1 to 256 neighbouring positions
- step_count: int32 [1], replicated, may hold values from 1 to 199999
- qkv_state: float32 [3, 768, 3, 768], P(None, 'dp', None, 'tensor'), as said below
- qv_bias_state: float32 [3, 2, 12, 64], P(None, None, 'tensor', 'dp'), as said below
- out_state: float32 [3, 768, 768], P(None, 'tensor', 'dp'), as said below
- up_state: float32 [3, 768, 3072], P(None, 'dp', 'tensor'), as said below
- up_bias_state: float32 [3, 24, 128], P(None, 'tensor', 'dp'), as said below
- down_state: float32 [3, 3072, 768], P(None, 'tensor', 'dp'), as said below
- vector_state: float32 [3, 6, 768], P(None, None, 'dp'), as said below
Outputs:
- hidden_out: bfloat16 [32, 512, 768], P('dp')
- grad_in: bfloat16 [32, 512, 768], P('dp')
- grad_qkv: float32 [768, 3, 768], P('dp', None, 'tensor')
- grad_qv_bias: float32 [2, 12, 64], P(None, 'tensor', 'dp')
- grad_out: float32 [768, 768], P('tensor', 'dp')
- grad_up: float32 [768, 3072], P('dp', 'tensor')
- grad_up_bias: float32 [24, 128], P('tensor', 'dp')
- grad_down: float32 [3072, 768], P('tensor', 'dp')
- grad_vectors: float32 [6, 768], P(None, 'dp')
- new_qkv_state: float32 [2, 768, 3, 768], P(None, 'dp', None, 'tensor')
- new_qv_bias_state: float32 [2, 2, 12, 64], P(None, None, 'tensor', 'dp')
- new_out_state: float32 [2, 768, 768], P(None, 'tensor', 'dp')
- new_up_state: float32 [2, 768, 3072], P(None, 'dp', 'tensor')
- new_up_bias_state: float32 [2, 24, 128], P(None, 'tensor', 'dp')
- new_down_state: float32 [2, 3072, 768], P(None, 'tensor', 'dp')
- new_vector_state: float32 [2, 6, 768], P(None, None, 'dp')
- plan: float32 [3], replicated
Inputs may be any that keep to these rules, and one draw needn't show every extreme that they name: `segment_ids`: within each packed row the fragment numbers never fall; a token attends exactly to the tokens of its own row with the same number. `qkv_state`: index 2 (second moments) is positive. `qv_bias_state`: index 2 (second moments) is positive. `out_state`: index 2 (second moments) is positive. `up_state`: index 2 (second moments) is positive. `up_bias_state`: index 2 (second moments) is positive. `down_state`: index 2 (second moments) is positive. `vector_state`: index 2 (second moments) is positive.
All inputs are finite; a program needn't handle non-finite values.
Results may differ from a plain program's by a relative error of at most 0.023.
The roundings to bfloat16 on the way count: a program that leaves them out, or rounds other values in their place, can miss the bound.
Values may be sent and summed in bfloat16 or wider, within the bound.
No kernel may reach another device: no remote copies, remote signals or barrier semaphores. Data moves between devices by JAX's collectives and lax.ppermute only.
A program may use at most 192 MiB of HBM per device.

v0:
```python
import math

import jax
import jax.numpy as jnp
from jax import lax
from jax.sharding import PartitionSpec as P

HD = 64


norm_eps = 1e-05
beta_first = 0.9
beta_second = 0.999
warm_steps = 10000.0
total_steps = 200000.0


def layer_norm(value, gain, shift):
    center = value - jnp.mean(value, axis=-1, keepdims=True)
    spread = jnp.mean(center * center, axis=-1, keepdims=True)
    return center * lax.rsqrt(spread + norm_eps) * gain + shift


def gelu_exact(value):
    return 0.5 * value * (1.0 + lax.erf(value * 0.7071067811865476))


def scores_of(query, key_rows, segments):
    raw = jnp.einsum(
        "bqhd,bkhd->bhqk", query, key_rows, preferred_element_type=jnp.float32
    ) * HD ** (-0.5)
    same = segments[:, :, None] == segments[:, None, :]
    return jnp.where(same[:, None], raw, -1e30)


def contract_rows(left, right):
    return lax.dot_general(
        left, right, (((0,), (0,)), ((), ())), preferred_element_type=jnp.float32
    )


def contract_cols(left, right):
    return lax.dot_general(
        left, right, (((1,), (1,)), ((), ())), preferred_element_type=jnp.float32
    )


def moment_update(state, grad):
    moment_one = beta_first * state[1] + (1.0 - beta_first) * grad
    moment_two = beta_second * state[2] + (1.0 - beta_second) * grad * grad
    return jnp.stack([moment_one, moment_two])


def body(
    hidden_in,
    out_grad,
    segment_ids,
    step_count,
    qkv_state,
    qv_bias_state,
    out_state,
    up_state,
    up_bias_state,
    down_state,
    vector_state,
):
    bf = jnp.bfloat16
    fl = jnp.float32
    w_qkv, b_qv, w_out, w_up, b_up, w_down, vectors = (
        lax.all_gather(qkv_state[0].astype(bf), "dp", axis=0, tiled=True),
        lax.all_gather(qv_bias_state[0].astype(bf), "dp", axis=2, tiled=True),
        lax.all_gather(out_state[0].astype(bf), "dp", axis=1, tiled=True),
        lax.all_gather(up_state[0].astype(bf), "dp", axis=0, tiled=True),
        lax.all_gather(up_bias_state[0].astype(bf), "dp", axis=1, tiled=True),
        lax.all_gather(down_state[0].astype(bf), "dp", axis=1, tiled=True),
        lax.all_gather(vector_state[0].astype(bf), "dp", axis=1, tiled=True),
    )
    count, length, width_model = hidden_in.shape
    rows = count * length
    heads_local = b_qv.shape[1]
    head_width = heads_local * HD
    ff_local = w_up.shape[1]
    scale = HD ** (-0.5)
    plain = hidden_in.reshape(rows, width_model)
    cotangent = out_grad.reshape(rows, width_model)
    vec = vectors.astype(fl)
    proj = jnp.einsum("td,dcf->tcf", plain, w_qkv, preferred_element_type=fl)
    bias_f = b_qv.astype(fl).reshape(2, head_width)
    bias = jnp.stack([bias_f[0], jnp.zeros((head_width,), fl), bias_f[1]])
    proj_b = (proj + bias[None]).astype(bf)
    heads = proj_b.reshape(count, length, 3, heads_local, HD)
    query = heads[:, :, 0]
    key_rows = heads[:, :, 1]
    value_rows = heads[:, :, 2]
    scores = scores_of(query, key_rows, segment_ids)
    top = jnp.max(scores, axis=-1, keepdims=True)
    expd = jnp.exp(scores - top)
    denom = jnp.sum(expd, axis=-1, keepdims=True)
    log_total = top + jnp.log(denom)
    probs_b = (expd / denom).astype(bf)
    context = (
        jnp.einsum("bhqk,bkhd->bqhd", probs_b, value_rows, preferred_element_type=fl)
        .astype(bf)
        .reshape(rows, head_width)
    )
    attn_part = jnp.dot(context, w_out, preferred_element_type=fl)
    attn = lax.psum(attn_part.astype(jnp.bfloat16), "tensor").astype(jnp.float32)
    first, first_pull = jax.vjp(layer_norm, plain.astype(fl) + attn + vec[4], vec[0], vec[1])
    first_b = first.astype(bf)
    up = jnp.dot(first_b, w_up, preferred_element_type=fl) + b_up.astype(fl).reshape(ff_local)
    act, gelu_pull = jax.vjp(gelu_exact, up)
    act_b = act.astype(bf)
    ffn_part = jnp.dot(act_b, w_down, preferred_element_type=fl)
    ffn = lax.psum(ffn_part.astype(jnp.bfloat16), "tensor").astype(jnp.float32)
    out, second_pull = jax.vjp(layer_norm, first + ffn + vec[5], vec[2], vec[3])
    grad_r2, grad_g2, grad_b2 = second_pull(cotangent.astype(fl))
    grad_ffn = grad_r2.astype(bf)
    grad_down = contract_rows(act_b, grad_ffn)
    grad_act = contract_cols(grad_ffn, w_down)
    grad_up_b = gelu_pull(grad_act)[0].astype(bf)
    grad_wup = contract_rows(first_b, grad_up_b)
    grad_bup = jnp.sum(grad_up_b, axis=0, dtype=fl).reshape(b_up.shape)
    feed_part = contract_cols(grad_up_b, w_up)
    feed_back = lax.psum(feed_part.astype(jnp.bfloat16), "tensor").astype(jnp.float32)
    grad_first = grad_r2 + feed_back.astype(bf).astype(fl)
    grad_r1, grad_g1, grad_b1 = first_pull(grad_first)
    grad_attn = grad_r1.astype(bf)
    grad_wout = contract_rows(context, grad_attn)
    grad_context = (
        contract_cols(grad_attn, w_out).astype(bf).reshape(count, length, heads_local, HD)
    )
    again = scores_of(query, key_rows, segment_ids)
    probs = jnp.exp(again - log_total)
    probs_again = probs.astype(bf)
    grad_probs = jnp.einsum("bqhd,bkhd->bhqk", grad_context, value_rows, preferred_element_type=fl)
    grad_value = jnp.einsum("bhqk,bqhd->bkhd", probs_again, grad_context, preferred_element_type=fl)
    row_dot = jnp.sum(probs * grad_probs, axis=-1, keepdims=True)
    grad_scores = (probs * (grad_probs - row_dot)).astype(bf)
    grad_query = (
        jnp.einsum("bhqk,bkhd->bqhd", grad_scores, key_rows, preferred_element_type=fl) * scale
    )
    grad_key = jnp.einsum("bhqk,bqhd->bkhd", grad_scores, query, preferred_element_type=fl) * scale
    grad_proj = (
        jnp.stack([grad_query, grad_key, grad_value], axis=2)
        .astype(bf)
        .reshape(rows, 3, head_width)
    )
    proj_sums = jnp.sum(grad_proj, axis=0, dtype=fl)
    grad_bqv = jnp.stack([proj_sums[0], proj_sums[2]]).reshape(2, heads_local, HD)
    grad_wqkv = jnp.einsum("td,tcf->dcf", plain, grad_proj, preferred_element_type=fl)
    input_part = jnp.einsum("tcf,dcf->td", grad_proj, w_qkv, preferred_element_type=fl)
    vec_part = jnp.stack(
        [grad_g1, grad_b1, grad_g2, grad_b2, jnp.sum(grad_r1, axis=0), jnp.sum(grad_r2, axis=0)]
    )
    input_back = lax.psum(input_part.astype(jnp.bfloat16), "tensor").astype(jnp.float32)
    grad_in = (grad_r1 + input_back.astype(bf).astype(fl)).astype(bf).reshape(hidden_in.shape)
    hidden_out = out.astype(bf).reshape(hidden_in.shape)
    summed = (
        lax.psum_scatter(grad_wqkv, "dp", scatter_dimension=0, tiled=True),
        lax.psum_scatter(grad_bqv, "dp", scatter_dimension=2, tiled=True),
        lax.psum_scatter(grad_wout, "dp", scatter_dimension=1, tiled=True),
        lax.psum_scatter(grad_wup, "dp", scatter_dimension=0, tiled=True),
        lax.psum_scatter(grad_bup, "dp", scatter_dimension=1, tiled=True),
        lax.psum_scatter(grad_down, "dp", scatter_dimension=1, tiled=True),
        lax.psum_scatter(vec_part, "dp", scatter_dimension=1, tiled=True),
    )
    steps_f = step_count[0].astype(fl)
    factor = jnp.minimum(steps_f / warm_steps, (total_steps - steps_f) / (total_steps - warm_steps))
    fix_first = 1.0 - jnp.exp(steps_f * math.log(beta_first))
    fix_second = 1.0 - jnp.exp(steps_f * math.log(beta_second))
    states = (
        qkv_state,
        qv_bias_state,
        out_state,
        up_state,
        up_bias_state,
        down_state,
        vector_state,
    )
    news = tuple((moment_update(s, g) for s, g in zip(states, summed)))
    plan = jnp.stack([factor, fix_first, fix_second])
    return (
        hidden_out,
        grad_in,
        summed[0],
        summed[1],
        summed[2],
        summed[3],
        summed[4],
        summed[5],
        summed[6],
        news[0],
        news[1],
        news[2],
        news[3],
        news[4],
        news[5],
        news[6],
        plan,
    )


def solution(mesh):
    return jax.shard_map(
        body,
        mesh=mesh,
        in_specs=(
            P("dp", None, None),
            P("dp", None, None),
            P("dp", None),
            P(),
            P(None, "dp", None, "tensor"),
            P(None, None, "tensor", "dp"),
            P(None, "tensor", "dp"),
            P(None, "dp", "tensor"),
            P(None, "tensor", "dp"),
            P(None, "tensor", "dp"),
            P(None, None, "dp"),
        ),
        out_specs=(
            P("dp", None, None),
            P("dp", None, None),
            P("dp", None, "tensor"),
            P(None, "tensor", "dp"),
            P("tensor", "dp"),
            P("dp", "tensor"),
            P("tensor", "dp"),
            P("tensor", "dp"),
            P(None, "dp"),
            P(None, "dp", None, "tensor"),
            P(None, None, "tensor", "dp"),
            P(None, "tensor", "dp"),
            P(None, "dp", "tensor"),
            P(None, "tensor", "dp"),
            P(None, "tensor", "dp"),
            P(None, None, "dp"),
            P(),
        ),
        check_vma=False,
    )
```

profile of v0, /device:TPU:0, one launch (start us, length us, event | category | flops | bytes accessed | tf_op | source)
XLA Modules:
  0.0 760.8 jit_solution(6386560561636301362)
XLA Ops:
  9.0 10.6 %all-gather.1 = bf16[1,2,3,64]{2,1,0,3:T(2,128)(2,1)S(1)} all-gather(bf16[1,2,3,8]{2,1,0,3:T(2,128)(2,1)S(1)} %copy.181), channel_id=3, replica_groups=mesh['dp'=8,'tensor'=4] {'dp'}, dimensions={3}, use_global_device_ids=true | all-gather | bytes 864 | tf_op jit(solution)/shard_map/all_gather | solution.py:71
  22.8 11.3 %all-gather.2 = bf16[1,192,768]{1,0,2:T(2,128)(2,1)} all-gather(bf16[1,192,96]{1,0,2:T(2,128)(2,1)S(1)} %copy.142), channel_id=4, replica_groups=mesh['dp'=8,'tensor'=4] {'dp'}, dimensions={2}, use_global_device_ids=true | all-gather | bytes 331776 | tf_op jit(solution)/shard_map/all_gather | solution.py:72
  38.6 15.8 %all-gather = bf16[1,768,3,192]{3,2,0,1:T(4,128)(2,1)} all-gather(bf16[1,96,3,192]{3,2,0,1:T(4,128)(2,1)} %copy.132), channel_id=2, replica_groups=mesh['dp'=8,'tensor'=4] {'dp'}, dimensions={1}, use_global_device_ids=true | all-gather | bytes 995328 | tf_op jit(solution)/shard_map/all_gather | solution.py:70
  62.9 6.2 reshape.215
  93.2 8.7 %all-gather.5 = bf16[1,6,128]{1,0,2:T(2,128)(2,1)S(1)} all-gather(bf16[1,6,16]{1,0,2:T(2,128)(2,1)} %copy.145), channel_id=7, replica_groups=mesh['dp'=8,'tensor'=4] {'dp'}, dimensions={2}, use_global_device_ids=true | all-gather | bytes 1728 | tf_op jit(solution)/shard_map/all_gather | solution.py:74
  103.2 10.8 %all-gather.3 = bf16[1,6,768]{1,0,2:T(2,128)(2,1)S(1)} all-gather(bf16[1,6,96]{1,0,2:T(2,128)(2,1)S(1)} %copy.185), channel_id=5, replica_groups=mesh['dp'=8,'tensor'=4] {'dp'}, dimensions={2}, use_global_device_ids=true | all-gather | bytes 10368 | tf_op jit(solution)/shard_map/all_gather | solution.py:76
  114.4 13.0 %slice_reduce_fusion.1 = (f32[768]{0:T(1024)S(1)}, f32[768]{0:T(1024)S(1)}, f32[768]{0:T(1024)S(1)}, f32[768]{0:T(1024)S(1)}, f32[768]{0:T(1024)S(1)}, /*index=5*/f32[768]{0:T(1024)S(1)}) fusion(f32[1,6,768]{1,0,2:T(1,128)S(1)} %convert_element_type.169), kind=kLoop, calls=%fused_computation.78 | loop fusion | bytes 36864 | tf_op jit(solution)/shard_map/slice | solution.py:115
  127.4 81.6 %all-reduce.6.cloned.1.call-done = bf16[2048,768]{1,0:T(8,128)(2,1)} async-done(((bf16[2048,768]{1,0:T(8,128)(2,1)}), bf16[2048,768]{1,0:T(8,128)(2,1)}) %all-reduce.6.cloned.1.call-update) | async-done | bytes 3145744 | tf_op jit(solution)/shard_map/psum | solution.py:107
  215.8 7.4 multiply_convert_fusion.1
  223.3 6.2 convolution_convert_fusion.1
  229.7 120.0 %all-reduce.8.cloned.1.call-done = bf16[2048,768]{1,0:T(8,128)(2,1)} async-done(((bf16[2048,768]{1,0:T(8,128)(2,1)}), bf16[2048,768]{1,0:T(8,128)(2,1)}) %all-reduce.8.cloned.1.call-update) | async-done | bytes 3145744 | tf_op jit(solution)/shard_map/psum | solution.py:114
  376.4 8.0 %fusion.60 = f32[768,768]{0,1:T(8,128)} fusion(bf16[2048,768]{1,0:T(8,128)(2,1)} %copy-done.36, f32[2048,768]{1,0:T(8,128)} %copy-done.2, f32[2048]{0:T(1024)S(1)} %negate_multiply_fusion.1), kind=kOutput, calls=%fused_computation.147 | convolution fusion | flops 2419064832 | bytes 11804672 | tf_op jit(solution)/shard_map/dot_general | solution.py:37
  384.5 8.0 %fusion.61 = f32[768,768]{1,0:T(8,128)} fusion(bf16[2048,768]{1,0:T(8,128)(2,1)} %copy-done.35, f32[2048,768]{1,0:T(8,128)} %get-tuple-element.123, f32[768]{0:T(1024)} %copy-done.24, f32[768]{0:T(1024)} %copy-done.22, f32[2048]{0:T(1024)S(1)} %fusion.49), kind=kOutput, calls=%fused_computation.148 | convolution fusion | flops 2422210560 | bytes 11810816 | tf_op jit(solution)/shard_map/dot_general | solution.py:37
  392.8 102.9 %all-reduce.10.cloned.1.call-done = bf16[2048,768]{1,0:T(8,128)(2,1)} async-done(((bf16[2048,768]{1,0:T(8,128)(2,1)}), bf16[2048,768]{1,0:T(8,128)(2,1)}) %all-reduce.10.cloned.1.call-update) | async-done | bytes 3145744 | tf_op jit(solution)/shard_map/psum | solution.py:124
  495.7 8.0 %multiply_reduce_fusion.1 = (f32[768]{0:T(1024)}, f32[2048]{0:T(1024)S(1)}, f32[768]{0:T(1024)}, f32[768]{0:T(1024)}) fusion(f32[2048,768]{1,0:T(8,128)} %get-tuple-element.123, f32[2048]{0:T(1024)S(1)} %fusion.49, bf16[2048,768]{1,0:T(8,128)(2,1)} %all-reduce.10.cloned.1.call-done, f32[2048,768]{1,0:T(8,128)} %copy-done.2, ...), kind=kLoop, calls=%fused_computation.19 | loop fusion | flops 17297152 | bytes 15765504 | tf_op jit(solution)/shard_map/transpose(jvp())/reduce_sum | solution.py:21
  503.7 6.1 fusion.65
  517.6 8.3 %multiply_reduce_fusion = (f32[4,3,512]{2,1,0:T(4,128)S(1)}, f32[4,3,512,512]{2,3,1,0:T(8,128)S(1)}) fusion(f32[4,3,512,512]{2,3,1,0:T(8,128)} %copy-done, f32[4,3,512]{2,1,0:T(4,128)S(1)} %log_add_fusion, bf16[4,512,1,3,64]{1,0,4,3,2:T(4,128)(2,1)} %copy-done.11, bf16[4,512,3,64]{1,0,3,2:T(4,128)(2,1)} %reshape.218), kind=kOutput, calls=%fused_computation.1 | convolution fusion | flops 412084224 | bytes 26787840 | tf_op jit(solution)/shard_map/bqhd,bkhd->bhqk/dot_general | solution.py:135
  526.0 6.9 multiply_convert_fusion
  558.4 7.7 %fusion.17 = bf16[4,512,3,64]{1,3,2,0:T(8,128)(2,1)} fusion(f32[4,3,512,512]{2,3,1,0:T(8,128)} %copy-done, f32[4,3,512]{2,1,0:T(4,128)S(1)} %log_add_fusion, bf16[4,512,3,64]{1,0,3,2:T(4,128)(2,1)} %reshape.218), kind=kOutput, calls=%fused_computation.53 | convolution fusion | flops 409337856 | bytes 14180352 | tf_op jit(solution)/shard_map/bhqk,bqhd->bkhd/dot_general | solution.py:136
  585.8 6.2 bitcast_convert_fusion
  601.6 14.3 %all-reduce = f32[2,3,64]{2,1,0:T(4,128)S(1)} all-reduce(f32[2,3,64]{2,1,0:T(4,128)S(1)} %reshape.220), channel_id=10, replica_groups=mesh['dp'=8,'tensor'=4] {'dp'}, use_global_device_ids=true, to_apply=%region_17.18.clone | all-reduce | flops 384 | bytes 3072
  623.8 19.7 %reduce-scatter.20.cloned.1.call-done = f32[96,576]{1,0:T(8,128)} async-done(((f32[768,576]{1,0:T(8,128)}), f32[96,576]{1,0:T(8,128)}) %reduce-scatter.20.cloned.1.call-update) | async-done | bytes 221200
  644.8 67.8 %all-reduce.12.cloned.1.call-done = bf16[2048,768]{1,0:T(8,128)(2,1)} async-done(((bf16[2048,768]{1,0:T(8,128)(2,1)}), bf16[2048,768]{1,0:T(8,128)(2,1)}) %all-reduce.12.cloned.1.call-update) | async-done | bytes 3145744 | tf_op jit(solution)/shard_map/psum | solution.py:155
  721.0 31.0 %reduce-scatter.26.cloned.1.call-done = f32[96,6]{1,0:T(8,128)} async-done(((f32[768,6]{1,0:T(8,128)}), f32[96,6]{1,0:T(8,128)}) %reduce-scatter.26.cloned.1.call-update) | async-done | bytes 2320
  (220 shorter events, 156.9 us)
Async XLA Ops:
  8.0 49.9 %copy-start.6 = (bf16[4,512,768]{2,1,0:T(8,128)(2,1)S(1)}, bf16[4,512,768]{2,1,0:T(8,128)(2,1)}, u32[]{:S(2)}) copy-start(bf16[4,512,768]{2,1,0:T(8,128)(2,1)} %param.11) | copy-start | bytes 9437188
  8.0 200.9 %all-reduce.6.cloned.1.call-start = ((), (), s32[]{:S(2)}) async-start(), calls=%async_computation.6 | async-start | bytes 6291456 | tf_op jit(solution)/shard_map/psum | solution.py:107
  87.5 128.3 %all-gather.10.cloned.1.call-start = ((), (), s32[]{:S(2)}) async-start(), calls=%async_computation.12 | async-start | bytes 1327104 | tf_op jit(solution)/shard_map/all_gather | solution.py:73
  89.2 134.1 %all-gather.12.cloned.1.call-start = ((), (), s32[]{:S(2)}) async-start(), calls=%async_computation.13 | async-start | bytes 1327104 | tf_op jit(solution)/shard_map/all_gather | solution.py:75
  90.9 258.8 %all-reduce.8.cloned.1.call-start = ((), (), s32[]{:S(2)}) async-start(), calls=%async_computation.7 | async-start | bytes 6291456 | tf_op jit(solution)/shard_map/psum | solution.py:114
  127.3 222.4 %copy-start.22 = (f32[768]{0:T(1024)}, f32[768]{0:T(1024)S(1)}, u32[]{:S(2)}) copy-start(f32[768]{0:T(1024)S(1)} %get-tuple-element.111) | copy-start | bytes 9220
  127.3 222.4 %copy-start.24 = (f32[768]{0:T(1024)}, f32[768]{0:T(1024)S(1)}, u32[]{:S(2)}) copy-start(f32[768]{0:T(1024)S(1)} %get-tuple-element.110) | copy-start | bytes 9220
  229.5 266.2 %all-reduce.10.cloned.1.call-start = ((), (), s32[]{:S(2)}) async-start(), calls=%async_computation.8 | async-start | bytes 6291456 | tf_op jit(solution)/shard_map/psum | solution.py:124
  375.5 222.1 %reduce-scatter.24.cloned.1.call-start = ((), (), s32[]{:S(2)}) async-start(), calls=%async_computation.16 | async-start | bytes 73728
  376.4 241.5 %reduce-scatter.18.cloned.1.call-start = ((), (), s32[]{:S(2)}) async-start(), calls=%async_computation.11 | async-start | bytes 2654208 | tf_op jit(solution)/shard_map/reduce_scatter | solution.py:164
  384.4 235.6 %reduce-scatter.16.cloned.1.call-start = ((), (), s32[]{:S(2)}) async-start(), calls=%async_computation.10 | async-start | bytes 2654208 | tf_op jit(solution)/shard_map/reduce_scatter | solution.py:162
  384.5 111.2 %copy-start.23 = (f32[768]{0:T(1024)S(1)}, f32[768]{0:T(1024)}, u32[]{:S(2)}) copy-start(f32[768]{0:T(1024)} %copy-done.22) | copy-start | bytes 9220
  392.5 111.2 %copy-start.21 = (f32[2048]{0:T(1024)S(1)}, f32[2048]{0:T(1024)}, u32[]{:S(2)}) copy-start(f32[2048]{0:T(1024)} %copy-done.20) | copy-start | bytes 24580
  392.6 229.5 %reduce-scatter.22.cloned.1.call-start = ((), (), s32[]{:S(2)}) async-start(), calls=%async_computation.15 | async-start | bytes 884736
  566.2 77.4 %reduce-scatter.20.cloned.1.call-start = ((), (), s32[]{:S(2)}) async-start(), calls=%async_computation.14 | async-start | bytes 2211840
  584.5 128.0 %all-reduce.12.cloned.1.call-start = ((), (), s32[]{:S(2)}) async-start(), calls=%async_computation.9 | async-start | bytes 6291456 | tf_op jit(solution)/shard_map/psum | solution.py:155
  585.8 15.2 %copy-start.26 = (f32[768]{0:T(1024)S(1)}, f32[768]{0:T(1024)}, u32[]{:S(2)}) copy-start(f32[768]{0:T(1024)} %get-tuple-element.107) | copy-start | bytes 9220
  592.1 31.0 %copy-start.15 = (f32[3,192,96]{2,1,0:T(8,128)S(1)}, f32[3,192,96]{2,1,0:T(8,128)}, u32[]{:S(2)}) copy-start(f32[3,192,96]{2,1,0:T(8,128)} %param.17) | copy-start | bytes 663556
  592.1 159.8 %reduce-scatter.26.cloned.1.call-start = ((), (), s32[]{:S(2)}) async-start(), calls=%async_computation.17 | async-start | bytes 442368
  598.4 119.6 %copy-start.28 = (f32[6,16]{1,0:T(8,128)}, f32[6,16]{1,0:T(8,128)S(1)}, u32[]{:S(2)}) copy-start(f32[6,16]{1,0:T(8,128)S(1)} %copy.176) | copy-start | bytes 1156
  616.6 101.3 %copy-start.30 = (f32[2,3,8]{2,0,1:T(2,128)}, f32[2,3,8]{2,0,1:T(2,128)S(1)}, u32[]{:S(2)}) copy-start(f32[2,3,8]{2,0,1:T(2,128)S(1)} %get-tuple-element.115) | copy-start | bytes 580
  623.1 94.8 %copy-start.14 = (f32[192,96]{1,0:T(8,128)}, f32[192,96]{1,0:T(8,128)S(1)}, u32[]{:S(2)}) copy-start(f32[192,96]{1,0:T(8,128)S(1)} %copy.174) | copy-start | bytes 221188
  644.7 73.2 %copy-start.31 = (f32[1,768]{1,0:T(1,128)S(1)}, f32[1,768]{1,0:T(1,128)}, u32[]{:S(2)}) copy-start(f32[1,768]{1,0:T(1,128)} %reshape.225) | copy-start | bytes 9220
  644.7 108.1 %copy-start.32 = (f32[3,6,96]{2,1,0:T(8,128)S(1)}, f32[3,6,96]{2,1,0:T(8,128)}, u32[]{:S(2)}) copy-start(f32[3,6,96]{2,1,0:T(8,128)} %param.21) | copy-start | bytes 20740
  (27 other events, 149.5 us)
Sparse Core Ops, SparseCore 0:
  87.6 121.2 all-reduce.5
  229.6 120.0 all-reduce.7
  375.6 120.0 all-reduce.9
  592.2 120.2 all-reduce.11
Sparse Core Ops, SparseCore 1:
  90.4 25.2 all-gather.9
  118.0 23.8 all-gather.11
  379.6 32.5 reduce-scatter.23
  416.1 42.2 reduce-scatter.17
  462.2 42.2 reduce-scatter.15
  566.2 33.9 reduce-scatter.21
  603.5 40.0 reduce-scatter.19
  719.0 32.9 reduce-scatter.25
where the time goes:
time: 772 us; the launch traced here: 761 us
  waiting for transfers between devices  423 us (55%)
  matrix products  94.3 us (12%)
  local copies, waits for them, and re-layouts  90.2 us (12%)
  blocking collectives  71.4 us (9%)
  other arithmetic  63 us (8%)
  between operations  17.6 us (2%)
    psum x1, waiting for transfers between devices, body(): ffn = lax.psum(ffn_part.astype(jnp.bfloat16), 'tensor').astype(jnp.float32)  120 us
    psum x1, waiting for transfers between devices, body(): lax.psum(feed_part.astype(jnp.bfloat16), 'tensor').astype(jnp.float32)  103 us
    psum x1, waiting for transfers between devices, body(): lax.psum(attn_part.astype(jnp.bfloat16), 'tensor').astype(jnp.float32)  81.6 us
    psum x1, waiting for transfers between devices, body(): lax.psum(input_part.astype(jnp.bfloat16), 'tensor').astype(jnp.float32)  67.8 us
    unnamed x16, waiting for transfers between devices  50.9 us
    unnamed x98, local copies, waits for them, and re-layouts  29.5 us
    reduce_sum x4, other arithmetic, layer_norm(): center = value - jnp.mean(value, axis=-1, keepdims=True)  18.3 us
    dot_general x2, matrix products, contract_rows(): lax.dot_general(left, right, (((0,), (0,)), ((), ())), preferred_element_...  16 us
  transfers between devices with their start and end apart: 12, of which 6 were waited for; matrix products, arithmetic and copies ran while one was open for 21% of the time, Pallas kernels for 0%

commit v1 on v0

v1 whole, which is shorter than its diff:
```python
import functools
import math

import jax
import jax.numpy as jnp
from jax import lax
from jax.experimental import pallas as pl
from jax.experimental.pallas import tpu as pltpu
from jax.sharding import PartitionSpec as P

HD = 64
LANES = 128
VMEM_LIMIT = 60 * 1024 * 1024

norm_eps = 1e-05
beta_first = 0.9
beta_second = 0.999
warm_steps = 10000.0
total_steps = 200000.0

bf = jnp.bfloat16
fl = jnp.float32

SLABS = 8
DEPTH = 96


def nt(left, right):
    return lax.dot_general(left, right, (((1,), (1,)), ((), ())), preferred_element_type=fl)


def nn(left, right):
    return lax.dot_general(left, right, (((1,), (0,)), ((), ())), preferred_element_type=fl)


def tn(left, right):
    return lax.dot_general(left, right, (((0,), (0,)), ((), ())), preferred_element_type=fl)


def low_lanes(shape):
    return lax.broadcasted_iota(jnp.int32, shape, 1) < HD


def assemble(where_ref, pieces, plan, weight_ref):
    for ref, (r, shifts) in zip(pieces, plan):
        slab = jnp.bitwise_xor(where_ref[0], r)
        for k, s in enumerate(shifts):
            group = jnp.bitwise_and(where_ref[1] + 4 - s, 3)
            weight_ref[group, slab] = ref[k]


def scatter_slabs(where_ref, group, value, out_ref):
    shift = jnp.bitwise_and(group + 4 - where_ref[1], 3)
    for j in range(SLABS):
        out_ref[jnp.bitwise_xor(where_ref[0], j), shift] = value[DEPTH * j : DEPTH * (j + 1)]


def matrix(ref, group):
    return ref[group].reshape(SLABS * DEPTH, ref.shape[-1])


def attn_fwd_kernel(plan, where_ref, x_ref, seg_row_ref, seg_col_ref, bias_ref, *refs):
    pieces, (proj_ref, ctx_ref, lse_ref, weight_ref) = refs[: len(plan)], refs[len(plan) :]
    assemble(where_ref, pieces, plan, weight_ref)
    scale = HD ** (-0.5)
    length = x_ref.shape[0]

    def group_step(g, carry):
        x = x_ref[...]
        proj = (nn(x, matrix(weight_ref, g)) + bias_ref[g]).astype(bf)
        proj_ref[g] = proj
        same = seg_col_ref[...] == seg_row_ref[...]
        low = low_lanes((length, LANES))
        none = jnp.zeros((length, LANES), bf)
        parts = [proj[:, LANES * k : LANES * (k + 1)] for k in range(6)]
        outs = []
        for head in range(3):
            query = parts[0] if head < 2 else parts[3]
            keys = parts[1] if head < 2 else parts[5]
            value = parts[2] if head < 2 else parts[3]
            query = jnp.where(low, none, query) if head == 1 else jnp.where(low, query, none)
            scores = jnp.where(same, nt(keys, query) * scale, -1e30)
            top = jnp.max(scores, axis=0, keepdims=True)
            expd = jnp.exp(scores - top)
            denom = jnp.sum(expd, axis=0, keepdims=True)
            lse_ref[g, head] = top + jnp.log(denom)
            probs = (expd / denom).astype(bf)
            outs.append(tn(probs, value).astype(bf))
        ctx_ref[g] = jnp.concatenate(
            [jnp.where(low, outs[0], outs[1]), jnp.where(low, none, outs[2])], axis=1
        )
        return carry

    lax.fori_loop(0, 4, group_step, 0)


def up_kernel(plan, where_ref, x_ref, ctx_ref, attn_weight_ref, vec_ref, b_up_ref, *refs):
    pieces, (xhat_ref, rstd_ref, first_ref, act_ref, slope_ref, weight_ref) = refs[: len(plan)], refs[len(plan) :]
    assemble(where_ref, pieces, plan, weight_ref)
    total = x_ref[...].astype(fl) + vec_ref[4:5]
    attn = None
    for g in range(4):
        w = attn_weight_ref[g][:, :, 512:768].reshape(SLABS * DEPTH, 256)
        part = nt(ctx_ref[g], w)
        attn = part if attn is None else attn + part
    total = total + attn
    center = total - jnp.mean(total, axis=-1, keepdims=True)
    rstd = lax.rsqrt(jnp.mean(center * center, axis=-1, keepdims=True) + norm_eps)
    xhat = center * rstd
    first = xhat * vec_ref[0:1] + vec_ref[1:2]
    xhat_ref[...] = xhat
    rstd_ref[...] = jnp.broadcast_to(rstd, rstd_ref.shape)
    first_ref[...] = first.astype(bf)

    def step(g, carry):
        up = nn(first_ref[...], matrix(weight_ref, g)) + b_up_ref[g]
        half = 0.5 * (1.0 + lax.erf(up * 0.7071067811865476))
        act_ref[g] = (up * half).astype(bf)
        slope_ref[g] = half + up * (jnp.exp(-0.5 * up * up) * 0.3989422804014327)
        return carry

    lax.fori_loop(0, 4, step, 0)


def down_kernel(plan, where_ref, xhat_ref, act_ref, slope_ref, dy_ref, vec_ref, *refs):
    pieces = refs[: len(plan)]
    out_ref, dr2_ref, dup_ref, grad_ref, small_ref, b_up_ref, weight_ref = refs[len(plan) :]
    assemble(where_ref, pieces, plan, weight_ref)
    ffn = None
    for g in range(4):
        part = nt(act_ref[g], matrix(weight_ref, g))
        ffn = part if ffn is None else ffn + part
    first = xhat_ref[...] * vec_ref[0:1] + vec_ref[1:2]
    total = first + ffn + vec_ref[5:6]
    center = total - jnp.mean(total, axis=-1, keepdims=True)
    rstd = lax.rsqrt(jnp.mean(center * center, axis=-1, keepdims=True) + norm_eps)
    xhat = center * rstd
    out_ref[...] = (xhat * vec_ref[2:3] + vec_ref[3:4]).astype(bf)
    dy = dy_ref[...].astype(fl)
    small_ref[0:1] = jnp.sum(dy * xhat, axis=0, keepdims=True)
    small_ref[1:2] = jnp.sum(dy, axis=0, keepdims=True)
    dxhat = dy * vec_ref[2:3]
    dr2 = rstd * (
        dxhat
        - jnp.mean(dxhat, axis=-1, keepdims=True)
        - xhat * jnp.mean(dxhat * xhat, axis=-1, keepdims=True)
    )
    dr2_ref[...] = dr2
    small_ref[2:3] = jnp.sum(dr2, axis=0, keepdims=True)

    def step(g, carry):
        dffn = dr2_ref[...].astype(bf)
        scatter_slabs(where_ref, g, tn(dffn, act_ref[g]).astype(bf), grad_ref)
        dup = (nn(dffn, matrix(weight_ref, g)) * slope_ref[g]).astype(bf)
        dup_ref[g] = dup
        b_up_ref[g] = jnp.sum(dup.astype(fl), axis=0, keepdims=True)
        return carry

    lax.fori_loop(0, 4, step, 0)


def up_bwd_kernel(where_ref, dr2_ref, dup_ref, xhat_ref, rstd_ref, first_ref, vec_ref, weight_ref, attn_weight_ref,
                  dr1_ref, dctx_ref, grad_ref, small_ref):
    feed = None
    for g in range(4):
        part = nt(dup_ref[g], matrix(weight_ref, g))
        feed = part if feed is None else feed + part
    dfirst = dr2_ref[...] + feed.astype(bf).astype(fl)
    xhat = xhat_ref[...]
    small_ref[0:1] = jnp.sum(dfirst * xhat, axis=0, keepdims=True)
    small_ref[1:2] = jnp.sum(dfirst, axis=0, keepdims=True)
    dxhat = dfirst * vec_ref[0:1]
    dr1 = rstd_ref[:, 0:1] * (
        dxhat
        - jnp.mean(dxhat, axis=-1, keepdims=True)
        - xhat * jnp.mean(dxhat * xhat, axis=-1, keepdims=True)
    )
    dr1_ref[...] = dr1
    small_ref[2:3] = jnp.sum(dr1, axis=0, keepdims=True)
    dattn = dr1.astype(bf)
    for g in range(4):
        w = attn_weight_ref[g][:, :, 512:768].reshape(SLABS * DEPTH, 256)
        dctx_ref[g] = nn(dattn, w).astype(bf)

    def step(g, carry):
        scatter_slabs(where_ref, g, tn(first_ref[...], dup_ref[g]).astype(bf), grad_ref)
        return carry

    lax.fori_loop(0, 4, step, 0)


def attn_bwd_kernel(where_ref, x_ref, seg_row_ref, seg_col_ref, proj_ref, ctx_ref, lse_ref, dr1_ref, dctx_ref, weight_ref,
                    grad_in_ref, grad_ref, bias_ref, dproj_ref, back_ref):
    scale = HD ** (-0.5)
    length = x_ref.shape[0]
    back_ref[...] = jnp.zeros_like(back_ref)

    def step(g, carry):
        same = seg_col_ref[...] == seg_row_ref[...]
        low = low_lanes((length, LANES))
        none = jnp.zeros((length, LANES), bf)
        parts = [proj_ref[g, :, LANES * k : LANES * (k + 1)] for k in range(6)]
        dctx = [dctx_ref[g, :, :LANES], dctx_ref[g, :, LANES:]]
        dq, dk, dv = [], [], []
        for head in range(3):
            query = parts[0] if head < 2 else parts[3]
            keys = parts[1] if head < 2 else parts[5]
            value = parts[2] if head < 2 else parts[3]
            dout = dctx[0] if head < 2 else dctx[1]
            query_in = jnp.where(low, none, query) if head == 1 else jnp.where(low, query, none)
            dout_in = jnp.where(low, dout, none) if head == 0 else jnp.where(low, none, dout)
            scores = jnp.where(same, nt(keys, query_in) * scale, -1e30)
            probs = jnp.exp(scores - lse_ref[g, head])
            dprobs = nt(value, dout_in)
            dv.append(nn(probs.astype(bf), dout))
            row_dot = jnp.sum(probs * dprobs, axis=0, keepdims=True)
            dscores = (probs * (dprobs - row_dot)).astype(bf)
            dq.append(tn(dscores, keys) * scale)
            dk.append(nn(dscores, query) * scale)
        dproj = jnp.concatenate(
            [
                jnp.where(low, dq[0], dq[1]).astype(bf),
                jnp.where(low, dk[0], dk[1]).astype(bf),
                jnp.where(low, dv[0], dv[1]).astype(bf),
                jnp.where(low, dq[2], dv[2]).astype(bf),
                none,
                jnp.where(low, dk[2].astype(bf), none),
            ],
            axis=1,
        )
        dproj_ref[g] = dproj
        bias_ref[g] = jnp.sum(dproj.astype(fl), axis=0, keepdims=True)
        back_ref[...] += nt(dproj, matrix(weight_ref, g))
        return carry

    lax.fori_loop(0, 4, step, 0)
    dr1 = dr1_ref[...]
    grad_in_ref[...] = (dr1 + back_ref[...].astype(bf).astype(fl)).astype(bf)

    def grads(g, carry):
        x = x_ref[...]
        main = tn(x, dproj_ref[g])
        side = tn(dr1_ref[...].astype(bf), ctx_ref[g])
        whole = jnp.concatenate([main[:, :512], main[:, 512:] + side], axis=1).astype(bf)
        scatter_slabs(where_ref, g, whole, grad_ref)
        return carry

    lax.fori_loop(0, 4, grads, 0)


def place_kernel(where_ref, *refs):
    out_ref = refs[-1]
    for s, ref in enumerate(refs[:-1]):
        out_ref[jnp.bitwise_and(where_ref[1] + 4 - s, 3)] = ref[...]


smem = pl.BlockSpec(memory_space=pltpu.SMEM)
vmem = pl.BlockSpec(memory_space=pltpu.VMEM)


def call(kernel, name, outs, where, *args, scratch=(), flops=0):
    size = sum(math.prod(a.shape) * a.dtype.itemsize for a in args)
    size += sum(math.prod(s) * jnp.dtype(d).itemsize for s, d in outs)
    return pl.pallas_call(
        kernel,
        name=name,
        out_shape=[jax.ShapeDtypeStruct(s, d) for s, d in outs],
        in_specs=[smem] + [vmem] * len(args),
        out_specs=[vmem] * len(outs),
        scratch_shapes=list(scratch),
        compiler_params=pltpu.CompilerParams(vmem_limit_bytes=VMEM_LIMIT),
        cost_estimate=pl.CostEstimate(flops=flops, bytes_accessed=size, transcendentals=0),
    )(where, *args)


def flip(value, bit):
    n = lax.axis_size("dp")
    return lax.ppermute(value, "dp", [(k, k ^ bit) for k in range(n)])


def shift(value, s):
    return lax.ppermute(value, "tensor", [(k, (k + s) % 4) for k in range(4)])


def gather_slabs(shard):
    own = jnp.stack([shard] + [shift(shard, s) for s in (1, 2, 3)])
    over_x = flip(own, 2)
    over_y = flip(own, 4)
    far_a = flip(over_x[:2], 4)
    far_b = flip(over_y[2:], 2)
    near = [(own, (0, (0, 1, 2, 3))), (over_x, (2, (0, 1, 2, 3))), (over_y, (4, (0, 1, 2, 3)))]
    near += [(far_a, (6, (0, 1))), (far_b, (6, (2, 3)))]
    return near + [(flip(a, 1), (r + 1, s)) for a, (r, s) in near]


def reduce_slabs(grad):
    pairs = grad.reshape(4, 2, 4, DEPTH, 768)
    half = (pairs[:, 0].astype(fl) + flip(pairs[:, 1], 1).astype(fl)).astype(bf)
    far_a = flip(half[3, :2], 2)
    far_b = flip(half[3, 2:], 4)
    to_y = jnp.concatenate([half[2, :2].astype(fl) + far_a.astype(fl), half[2, 2:].astype(fl)]).astype(bf)
    to_x = jnp.concatenate([half[1, :2].astype(fl), half[1, 2:].astype(fl) + far_b.astype(fl)]).astype(bf)
    plane = (half[0].astype(fl) + flip(to_x, 2).astype(fl) + flip(to_y, 4).astype(fl)).astype(bf)
    total = plane[0].astype(fl)
    for s in (1, 2, 3):
        total = total + shift(plane[s], s).astype(fl)
    return total


def gather_plain(shard):
    whole = lax.all_gather(lax.all_gather(shard, "dp", axis=0, tiled=True), "tensor", axis=0)
    whole = whole.reshape(4, SLABS, DEPTH, 768)
    order = [(4 - s) % 4 for s in range(4)]
    return [(jnp.stack([whole[t, r] for t in order]), (r, (0, 1, 2, 3))) for r in range(SLABS)]


def reduce_plain(grad):
    whole = grad.transpose(1, 0, 2, 3).reshape(4, SLABS * DEPTH, 768)
    part = lax.psum_scatter(whole.astype(fl), "tensor", scatter_dimension=0, tiled=True)
    return lax.psum_scatter(part[0], "dp", scatter_dimension=0, tiled=True)


def gather_row(row, where):
    rows = [row] + [shift(row, s) for s in (1, 2, 3)]
    return call(place_kernel, "place_rows", [((4,) + row.shape, row.dtype)], where, *rows)[0]


def moment_update(state, grad):
    moment_one = beta_first * state[1] + (1.0 - beta_first) * grad
    moment_two = beta_second * state[2] + (1.0 - beta_second) * grad * grad
    return jnp.stack([moment_one, moment_two])


def body(
    hidden_in,
    out_grad,
    segment_ids,
    step_count,
    qkv_state,
    qv_bias_state,
    out_state,
    up_state,
    up_bias_state,
    down_state,
    vector_state,
):
    n_dp = lax.axis_size("dp")
    place = lax.axis_index("tensor")
    fast = n_dp == SLABS
    spot = lax.axis_index("dp") if fast else 0
    where = jnp.stack([jnp.int32(spot), (place if fast else 0) * jnp.int32(1)])
    spin = jnp.stack([jnp.int32(0), place * jnp.int32(1)])
    gather = gather_slabs if fast else gather_plain
    reduce = reduce_slabs if fast else reduce_plain
    rows, width = qkv_state.shape[1], hidden_in.shape[2]

    q, k, v = (qkv_state[0, :, c].astype(bf) for c in range(3))
    o = out_state[0].T.astype(bf)
    cut = 2 * HD
    attn_shard = jnp.concatenate(
        [q[:, :cut], k[:, :cut], v[:, :cut], q[:, cut:], v[:, cut:], o[:, :cut], k[:, cut:], o[:, cut:]], axis=1
    )
    up_shard = up_state[0].astype(bf)
    down_shard = down_state[0].T.astype(bf)
    attn_pieces = gather(attn_shard)
    up_pieces = gather(up_shard)
    down_pieces = gather(down_shard)

    sizes = (qv_bias_state[0].size, up_bias_state[0].size, vector_state[0].size)
    small = jnp.concatenate([s[0].reshape(-1).astype(bf) for s in (qv_bias_state, up_bias_state, vector_state)])
    small = lax.all_gather(small, ("dp", "tensor")).reshape(n_dp, 4, -1).astype(fl)
    a, b = sizes[0], sizes[0] + sizes[1]
    qv = small[:, :, :a].reshape(n_dp, 4, 2, 3, -1).transpose(1, 2, 3, 0, 4).reshape(4, 2, 3 * HD)
    b_up = small[:, :, a:b].reshape(n_dp, 4, 6, -1).transpose(1, 2, 0, 3).reshape(4, 1, 768)
    vec = small[:, 0, b:].reshape(n_dp, 6, -1).transpose(1, 0, 2).reshape(6, width)
    gap = jnp.zeros((4, cut), fl)
    bias = jnp.concatenate(
        [qv[:, 0, :cut], gap, qv[:, 1, :cut], qv[:, 0, cut:], qv[:, 1, cut:], gap, gap], axis=1
    ).reshape(4, 1, 768)

    x = lax.dynamic_index_in_dim(hidden_in, place, 0, keepdims=False)
    dy = lax.dynamic_index_in_dim(out_grad, place, 0, keepdims=False)
    seg = lax.dynamic_index_in_dim(segment_ids, place, 0, keepdims=True)
    seg_col = seg.reshape(-1, 1)
    length = x.shape[0]
    wide = (4, length, 768)
    whole = ((4, SLABS, DEPTH, 768), bf)
    grad_shape = ((SLABS, 4, DEPTH, 768), bf)

    def split(pieces):
        return [p for p, _ in pieces], tuple(w for _, w in pieces)

    pieces, plan = split(attn_pieces)
    proj, ctx, lse, attn_w = call(
        functools.partial(attn_fwd_kernel, plan), "attn_fwd",
        [(wide, bf), ((4, length, 256), bf), ((4, 3, 1, length), fl), whole],
        where, x, seg, seg_col, bias, *pieces, flops=6 * 10**9,
    )
    pieces, plan = split(up_pieces)
    xhat, rstd, first, act, slope, up_w = call(
        functools.partial(up_kernel, plan), "up_fwd",
        [((length, width), fl), ((length, LANES), fl), ((length, width), bf), (wide, bf), (wide, fl), whole],
        where, x, ctx, attn_w, vec, b_up, *pieces, flops=4 * 10**9,
    )
    pieces, plan = split(down_pieces)
    out, dr2, dup, down_grad, small_two, b_up_grad = call(
        functools.partial(down_kernel, plan), "down_fwd_bwd",
        [((length, width), bf), ((length, width), fl), (wide, bf), grad_shape, ((3, width), fl), ((4, 1, 768), fl)],
        where, xhat, act, slope, dy, vec, *pieces, flops=8 * 10**9,
        scratch=[pltpu.VMEM(*whole)],
    )
    hidden_out = gather_row(out, spin)
    down_sum = reduce(down_grad)
    dr1, dctx, up_grad, small_one = call(
        up_bwd_kernel, "up_bwd",
        [((length, width), fl), ((4, length, 256), bf), grad_shape, ((3, width), fl)],
        where, dr2, dup, xhat, rstd, first, vec, up_w, attn_w, flops=6 * 10**9,
    )
    up_sum = reduce(up_grad)
    grad_row, attn_grad, bias_grad = call(
        attn_bwd_kernel, "attn_bwd",
        [((length, width), bf), grad_shape, ((4, 1, 768), fl)],
        where, x, seg, seg_col, proj, ctx, lse, dr1, dctx, attn_w, flops=10 * 10**9,
        scratch=[pltpu.VMEM(wide, bf), pltpu.VMEM((length, width), fl)],
    )
    grad_in = gather_row(grad_row, spin)
    attn_sum = reduce(attn_grad)

    bias_grad = bias_grad.reshape(4, 768)
    gq = jnp.concatenate([bias_grad[:, :cut], bias_grad[:, 384 : 384 + HD]], axis=1)
    gv = jnp.concatenate([bias_grad[:, 256 : 256 + cut], bias_grad[:, 384 + HD : 512]], axis=1)
    gqv = jnp.stack([gq, gv], axis=1).reshape(4, 2, 3, n_dp, -1).transpose(3, 0, 1, 2, 4).reshape(n_dp, 4, -1)
    gup = b_up_grad.reshape(4, 6, n_dp, -1).transpose(2, 0, 1, 3).reshape(n_dp, 4, -1)
    gvec = jnp.concatenate([small_one[:2], small_two[:2], small_one[2:], small_two[2:]])
    gvec = gvec.reshape(6, n_dp, -1).transpose(1, 0, 2).reshape(n_dp, 1, -1)
    gvec = jnp.broadcast_to(gvec, (n_dp, 4, gvec.shape[-1]))
    shares = jnp.concatenate([gqv, gup, gvec], axis=2).reshape(n_dp * 4, -1)
    shares = lax.all_to_all(shares, ("dp", "tensor"), 0, 0, tiled=True)
    sums = jnp.sum(shares, axis=0)

    gk = [attn_sum[:, 128 * n : 128 * (n + 1)] for n in range(6)]
    grad_qkv = jnp.stack(
        [
            jnp.concatenate([gk[0], gk[3][:, :HD]], axis=1),
            jnp.concatenate([gk[1], gk[5][:, :HD]], axis=1),
            jnp.concatenate([gk[2], gk[3][:, HD:]], axis=1),
        ],
        axis=1,
    )
    grad_out = jnp.concatenate([gk[4], gk[5][:, HD:]], axis=1).T
    summed = (
        grad_qkv,
        sums[:a].reshape(qv_bias_state.shape[1:]),
        grad_out,
        up_sum,
        sums[a:b].reshape(up_bias_state.shape[1:]),
        down_sum.T,
        sums[b:].reshape(vector_state.shape[1:]),
    )
    steps_f = step_count[0].astype(fl)
    factor = jnp.minimum(steps_f / warm_steps, (total_steps - steps_f) / (total_steps - warm_steps))
    fix_first = 1.0 - jnp.exp(steps_f * math.log(beta_first))
    fix_second = 1.0 - jnp.exp(steps_f * math.log(beta_second))
    states = (qkv_state, qv_bias_state, out_state, up_state, up_bias_state, down_state, vector_state)
    news = tuple((moment_update(s, g) for s, g in zip(states, summed)))
    plan_out = jnp.stack([factor, fix_first, fix_second])
    return (hidden_out, grad_in, *summed, *news, plan_out)


def solution(mesh):
    return jax.shard_map(
        body,
        mesh=mesh,
        in_specs=(
            P("dp", None, None),
            P("dp", None, None),
            P("dp", None),
            P(),
            P(None, "dp", None, "tensor"),
            P(None, None, "tensor", "dp"),
            P(None, "tensor", "dp"),
            P(None, "dp", "tensor"),
            P(None, "tensor", "dp"),
            P(None, "tensor", "dp"),
            P(None, None, "dp"),
        ),
        out_specs=(
            P("dp", None, None),
            P("dp", None, None),
            P("dp", None, "tensor"),
            P(None, "tensor", "dp"),
            P("tensor", "dp"),
            P("dp", "tensor"),
            P("tensor", "dp"),
            P("tensor", "dp"),
            P(None, "dp"),
            P(None, "dp", None, "tensor"),
            P(None, None, "tensor", "dp"),
            P(None, "tensor", "dp"),
            P(None, "dp", "tensor"),
            P(None, "tensor", "dp"),
            P(None, "tensor", "dp"),
            P(None, None, "dp"),
            P(),
        ),
        check_vma=False,
    )
```

time: 772 us -> 494 us (0.64); the launches traced: 761 us -> 493 us
  waiting for transfers between devices: 423 us -> 171 us
  starting transfers between devices: 1.07 us -> 106 us
  Pallas kernels: 0 us -> 101 us
  matrix products: 94.3 us -> 0 us
  local copies, waits for them, and re-layouts: 90.2 us -> 39.5 us
  other arithmetic: 63 us -> 25.8 us
  blocking collectives: 71.4 us -> 47.8 us
  between operations: 17.6 us -> 2.34 us
    psum x4 -> x0, waiting for transfers between devices: 372 us -> none  [the longest x1 120 us: body(): ffn = lax.psum(ffn_part.astype(jnp.bfloat16), 'tensor').astype(jnp.float32)]
    ppermute x0 -> x66, waiting for transfers between devices: none -> 137 us  [the longest x24 108 us: shift(): return lax.ppermute(value, 'tensor', [(k, (k + s) % 4) for k in range(4)])]
    pallas_call x0 -> x7, Pallas kernels: none -> 101 us  [call(): pl.pallas_call(kernel, name=name, out_shape=[jax.ShapeDtypeStruct(s, d) f...]
    ppermute x0 -> x66, starting transfers between devices: none -> 101 us  [the longest x24 69.4 us: shift(): return lax.ppermute(value, 'tensor', [(k, (k + s) % 4) for k in range(4)])]
    dot_general x16 -> x0, matrix products: 85.5 us -> none  [the longest x2 16 us: contract_rows(): lax.dot_general(left, right, (((0,), (0,)), ((), ())), preferred_element_...]
    all_gather x5 -> x0, blocking collectives: 57.1 us -> none  [the longest x1 15.8 us: body(): lax.all_gather(qkv_state[0].astype(bf), 'dp', axis=0, tiled=True)]
    unnamed x16 -> x0, waiting for transfers between devices: 50.9 us -> none
    reduce_sum x12 -> x1, other arithmetic: 42.5 us -> 0.08 us  [body(): sums = jnp.sum(shares, axis=0)]
  transfers between devices with their start and end apart: 12 -> 67, of which waited for: 6 -> 20; matrix products, arithmetic and copies ran while one was open for 21% -> 9% of each run, Pallas kernels for 0% -> 8%
where the time goes in v1:
time: 494 us; the launch traced here: 493 us
  waiting for transfers between devices  171 us (35%)
  starting transfers between devices  106 us (21%)
  Pallas kernels  101 us (20%)
  blocking collectives  47.8 us (10%)
  local copies, waits for them, and re-layouts  39.5 us (8%)
  other arithmetic  25.8 us (5%)
    ppermute x24, waiting for transfers between devices, shift(): return lax.ppermute(value, 'tensor', [(k, (k + s) % 4) for k in range(4)])  108 us
    pallas_call x7, Pallas kernels, call(): pl.pallas_call(kernel, name=name, out_shape=[jax.ShapeDtypeStruct(s, d) f...  101 us
    ppermute x24, starting transfers between devices, shift(): return lax.ppermute(value, 'tensor', [(k, (k + s) % 4) for k in range(4)])  69.4 us
    unnamed x1, blocking collectives  47.8 us
    all_to_all x1, waiting for transfers between devices, body(): shares = lax.all_to_all(shares, ('dp', 'tensor'), 0, 0, tiled=True)  34.4 us
    ppermute x42, starting transfers between devices, flip(): return lax.ppermute(value, 'dp', [(k, k ^ bit) for k in range(n)])  31.1 us
    ppermute x42, waiting for transfers between devices, flip(): return lax.ppermute(value, 'dp', [(k, k ^ bit) for k in range(n)])  28.4 us
    squeeze x3, local copies, waits for them, and re-layouts, reduce_slabs(): half = (pairs[:, 0].astype(fl) + flip(pairs[:, 1], 1).astype(fl)).astype(bf)  9.92 us
  transfers between devices with their start and end apart: 67, of which 20 were waited for; matrix products, arithmetic and copies ran while one was open for 9% of the time, Pallas kernels for 8%

profile of v1, /device:TPU:0, one launch (start us, length us, event | category | flops | bytes accessed | tf_op | source)
XLA Modules:
  0.0 493.1 jit_solution(6112605176244705071)
XLA Ops:
  25.7 5.7 %collective-permute-done.13 = bf16[96,768]{1,0:T(8,128)(2,1)S(1)} collective-permute-done((bf16[96,768]{1,0:T(8,128)(2,1)S(1)}, bf16[96,768]{1,0:T(8,128)(2,1)S(1)}, u32[]{:S(2)}, u32[]{:S(2)}) %collective-permute-start.13) | collective-permute-done | bytes 147488 | tf_op jit(solution)/shard_map/ppermute | solution.py:282
  40.7 4.3 collective-permute-done.24
  60.7 47.8 %all-reduce = bf16[23040]{0:T(1024)(128)(2,1)S(1)} all-reduce(bf16[23040]{0:T(1024)(128)(2,1)S(1)} %dynamic-update-slice), channel_id=2, replica_groups=mesh['dp'=8,'tensor'=4] {'dp','tensor'}, use_global_device_ids=true, to_apply=%add | all-reduce | flops 23040 | bytes 92160
  128.1 4.7 collective-permute-done.18.refs_4_
  143.5 14.9 %attn_fwd.1 = (bf16[4,512,768]{2,1,0:T(8,128)(2,1)}, bf16[4,512,256]{2,1,0:T(8,128)(2,1)}, f32[4,3,1,512]{3,2,1,0:T(1,128)}, bf16[4,8,96,768]{3,2,1,0:T(8,128)(2,1)}) custom-call(s32[2]{0:T(128)} %pad_add_fusion.1.where_ref, bf16[512,768]{1,0:T(8,128)(2,1)} %dynamic-slice_bitcast_fusion.1.x_ref, s32[1,512]{1,0:T(1,128)} %constant_dynamic-slice_fusion.seg_row_ref, ...), custom_call_target="tpu_custom_call" | custom-call | flops 6000000000 | bytes 14458880 | tf_op jit(solution)/shard_map/attn_fwd/pallas_call | solution.py:264
  159.0 15.8 %up_fwd.1 = (f32[512,768]{1,0:T(8,128)}, f32[512,128]{1,0:T(8,128)}, bf16[512,768]{1,0:T(8,128)(2,1)}, bf16[4,512,768]{2,1,0:T(8,128)(2,1)}, f32[4,512,768]{2,1,0:T(8,128)}, /*index=5*/bf16[4,8,96,768]{3,2,1,0:T(8,128)(2,1)}) custom-call(s32[2]{0:T(128)} %pad_add_fusion.1.where_ref, bf16[512,768]{1,0:T(8,128)(2,1)} %dynamic-slice_bitcast_fusion.1.x_ref, ...), custom_call_target="tpu_custom_call" | custom-call | flops 4000000000 | bytes 28080128 | tf_op jit(solution)/shard_map/up_fwd/pallas_call | solution.py:264
  175.8 19.3 %down_fwd_bwd.1 = (bf16[512,768]{1,0:T(8,128)(2,1)}, f32[512,768]{1,0:T(8,128)}, bf16[4,512,768]{2,1,0:T(8,128)(2,1)}, bf16[8,4,96,768]{3,2,1,0:T(8,128)(2,1)}, f32[3,768]{1,0:T(4,128)}, /*index=5*/f32[4,1,768]{2,1,0:T(1,128)}) custom-call(s32[2]{0:T(128)} %pad_add_fusion.1.where_ref, f32[512,768]{1,0:T(8,128)} %get-tuple-element.42.xhat_ref, ...), custom_call_target="tpu_custom_call" | custom-call | flops 8000000000 | bytes 26778624 | tf_op jit(solution)/shard_map/down_fwd_bwd/pallas_call | solution.py:264
  195.0 17.4 %up_bwd.1 = (f32[512,768]{1,0:T(8,128)}, bf16[4,512,256]{2,1,0:T(8,128)(2,1)}, bf16[8,4,96,768]{3,2,1,0:T(8,128)(2,1)}, f32[3,768]{1,0:T(4,128)}) custom-call(s32[2]{0:T(128)} %pad_add_fusion.1.where_ref, f32[512,768]{1,0:T(8,128)} %get-tuple-element.48.dr2_ref, bf16[4,512,768]{2,1,0:T(8,128)(2,1)} %get-tuple-element.49.dup_ref, ...), custom_call_target="tpu_custom_call" | custom-call | flops 6000000000 | bytes 24144896 | tf_op jit(solution)/shard_map/up_bwd/pallas_call | solution.py:264
  212.5 26.2 %attn_bwd.1 = (bf16[512,768]{1,0:T(8,128)(2,1)}, bf16[8,4,96,768]{3,2,1,0:T(8,128)(2,1)}, f32[4,1,768]{2,1,0:T(1,128)}) custom-call(s32[2]{0:T(128)} %pad_add_fusion.1.where_ref, bf16[512,768]{1,0:T(8,128)(2,1)} %dynamic-slice_bitcast_fusion.1.x_ref, s32[1,512]{1,0:T(1,128)} %constant_dynamic-slice_fusion.seg_row_ref, s32[512,1]{1,0:T(8,128)} %copy.107.seg_col_ref, ...), custom_call_target="tpu_custom_call" | custom-call | flops 10000000000 | bytes 17866752 | tf_op jit(solution)/shard_map/attn_bwd/pallas_call | solution.py:264
  251.2 14.3 %collective-permute-done.39.refs_1_ = bf16[512,768]{1,0:T(8,128)(2,1)} collective-permute-done((bf16[512,768]{1,0:T(8,128)(2,1)}, bf16[512,768]{1,0:T(8,128)(2,1)}, u32[]{:S(2)}, u32[]{:S(2)}) %collective-permute-start.39) | collective-permute-done | bytes 786464 | tf_op jit(solution)/shard_map/ppermute | solution.py:282
  266.4 5.1 %all-to-all-start = ((f32[32,1,720]{2,1,0:T(1,128)}), f32[32,1,720]{2,1,0:T(1,128)S(1)}, u32[]{:S(2)}, u32[]{:S(2)}) async-start(f32[32,1,720]{2,1,0:T(1,128)} %all_to_all.6), calls=%async_computation | async-start | bytes 196608 | tf_op jit(solution)/shard_map/all_to_all | solution.py:438
  274.7 24.2 %collective-permute-done.40.refs_2_ = bf16[512,768]{1,0:T(8,128)(2,1)} collective-permute-done((bf16[512,768]{1,0:T(8,128)(2,1)}, bf16[512,768]{1,0:T(8,128)(2,1)}, u32[]{:S(2)}, u32[]{:S(2)}) %collective-permute-start.40) | collective-permute-done | bytes 786464 | tf_op jit(solution)/shard_map/ppermute | solution.py:282
  299.6 34.4 %all-to-all-done = f32[32,1,720]{2,1,0:T(1,128)S(1)} async-done(((f32[32,1,720]{2,1,0:T(1,128)}), f32[32,1,720]{2,1,0:T(1,128)S(1)}, u32[]{:S(2)}, u32[]{:S(2)}) %all-to-all-start) | async-done | bytes 92192 | tf_op jit(solution)/shard_map/all_to_all | solution.py:438
  345.2 28.0 %collective-permute-done.37.refs_2_ = bf16[512,768]{1,0:T(8,128)(2,1)S(1)} collective-permute-done((bf16[512,768]{1,0:T(8,128)(2,1)S(1)}, bf16[512,768]{1,0:T(8,128)(2,1)S(1)}, u32[]{:S(2)}, u32[]{:S(2)}) %collective-permute-start.37) | collective-permute-done | bytes 786464 | tf_op jit(solution)/shard_map/ppermute | solution.py:282
  374.1 3.8 place_rows.2
  392.9 3.9 collective-permute-done.51
  399.1 4.0 collective-permute-done.43
  405.4 11.1 %collective-permute-done.60 = bf16[4,96,768]{2,1,0:T(8,128)(2,1)S(1)} collective-permute-done((bf16[4,96,768]{2,1,0:T(8,128)(2,1)S(1)}, bf16[4,96,768]{2,1,0:T(8,128)(2,1)S(1)}, u32[]{:S(2)}, u32[]{:S(2)}) %collective-permute-start.60) | collective-permute-done | bytes 589856 | tf_op jit(solution)/shard_map/ppermute | solution.py:278
  418.0 16.6 %collective-permute-start.63 = (bf16[96,768]{1,0:T(8,128)(2,1)S(1)}, bf16[96,768]{1,0:T(8,128)(2,1)S(1)}, u32[]{:S(2)}, u32[]{:S(2)}) collective-permute-start(bf16[96,768]{1,0:T(8,128)(2,1)S(1)} %get-tuple-element.157), channel_id=1, source_target_pairs={{0,1},{1,2},{2,3},{3,0},{4,5},{5,6},{6,7},{7,4},{8,9},{9,10},{10,1... | collective-permute-start | bytes 442376 | tf_op jit(solution)/shard_map/ppermute | solution.py:282
  434.6 10.0 %collective-permute-start.64 = (bf16[96,768]{1,0:T(8,128)(2,1)S(1)}, bf16[96,768]{1,0:T(8,128)(2,1)S(1)}, u32[]{:S(2)}, u32[]{:S(2)}) collective-permute-start(bf16[96,768]{1,0:T(8,128)(2,1)S(1)} %get-tuple-element.159), channel_id=1, source_target_pairs={{0,2},{1,3},{2,0},{3,1},{4,6},{5,7},{6,4},{7,5},{8,10},{9,11},{10,... | collective-permute-start | bytes 442376 | tf_op jit(solution)/shard_map/ppermute | solution.py:282
  448.4 8.8 %collective-permute-start.55 = (bf16[96,768]{1,0:T(8,128)(2,1)S(1)}, bf16[96,768]{1,0:T(8,128)(2,1)S(1)}, u32[]{:S(2)}, u32[]{:S(2)}) collective-permute-start(bf16[96,768]{1,0:T(8,128)(2,1)S(1)} %get-tuple-element.160), channel_id=1, source_target_pairs={{0,1},{1,2},{2,3},{3,0},{4,5},{5,6},{6,7},{7,4},{8,9},{9,10},{10,1... | collective-permute-start | bytes 442376 | tf_op jit(solution)/shard_map/ppermute | solution.py:282
  463.6 4.2 collective-permute-done.47
  467.8 8.3 %collective-permute-done.48 = bf16[96,768]{1,0:T(8,128)(2,1)S(1)} collective-permute-done((bf16[96,768]{1,0:T(8,128)(2,1)S(1)}, bf16[96,768]{1,0:T(8,128)(2,1)S(1)}, u32[]{:S(2)}, u32[]{:S(2)}) %collective-permute-start.48) | collective-permute-done | bytes 147488 | tf_op jit(solution)/shard_map/ppermute | solution.py:282
  477.5 5.8 %collective-permute-done.57 = bf16[96,768]{1,0:T(8,128)(2,1)S(1)} collective-permute-done((bf16[96,768]{1,0:T(8,128)(2,1)S(1)}, bf16[96,768]{1,0:T(8,128)(2,1)S(1)}, u32[]{:S(2)}, u32[]{:S(2)}) %collective-permute-start.57) | collective-permute-done | bytes 147488 | tf_op jit(solution)/shard_map/ppermute | solution.py:282
  (335 shorter events, 152.4 us)
Async XLA Ops:
  22.7 35.2 %collective-permute-start.3 = (bf16[4,96,768]{2,1,0:T(8,128)(2,1)}, bf16[4,96,768]{2,1,0:T(8,128)(2,1)}, u32[]{:S(2)}, u32[]{:S(2)}) collective-permute-start(bf16[4,96,768]{2,1,0:T(8,128)(2,1)} %pad_maximum_fusion.refs_0_), channel_id=1, source_target_pairs={{0,8},{4,12},{8,0},{12,4},{16,24},{20,28},{24,16},{28,20},{1,9},{5... | collective-permute-start | bytes 1769480 | tf_op jit(solution)/shard_map/ppermute | solution.py:278
  24.2 34.2 %collective-permute-start.4 = (bf16[4,96,768]{2,1,0:T(8,128)(2,1)}, bf16[4,96,768]{2,1,0:T(8,128)(2,1)}, u32[]{:S(2)}, u32[]{:S(2)}) collective-permute-start(bf16[4,96,768]{2,1,0:T(8,128)(2,1)} %pad_maximum_fusion.refs_0_), channel_id=1, source_target_pairs={{0,16},{4,20},{8,24},{12,28},{16,0},{20,4},{24,8},{28,12},{1,17},{... | collective-permute-start | bytes 1769480 | tf_op jit(solution)/shard_map/ppermute | solution.py:278
  45.0 66.0 %collective-permute-start.16 = (bf16[4,96,768]{2,1,0:T(8,128)(2,1)}, bf16[4,96,768]{2,1,0:T(8,128)(2,1)}, u32[]{:S(2)}, u32[]{:S(2)}) collective-permute-start(bf16[4,96,768]{2,1,0:T(8,128)(2,1)} %pad_maximum_fusion.1.refs_0_), channel_id=1, source_target_pairs={{0,16},{4,20},{8,24},{12,28},{16,0},{20,4},{24,8},{28,12},{1,17},{... | collective-permute-start | bytes 1769480 | tf_op jit(solution)/shard_map/ppermute | solution.py:278
  56.0 62.0 %collective-permute-start.7 = (bf16[4,96,768]{2,1,0:T(8,128)(2,1)}, bf16[4,96,768]{2,1,0:T(8,128)(2,1)}, u32[]{:S(2)}, u32[]{:S(2)}) collective-permute-start(bf16[4,96,768]{2,1,0:T(8,128)(2,1)} %pad_maximum_fusion.refs_0_), channel_id=1, source_target_pairs={{0,4},{4,0},{8,12},{12,8},{16,20},{20,16},{24,28},{28,24},{1,5},{5... | collective-permute-start | bytes 1769480 | tf_op jit(solution)/shard_map/ppermute | solution.py:278
  57.9 61.7 %collective-permute-start.19 = (bf16[4,96,768]{2,1,0:T(8,128)(2,1)}, bf16[4,96,768]{2,1,0:T(8,128)(2,1)}, u32[]{:S(2)}, u32[]{:S(2)}) collective-permute-start(bf16[4,96,768]{2,1,0:T(8,128)(2,1)} %pad_maximum_fusion.1.refs_0_), channel_id=1, source_target_pairs={{0,4},{4,0},{8,12},{12,8},{16,20},{20,16},{24,28},{28,24},{1,5},{5... | collective-permute-start | bytes 1769480 | tf_op jit(solution)/shard_map/ppermute | solution.py:278
  58.4 58.1 %collective-permute-start.27 = (bf16[4,96,768]{2,1,0:T(8,128)(2,1)}, bf16[4,96,768]{2,1,0:T(8,128)(2,1)}, u32[]{:S(2)}, u32[]{:S(2)}) collective-permute-start(bf16[4,96,768]{2,1,0:T(8,128)(2,1)} %pad_maximum_fusion.2.refs_0_), channel_id=1, source_target_pairs={{0,8},{4,12},{8,0},{12,4},{16,24},{20,28},{24,16},{28,20},{1,9},{5... | collective-permute-start | bytes 1769480 | tf_op jit(solution)/shard_map/ppermute | solution.py:278
  58.9 60.8 %collective-permute-start.28 = (bf16[4,96,768]{2,1,0:T(8,128)(2,1)}, bf16[4,96,768]{2,1,0:T(8,128)(2,1)}, u32[]{:S(2)}, u32[]{:S(2)}) collective-permute-start(bf16[4,96,768]{2,1,0:T(8,128)(2,1)} %pad_maximum_fusion.2.refs_0_), channel_id=1, source_target_pairs={{0,16},{4,20},{8,24},{12,28},{16,0},{20,4},{24,8},{28,12},{1,17},{... | collective-permute-start | bytes 1769480 | tf_op jit(solution)/shard_map/ppermute | solution.py:278
  141.7 33.1 %collective-permute-start.31 = (bf16[4,96,768]{2,1,0:T(8,128)(2,1)}, bf16[4,96,768]{2,1,0:T(8,128)(2,1)S(1)}, u32[]{:S(2)}, u32[]{:S(2)}) collective-permute-start(bf16[4,96,768]{2,1,0:T(8,128)(2,1)} %pad_maximum_fusion.2.refs_0_), channel_id=1, source_target_pairs={{0,4},{4,0},{8,12},{12,8},{16,20},{20,16},{24,28},{28,24},{1,5},{5... | collective-permute-start | bytes 1769480 | tf_op jit(solution)/shard_map/ppermute | solution.py:278
  141.9 32.9 %collective-permute-start.32 = (bf16[4,96,768]{2,1,0:T(8,128)(2,1)}, bf16[4,96,768]{2,1,0:T(8,128)(2,1)}, u32[]{:S(2)}, u32[]{:S(2)}) collective-permute-start(bf16[4,96,768]{2,1,0:T(8,128)(2,1)} %collective-permute-done.27.refs_1_), channel_id=1, source_target_pairs={{0,4},{4,0},{8,12},{12,8},{16,20},{20,16},{24,28},{28,24},{1,5},{5... | collective-permute-start | bytes 1769480 | tf_op jit(solution)/shard_map/ppermute | solution.py:278
  142.3 32.5 %collective-permute-start.33 = (bf16[4,96,768]{2,1,0:T(8,128)(2,1)}, bf16[4,96,768]{2,1,0:T(8,128)(2,1)}, u32[]{:S(2)}, u32[]{:S(2)}) collective-permute-start(bf16[4,96,768]{2,1,0:T(8,128)(2,1)} %collective-permute-done.28.refs_2_), channel_id=1, source_target_pairs={{0,4},{4,0},{8,12},{12,8},{16,20},{20,16},{24,28},{28,24},{1,5},{5... | collective-permute-start | bytes 1769480 | tf_op jit(solution)/shard_map/ppermute | solution.py:278
  242.7 135.1 %collective-permute-start.58 = (bf16[4,4,96,768]{3,2,1,0:T(8,128)(2,1)}, bf16[4,4,96,768]{3,2,1,0:T(8,128)(2,1)S(1)}, u32[]{:S(2)}, u32[]{:S(2)}) collective-permute-start(bf16[4,4,96,768]{3,2,1,0:T(8,128)(2,1)} %slice_bitcast_fusion), channel_id=1, source_target_pairs={{0,4},{4,0},{8,12},{12,8},{16,20},{20,16},{24,28},{28,24},{1,5},{5... | collective-permute-start | bytes 7077896 | tf_op jit(solution)/shard_map/ppermute | solution.py:278
  243.0 56.0 %collective-permute-start.40 = (bf16[512,768]{1,0:T(8,128)(2,1)}, bf16[512,768]{1,0:T(8,128)(2,1)}, u32[]{:S(2)}, u32[]{:S(2)}) collective-permute-start(bf16[512,768]{1,0:T(8,128)(2,1)} %get-tuple-element.55.refs_0_), channel_id=1, source_target_pairs={{0,2},{1,3},{2,0},{3,1},{4,6},{5,7},{6,4},{7,5},{8,10},{9,11},{10,... | collective-permute-start | bytes 2359304 | tf_op jit(solution)/shard_map/ppermute | solution.py:282
  245.2 90.7 %collective-permute-start.41 = (bf16[512,768]{1,0:T(8,128)(2,1)}, bf16[512,768]{1,0:T(8,128)(2,1)}, u32[]{:S(2)}, u32[]{:S(2)}) collective-permute-start(bf16[512,768]{1,0:T(8,128)(2,1)} %get-tuple-element.55.refs_0_), channel_id=1, source_target_pairs={{0,3},{1,0},{2,1},{3,2},{4,7},{5,4},{6,5},{7,6},{8,11},{9,8},{10,9... | collective-permute-start | bytes 2359304 | tf_op jit(solution)/shard_map/ppermute | solution.py:282
  250.7 131.9 %collective-permute-start.50 = (bf16[4,4,96,768]{3,2,1,0:T(8,128)(2,1)}, bf16[4,4,96,768]{3,2,1,0:T(8,128)(2,1)}, u32[]{:S(2)}, u32[]{:S(2)}) collective-permute-start(bf16[4,4,96,768]{3,2,1,0:T(8,128)(2,1)} %slice_bitcast_fusion.2), channel_id=1, source_target_pairs={{0,4},{4,0},{8,12},{12,8},{16,20},{20,16},{24,28},{28,24},{1,5},{5... | collective-permute-start | bytes 7077896 | tf_op jit(solution)/shard_map/ppermute | solution.py:278
  265.6 70.4 %collective-permute-start.36 = (bf16[512,768]{1,0:T(8,128)(2,1)S(1)}, bf16[512,768]{1,0:T(8,128)(2,1)}, u32[]{:S(2)}, u32[]{:S(2)}) collective-permute-start(bf16[512,768]{1,0:T(8,128)(2,1)S(1)} %copy-done.5), channel_id=1, source_target_pairs={{0,1},{1,2},{2,3},{3,0},{4,5},{5,6},{6,7},{7,4},{8,9},{9,10},{10,1... | collective-permute-start | bytes 2359304 | tf_op jit(solution)/shard_map/ppermute | solution.py:282
  266.4 67.6 %all-to-all-start = ((f32[32,1,720]{2,1,0:T(1,128)}), f32[32,1,720]{2,1,0:T(1,128)S(1)}, u32[]{:S(2)}, u32[]{:S(2)}) async-start(f32[32,1,720]{2,1,0:T(1,128)} %all_to_all.6), calls=%async_computation | async-start | bytes 196608 | tf_op jit(solution)/shard_map/all_to_all | solution.py:438
  299.0 88.2 %collective-permute-start.42 = (bf16[4,4,96,768]{3,2,1,0:T(8,128)(2,1)}, bf16[4,4,96,768]{3,2,1,0:T(8,128)(2,1)}, u32[]{:S(2)}, u32[]{:S(2)}) collective-permute-start(bf16[4,4,96,768]{3,2,1,0:T(8,128)(2,1)} %slice_bitcast_fusion.4), channel_id=1, source_target_pairs={{0,4},{4,0},{8,12},{12,8},{16,20},{20,16},{24,28},{28,24},{1,5},{5... | collective-permute-start | bytes 7077896 | tf_op jit(solution)/shard_map/ppermute | solution.py:278
  335.9 37.3 %collective-permute-start.37 = (bf16[512,768]{1,0:T(8,128)(2,1)S(1)}, bf16[512,768]{1,0:T(8,128)(2,1)S(1)}, u32[]{:S(2)}, u32[]{:S(2)}) collective-permute-start(bf16[512,768]{1,0:T(8,128)(2,1)S(1)} %copy-done.5), channel_id=1, source_target_pairs={{0,2},{1,3},{2,0},{3,1},{4,6},{5,7},{6,4},{7,5},{8,10},{9,11},{10,... | collective-permute-start | bytes 2359304 | tf_op jit(solution)/shard_map/ppermute | solution.py:282
  336.0 38.1 %collective-permute-start.38 = (bf16[512,768]{1,0:T(8,128)(2,1)S(1)}, bf16[512,768]{1,0:T(8,128)(2,1)}, u32[]{:S(2)}, u32[]{:S(2)}) collective-permute-start(bf16[512,768]{1,0:T(8,128)(2,1)S(1)} %copy-done.5), channel_id=1, source_target_pairs={{0,3},{1,0},{2,1},{3,2},{4,7},{5,4},{6,5},{7,6},{8,11},{9,8},{10,9... | collective-permute-start | bytes 2359304 | tf_op jit(solution)/shard_map/ppermute | solution.py:282
  397.8 36.8 %collective-permute-start.52 = (bf16[4,96,768]{2,1,0:T(8,128)(2,1)S(1)}, bf16[4,96,768]{2,1,0:T(8,128)(2,1)S(1)}, u32[]{:S(2)}, u32[]{:S(2)}) collective-permute-start(bf16[4,96,768]{2,1,0:T(8,128)(2,1)S(1)} %pad_maximum_fusion.5), channel_id=1, source_target_pairs={{0,8},{4,12},{8,0},{12,4},{16,24},{20,28},{24,16},{28,20},{1,9},{5... | collective-permute-start | bytes 1769480 | tf_op jit(solution)/shard_map/ppermute | solution.py:278
  403.1 41.5 %collective-permute-start.54 = (bf16[4,96,768]{2,1,0:T(8,128)(2,1)S(1)}, bf16[4,96,768]{2,1,0:T(8,128)(2,1)S(1)}, u32[]{:S(2)}, u32[]{:S(2)}) collective-permute-start(bf16[4,96,768]{2,1,0:T(8,128)(2,1)S(1)} %pad_maximum_fusion.6), channel_id=1, source_target_pairs={{0,16},{4,20},{8,24},{12,28},{16,0},{20,4},{24,8},{28,12},{1,17},{... | collective-permute-start | bytes 1769480 | tf_op jit(solution)/shard_map/ppermute | solution.py:278
  404.1 44.3 %collective-permute-start.44 = (bf16[4,96,768]{2,1,0:T(8,128)(2,1)S(1)}, bf16[4,96,768]{2,1,0:T(8,128)(2,1)S(1)}, u32[]{:S(2)}, u32[]{:S(2)}) collective-permute-start(bf16[4,96,768]{2,1,0:T(8,128)(2,1)S(1)} %pad_maximum_fusion.3), channel_id=1, source_target_pairs={{0,8},{4,12},{8,0},{12,4},{16,24},{20,28},{24,16},{28,20},{1,9},{5... | collective-permute-start | bytes 1769480 | tf_op jit(solution)/shard_map/ppermute | solution.py:278
  416.5 40.6 %collective-permute-start.46 = (bf16[4,96,768]{2,1,0:T(8,128)(2,1)S(1)}, bf16[4,96,768]{2,1,0:T(8,128)(2,1)S(1)}, u32[]{:S(2)}, u32[]{:S(2)}) collective-permute-start(bf16[4,96,768]{2,1,0:T(8,128)(2,1)S(1)} %pad_maximum_fusion.4), channel_id=1, source_target_pairs={{0,16},{4,20},{8,24},{12,28},{16,0},{20,4},{24,8},{28,12},{1,17},{... | collective-permute-start | bytes 1769480 | tf_op jit(solution)/shard_map/ppermute | solution.py:278
  418.0 39.8 %collective-permute-start.63 = (bf16[96,768]{1,0:T(8,128)(2,1)S(1)}, bf16[96,768]{1,0:T(8,128)(2,1)S(1)}, u32[]{:S(2)}, u32[]{:S(2)}) collective-permute-start(bf16[96,768]{1,0:T(8,128)(2,1)S(1)} %get-tuple-element.157), channel_id=1, source_target_pairs={{0,1},{1,2},{2,3},{3,0},{4,5},{5,6},{6,7},{7,4},{8,9},{9,10},{10,1... | collective-permute-start | bytes 442376 | tf_op jit(solution)/shard_map/ppermute | solution.py:282
  (74 other events, 1083.9 us)

commit v2 on v1

v2 whole, which is shorter than its diff:
```python
import functools
import math

import jax
import jax.numpy as jnp
from jax import lax
from jax.experimental import pallas as pl
from jax.experimental.pallas import tpu as pltpu
from jax.sharding import PartitionSpec as P

HD = 64
LANES = 128
VMEM_LIMIT = 60 * 1024 * 1024

norm_eps = 1e-05
beta_first = 0.9
beta_second = 0.999
warm_steps = 10000.0
total_steps = 200000.0

bf = jnp.bfloat16
fl = jnp.float32

SLABS = 8
DEPTH = 96
EXTRA = 16


def nt(left, right):
    return lax.dot_general(left, right, (((1,), (1,)), ((), ())), preferred_element_type=fl)


def nn(left, right):
    return lax.dot_general(left, right, (((1,), (0,)), ((), ())), preferred_element_type=fl)


def tn(left, right):
    return lax.dot_general(left, right, (((0,), (0,)), ((), ())), preferred_element_type=fl)


def low_lanes(shape):
    return lax.broadcasted_iota(jnp.int32, shape, 1) < HD


def assemble(where_ref, pieces, plan, *targets):
    for ref, (r, shifts) in zip(pieces, plan):
        slab = jnp.bitwise_xor(where_ref[0], r)
        for k, s in enumerate(shifts):
            group = jnp.bitwise_and(where_ref[1] + 4 - s, 3)
            first = 0
            for target in targets:
                last = first + target.shape[2]
                target[group, slab] = ref[k, first:last]
                first = last


def scatter_slabs(where_ref, group, value, near_ref, far_ref, extra=None):
    shift = jnp.bitwise_and(group + 4 - where_ref[1], 3)
    chip = jnp.right_shift(where_ref[0], 1)
    core = jnp.bitwise_and(where_ref[0], 1)

    def put(even_ref, odd_ref):
        for j in range(SLABS):
            out_ref = odd_ref if j % 2 else even_ref
            place = jnp.bitwise_xor(chip, j // 2)
            out_ref[place, shift, :DEPTH] = value[DEPTH * j : DEPTH * (j + 1)]
            if extra is not None:
                out_ref[place, shift, DEPTH:] = extra

    @pl.when(core == 0)
    def _():
        put(near_ref, far_ref)

    @pl.when(core == 1)
    def _():
        put(far_ref, near_ref)


def matrix(ref, group):
    return ref[group][:, :DEPTH].reshape(SLABS * DEPTH, ref.shape[-1])


def out_matrix(ref, group):
    return ref[group][:, :DEPTH, 512:768].reshape(SLABS * DEPTH, 256)


def attn_fwd_kernel(plan, where_ref, x_ref, seg_row_ref, seg_col_ref, *refs):
    pieces = refs[: len(plan)]
    proj_ref, ctx_ref, lse_ref, weight_ref, xhat_ref, rstd_ref, first_ref, vec_ref, b_up_ref = refs[-9:]
    assemble(where_ref, pieces, plan, weight_ref)
    scale = HD ** (-0.5)
    length = x_ref.shape[0]

    def group_step(g, carry):
        small = jnp.sum(weight_ref[g, :, DEPTH:].astype(fl), axis=0)
        vec_ref[...] = small[:8]
        b_up_ref[g] = small[7:8]
        x = x_ref[...]
        proj = (nn(x, matrix(weight_ref, g)) + small[6:7]).astype(bf)
        proj_ref[g] = proj
        same = seg_col_ref[...] == seg_row_ref[...]
        low = low_lanes((length, LANES))
        none = jnp.zeros((length, LANES), bf)
        parts = [proj[:, LANES * k : LANES * (k + 1)] for k in range(6)]
        outs = []
        for head in range(3):
            query = parts[0] if head < 2 else parts[3]
            keys = parts[1] if head < 2 else parts[5]
            value = parts[2] if head < 2 else parts[3]
            query = jnp.where(low, none, query) if head == 1 else jnp.where(low, query, none)
            scores = jnp.where(same, nt(keys, query) * scale, -1e30)
            top = jnp.max(scores, axis=0, keepdims=True)
            expd = jnp.exp(scores - top)
            denom = jnp.sum(expd, axis=0, keepdims=True)
            lse_ref[g, head] = top + jnp.log(denom)
            probs = (expd / denom).astype(bf)
            outs.append(tn(probs, value).astype(bf))
        ctx_ref[g] = jnp.concatenate(
            [jnp.where(low, outs[0], outs[1]), jnp.where(low, none, outs[2])], axis=1
        )
        return carry

    lax.fori_loop(0, 4, group_step, 0)
    total = x_ref[...].astype(fl) + vec_ref[4:5]
    attn = None
    for g in range(4):
        part = nt(ctx_ref[g], out_matrix(weight_ref, g))
        attn = part if attn is None else attn + part
    total = total + attn
    center = total - jnp.mean(total, axis=-1, keepdims=True)
    rstd = lax.rsqrt(jnp.mean(center * center, axis=-1, keepdims=True) + norm_eps)
    xhat = center * rstd
    xhat_ref[...] = xhat
    rstd_ref[...] = jnp.broadcast_to(rstd, rstd_ref.shape)
    first_ref[...] = (xhat * vec_ref[0:1] + vec_ref[1:2]).astype(bf)


def ffn_fwd_kernel(plan, where_ref, xhat_ref, first_ref, dy_ref, vec_ref, b_up_ref, *refs):
    pieces, refs = refs[: len(plan)], refs[len(plan) :]
    out_ref, dr2_ref, act_ref, slope_ref, small_ref, up_w_ref, down_w_ref = refs
    assemble(where_ref, pieces, plan, up_w_ref, down_w_ref)

    def step(g, carry):
        up = nn(first_ref[...], matrix(up_w_ref, g)) + b_up_ref[g]
        half = 0.5 * (1.0 + lax.erf(up * 0.7071067811865476))
        act_ref[g] = (up * half).astype(bf)
        slope_ref[g] = half + up * (jnp.exp(-0.5 * up * up) * 0.3989422804014327)
        return carry

    lax.fori_loop(0, 4, step, 0)
    ffn = None
    for g in range(4):
        part = nt(act_ref[g], matrix(down_w_ref, g))
        ffn = part if ffn is None else ffn + part
    first = xhat_ref[...] * vec_ref[0:1] + vec_ref[1:2]
    total = first + ffn + vec_ref[5:6]
    center = total - jnp.mean(total, axis=-1, keepdims=True)
    rstd = lax.rsqrt(jnp.mean(center * center, axis=-1, keepdims=True) + norm_eps)
    xhat = center * rstd
    out_ref[...] = (xhat * vec_ref[2:3] + vec_ref[3:4]).astype(bf)
    dy = dy_ref[...].astype(fl)
    small_ref[0:1] = jnp.sum(dy * xhat, axis=0, keepdims=True)
    small_ref[1:2] = jnp.sum(dy, axis=0, keepdims=True)
    dxhat = dy * vec_ref[2:3]
    dr2 = rstd * (
        dxhat
        - jnp.mean(dxhat, axis=-1, keepdims=True)
        - xhat * jnp.mean(dxhat * xhat, axis=-1, keepdims=True)
    )
    dr2_ref[...] = dr2
    small_ref[2:3] = jnp.sum(dr2, axis=0, keepdims=True)


def down_weights_kernel(where_ref, dr2_ref, act_ref, near_ref, far_ref):
    def step(g, carry):
        dffn = dr2_ref[...].astype(bf)
        scatter_slabs(where_ref, g, tn(dffn, act_ref[g]).astype(bf), near_ref, far_ref)
        return carry

    lax.fori_loop(0, 4, step, 0)


def down_bwd_kernel(where_ref, dr2_ref, slope_ref, weight_ref, dup_ref, b_up_ref):
    def step(g, carry):
        dffn = dr2_ref[...].astype(bf)
        dup = (nn(dffn, matrix(weight_ref, g)) * slope_ref[g]).astype(bf)
        dup_ref[g] = dup
        b_up_ref[g] = jnp.sum(dup.astype(fl), axis=0, keepdims=True)
        return carry

    lax.fori_loop(0, 4, step, 0)


def up_weights_kernel(where_ref, first_ref, dup_ref, *refs):
    near_ref, far_ref = refs[-2:]

    def step(g, carry):
        scatter_slabs(where_ref, g, tn(first_ref[...], dup_ref[g]).astype(bf), near_ref, far_ref)
        return carry

    lax.fori_loop(0, 4, step, 0)


def up_bwd_kernel(where_ref, dr2_ref, dup_ref, xhat_ref, rstd_ref, vec_ref, weight_ref, attn_weight_ref, *refs):
    dr1_ref, dctx_ref, small_ref = refs[-3:]
    feed = None
    for g in range(4):
        part = nt(dup_ref[g], matrix(weight_ref, g))
        feed = part if feed is None else feed + part
    dfirst = dr2_ref[...] + feed.astype(bf).astype(fl)
    xhat = xhat_ref[...]
    small_ref[0:1] = jnp.sum(dfirst * xhat, axis=0, keepdims=True)
    small_ref[1:2] = jnp.sum(dfirst, axis=0, keepdims=True)
    dxhat = dfirst * vec_ref[0:1]
    dr1 = rstd_ref[:, 0:1] * (
        dxhat
        - jnp.mean(dxhat, axis=-1, keepdims=True)
        - xhat * jnp.mean(dxhat * xhat, axis=-1, keepdims=True)
    )
    dr1_ref[...] = dr1
    small_ref[2:3] = jnp.sum(dr1, axis=0, keepdims=True)
    dattn = dr1.astype(bf)
    for g in range(4):
        dctx_ref[g] = nn(dattn, out_matrix(attn_weight_ref, g)).astype(bf)


def attn_bwd_kernel(where_ref, seg_row_ref, seg_col_ref, proj_ref, lse_ref, dr1_ref, dctx_ref, weight_ref, *refs):
    grad_in_ref, dproj_ref, bias_ref, back_ref = refs[-4:]
    scale = HD ** (-0.5)
    length = dr1_ref.shape[0]
    back_ref[...] = jnp.zeros_like(back_ref)

    def step(g, carry):
        same = seg_col_ref[...] == seg_row_ref[...]
        low = low_lanes((length, LANES))
        none = jnp.zeros((length, LANES), bf)
        parts = [proj_ref[g, :, LANES * k : LANES * (k + 1)] for k in range(6)]
        dctx = [dctx_ref[g, :, :LANES], dctx_ref[g, :, LANES:]]
        dq, dk, dv = [], [], []
        for head in range(3):
            query = parts[0] if head < 2 else parts[3]
            keys = parts[1] if head < 2 else parts[5]
            value = parts[2] if head < 2 else parts[3]
            dout = dctx[0] if head < 2 else dctx[1]
            query_in = jnp.where(low, none, query) if head == 1 else jnp.where(low, query, none)
            dout_in = jnp.where(low, dout, none) if head == 0 else jnp.where(low, none, dout)
            scores = jnp.where(same, nt(keys, query_in) * scale, -1e30)
            probs = jnp.exp(scores - lse_ref[g, head])
            dprobs = nt(value, dout_in)
            dv.append(nn(probs.astype(bf), dout))
            row_dot = jnp.sum(probs * dprobs, axis=0, keepdims=True)
            dscores = (probs * (dprobs - row_dot)).astype(bf)
            dq.append(tn(dscores, keys) * scale)
            dk.append(nn(dscores, query) * scale)
        dproj = jnp.concatenate(
            [
                jnp.where(low, dq[0], dq[1]).astype(bf),
                jnp.where(low, dk[0], dk[1]).astype(bf),
                jnp.where(low, dv[0], dv[1]).astype(bf),
                jnp.where(low, dq[2], dv[2]).astype(bf),
                none,
                jnp.where(low, dk[2].astype(bf), none),
            ],
            axis=1,
        )
        dproj_ref[g] = dproj
        bias_ref[g] = jnp.sum(dproj.astype(fl), axis=0, keepdims=True)
        back_ref[...] += nt(dproj, matrix(weight_ref, g))
        return carry

    lax.fori_loop(0, 4, step, 0)
    dr1 = dr1_ref[...]
    grad_in_ref[...] = (dr1 + back_ref[...].astype(bf).astype(fl)).astype(bf)


def attn_weights_kernel(where_ref, x_ref, dproj_ref, ctx_ref, dr1_ref, bias_ref, b_up_ref, one_ref, two_ref, *refs):
    near_ref, far_ref, small_ref = refs[-3:]
    small_ref[...] = jnp.zeros_like(small_ref)
    small_ref[0:2] = one_ref[0:2]
    small_ref[2:4] = two_ref[0:2]
    small_ref[4:5] = one_ref[2:3]
    small_ref[5:6] = two_ref[2:3]

    def grads(g, carry):
        small_ref[6:7] = bias_ref[g]
        small_ref[7:8] = b_up_ref[g]
        main = tn(x_ref[...], dproj_ref[g])
        side = tn(dr1_ref[...].astype(bf), ctx_ref[g])
        whole = jnp.concatenate([main[:, :512], main[:, 512:] + side], axis=1).astype(bf)
        scatter_slabs(where_ref, g, whole, near_ref, far_ref, small_ref[...].astype(bf))
        return carry

    lax.fori_loop(0, 4, grads, 0)


def place_kernel(where_ref, own_ref, *refs):
    out_ref = refs[-1]
    spot = where_ref[1]
    out_ref[spot] = own_ref[...]
    for d in (1, 2, 3):
        up_ref, down_ref = refs[2 * d - 2], refs[2 * d - 1]

        @pl.when(spot >= d)
        def _():
            out_ref[jnp.maximum(spot - d, 0)] = up_ref[...]

        @pl.when(spot + d < 4)
        def _():
            out_ref[jnp.minimum(spot + d, 3)] = down_ref[...]


smem = pl.BlockSpec(memory_space=pltpu.SMEM)
vmem = pl.BlockSpec(memory_space=pltpu.VMEM)


def call(kernel, name, outs, where, *args, scratch=(), after=()):
    return pl.pallas_call(
        kernel,
        name=name,
        out_shape=[jax.ShapeDtypeStruct(s, d) for s, d in outs],
        in_specs=[smem] + [vmem] * len(args) + [pl.BlockSpec(memory_space=pl.ANY)] * len(after),
        out_specs=[vmem] * len(outs),
        scratch_shapes=list(scratch),
        compiler_params=pltpu.CompilerParams(vmem_limit_bytes=VMEM_LIMIT),
        cost_estimate=pl.CostEstimate(flops=COST, bytes_accessed=COST, transcendentals=0),
    )(where, *args, *after)


COST = 1000


def flip(value, bits):
    n = lax.axis_size("dp")
    return lax.ppermute(value, "dp", [(k, k ^ bits) for k in range(n)])


def shift(value, s):
    return lax.ppermute(value, "tensor", [(k, (k + s) % 4) for k in range(4)])


def along(value, step, senders):
    return lax.ppermute(value, "tensor", [(k, k + step) for k in senders])


def with_core(near):
    return near + [(flip(a, 1), (r + 1, s)) for a, (r, s) in near]


ALL = (0, 1, 2, 3)


def tensor_stack(shard):
    return jnp.stack([shard] + [shift(shard, s) for s in (1, 2, 3)])


def gather_direct(own):
    return with_core([(own, (0, ALL))] + [(flip(own, r), (r, ALL)) for r in (2, 4, 6)])


def late(values, gate):
    return list(lax.optimization_barrier((*values, gate))[:-1])


def gather_staged(own, gate):
    over_x = flip(own, 2)
    over_y = flip(own, 4)
    half_x, half_y = late([over_x[:2], over_y[2:]], gate)
    far_a = flip(half_x, 4)
    far_b = flip(half_y, 2)
    near = [(own, (0, ALL)), (over_x, (2, ALL)), (over_y, (4, ALL))]
    return with_core(near + [(far_a, (6, (0, 1))), (far_b, (6, (2, 3)))])


def add(*values):
    total = values[0].astype(fl)
    for value in values[1:]:
        total = total + value.astype(fl)
    return total


def reduce_core(near, far, gate):
    (got,) = late([flip(far, 1)], gate)
    return [add(near[r], got[r]).astype(bf) for r in range(4)]


def reduce_plane(half, gate):
    got = late([flip(half[r], 2 * r) for r in (1, 2, 3)], gate)
    sums = [add(half[0][s], *[g[s] for g in got]) for s in range(4)]
    return [sums[0]] + [v.astype(bf) for v in sums[1:]]


def reduce_tensor(plane, gate):
    return [plane[0]] + late([shift(plane[s], s) for s in (1, 2, 3)], gate)


def gather_plain(shard, extra=None):
    whole = lax.all_gather(lax.all_gather(shard, "dp", axis=0, tiled=True), "tensor", axis=0)
    whole = whole.reshape(4, SLABS, -1, 768)
    if extra is not None:
        extra = lax.all_gather(lax.psum(extra, "dp"), "tensor", axis=0)[:, None].astype(bf)
        extra = jnp.concatenate([extra] + [jnp.zeros_like(extra)] * (SLABS - 1), axis=1)
        whole = jnp.concatenate([whole, extra], axis=2)
    order = [(4 - s) % 4 for s in range(4)]
    return [(jnp.stack([whole[t, r] for t in order]), (r, ALL)) for r in range(SLABS)]


def reduce_plain(near, far):
    grad = jnp.stack([near, far], axis=1).reshape(SLABS, 4, -1, 768).astype(fl)
    whole = grad[:, :, :DEPTH].transpose(1, 0, 2, 3).reshape(4, SLABS * DEPTH, 768)
    part = lax.psum_scatter(whole, "tensor", scatter_dimension=0, tiled=True)
    part = lax.psum_scatter(part[0], "dp", scatter_dimension=0, tiled=True)
    if near.shape[2] == DEPTH:
        return part
    extra = lax.psum_scatter(lax.psum(grad[0, :, DEPTH:], "dp"), "tensor", scatter_dimension=0, tiled=True)[0]
    return jnp.concatenate([part, extra])


def forward_rows(up, down, d, gate):
    return late([along(up, 1, range(d - 1, 3)), along(down, -1, range(1, 5 - d))], gate)


def place_rows(row, steps, where):
    pieces = [piece for step in steps for piece in step]
    return call(place_kernel, "place_rows", [((4,) + row.shape, row.dtype)], where, row, *pieces)[0]


def moment_update(state, grad):
    moment_one = beta_first * state[1] + (1.0 - beta_first) * grad
    moment_two = beta_second * state[2] + (1.0 - beta_second) * grad * grad
    return jnp.stack([moment_one, moment_two])


def body(
    hidden_in,
    out_grad,
    segment_ids,
    step_count,
    qkv_state,
    qv_bias_state,
    out_state,
    up_state,
    up_bias_state,
    down_state,
    vector_state,
):
    n_dp = lax.axis_size("dp")
    place = lax.axis_index("tensor")
    fast = n_dp == SLABS
    spot = lax.axis_index("dp") if fast else 0
    where = jnp.stack([jnp.int32(spot), (place if fast else 0) * jnp.int32(1)])
    spin = jnp.stack([jnp.int32(0), place * jnp.int32(1)])
    rows, width = qkv_state.shape[1], hidden_in.shape[2]
    cut = 2 * HD

    def spread(value, axis, whole):
        full = jnp.zeros(value.shape[:-1] + (whole,), bf)
        return lax.dynamic_update_slice_in_dim(full, value.astype(bf), axis * value.shape[-1], value.ndim - 1)

    dp = lax.axis_index("dp")
    q, k, v = (qkv_state[0, :, c].astype(bf) for c in range(3))
    o = out_state[0].T.astype(bf)
    attn_shard = jnp.concatenate(
        [q[:, :cut], k[:, :cut], v[:, :cut], q[:, cut:], v[:, cut:], o[:, :cut], k[:, cut:], o[:, cut:]], axis=1
    )
    bq, bv = spread(qv_bias_state[0], dp, HD).reshape(2, 3 * HD)
    gap = jnp.zeros((cut,), bf)
    bias = jnp.concatenate([bq[:cut], gap, bv[:cut], bq[cut:], bv[cut:], gap, gap])
    b_up = spread(up_bias_state[0], dp, LANES).reshape(1, 768)
    extra = jnp.concatenate(
        [spread(vector_state[0], dp, width), bias[None], b_up, jnp.zeros((EXTRA - 8, width), bf)]
    )
    up_shard = up_state[0].astype(bf)
    down_shard = down_state[0].T.astype(bf)

    x = lax.dynamic_index_in_dim(hidden_in, place, 0, keepdims=False)
    dy = lax.dynamic_index_in_dim(out_grad, place, 0, keepdims=False)
    seg = lax.dynamic_index_in_dim(segment_ids, place, 0, keepdims=True)
    seg_col = seg.reshape(-1, 1)
    length = x.shape[0]
    wide = (4, length, 768)
    row_f, row_b = ((length, width), fl), ((length, width), bf)
    whole = ((4, SLABS, DEPTH, 768), bf)
    attn_whole = ((4, SLABS, DEPTH + EXTRA, 768), bf)
    grad_shape = ((4, 4, DEPTH, 768), bf)
    attn_grad_shape = ((4, 4, DEPTH + EXTRA, 768), bf)
    thin = ((4, 1, 768), fl)

    if fast:
        own = tensor_stack(jnp.concatenate([attn_shard, extra]))
        attn_pieces = gather_direct(own)
        (ffn_shard,) = late([jnp.concatenate([up_shard, down_shard])], attn_pieces[4][0])
        ffn_own = tensor_stack(ffn_shard)
        wait = [ffn_own]
    else:
        attn_pieces = gather_plain(attn_shard, extra)
        ups, downs = gather_plain(up_shard), gather_plain(down_shard)
        ffn_pieces = [(jnp.concatenate([u, d], axis=1), w) for (u, w), (d, _) in zip(ups, downs)]
        wait = []

    def split(pieces):
        return [p for p, _ in pieces], tuple(w for _, w in pieces)

    pieces, plan = split(attn_pieces)
    proj, ctx, lse, attn_w, xhat, rstd, first, vec, b_up = call(
        functools.partial(attn_fwd_kernel, plan), "attn_fwd",
        [(wide, bf), ((4, length, 256), bf), ((4, 3, 1, length), fl), attn_whole, row_f, ((length, LANES), fl), row_b,
         ((8, width), fl), thin],
        where, x, seg, seg_col, *pieces, after=wait,
    )
    if fast:
        ffn_pieces = gather_staged(ffn_own, vec)
    pieces, plan = split(ffn_pieces)
    out, dr2, act, slope, small_two, up_w, down_w = call(
        functools.partial(ffn_fwd_kernel, plan), "ffn_fwd",
        [row_b, row_f, (wide, bf), (wide, fl), ((3, width), fl), whole, whole],
        where, xhat, first, dy, vec, b_up, *pieces,
    )
    down_near, down_far = call(
        down_weights_kernel, "down_weights", [grad_shape, grad_shape], where, dr2, act,
    )
    dup, b_up_grad = call(down_bwd_kernel, "down_bwd", [(wide, bf), thin], where, dr2, slope, down_w)
    down_half = reduce_core(down_near, down_far, b_up_grad) if fast else []
    out_one = forward_rows(out, out, 1, b_up_grad)
    up_near, up_far = call(
        up_weights_kernel, "up_weights", [grad_shape, grad_shape], where, first, dup, after=out_one,
    )
    dr1, dctx, small_one = call(
        up_bwd_kernel, "up_bwd", [row_f, ((4, length, 256), bf), ((3, width), fl)],
        where, dr2, dup, xhat, rstd, vec, up_w, attn_w, after=down_half,
    )
    out_two = forward_rows(*out_one, 2, small_one)
    down_plane = reduce_plane(down_half, small_one) if fast else []
    up_half = reduce_core(up_near, up_far, small_one) if fast else []
    grad_row, dproj, bias_grad = call(
        attn_bwd_kernel, "attn_bwd", [row_b, (wide, bf), thin],
        where, seg, seg_col, proj, lse, dr1, dctx, attn_w, after=out_two + down_plane + up_half,
        scratch=[pltpu.VMEM((length, width), fl)],
    )
    out_three = forward_rows(*out_two, 3, bias_grad)
    down_parts = reduce_tensor(down_plane, bias_grad) if fast else []
    up_plane = reduce_plane(up_half, bias_grad) if fast else []
    attn_near, attn_far = call(
        attn_weights_kernel, "attn_weights", [attn_grad_shape, attn_grad_shape],
        where, x, dproj, ctx, dr1, bias_grad, b_up_grad, small_one, small_two,
        scratch=[pltpu.VMEM((EXTRA, width), fl)], after=out_three + down_parts + up_plane,
    )
    in_one = forward_rows(grad_row, grad_row, 1, attn_near)
    in_two = forward_rows(*in_one, 2, attn_near)
    in_three = forward_rows(*in_two, 3, attn_near)
    hidden_out = place_rows(out, (out_one, out_two, out_three), spin)
    grad_in = place_rows(grad_row, (in_one, in_two, in_three), spin)
    if fast:
        down_sum = add(*down_parts)
        up_sum = add(*reduce_tensor(up_plane, attn_near))
        attn_half = reduce_core(attn_near, attn_far, attn_near)
        attn_sum = add(*reduce_tensor(reduce_plane(attn_half, attn_near), attn_near))
    else:
        down_sum = reduce_plain(down_near, down_far)
        up_sum = reduce_plain(up_near, up_far)
        attn_sum = reduce_plain(attn_near, attn_far)

    def own_part(value):
        size = value.shape[-1] // n_dp
        return lax.dynamic_slice_in_dim(value, dp * size, size, value.ndim - 1)

    small = attn_sum[rows:]
    gq = jnp.concatenate([small[6, :cut], small[6, 384 : 384 + HD]])
    gv = jnp.concatenate([small[6, 256 : 256 + cut], small[6, 384 + HD : 512]])
    grad_qv = own_part(jnp.stack([gq, gv]).reshape(2, 3, HD))
    grad_b_up = own_part(small[7].reshape(6, LANES))
    grad_vectors = own_part(small[:6])

    gk = [attn_sum[:rows, 128 * n : 128 * (n + 1)] for n in range(6)]
    grad_qkv = jnp.stack(
        [
            jnp.concatenate([gk[0], gk[3][:, :HD]], axis=1),
            jnp.concatenate([gk[1], gk[5][:, :HD]], axis=1),
            jnp.concatenate([gk[2], gk[3][:, HD:]], axis=1),
        ],
        axis=1,
    )
    grad_out = jnp.concatenate([gk[4], gk[5][:, HD:]], axis=1).T
    summed = (grad_qkv, grad_qv, grad_out, up_sum, grad_b_up, down_sum.T, grad_vectors)
    steps_f = step_count[0].astype(fl)
    factor = jnp.minimum(steps_f / warm_steps, (total_steps - steps_f) / (total_steps - warm_steps))
    fix_first = 1.0 - jnp.exp(steps_f * math.log(beta_first))
    fix_second = 1.0 - jnp.exp(steps_f * math.log(beta_second))
    states = (qkv_state, qv_bias_state, out_state, up_state, up_bias_state, down_state, vector_state)
    news = tuple((moment_update(s, g) for s, g in zip(states, summed)))
    plan_out = jnp.stack([factor, fix_first, fix_second])
    return (hidden_out, grad_in, *summed, *news, plan_out)


def solution(mesh):
    return jax.shard_map(
        body,
        mesh=mesh,
        in_specs=(
            P("dp", None, None),
            P("dp", None, None),
            P("dp", None),
            P(),
            P(None, "dp", None, "tensor"),
            P(None, None, "tensor", "dp"),
            P(None, "tensor", "dp"),
            P(None, "dp", "tensor"),
            P(None, "tensor", "dp"),
            P(None, "tensor", "dp"),
            P(None, None, "dp"),
        ),
        out_specs=(
            P("dp", None, None),
            P("dp", None, None),
            P("dp", None, "tensor"),
            P(None, "tensor", "dp"),
            P("tensor", "dp"),
            P("dp", "tensor"),
            P("tensor", "dp"),
            P("tensor", "dp"),
            P(None, "dp"),
            P(None, "dp", None, "tensor"),
            P(None, None, "tensor", "dp"),
            P(None, "tensor", "dp"),
            P(None, "dp", "tensor"),
            P(None, "tensor", "dp"),
            P(None, "tensor", "dp"),
            P(None, None, "dp"),
            P(),
        ),
        check_vma=False,
    )
```

time: 494 us -> 377 us (0.76)
  waiting for transfers between devices: 171 us -> 115 us
  blocking collectives: 47.8 us -> 0 us
  local copies, waits for them, and re-layouts: 39.5 us -> 22.4 us
  starting transfers between devices: 106 us -> 93 us
  Pallas kernels: 101 us -> 111 us
  other arithmetic: 25.8 us -> 32.3 us
    ppermute x24 -> x15, waiting for transfers between devices: 108 us -> 39.4 us  [shift(): return lax.ppermute(value, 'tensor', [(k, (k + s) % 4) for k in range(4)])]
    unnamed x1 -> x0, blocking collectives: 47.8 us -> none
    ppermute x42 -> x40, waiting for transfers between devices: 28.4 us -> 75.6 us  [the longest x28 50.5 us: flip(): return lax.ppermute(value, 'dp', [(k, k ^ bits) for k in range(n)])]
    all_to_all x1 -> x0, waiting for transfers between devices: 34.4 us -> none  [body(): shares = lax.all_to_all(shares, ('dp', 'tensor'), 0, 0, tiled=True)]
    ppermute x24 -> x15, starting transfers between devices: 69.4 us -> 53.3 us  [shift(): return lax.ppermute(value, 'tensor', [(k, (k + s) % 4) for k in range(4)])]
    squeeze x8 -> x2, local copies, waits for them, and re-layouts: 10 us -> 0.08 us  [body(): gq = jnp.concatenate([small[6, :cut], small[6, 384:384 + HD]])]
    pallas_call x7 -> x10, Pallas kernels: 101 us -> 111 us  [call(): pl.pallas_call(kernel, name=name, out_shape=[jax.ShapeDtypeStruct(s, d) f...]
    add x1 -> x4, other arithmetic: 0.07 us -> 9.38 us  [add(): total = total + value.astype(fl)]
  transfers between devices with their start and end apart: 67 -> 55, of which waited for: 20 -> 20; matrix products, arithmetic and copies ran while one was open for 9% -> 9% of each run, Pallas kernels for 8% -> 20%
where the time goes in v2:
time: 377 us; the launch traced here: 376 us
  waiting for transfers between devices  115 us (31%)
  Pallas kernels  111 us (29%)
  starting transfers between devices  93 us (25%)
  other arithmetic  32.3 us (9%)
  local copies, waits for them, and re-layouts  22.4 us (6%)
    pallas_call x10, Pallas kernels, call(): pl.pallas_call(kernel, name=name, out_shape=[jax.ShapeDtypeStruct(s, d) f...  111 us
    ppermute x15, starting transfers between devices, shift(): return lax.ppermute(value, 'tensor', [(k, (k + s) % 4) for k in range(4)])  53.3 us
    ppermute x28, waiting for transfers between devices, flip(): return lax.ppermute(value, 'dp', [(k, k ^ bits) for k in range(n)])  50.5 us
    ppermute x15, waiting for transfers between devices, shift(): return lax.ppermute(value, 'tensor', [(k, (k + s) % 4) for k in range(4)])  39.4 us
    ppermute x12, waiting for transfers between devices, along(): return lax.ppermute(value, 'tensor', [(k, k + step) for k in senders])  25.2 us
    ppermute x28, starting transfers between devices, flip(): return lax.ppermute(value, 'dp', [(k, k ^ bits) for k in range(n)])  22.5 us
    ppermute x12, starting transfers between devices, along(): return lax.ppermute(value, 'tensor', [(k, k + step) for k in senders])  17.2 us
    convert_element_type x3, other arithmetic, reduce_core(): return [add(near[r], got[r]).astype(bf) for r in range(4)]  10.8 us
  transfers between devices with their start and end apart: 55, of which 20 were waited for; matrix products, arithmetic and copies ran while one was open for 9% of the time, Pallas kernels for 20%

profile of v2, /device:TPU:0, one launch (start us, length us, event | category | flops | bytes accessed | tf_op | source)
XLA Modules:
  0.0 375.8 jit_solution(5264752490519607436)
XLA Ops:
  17.9 7.0 %collective-permute-done.1 = bf16[112,768]{1,0:T(8,128)(2,1)S(1)} collective-permute-done((bf16[112,768]{1,0:T(8,128)(2,1)S(1)}, bf16[112,768]{1,0:T(8,128)(2,1)S(1)}, u32[]{:S(2)}, u32[]{:S(2)}) %collective-permute-start.1) | collective-permute-done | bytes 172064 | tf_op jit(solution)/shard_map/ppermute | solution.py:338
  27.2 4.2 %collective-permute-start.10 = (bf16[192,768]{1,0:T(8,128)(2,1)S(1)}, bf16[192,768]{1,0:T(8,128)(2,1)S(1)}, u32[]{:S(2)}, u32[]{:S(2)}) collective-permute-start(bf16[192,768]{1,0:T(8,128)(2,1)S(1)} %pad_maximum_fusion.5), channel_id=1, source_target_pairs={{0,1},{1,2},{2,3},{3,0},{4,5},{5,6},{6,7},{7,4},{8,9},{9,10},{10,1... | collective-permute-start | bytes 884744 | tf_op jit(solution)/shard_map/ppermute | solution.py:338
  42.9 9.8 %collective-permute-done.11 = bf16[192,768]{1,0:T(8,128)(2,1)S(1)} collective-permute-done((bf16[192,768]{1,0:T(8,128)(2,1)S(1)}, bf16[192,768]{1,0:T(8,128)(2,1)S(1)}, u32[]{:S(2)}, u32[]{:S(2)}) %collective-permute-start.11) | collective-permute-done | bytes 294944 | tf_op jit(solution)/shard_map/ppermute | solution.py:338
  56.9 10.2 %collective-permute-done.4.refs_2_ = bf16[4,112,768]{2,1,0:T(8,128)(2,1)} collective-permute-done((bf16[4,112,768]{2,1,0:T(8,128)(2,1)S(1)}, bf16[4,112,768]{2,1,0:T(8,128)(2,1)}, u32[]{:S(2)}, u32[]{:S(2)}) %collective-permute-start.4) | collective-permute-done | bytes 688160 | tf_op jit(solution)/shard_map/ppermute | solution.py:334
  71.6 15.5 %attn_fwd.1 = (bf16[4,512,768]{2,1,0:T(8,128)(2,1)}, bf16[4,512,256]{2,1,0:T(8,128)(2,1)}, f32[4,3,1,512]{3,2,1,0:T(1,128)}, bf16[4,8,112,768]{3,2,1,0:T(8,128)(...) custom-call(s32[2]{0:T(128)} %pad_add_fusion.1.where_ref, ...), custom_call_target="tpu_custom_call" | custom-call | flops 1000 | bytes 1000 | tf_op jit(solution)/shard_map/attn_fwd/pallas_call | solution.py:317
  96.9 11.7 %collective-permute-done.15.refs_3_ = bf16[2,192,768]{2,1,0:T(8,128)(2,1)S(1)} collective-permute-done((bf16[2,192,768]{2,1,0:T(8,128)(2,1)S(1)}, bf16[2,192,768]{2,1,0:T(8,128)(2,1)S(1)}, u32[]{:S(2)}, u32[]{:S(2)}) %collective-permute-start.15) | collective-permute-done | bytes 589856 | tf_op jit(solution)/shard_map/ppermute | solution.py:334
  113.2 17.5 %ffn_fwd.1 = (bf16[512,768]{1,0:T(8,128)(2,1)}, f32[512,768]{1,0:T(8,128)}, bf16[4,512,768]{2,1,0:T(8,128)(2,1)}, f32[4,512,768]{2,1,0:T(8,128)}, f32[3,768]{1,0...) custom-call(s32[2]{0:T(128)} %pad_add_fusion.1.where_ref, ...), custom_call_target="tpu_custom_call" | custom-call | flops 1000 | bytes 1000 | tf_op jit(solution)/shard_map/ffn_fwd/pallas_call | solution.py:317
  130.6 8.4 %down_weights.1 = (bf16[4,4,96,768]{3,2,1,0:T(8,128)(2,1)}, bf16[4,4,96,768]{3,2,1,0:T(8,128)(2,1)}) custom-call(s32[2]{0:T(128)} %pad_add_fusion.1.where_ref, f32[512,768]{1,0:T(8,128)} %get-tuple-element.91.dr2_ref, bf16[4,512,768]{2,1,0:T(8,128)(2,1)} %get-tuple-element.101.act_ref), custom_call_target="tpu_custom_call" | custom-call | flops 1000 | bytes 1000 | tf_op jit(solution)/shard_map/down_weights/pallas_call | solution.py:317
  143.7 9.5 %down_bwd.1 = (bf16[4,512,768]{2,1,0:T(8,128)(2,1)}, f32[4,1,768]{2,1,0:T(1,128)}) custom-call(s32[2]{0:T(128)} %pad_add_fusion.1.where_ref, f32[512,768]{1,0:T(8,128)} %get-tuple-element.91.dr2_ref, f32[4,512,768]{2,1,0:T(8,128)} %get-tuple-element.92.slope_ref, bf16[4,8,96,768]{3,2,1,0:T(8,128)(2,1)} %get-tuple-element.93.weight_ref), custom_call_target="tpu_custom_call" | custom-call | flops 1000 | bytes 1000 | tf_op jit(solution)/shard_map/down_bwd/pallas_call | solution.py:317
  153.2 6.2 %collective-permute-done.22.refs_0_ = bf16[512,768]{1,0:T(8,128)(2,1)S(1)} collective-permute-done((bf16[512,768]{1,0:T(8,128)(2,1)S(1)}, bf16[512,768]{1,0:T(8,128)(2,1)S(1)}, u32[]{:S(2)}, u32[]{:S(2)}) %collective-permute-start.22) | collective-permute-done | bytes 786464 | tf_op jit(solution)/shard_map/ppermute | solution.py:342
  164.4 8.1 %up_weights.1 = (bf16[4,4,96,768]{3,2,1,0:T(8,128)(2,1)}, bf16[4,4,96,768]{3,2,1,0:T(8,128)(2,1)}) custom-call(s32[2]{0:T(128)} %pad_add_fusion.1.where_ref, bf16[512,768]{1,0:T(8,128)(2,1)} %get-tuple-element.85.first_ref, bf16[4,512,768]{2,1,0:T(8,128)(2,1)} %get-tuple-element.97.dup_ref, bf16[512,768]{1,0:T(8,128)(2,1)} %copy-done.9, ...), custom_call_target="tpu_custom_call" | custom-call | flops 1000 | bytes 1000 | tf_op jit(solution)/shard_map/up_weights/pallas_call | solution.py:317
  182.0 12.3 %up_bwd.1 = (f32[512,768]{1,0:T(8,128)}, bf16[4,512,256]{2,1,0:T(8,128)(2,1)}, f32[3,768]{1,0:T(4,128)}) custom-call(s32[2]{0:T(128)} %pad_add_fusion.1.where_ref, f32[512,768]{1,0:T(8,128)} %get-tuple-element.91.dr2_ref, bf16[4,512,768]{2,1,0:T(8,128)(2,1)} %get-tuple-element.97.dup_ref, f32[512,768]{1,0:T(8,128)} %get-tuple-element.84.xhat_ref, ...), custom_call_target="tpu_custom_call" | custom-call | flops 1000 | bytes 1000 | tf_op jit(solution)/shard_map/up_bwd/pallas_call | solution.py:317
  198.6 9.7 %collective-permute-done.30 = bf16[4,96,768]{2,1,0:T(8,128)(2,1)} collective-permute-done((bf16[4,96,768]{2,1,0:T(8,128)(2,1)}, bf16[4,96,768]{2,1,0:T(8,128)(2,1)}, u32[]{:S(2)}, u32[]{:S(2)}) %collective-permute-start.30) | collective-permute-done | bytes 589856 | tf_op jit(solution)/shard_map/ppermute | solution.py:334
  225.8 11.5 %collective-permute-done.37.refs_5_ = bf16[96,768]{1,0:T(8,128)(2,1)S(1)} collective-permute-done((bf16[96,768]{1,0:T(8,128)(2,1)S(1)}, bf16[96,768]{1,0:T(8,128)(2,1)S(1)}, u32[]{:S(2)}, u32[]{:S(2)}) %collective-permute-start.37) | collective-permute-done | bytes 147488 | tf_op jit(solution)/shard_map/ppermute | solution.py:338
  238.1 20.4 %attn_bwd.1 = (bf16[512,768]{1,0:T(8,128)(2,1)}, bf16[4,512,768]{2,1,0:T(8,128)(2,1)}, f32[4,1,768]{2,1,0:T(1,128)}) custom-call(s32[2]{0:T(128)} %pad_add_fusion.1.where_ref, s32[1,512]{1,0:T(1,128)} %constant_dynamic-slice_fusion.2.seg_row_ref, s32[512,1]{1,0:T(8,128)} %copy.38.seg_col_ref, bf16[4,512,768]{2,1,0:T(8,128)(2,1)} %get-tuple-element.108.proj_ref, ...), custom_call_target="tpu_custom_call" | custom-call | flops 1000 | bytes 1000 | tf_op jit(solution)/shard_map/attn_bwd/pallas_call | solution.py:317
  261.7 9.9 %attn_weights.1 = (bf16[4,4,112,768]{3,2,1,0:T(8,128)(2,1)}, bf16[4,4,112,768]{3,2,1,0:T(8,128)(2,1)}) custom-call(s32[2]{0:T(128)} %pad_add_fusion.1.where_ref, bf16[512,768]{1,0:T(8,128)(2,1)} %dynamic-slice_bitcast_fusion.1.x_ref, bf16[4,512,768]{2,1,0:T(8,128)(2,1)} %get-tuple-element.122.dproj_ref, bf16[4,512,256]{2,1,0:T(8,128)(2,1)} %get-tuple-element.123.ctx_ref, ...), custom_call_target="tpu_custom_call" | custom-call | flops 1000 | bytes 1000 | tf_op jit(solution)/shard_map/attn_weights/pallas_call | solution.py:317
  278.7 8.2 %collective-permute-start.52 = (bf16[96,768]{1,0:T(8,128)(2,1)}, bf16[96,768]{1,0:T(8,128)(2,1)S(1)}, u32[]{:S(2)}, u32[]{:S(2)}) collective-permute-start(bf16[96,768]{1,0:T(8,128)(2,1)} %get-tuple-element.210.refs_7_), channel_id=1, source_target_pairs={{0,1},{1,2},{2,3},{3,0},{4,5},{5,6},{6,7},{7,4},{8,9},{9,10},{10,1... | collective-permute-start | bytes 442376 | tf_op jit(solution)/shard_map/ppermute | solution.py:338
  287.0 4.8 %collective-permute-start.53 = (bf16[96,768]{1,0:T(8,128)(2,1)S(1)}, bf16[96,768]{1,0:T(8,128)(2,1)S(1)}, u32[]{:S(2)}, u32[]{:S(2)}) collective-permute-start(bf16[96,768]{1,0:T(8,128)(2,1)S(1)} %copy-done.38), channel_id=1, source_target_pairs={{0,2},{1,3},{2,0},{3,1},{4,6},{5,7},{6,4},{7,5},{8,10},{9,11},{10,... | collective-permute-start | bytes 442376 | tf_op jit(solution)/shard_map/ppermute | solution.py:338
  291.8 11.9 %collective-permute-start.54 = (bf16[96,768]{1,0:T(8,128)(2,1)S(1)}, bf16[96,768]{1,0:T(8,128)(2,1)S(1)}, u32[]{:S(2)}, u32[]{:S(2)}) collective-permute-start(bf16[96,768]{1,0:T(8,128)(2,1)S(1)} %copy-done.37), channel_id=1, source_target_pairs={{0,3},{1,0},{2,1},{3,2},{4,7},{5,4},{6,5},{7,6},{8,11},{9,8},{10,9... | collective-permute-start | bytes 442376 | tf_op jit(solution)/shard_map/ppermute | solution.py:338
  317.3 4.6 %place_rows.2 = bf16[4,512,768]{2,1,0:T(8,128)(2,1)} custom-call(s32[2]{0:T(128)} %pad_add_fusion.where_ref, bf16[512,768]{1,0:T(8,128)(2,1)} %get-tuple-element.90.own_ref, bf16[512,768]{1,0:T(8,128)(2,1)} %copy-done.9, bf16[512,768]{1,0:T(8,128)(2,1)} %copy-done.10, bf16[512,768]{1,0:T(8,128)(2,1)} %copy-done.5, bf16[512,768]{1,0:T(8,128)(2,1)} %copy-done.6, ...), custom_call_target="tpu_custom_call" | custom-call | flops 1000 | bytes 1000 | tf_op jit(solution)/shard_map/place_rows/pallas_call | solution.py:317
  323.9 5.8 %collective-permute-done.42.refs_3_ = bf16[512,768]{1,0:T(8,128)(2,1)} collective-permute-done((bf16[512,768]{1,0:T(8,128)(2,1)}, bf16[512,768]{1,0:T(8,128)(2,1)}, u32[]{:S(2)}, u32[]{:S(2)}) %collective-permute-start.42) | collective-permute-done | bytes 786464 | tf_op jit(solution)/shard_map/ppermute | solution.py:342
  331.8 13.3 %collective-permute-done.47 = bf16[4,112,768]{2,1,0:T(8,128)(2,1)} collective-permute-done((bf16[4,112,768]{2,1,0:T(8,128)(2,1)}, bf16[4,112,768]{2,1,0:T(8,128)(2,1)}, u32[]{:S(2)}, u32[]{:S(2)}) %collective-permute-start.47) | collective-permute-done | bytes 688160 | tf_op jit(solution)/shard_map/ppermute | solution.py:334
  354.7 7.0 %collective-permute-done.44.refs_5_ = bf16[512,768]{1,0:T(8,128)(2,1)S(1)} collective-permute-done((bf16[512,768]{1,0:T(8,128)(2,1)}, bf16[512,768]{1,0:T(8,128)(2,1)S(1)}, u32[]{:S(2)}, u32[]{:S(2)}) %collective-permute-start.44) | collective-permute-done | bytes 786464 | tf_op jit(solution)/shard_map/ppermute | solution.py:342
  362.7 4.5 %place_rows.3 = bf16[4,512,768]{2,1,0:T(8,128)(2,1)} custom-call(s32[2]{0:T(128)} %pad_add_fusion.where_ref, bf16[512,768]{1,0:T(8,128)(2,1)} %get-tuple-element.121.own_ref, bf16[512,768]{1,0:T(8,128)(2,1)} %collective-permute-done.33.refs_0_, bf16[512,768]{1,0:T(8,128)(2,1)} %collective-permute-done.34.refs_1_, ...), custom_call_target="tpu_custom_call" | custom-call | flops 1000 | bytes 1000 | tf_op jit(solution)/shard_map/place_rows/pallas_call | solution.py:317
  (301 shorter events, 141.5 us)
Async XLA Ops:
  33.9 23.0 %collective-permute-start.3 = (bf16[4,112,768]{2,1,0:T(8,128)(2,1)S(1)}, bf16[4,112,768]{2,1,0:T(8,128)(2,1)}, u32[]{:S(2)}, u32[]{:S(2)}) collective-permute-start(bf16[4,112,768]{2,1,0:T(8,128)(2,1)S(1)} %pad_maximum_fusion.1.refs_0_), channel_id=1, source_target_pairs={{0,8},{4,12},{8,0},{12,4},{16,24},{20,28},{24,16},{28,20},{1,9},{5... | collective-permute-start | bytes 2064392 | tf_op jit(solution)/shard_map/ppermute | solution.py:334
  35.4 31.7 %collective-permute-start.4 = (bf16[4,112,768]{2,1,0:T(8,128)(2,1)S(1)}, bf16[4,112,768]{2,1,0:T(8,128)(2,1)}, u32[]{:S(2)}, u32[]{:S(2)}) collective-permute-start(bf16[4,112,768]{2,1,0:T(8,128)(2,1)S(1)} %pad_maximum_fusion.1.refs_0_), channel_id=1, source_target_pairs={{0,16},{4,20},{8,24},{12,28},{16,0},{20,4},{24,8},{28,12},{1,17},{... | collective-permute-start | bytes 2064392 | tf_op jit(solution)/shard_map/ppermute | solution.py:334
  40.5 27.5 %collective-permute-start.5 = (bf16[4,112,768]{2,1,0:T(8,128)(2,1)S(1)}, bf16[4,112,768]{2,1,0:T(8,128)(2,1)}, u32[]{:S(2)}, u32[]{:S(2)}) collective-permute-start(bf16[4,112,768]{2,1,0:T(8,128)(2,1)S(1)} %pad_maximum_fusion.1.refs_0_), channel_id=1, source_target_pairs={{0,24},{4,28},{8,16},{12,20},{16,8},{20,12},{24,0},{28,4},{1,25},{... | collective-permute-start | bytes 2064392 | tf_op jit(solution)/shard_map/ppermute | solution.py:334
  53.9 37.2 %collective-permute-start.13 = (bf16[4,192,768]{2,1,0:T(8,128)(2,1)}, bf16[4,192,768]{2,1,0:T(8,128)(2,1)}, u32[]{:S(2)}, u32[]{:S(2)}) collective-permute-start(bf16[4,192,768]{2,1,0:T(8,128)(2,1)} %pad_maximum_fusion.refs_8_.refs_0_), channel_id=1, source_target_pairs={{0,8},{4,12},{8,0},{12,4},{16,24},{20,28},{24,16},{28,20},{1,9},{5... | collective-permute-start | bytes 3538952 | tf_op jit(solution)/shard_map/ppermute | solution.py:334
  55.4 36.9 %collective-permute-start.14 = (bf16[4,192,768]{2,1,0:T(8,128)(2,1)}, bf16[4,192,768]{2,1,0:T(8,128)(2,1)}, u32[]{:S(2)}, u32[]{:S(2)}) collective-permute-start(bf16[4,192,768]{2,1,0:T(8,128)(2,1)} %pad_maximum_fusion.refs_8_.refs_0_), channel_id=1, source_target_pairs={{0,16},{4,20},{8,24},{12,28},{16,0},{20,4},{24,8},{28,12},{1,17},{... | collective-permute-start | bytes 3538952 | tf_op jit(solution)/shard_map/ppermute | solution.py:334
  71.1 40.2 %collective-permute-start.17 = (bf16[4,192,768]{2,1,0:T(8,128)(2,1)}, bf16[4,192,768]{2,1,0:T(8,128)(2,1)S(1)}, u32[]{:S(2)}, u32[]{:S(2)}) collective-permute-start(bf16[4,192,768]{2,1,0:T(8,128)(2,1)} %pad_maximum_fusion.refs_8_.refs_0_), channel_id=1, source_target_pairs={{0,4},{4,0},{8,12},{12,8},{16,20},{20,16},{24,28},{28,24},{1,5},{5... | collective-permute-start | bytes 3538952 | tf_op jit(solution)/shard_map/ppermute | solution.py:334
  139.1 35.4 %collective-permute-start.26 = (bf16[4,4,96,768]{3,2,1,0:T(8,128)(2,1)}, bf16[4,4,96,768]{3,2,1,0:T(8,128)(2,1)}, u32[]{:S(2)}, u32[]{:S(2)}) collective-permute-start(bf16[4,4,96,768]{3,2,1,0:T(8,128)(2,1)} %get-tuple-element.103), channel_id=1, source_target_pairs={{0,4},{4,0},{8,12},{12,8},{16,20},{20,16},{24,28},{28,24},{1,5},{5... | collective-permute-start | bytes 7077896 | tf_op jit(solution)/shard_map/ppermute | solution.py:334
  172.5 43.7 %collective-permute-start.32 = (bf16[4,4,96,768]{3,2,1,0:T(8,128)(2,1)}, bf16[4,4,96,768]{3,2,1,0:T(8,128)(2,1)}, u32[]{:S(2)}, u32[]{:S(2)}) collective-permute-start(bf16[4,4,96,768]{3,2,1,0:T(8,128)(2,1)} %get-tuple-element.116), channel_id=1, source_target_pairs={{0,4},{4,0},{8,12},{12,8},{16,20},{20,16},{24,28},{28,24},{1,5},{5... | collective-permute-start | bytes 7077896 | tf_op jit(solution)/shard_map/ppermute | solution.py:334
  173.2 23.1 %collective-permute-start.25 = (bf16[512,768]{1,0:T(8,128)(2,1)}, bf16[512,768]{1,0:T(8,128)(2,1)S(1)}, u32[]{:S(2)}, u32[]{:S(2)}) collective-permute-start(bf16[512,768]{1,0:T(8,128)(2,1)} %copy-done.10), channel_id=1, source_target_pairs={{1,0},{2,1},{5,4},{6,5},{9,8},{10,9},{13,12},{14,13},{17,16},{18,1... | collective-permute-start | bytes 2359304 | tf_op jit(solution)/shard_map/ppermute | solution.py:342
  179.9 28.4 %collective-permute-start.30 = (bf16[4,96,768]{2,1,0:T(8,128)(2,1)}, bf16[4,96,768]{2,1,0:T(8,128)(2,1)}, u32[]{:S(2)}, u32[]{:S(2)}) collective-permute-start(bf16[4,96,768]{2,1,0:T(8,128)(2,1)} %get-tuple-element.202.refs_2_), channel_id=1, source_target_pairs={{0,16},{4,20},{8,24},{12,28},{16,0},{20,4},{24,8},{28,12},{1,17},{... | collective-permute-start | bytes 1769480 | tf_op jit(solution)/shard_map/ppermute | solution.py:334
  181.2 27.1 %collective-permute-start.31 = (bf16[4,96,768]{2,1,0:T(8,128)(2,1)}, bf16[4,96,768]{2,1,0:T(8,128)(2,1)}, u32[]{:S(2)}, u32[]{:S(2)}) collective-permute-start(bf16[4,96,768]{2,1,0:T(8,128)(2,1)} %get-tuple-element.201.refs_3_), channel_id=1, source_target_pairs={{0,24},{4,28},{8,16},{12,20},{16,8},{20,12},{24,0},{28,4},{1,25},{... | collective-permute-start | bytes 1769480 | tf_op jit(solution)/shard_map/ppermute | solution.py:334
  196.3 62.1 %collective-permute-start.27 = (bf16[512,768]{1,0:T(8,128)(2,1)S(1)}, bf16[512,768]{1,0:T(8,128)(2,1)S(1)}, u32[]{:S(2)}, u32[]{:S(2)}) collective-permute-start(bf16[512,768]{1,0:T(8,128)(2,1)S(1)} %collective-permute-done.24.refs_0_.refs_2_), channel_id=1, source_target_pairs={{2,3},{6,7},{10,11},{14,15},{18,19},{22,23},{26,27},{30,31}} | collective-permute-start | bytes 2359304 | tf_op jit(solution)/shard_map/ppermute | solution.py:342
  197.2 61.3 %collective-permute-start.28 = (bf16[512,768]{1,0:T(8,128)(2,1)S(1)}, bf16[512,768]{1,0:T(8,128)(2,1)S(1)}, u32[]{:S(2)}, u32[]{:S(2)}) collective-permute-start(bf16[512,768]{1,0:T(8,128)(2,1)S(1)} %collective-permute-done.25.refs_1_.refs_3_), channel_id=1, source_target_pairs={{1,0},{5,4},{9,8},{13,12},{17,16},{21,20},{25,24},{29,28}} | collective-permute-start | bytes 2359304 | tf_op jit(solution)/shard_map/ppermute | solution.py:342
  222.6 35.9 %collective-permute-start.38 = (bf16[4,96,768]{2,1,0:T(8,128)(2,1)}, bf16[4,96,768]{2,1,0:T(8,128)(2,1)}, u32[]{:S(2)}, u32[]{:S(2)}) collective-permute-start(bf16[4,96,768]{2,1,0:T(8,128)(2,1)} %get-tuple-element.199.refs_7_), channel_id=1, source_target_pairs={{0,8},{4,12},{8,0},{12,4},{16,24},{20,28},{24,16},{28,20},{1,9},{5... | collective-permute-start | bytes 1769480 | tf_op jit(solution)/shard_map/ppermute | solution.py:334
  225.1 33.4 %collective-permute-start.39 = (bf16[4,96,768]{2,1,0:T(8,128)(2,1)}, bf16[4,96,768]{2,1,0:T(8,128)(2,1)}, u32[]{:S(2)}, u32[]{:S(2)}) collective-permute-start(bf16[4,96,768]{2,1,0:T(8,128)(2,1)} %get-tuple-element.198.refs_8_), channel_id=1, source_target_pairs={{0,16},{4,20},{8,24},{12,28},{16,0},{20,4},{24,8},{28,12},{1,17},{... | collective-permute-start | bytes 1769480 | tf_op jit(solution)/shard_map/ppermute | solution.py:334
  271.6 33.8 %collective-permute-start.45 = (bf16[4,4,112,768]{3,2,1,0:T(8,128)(2,1)}, bf16[4,4,112,768]{3,2,1,0:T(8,128)(2,1)S(1)}, u32[]{:S(2)}, u32[]{:S(2)}) collective-permute-start(bf16[4,4,112,768]{3,2,1,0:T(8,128)(2,1)} %get-tuple-element.138), channel_id=1, source_target_pairs={{0,4},{4,0},{8,12},{12,8},{16,20},{20,16},{24,28},{28,24},{1,5},{5... | collective-permute-start | bytes 8257544 | tf_op jit(solution)/shard_map/ppermute | solution.py:334
  274.0 29.7 %collective-permute-start.34 = (bf16[512,768]{1,0:T(8,128)(2,1)}, bf16[512,768]{1,0:T(8,128)(2,1)}, u32[]{:S(2)}, u32[]{:S(2)}) collective-permute-start(bf16[512,768]{1,0:T(8,128)(2,1)} %get-tuple-element.121.own_ref), channel_id=1, source_target_pairs={{1,0},{2,1},{3,2},{5,4},{6,5},{7,6},{9,8},{10,9},{11,10},{13,12},{... | collective-permute-start | bytes 2359304 | tf_op jit(solution)/shard_map/ppermute | solution.py:342
  278.7 31.4 %collective-permute-start.52 = (bf16[96,768]{1,0:T(8,128)(2,1)}, bf16[96,768]{1,0:T(8,128)(2,1)S(1)}, u32[]{:S(2)}, u32[]{:S(2)}) collective-permute-start(bf16[96,768]{1,0:T(8,128)(2,1)} %get-tuple-element.210.refs_7_), channel_id=1, source_target_pairs={{0,1},{1,2},{2,3},{3,0},{4,5},{5,6},{6,7},{7,4},{8,9},{9,10},{10,1... | collective-permute-start | bytes 442376 | tf_op jit(solution)/shard_map/ppermute | solution.py:338
  287.0 26.6 %collective-permute-start.53 = (bf16[96,768]{1,0:T(8,128)(2,1)S(1)}, bf16[96,768]{1,0:T(8,128)(2,1)S(1)}, u32[]{:S(2)}, u32[]{:S(2)}) collective-permute-start(bf16[96,768]{1,0:T(8,128)(2,1)S(1)} %copy-done.38), channel_id=1, source_target_pairs={{0,2},{1,3},{2,0},{3,1},{4,6},{5,7},{6,4},{7,5},{8,10},{9,11},{10,... | collective-permute-start | bytes 442376 | tf_op jit(solution)/shard_map/ppermute | solution.py:338
  305.4 24.2 %collective-permute-start.42 = (bf16[512,768]{1,0:T(8,128)(2,1)}, bf16[512,768]{1,0:T(8,128)(2,1)}, u32[]{:S(2)}, u32[]{:S(2)}) collective-permute-start(bf16[512,768]{1,0:T(8,128)(2,1)} %collective-permute-done.34.refs_1_), channel_id=1, source_target_pairs={{1,0},{2,1},{5,4},{6,5},{9,8},{10,9},{13,12},{14,13},{17,16},{18,1... | collective-permute-start | bytes 2359304 | tf_op jit(solution)/shard_map/ppermute | solution.py:342
  313.5 31.6 %collective-permute-start.47 = (bf16[4,112,768]{2,1,0:T(8,128)(2,1)}, bf16[4,112,768]{2,1,0:T(8,128)(2,1)}, u32[]{:S(2)}, u32[]{:S(2)}) collective-permute-start(bf16[4,112,768]{2,1,0:T(8,128)(2,1)} %get-tuple-element.194), channel_id=1, source_target_pairs={{0,16},{4,20},{8,24},{12,28},{16,0},{20,4},{24,8},{28,12},{1,17},{... | collective-permute-start | bytes 2064392 | tf_op jit(solution)/shard_map/ppermute | solution.py:334
  314.3 30.8 %collective-permute-start.48 = (bf16[4,112,768]{2,1,0:T(8,128)(2,1)}, bf16[4,112,768]{2,1,0:T(8,128)(2,1)}, u32[]{:S(2)}, u32[]{:S(2)}) collective-permute-start(bf16[4,112,768]{2,1,0:T(8,128)(2,1)} %get-tuple-element.193), channel_id=1, source_target_pairs={{0,24},{4,28},{8,16},{12,20},{16,8},{20,12},{24,0},{28,4},{1,25},{... | collective-permute-start | bytes 2064392 | tf_op jit(solution)/shard_map/ppermute | solution.py:334
  329.6 25.1 %collective-permute-start.43 = (bf16[512,768]{1,0:T(8,128)(2,1)}, bf16[512,768]{1,0:T(8,128)(2,1)S(1)}, u32[]{:S(2)}, u32[]{:S(2)}) collective-permute-start(bf16[512,768]{1,0:T(8,128)(2,1)} %collective-permute-done.41.refs_2_), channel_id=1, source_target_pairs={{2,3},{6,7},{10,11},{14,15},{18,19},{22,23},{26,27},{30,31}} | collective-permute-start | bytes 2359304 | tf_op jit(solution)/shard_map/ppermute | solution.py:342
  330.3 31.4 %collective-permute-start.44 = (bf16[512,768]{1,0:T(8,128)(2,1)}, bf16[512,768]{1,0:T(8,128)(2,1)S(1)}, u32[]{:S(2)}, u32[]{:S(2)}) collective-permute-start(bf16[512,768]{1,0:T(8,128)(2,1)} %collective-permute-done.42.refs_3_), channel_id=1, source_target_pairs={{1,0},{5,4},{9,8},{13,12},{17,16},{21,20},{25,24},{29,28}} | collective-permute-start | bytes 2359304 | tf_op jit(solution)/shard_map/ppermute | solution.py:342
  (86 other events, 1056.4 us)

commit v3 on v2

--- a/solution.py
+++ b/solution.py
@@ -43,10 +43,10 @@
 
 
 def assemble(where_ref, pieces, plan, *targets):
-    for ref, (r, shifts) in zip(pieces, plan):
+    for ref, (r, hops) in zip(pieces, plan):
         slab = jnp.bitwise_xor(where_ref[0], r)
-        for k, s in enumerate(shifts):
-            group = jnp.bitwise_and(where_ref[1] + 4 - s, 3)
+        for k, hop in enumerate(hops):
+            group = jnp.bitwise_xor(where_ref[1], hop)
             first = 0
             for target in targets:
                 last = first + target.shape[2]
@@ -54,26 +54,30 @@
                 first = last
 
 
-def scatter_slabs(where_ref, group, value, near_ref, far_ref, extra=None):
-    shift = jnp.bitwise_and(group + 4 - where_ref[1], 3)
+def scatter_slabs(where_ref, group, value, near_ref, far_refs, extra=None, x_last=False):
+    hop = jnp.bitwise_xor(group, where_ref[1])
+    hop = 2 * jnp.bitwise_and(hop, 1) + jnp.right_shift(hop, 1)
     chip = jnp.right_shift(where_ref[0], 1)
     core = jnp.bitwise_and(where_ref[0], 1)
 
-    def put(even_ref, odd_ref):
-        for j in range(SLABS):
-            out_ref = odd_ref if j % 2 else even_ref
-            place = jnp.bitwise_xor(chip, j // 2)
-            out_ref[place, shift, :DEPTH] = value[DEPTH * j : DEPTH * (j + 1)]
-            if extra is not None:
-                out_ref[place, shift, DEPTH:] = extra
-
-    @pl.when(core == 0)
-    def _():
-        put(near_ref, far_ref)
-
-    @pl.when(core == 1)
-    def _():
-        put(far_ref, near_ref)
+    def put(near, far):
+        for j in range(SLABS // 2):
+            place = jnp.bitwise_xor(chip, j)
+            if x_last:
+                place = 2 * jnp.bitwise_and(place, 1) + jnp.right_shift(place, 1)
+            half, low = jnp.right_shift(place, 1), jnp.bitwise_and(place, 1)
+
+            def store(ref, index, slab):
+                ref[index, hop, :DEPTH] = value[DEPTH * slab : DEPTH * (slab + 1)]
+                if extra is not None:
+                    ref[index, hop, DEPTH:] = extra
+
+            store(near_ref, place, 2 * j + near)
+            for k in (0, 1):
+                pl.when(half == k)(functools.partial(store, far_refs[k], low, 2 * j + far))
+
+    pl.when(core == 0)(functools.partial(put, 0, 1))
+    pl.when(core == 1)(functools.partial(put, 1, 0))
 
 
 def matrix(ref, group):
@@ -171,10 +175,10 @@
     small_ref[2:3] = jnp.sum(dr2, axis=0, keepdims=True)
 
 
-def down_weights_kernel(where_ref, dr2_ref, act_ref, near_ref, far_ref):
+def down_weights_kernel(where_ref, dr2_ref, act_ref, near_ref, *far_refs):
     def step(g, carry):
         dffn = dr2_ref[...].astype(bf)
-        scatter_slabs(where_ref, g, tn(dffn, act_ref[g]).astype(bf), near_ref, far_ref)
+        scatter_slabs(where_ref, g, tn(dffn, act_ref[g]).astype(bf), near_ref, far_refs, x_last=True)
         return carry
 
     lax.fori_loop(0, 4, step, 0)
@@ -192,10 +196,10 @@
 
 
 def up_weights_kernel(where_ref, first_ref, dup_ref, *refs):
-    near_ref, far_ref = refs[-2:]
+    near_ref, *far_refs = refs
 
     def step(g, carry):
-        scatter_slabs(where_ref, g, tn(first_ref[...], dup_ref[g]).astype(bf), near_ref, far_ref)
+        scatter_slabs(where_ref, g, tn(first_ref[...], dup_ref[g]).astype(bf), near_ref, far_refs)
         return carry
 
     lax.fori_loop(0, 4, step, 0)
@@ -274,7 +278,7 @@
 
 
 def attn_weights_kernel(where_ref, x_ref, dproj_ref, ctx_ref, dr1_ref, bias_ref, b_up_ref, one_ref, two_ref, *refs):
-    near_ref, far_ref, small_ref = refs[-3:]
+    near_ref, *far_refs, small_ref = refs
     small_ref[...] = jnp.zeros_like(small_ref)
     small_ref[0:2] = one_ref[0:2]
     small_ref[2:4] = two_ref[0:2]
@@ -287,26 +291,16 @@
         main = tn(x_ref[...], dproj_ref[g])
         side = tn(dr1_ref[...].astype(bf), ctx_ref[g])
         whole = jnp.concatenate([main[:, :512], main[:, 512:] + side], axis=1).astype(bf)
-        scatter_slabs(where_ref, g, whole, near_ref, far_ref, small_ref[...].astype(bf))
+        scatter_slabs(where_ref, g, whole, near_ref, far_refs, small_ref[...].astype(bf))
         return carry
 
     lax.fori_loop(0, 4, grads, 0)
 
 
-def place_kernel(where_ref, own_ref, *refs):
+def place_kernel(where_ref, *refs):
     out_ref = refs[-1]
-    spot = where_ref[1]
-    out_ref[spot] = own_ref[...]
-    for d in (1, 2, 3):
-        up_ref, down_ref = refs[2 * d - 2], refs[2 * d - 1]
-
-        @pl.when(spot >= d)
-        def _():
-            out_ref[jnp.maximum(spot - d, 0)] = up_ref[...]
-
-        @pl.when(spot + d < 4)
-        def _():
-            out_ref[jnp.minimum(spot + d, 3)] = down_ref[...]
+    for d, ref in enumerate(refs[:-1]):
+        out_ref[jnp.bitwise_and(where_ref[1] + 4 - d, 3)] = ref[...]
 
 
 smem = pl.BlockSpec(memory_space=pltpu.SMEM)
@@ -314,16 +308,18 @@
 
 
 def call(kernel, name, outs, where, *args, scratch=(), after=()):
+    if after:
+        (where,) = late([where], *after)
     return pl.pallas_call(
         kernel,
         name=name,
         out_shape=[jax.ShapeDtypeStruct(s, d) for s, d in outs],
-        in_specs=[smem] + [vmem] * len(args) + [pl.BlockSpec(memory_space=pl.ANY)] * len(after),
+        in_specs=[smem] + [vmem] * len(args),
         out_specs=[vmem] * len(outs),
         scratch_shapes=list(scratch),
         compiler_params=pltpu.CompilerParams(vmem_limit_bytes=VMEM_LIMIT),
         cost_estimate=pl.CostEstimate(flops=COST, bytes_accessed=COST, transcendentals=0),
-    )(where, *args, *after)
+    )(where, *args)
 
 
 COST = 1000
@@ -334,12 +330,16 @@
     return lax.ppermute(value, "dp", [(k, k ^ bits) for k in range(n)])
 
 
-def shift(value, s):
-    return lax.ppermute(value, "tensor", [(k, (k + s) % 4) for k in range(4)])
-
-
-def along(value, step, senders):
-    return lax.ppermute(value, "tensor", [(k, k + step) for k in senders])
+def cross(value, bits):
+    return lax.ppermute(value, "tensor", [(k, k ^ bits) for k in range(4)])
+
+
+def rotate(value):
+    return lax.ppermute(value, "tensor", [(k, (k + 1) % 4) for k in range(4)])
+
+
+def late(values, *gates):
+    return list(lax.optimization_barrier((*values, *gates))[: len(values)])
 
 
 def with_core(near):
@@ -350,15 +350,16 @@
 
 
 def tensor_stack(shard):
-    return jnp.stack([shard] + [shift(shard, s) for s in (1, 2, 3)])
+    return jnp.stack([shard] + [cross(shard, hop) for hop in (1, 2, 3)])
+
+
+def tensor_stack_doubling(shard):
+    pair = jnp.stack([shard, cross(shard, 1)])
+    return jnp.concatenate([pair, cross(pair, 2)])
 
 
 def gather_direct(own):
     return with_core([(own, (0, ALL))] + [(flip(own, r), (r, ALL)) for r in (2, 4, 6)])
-
-
-def late(values, gate):
-    return list(lax.optimization_barrier((*values, gate))[:-1])
 
 
 def gather_staged(own, gate):
@@ -378,19 +379,33 @@
     return total
 
 
-def reduce_core(near, far, gate):
-    (got,) = late([flip(far, 1)], gate)
-    return [add(near[r], got[r]).astype(bf) for r in range(4)]
+def reduce_core(near, far, gate, cuts=(0, 2)):
+    got = late([flip(half, 1) for half in far], gate)
+    return [
+        add(near[2 * k + a : 2 * k + b], got[k][a:b]).astype(bf) for k in (0, 1) for a, b in zip(cuts, cuts[1:])
+    ]
+
+
+def reduce_pair(half, axis, gate):
+    (got,) = late([flip(half[1], 2 * axis)], gate)
+    return [add(half[0][k], got[k]).astype(bf) for k in (0, 1)]
+
+
+def reduce_chip(pair, axis, gate):
+    (got,) = late([flip(pair[1], 2 * axis)], gate)
+    return [add(pair[0][:2], got[:2]).astype(bf), add(pair[0][2:], got[2:]).astype(bf)]
 
 
 def reduce_plane(half, gate):
+    half = [h[0] for h in half]
     got = late([flip(half[r], 2 * r) for r in (1, 2, 3)], gate)
-    sums = [add(half[0][s], *[g[s] for g in got]) for s in range(4)]
-    return [sums[0]] + [v.astype(bf) for v in sums[1:]]
+    return [add(half[0][k : k + 2], *[g[k : k + 2] for g in got]).astype(bf) for k in (0, 2)]
 
 
 def reduce_tensor(plane, gate):
-    return [plane[0]] + late([shift(plane[s], s) for s in (1, 2, 3)], gate)
+    (got,) = late([cross(plane[1], 1)], gate)
+    near, far = add(plane[0][0], got[0]), add(plane[0][1], got[1]).astype(bf)
+    return add(near, cross(far, 2))
 
 
 def gather_plain(shard, extra=None):
@@ -400,12 +415,13 @@
         extra = lax.all_gather(lax.psum(extra, "dp"), "tensor", axis=0)[:, None].astype(bf)
         extra = jnp.concatenate([extra] + [jnp.zeros_like(extra)] * (SLABS - 1), axis=1)
         whole = jnp.concatenate([whole, extra], axis=2)
-    order = [(4 - s) % 4 for s in range(4)]
-    return [(jnp.stack([whole[t, r] for t in order]), (r, ALL)) for r in range(SLABS)]
-
-
-def reduce_plain(near, far):
-    grad = jnp.stack([near, far], axis=1).reshape(SLABS, 4, -1, 768).astype(fl)
+    return [(whole[:, r], (r, ALL)) for r in range(SLABS)]
+
+
+def reduce_plain(near, far, x_last=False):
+    order = jnp.array([0, 2, 1, 3])
+    grad = jnp.stack([near, jnp.concatenate(far)], axis=1)[:, :, order]
+    grad = (grad[order] if x_last else grad).reshape(SLABS, 4, -1, 768).astype(fl)
     whole = grad[:, :, :DEPTH].transpose(1, 0, 2, 3).reshape(4, SLABS * DEPTH, 768)
     part = lax.psum_scatter(whole, "tensor", scatter_dimension=0, tiled=True)
     part = lax.psum_scatter(part[0], "dp", scatter_dimension=0, tiled=True)
@@ -415,13 +431,13 @@
     return jnp.concatenate([part, extra])
 
 
-def forward_rows(up, down, d, gate):
-    return late([along(up, 1, range(d - 1, 3)), along(down, -1, range(1, 5 - d))], gate)
-
-
-def place_rows(row, steps, where):
-    pieces = [piece for step in steps for piece in step]
-    return call(place_kernel, "place_rows", [((4,) + row.shape, row.dtype)], where, row, *pieces)[0]
+def next_row(row, gate):
+    (row,) = late([rotate(row)], gate)
+    return row
+
+
+def place_rows(rows, where):
+    return call(place_kernel, "place_rows", [((4,) + rows[0].shape, rows[0].dtype)], where, *rows)[0]
 
 
 def moment_update(state, grad):
@@ -481,15 +497,15 @@
     row_f, row_b = ((length, width), fl), ((length, width), bf)
     whole = ((4, SLABS, DEPTH, 768), bf)
     attn_whole = ((4, SLABS, DEPTH + EXTRA, 768), bf)
-    grad_shape = ((4, 4, DEPTH, 768), bf)
-    attn_grad_shape = ((4, 4, DEPTH + EXTRA, 768), bf)
+    grad_shapes = [((n, 4, DEPTH, 768), bf) for n in (4, 2, 2)]
+    attn_grad_shapes = [((n, 4, DEPTH + EXTRA, 768), bf) for n in (4, 2, 2)]
     thin = ((4, 1, 768), fl)
 
     if fast:
         own = tensor_stack(jnp.concatenate([attn_shard, extra]))
         attn_pieces = gather_direct(own)
-        (ffn_shard,) = late([jnp.concatenate([up_shard, down_shard])], attn_pieces[4][0])
-        ffn_own = tensor_stack(ffn_shard)
+        (ffn_shard,) = late([jnp.concatenate([up_shard, down_shard])], own)
+        ffn_own = tensor_stack_doubling(ffn_shard)
         wait = [ffn_own]
     else:
         attn_pieces = gather_plain(attn_shard, extra)
@@ -515,47 +531,55 @@
         [row_b, row_f, (wide, bf), (wide, fl), ((3, width), fl), whole, whole],
         where, xhat, first, dy, vec, b_up, *pieces,
     )
-    down_near, down_far = call(
-        down_weights_kernel, "down_weights", [grad_shape, grad_shape], where, dr2, act,
+    down_near, *down_far = call(
+        down_weights_kernel, "down_weights", grad_shapes, where, dr2, act,
     )
     dup, b_up_grad = call(down_bwd_kernel, "down_bwd", [(wide, bf), thin], where, dr2, slope, down_w)
-    down_half = reduce_core(down_near, down_far, b_up_grad) if fast else []
-    out_one = forward_rows(out, out, 1, b_up_grad)
-    up_near, up_far = call(
-        up_weights_kernel, "up_weights", [grad_shape, grad_shape], where, first, dup, after=out_one,
-    )
+    out_one = next_row(out, b_up_grad)
+    wait = [out_one]
+    if fast:
+        down_half = reduce_core(down_near, down_far, b_up_grad)
+        wait += down_half
     dr1, dctx, small_one = call(
         up_bwd_kernel, "up_bwd", [row_f, ((4, length, 256), bf), ((3, width), fl)],
-        where, dr2, dup, xhat, rstd, vec, up_w, attn_w, after=down_half,
-    )
-    out_two = forward_rows(*out_one, 2, small_one)
-    down_plane = reduce_plane(down_half, small_one) if fast else []
-    up_half = reduce_core(up_near, up_far, small_one) if fast else []
+        where, dr2, dup, xhat, rstd, vec, up_w, attn_w, after=wait,
+    )
+    out_two = next_row(out_one, small_one)
+    up_near, *up_far = call(
+        up_weights_kernel, "up_weights", grad_shapes, where, first, dup, after=[small_one, out_two],
+    )
+    wait = [up_near]
+    if fast:
+        down_pair = reduce_pair(down_half, 1, up_near)
+        up_half = reduce_core(up_near, up_far, up_near)
+        wait += down_pair + up_half
     grad_row, dproj, bias_grad = call(
         attn_bwd_kernel, "attn_bwd", [row_b, (wide, bf), thin],
-        where, seg, seg_col, proj, lse, dr1, dctx, attn_w, after=out_two + down_plane + up_half,
+        where, seg, seg_col, proj, lse, dr1, dctx, attn_w, after=wait,
         scratch=[pltpu.VMEM((length, width), fl)],
     )
-    out_three = forward_rows(*out_two, 3, bias_grad)
-    down_parts = reduce_tensor(down_plane, bias_grad) if fast else []
-    up_plane = reduce_plane(up_half, bias_grad) if fast else []
-    attn_near, attn_far = call(
-        attn_weights_kernel, "attn_weights", [attn_grad_shape, attn_grad_shape],
+    out_three = next_row(out_two, bias_grad)
+    wait = [out_three]
+    if fast:
+        down_plane = reduce_chip(down_pair, 2, bias_grad)
+        wait += down_plane
+    attn_near, *attn_far = call(
+        attn_weights_kernel, "attn_weights", attn_grad_shapes,
         where, x, dproj, ctx, dr1, bias_grad, b_up_grad, small_one, small_two,
-        scratch=[pltpu.VMEM((EXTRA, width), fl)], after=out_three + down_parts + up_plane,
-    )
-    in_one = forward_rows(grad_row, grad_row, 1, attn_near)
-    in_two = forward_rows(*in_one, 2, attn_near)
-    in_three = forward_rows(*in_two, 3, attn_near)
-    hidden_out = place_rows(out, (out_one, out_two, out_three), spin)
-    grad_in = place_rows(grad_row, (in_one, in_two, in_three), spin)
+        scratch=[pltpu.VMEM((EXTRA, width), fl)], after=wait,
+    )
+    in_one = next_row(grad_row, attn_near)
+    in_two = rotate(in_one)
+    hidden_out = place_rows([out, out_one, out_two, out_three], spin)
+    grad_in = place_rows([grad_row, in_one, in_two, rotate(in_two)], spin)
     if fast:
-        down_sum = add(*down_parts)
-        up_sum = add(*reduce_tensor(up_plane, attn_near))
-        attn_half = reduce_core(attn_near, attn_far, attn_near)
-        attn_sum = add(*reduce_tensor(reduce_plane(attn_half, attn_near), attn_near))
+        down_sum = reduce_tensor(down_plane, attn_near)
+        up_plane = reduce_chip(reduce_pair(up_half, 2, attn_near), 1, attn_near)
+        up_sum = reduce_tensor(up_plane, attn_near)
+        attn_plane = reduce_plane(reduce_core(attn_near, attn_far, attn_near, (0, 1, 2)), attn_near)
+        attn_sum = reduce_tensor([attn_plane[0]] + late(attn_plane[1:], in_two), attn_near)
     else:
-        down_sum = reduce_plain(down_near, down_far)
+        down_sum = reduce_plain(down_near, down_far, x_last=True)
         up_sum = reduce_plain(up_near, up_far)
         attn_sum = reduce_plain(attn_near, attn_far)
 

time: 377 us -> 341 us (0.905)
  starting transfers between devices: 93 us -> 34.9 us
  waiting for transfers between devices: 115 us -> 146 us
  other arithmetic: 32.3 us -> 24.7 us
    ppermute x27 -> x17, starting transfers between devices: 70.5 us -> 16.8 us  [the longest x11 14.4 us: cross(): return lax.ppermute(value, 'tensor', [(k, k ^ bits) for k in range(4)])]
    ppermute x27 -> x17, waiting for transfers between devices: 64.6 us -> 118 us  [the longest x11 101 us: cross(): return lax.ppermute(value, 'tensor', [(k, k ^ bits) for k in range(4)])]
    ppermute x28 -> x29, waiting for transfers between devices: 50.5 us -> 28 us  [flip(): return lax.ppermute(value, 'dp', [(k, k ^ bits) for k in range(n)])]
    add x4 -> x1, other arithmetic: 9.38 us -> 0.06 us  [add(): total = total + value.astype(fl)]
    ppermute x28 -> x29, starting transfers between devices: 22.5 us -> 18.1 us  [flip(): return lax.ppermute(value, 'dp', [(k, k ^ bits) for k in range(n)])]
    unnamed x118 -> x70, local copies, waits for them, and re-layouts: 8.56 us -> 9.19 us
    convert_element_type x3 -> x10, other arithmetic: 10.8 us -> 11.2 us  [the longest x2 4.06 us: reduce_core(): add(near[2 * k + a:2 * k + b], got[k][a:b]).astype(bf)]
  transfers between devices with their start and end apart: 55 -> 46, of which waited for: 20 -> 22; matrix products, arithmetic and copies ran while one was open for 9% -> 9% of each run, Pallas kernels for 20% -> 25%
where the time goes in v3:
time: 341 us; the launch traced here: 340 us
  waiting for transfers between devices  146 us (43%)
  Pallas kernels  110 us (32%)
  starting transfers between devices  34.9 us (10%)
  other arithmetic  24.7 us (7%)
  local copies, waits for them, and re-layouts  23.1 us (7%)
    pallas_call x10, Pallas kernels, call(): pl.pallas_call(kernel, name=name, out_shape=[jax.ShapeDtypeStruct(s, d) f...  110 us
    ppermute x11, waiting for transfers between devices, cross(): return lax.ppermute(value, 'tensor', [(k, k ^ bits) for k in range(4)])  101 us
    ppermute x29, waiting for transfers between devices, flip(): return lax.ppermute(value, 'dp', [(k, k ^ bits) for k in range(n)])  28 us
    ppermute x29, starting transfers between devices, flip(): return lax.ppermute(value, 'dp', [(k, k ^ bits) for k in range(n)])  18.1 us
    ppermute x6, waiting for transfers between devices, rotate(): return lax.ppermute(value, 'tensor', [(k, (k + 1) % 4) for k in range(4)])  17.1 us
    ppermute x11, starting transfers between devices, cross(): return lax.ppermute(value, 'tensor', [(k, k ^ bits) for k in range(4)])  14.4 us
    unnamed x70, local copies, waits for them, and re-layouts  9.19 us
  transfers between devices with their start and end apart: 46, of which 22 were waited for; matrix products, arithmetic and copies ran while one was open for 9% of the time, Pallas kernels for 25%

profile of v3, /device:TPU:0, one launch (start us, length us, event | category | flops | bytes accessed | tf_op | source)
XLA Modules:
  0.0 340.2 jit_solution(191849509710413973)
XLA Ops:
  15.1 3.4 %collective-permute-done = bf16[112,768]{1,0:T(8,128)(2,1)S(1)} collective-permute-done((bf16[112,768]{1,0:T(8,128)(2,1)S(1)}, bf16[112,768]{1,0:T(8,128)(2,1)S(1)}, u32[]{:S(2)}, u32[]{:S(2)}) %collective-permute-start) | collective-permute-done | bytes 172064 | tf_op jit(solution)/shard_map/ppermute | solution.py:334
  18.5 7.6 %collective-permute-done.1 = bf16[112,768]{1,0:T(8,128)(2,1)S(1)} collective-permute-done((bf16[112,768]{1,0:T(8,128)(2,1)S(1)}, bf16[112,768]{1,0:T(8,128)(2,1)S(1)}, u32[]{:S(2)}, u32[]{:S(2)}) %collective-permute-start.1) | collective-permute-done | bytes 172064 | tf_op jit(solution)/shard_map/ppermute | solution.py:334
  26.2 3.4 collective-permute-start.3
  29.6 6.3 %collective-permute-done.3 = bf16[192,768]{1,0:T(8,128)(2,1)S(1)} collective-permute-done((bf16[192,768]{1,0:T(8,128)(2,1)S(1)}, bf16[192,768]{1,0:T(8,128)(2,1)S(1)}, u32[]{:S(2)}, u32[]{:S(2)}) %collective-permute-start.3) | collective-permute-done | bytes 294944 | tf_op jit(solution)/shard_map/ppermute | solution.py:334
  42.3 21.1 %collective-permute-done.4 = bf16[2,192,768]{2,1,0:T(8,128)(2,1)S(1)} collective-permute-done((bf16[2,192,768]{2,1,0:T(8,128)(2,1)S(1)}, bf16[2,192,768]{2,1,0:T(8,128)(2,1)S(1)}, u32[]{:S(2)}, u32[]{:S(2)}) %collective-permute-start.4) | collective-permute-done | bytes 589856 | tf_op jit(solution)/shard_map/ppermute | solution.py:334
  65.2 3.8 %collective-permute-done.6.refs_2_ = bf16[4,112,768]{2,1,0:T(8,128)(2,1)} collective-permute-done((bf16[4,112,768]{2,1,0:T(8,128)(2,1)S(1)}, bf16[4,112,768]{2,1,0:T(8,128)(2,1)}, u32[]{:S(2)}, u32[]{:S(2)}) %collective-permute-start.6) | collective-permute-done | bytes 688160 | tf_op jit(solution)/shard_map/ppermute | solution.py:330
  69.9 3.5 %collective-permute-done.5.refs_1_ = bf16[4,112,768]{2,1,0:T(8,128)(2,1)} collective-permute-done((bf16[4,112,768]{2,1,0:T(8,128)(2,1)S(1)}, bf16[4,112,768]{2,1,0:T(8,128)(2,1)}, u32[]{:S(2)}, u32[]{:S(2)}) %collective-permute-start.5) | collective-permute-done | bytes 688160 | tf_op jit(solution)/shard_map/ppermute | solution.py:330
  77.9 15.5 %attn_fwd.1 = (bf16[4,512,768]{2,1,0:T(8,128)(2,1)}, bf16[4,512,256]{2,1,0:T(8,128)(2,1)}, f32[4,3,1,512]{3,2,1,0:T(1,128)}, bf16[4,8,112,768]{3,2,1,0:T(8,128)(...) custom-call(s32[2]{0:T(128)} %pad_add_fusion.1.where_ref, ...), custom_call_target="tpu_custom_call" | custom-call | flops 1000 | bytes 1000 | tf_op jit(solution)/shard_map/attn_fwd/pallas_call | solution.py:313
  100.6 10.8 %collective-permute-done.14.refs_3_ = bf16[2,192,768]{2,1,0:T(8,128)(2,1)S(1)} collective-permute-done((bf16[2,192,768]{2,1,0:T(8,128)(2,1)S(1)}, bf16[2,192,768]{2,1,0:T(8,128)(2,1)S(1)}, u32[]{:S(2)}, u32[]{:S(2)}) %collective-permute-start.14) | collective-permute-done | bytes 589856 | tf_op jit(solution)/shard_map/ppermute | solution.py:330
  116.8 17.7 %ffn_fwd.1 = (bf16[512,768]{1,0:T(8,128)(2,1)}, f32[512,768]{1,0:T(8,128)}, bf16[4,512,768]{2,1,0:T(8,128)(2,1)}, f32[4,512,768]{2,1,0:T(8,128)}, f32[3,768]{1,0...) custom-call(s32[2]{0:T(128)} %pad_add_fusion.1.where_ref, ...), custom_call_target="tpu_custom_call" | custom-call | flops 1000 | bytes 1000 | tf_op jit(solution)/shard_map/ffn_fwd/pallas_call | solution.py:313
  134.5 8.5 %down_weights.1 = (bf16[4,4,96,768]{3,2,1,0:T(8,128)(2,1)}, bf16[2,4,96,768]{3,2,1,0:T(8,128)(2,1)}, bf16[2,4,96,768]{3,2,1,0:T(8,128)(2,1)}) custom-call(s32[2]{0:T(128)} %pad_add_fusion.1.where_ref, f32[512,768]{1,0:T(8,128)} %get-tuple-element.88.dr2_ref, bf16[4,512,768]{2,1,0:T(8,128)(2,1)} %get-tuple-element.93.act_ref), custom_call_target="tpu_custom_call" | custom-call | flops 1000 | bytes 1000 | tf_op jit(solution)/shard_map/down_weights/pallas_call | solution.py:313
  143.8 9.6 %down_bwd.1 = (bf16[4,512,768]{2,1,0:T(8,128)(2,1)}, f32[4,1,768]{2,1,0:T(1,128)}) custom-call(s32[2]{0:T(128)} %pad_add_fusion.1.where_ref, f32[512,768]{1,0:T(8,128)} %get-tuple-element.88.dr2_ref, f32[4,512,768]{2,1,0:T(8,128)} %get-tuple-element.89.slope_ref, bf16[4,8,96,768]{3,2,1,0:T(8,128)(2,1)} %get-tuple-element.90.weight_ref), custom_call_target="tpu_custom_call" | custom-call | flops 1000 | bytes 1000 | tf_op jit(solution)/shard_map/down_bwd/pallas_call | solution.py:313
  153.4 11.7 %collective-permute-done.21.refs_1_ = bf16[512,768]{1,0:T(8,128)(2,1)} collective-permute-done((bf16[512,768]{1,0:T(8,128)(2,1)S(1)}, bf16[512,768]{1,0:T(8,128)(2,1)}, u32[]{:S(2)}, u32[]{:S(2)}) %collective-permute-start.21) | collective-permute-done | bytes 786464 | tf_op jit(solution)/shard_map/ppermute | solution.py:338
  170.0 12.3 %up_bwd.1 = (f32[512,768]{1,0:T(8,128)}, bf16[4,512,256]{2,1,0:T(8,128)(2,1)}, f32[3,768]{1,0:T(4,128)}) custom-call(s32[2]{0:T(128)} %pad_add_fusion.1.where_ref, f32[512,768]{1,0:T(8,128)} %get-tuple-element.88.dr2_ref, bf16[4,512,768]{2,1,0:T(8,128)(2,1)} %get-tuple-element.100.dup_ref, f32[512,768]{1,0:T(8,128)} %get-tuple-element.81.xhat_ref, ...), custom_call_target="tpu_custom_call" | custom-call | flops 1000 | bytes 1000 | tf_op jit(solution)/shard_map/up_bwd/pallas_call | solution.py:313
  182.3 3.9 %collective-permute-done.22.refs_2_ = bf16[512,768]{1,0:T(8,128)(2,1)} collective-permute-done((bf16[512,768]{1,0:T(8,128)(2,1)}, bf16[512,768]{1,0:T(8,128)(2,1)}, u32[]{:S(2)}, u32[]{:S(2)}) %collective-permute-start.22) | collective-permute-done | bytes 786464 | tf_op jit(solution)/shard_map/ppermute | solution.py:338
  186.2 8.1 %up_weights.1 = (bf16[4,4,96,768]{3,2,1,0:T(8,128)(2,1)}, bf16[2,4,96,768]{3,2,1,0:T(8,128)(2,1)}, bf16[2,4,96,768]{3,2,1,0:T(8,128)(2,1)}) custom-call(s32[2]{0:T(128)} %pad_add_fusion.1.where_ref, bf16[512,768]{1,0:T(8,128)(2,1)} %get-tuple-element.82.first_ref, bf16[4,512,768]{2,1,0:T(8,128)(2,1)} %get-tuple-element.100.dup_ref), custom_call_target="tpu_custom_call" | custom-call | flops 1000 | bytes 1000 | tf_op jit(solution)/shard_map/up_weights/pallas_call | solution.py:313
  200.6 20.3 %attn_bwd.1 = (bf16[512,768]{1,0:T(8,128)(2,1)}, bf16[4,512,768]{2,1,0:T(8,128)(2,1)}, f32[4,1,768]{2,1,0:T(1,128)}) custom-call(s32[2]{0:T(128)} %pad_add_fusion.1.where_ref, s32[1,512]{1,0:T(1,128)} %constant_dynamic-slice_fusion.2.seg_row_ref, s32[512,1]{1,0:T(8,128)} %copy.38.seg_col_ref, bf16[4,512,768]{2,1,0:T(8,128)(2,1)} %get-tuple-element.114.proj_ref, ...), custom_call_target="tpu_custom_call" | custom-call | flops 1000 | bytes 1000 | tf_op jit(solution)/shard_map/attn_bwd/pallas_call | solution.py:313
  223.0 10.0 %attn_weights.1 = (bf16[4,4,112,768]{3,2,1,0:T(8,128)(2,1)}, bf16[2,4,112,768]{3,2,1,0:T(8,128)(2,1)}, bf16[2,4,112,768]{3,2,1,0:T(8,128)(2,1)}) custom-call(s32[2]{0:T(128)} %pad_add_fusion.1.where_ref, bf16[512,768]{1,0:T(8,128)(2,1)} %dynamic-slice_bitcast_fusion.1.x_ref, bf16[4,512,768]{2,1,0:T(8,128)(2,1)} %get-tuple-element.123.dproj_ref, ...), custom_call_target="tpu_custom_call" | custom-call | flops 1000 | bytes 1000 | tf_op jit(solution)/shard_map/attn_weights/pallas_call | solution.py:313
  241.9 3.9 %place_rows.2 = bf16[4,512,768]{2,1,0:T(8,128)(2,1)} custom-call(s32[2]{0:T(128)} %pad_add_fusion.where_ref, bf16[512,768]{1,0:T(8,128)(2,1)} %get-tuple-element.87.refs_0_, bf16[512,768]{1,0:T(8,128)(2,1)} %collective-permute-done.21.refs_1_, bf16[512,768]{1,0:T(8,128)(2,1)} %collective-permute-done.22.refs_2_, bf16[512,768]{1,0:T(8,128)(2,1)} %copy-done.12), custom_call_target="tpu_custom_call" | custom-call | flops 1000 | bytes 1000 | tf_op jit(solution)/shard_map/place_rows/pallas_call | solution.py:313
  245.8 14.9 %collective-permute-done.44 = bf16[2,96,768]{2,1,0:T(8,128)(2,1)} collective-permute-done((bf16[2,96,768]{2,1,0:T(8,128)(2,1)S(1)}, bf16[2,96,768]{2,1,0:T(8,128)(2,1)}, u32[]{:S(2)}, u32[]{:S(2)}) %collective-permute-start.44) | collective-permute-done | bytes 294944 | tf_op jit(solution)/shard_map/ppermute | solution.py:334
  271.3 15.4 %collective-permute-done.45 = bf16[96,768]{1,0:T(8,128)(2,1)S(1)} collective-permute-done((bf16[96,768]{1,0:T(8,128)(2,1)S(1)}, bf16[96,768]{1,0:T(8,128)(2,1)S(1)}, u32[]{:S(2)}, u32[]{:S(2)}) %collective-permute-start.45) | collective-permute-done | bytes 147488 | tf_op jit(solution)/shard_map/ppermute | solution.py:334
  287.8 7.9 %collective-permute-done.42 = bf16[2,96,768]{2,1,0:T(8,128)(2,1)S(1)} collective-permute-done((bf16[2,96,768]{2,1,0:T(8,128)(2,1)S(1)}, bf16[2,96,768]{2,1,0:T(8,128)(2,1)S(1)}, u32[]{:S(2)}, u32[]{:S(2)}) %collective-permute-start.42) | collective-permute-done | bytes 294944 | tf_op jit(solution)/shard_map/ppermute | solution.py:334
  304.9 20.0 %collective-permute-done.38 = bf16[2,112,768]{2,1,0:T(8,128)(2,1)S(1)} collective-permute-done((bf16[2,112,768]{2,1,0:T(8,128)(2,1)S(1)}, bf16[2,112,768]{2,1,0:T(8,128)(2,1)S(1)}, u32[]{:S(2)}, u32[]{:S(2)}) %collective-permute-start.38) | collective-permute-done | bytes 344096 | tf_op jit(solution)/shard_map/ppermute | solution.py:334
  328.3 3.7 %place_rows.3 = bf16[4,512,768]{2,1,0:T(8,128)(2,1)} custom-call(s32[2]{0:T(128)} %pad_add_fusion.where_ref, bf16[512,768]{1,0:T(8,128)(2,1)} %get-tuple-element.120.refs_0_, bf16[512,768]{1,0:T(8,128)(2,1)} %collective-permute-done.29.refs_1_, bf16[512,768]{1,0:T(8,128)(2,1)} %copy-done.13, bf16[512,768]{1,0:T(8,128)(2,1)} %copy-done.14), custom_call_target="tpu_custom_call" | custom-call | flops 1000 | bytes 1000 | tf_op jit(solution)/shard_map/place_rows/pallas_call | solution.py:313
  (241 shorter events, 94.7 us)
Async XLA Ops:
  36.0 27.4 %collective-permute-start.4 = (bf16[2,192,768]{2,1,0:T(8,128)(2,1)S(1)}, bf16[2,192,768]{2,1,0:T(8,128)(2,1)S(1)}, u32[]{:S(2)}, u32[]{:S(2)}) collective-permute-start(bf16[2,192,768]{2,1,0:T(8,128)(2,1)S(1)} %pad_maximum_fusion.2), channel_id=1, source_target_pairs={{0,2},{1,3},{2,0},{3,1},{4,6},{5,7},{6,4},{7,5},{8,10},{9,11},{10,... | collective-permute-start | bytes 1769480 | tf_op jit(solution)/shard_map/ppermute | solution.py:334
  38.8 30.2 %collective-permute-start.6 = (bf16[4,112,768]{2,1,0:T(8,128)(2,1)S(1)}, bf16[4,112,768]{2,1,0:T(8,128)(2,1)}, u32[]{:S(2)}, u32[]{:S(2)}) collective-permute-start(bf16[4,112,768]{2,1,0:T(8,128)(2,1)S(1)} %pad_maximum_fusion.1.refs_0_), channel_id=1, source_target_pairs={{0,16},{4,20},{8,24},{12,28},{16,0},{20,4},{24,8},{28,12},{1,17},{... | collective-permute-start | bytes 2064392 | tf_op jit(solution)/shard_map/ppermute | solution.py:330
  40.0 29.9 %collective-permute-start.7 = (bf16[4,112,768]{2,1,0:T(8,128)(2,1)S(1)}, bf16[4,112,768]{2,1,0:T(8,128)(2,1)}, u32[]{:S(2)}, u32[]{:S(2)}) collective-permute-start(bf16[4,112,768]{2,1,0:T(8,128)(2,1)S(1)} %pad_maximum_fusion.1.refs_0_), channel_id=1, source_target_pairs={{0,24},{4,28},{8,16},{12,20},{16,8},{20,12},{24,0},{28,4},{1,25},{... | collective-permute-start | bytes 2064392 | tf_op jit(solution)/shard_map/ppermute | solution.py:330
  41.4 32.0 %collective-permute-start.5 = (bf16[4,112,768]{2,1,0:T(8,128)(2,1)S(1)}, bf16[4,112,768]{2,1,0:T(8,128)(2,1)}, u32[]{:S(2)}, u32[]{:S(2)}) collective-permute-start(bf16[4,112,768]{2,1,0:T(8,128)(2,1)S(1)} %pad_maximum_fusion.1.refs_0_), channel_id=1, source_target_pairs={{0,8},{4,12},{8,0},{12,4},{16,24},{20,28},{24,16},{28,20},{1,9},{5... | collective-permute-start | bytes 2064392 | tf_op jit(solution)/shard_map/ppermute | solution.py:330
  42.3 31.1 %collective-permute-start.8 = (bf16[4,112,768]{2,1,0:T(8,128)(2,1)S(1)}, bf16[4,112,768]{2,1,0:T(8,128)(2,1)S(1)}, u32[]{:S(2)}, u32[]{:S(2)}) collective-permute-start(bf16[4,112,768]{2,1,0:T(8,128)(2,1)S(1)} %pad_maximum_fusion.1.refs_0_), channel_id=1, source_target_pairs={{0,4},{4,0},{8,12},{12,8},{16,20},{20,16},{24,28},{28,24},{1,5},{5... | collective-permute-start | bytes 2064392 | tf_op jit(solution)/shard_map/ppermute | solution.py:330
  64.6 31.0 %collective-permute-start.12 = (bf16[4,192,768]{2,1,0:T(8,128)(2,1)}, bf16[4,192,768]{2,1,0:T(8,128)(2,1)}, u32[]{:S(2)}, u32[]{:S(2)}) collective-permute-start(bf16[4,192,768]{2,1,0:T(8,128)(2,1)} %pad_maximum_fusion.refs_0_), channel_id=1, source_target_pairs={{0,8},{4,12},{8,0},{12,4},{16,24},{20,28},{24,16},{28,20},{1,9},{5... | collective-permute-start | bytes 3538952 | tf_op jit(solution)/shard_map/ppermute | solution.py:330
  69.0 27.6 %collective-permute-start.13 = (bf16[4,192,768]{2,1,0:T(8,128)(2,1)}, bf16[4,192,768]{2,1,0:T(8,128)(2,1)}, u32[]{:S(2)}, u32[]{:S(2)}) collective-permute-start(bf16[4,192,768]{2,1,0:T(8,128)(2,1)} %pad_maximum_fusion.refs_0_), channel_id=1, source_target_pairs={{0,16},{4,20},{8,24},{12,28},{16,0},{20,4},{24,8},{28,12},{1,17},{... | collective-permute-start | bytes 3538952 | tf_op jit(solution)/shard_map/ppermute | solution.py:330
  77.9 36.8 %collective-permute-start.16 = (bf16[4,192,768]{2,1,0:T(8,128)(2,1)}, bf16[4,192,768]{2,1,0:T(8,128)(2,1)S(1)}, u32[]{:S(2)}, u32[]{:S(2)}) collective-permute-start(bf16[4,192,768]{2,1,0:T(8,128)(2,1)} %pad_maximum_fusion.refs_0_), channel_id=1, source_target_pairs={{0,4},{4,0},{8,12},{12,8},{16,20},{20,16},{24,28},{28,24},{1,5},{5... | collective-permute-start | bytes 3538952 | tf_op jit(solution)/shard_map/ppermute | solution.py:330
  168.5 27.5 %collective-permute-start.26 = (bf16[2,4,96,768]{3,2,1,0:T(8,128)(2,1)}, bf16[2,4,96,768]{3,2,1,0:T(8,128)(2,1)S(1)}, u32[]{:S(2)}, u32[]{:S(2)}) collective-permute-start(bf16[2,4,96,768]{3,2,1,0:T(8,128)(2,1)} %get-tuple-element.199), channel_id=1, source_target_pairs={{0,8},{4,12},{8,0},{12,4},{16,24},{20,28},{24,16},{28,20},{1,9},{5... | collective-permute-start | bytes 3538952 | tf_op jit(solution)/shard_map/ppermute | solution.py:330
  194.8 26.1 %collective-permute-start.25 = (bf16[512,768]{1,0:T(8,128)(2,1)}, bf16[512,768]{1,0:T(8,128)(2,1)S(1)}, u32[]{:S(2)}, u32[]{:S(2)}) collective-permute-start(bf16[512,768]{1,0:T(8,128)(2,1)} %collective-permute-done.22.refs_2_), channel_id=1, source_target_pairs={{0,1},{1,2},{2,3},{3,0},{4,5},{5,6},{6,7},{7,4},{8,9},{9,10},{10,1... | collective-permute-start | bytes 2359304 | tf_op jit(solution)/shard_map/ppermute | solution.py:338
  197.2 23.8 %collective-permute-start.30 = (bf16[4,96,768]{2,1,0:T(8,128)(2,1)}, bf16[4,96,768]{2,1,0:T(8,128)(2,1)}, u32[]{:S(2)}, u32[]{:S(2)}) collective-permute-start(bf16[4,96,768]{2,1,0:T(8,128)(2,1)} %get-tuple-element.196), channel_id=1, source_target_pairs={{0,16},{4,20},{8,24},{12,28},{16,0},{20,4},{24,8},{28,12},{1,17},{... | collective-permute-start | bytes 1769480 | tf_op jit(solution)/shard_map/ppermute | solution.py:330
  199.7 37.0 %collective-permute-start.40 = (bf16[2,4,96,768]{3,2,1,0:T(8,128)(2,1)S(1)}, bf16[2,4,96,768]{3,2,1,0:T(8,128)(2,1)}, u32[]{:S(2)}, u32[]{:S(2)}) collective-permute-start(bf16[2,4,96,768]{3,2,1,0:T(8,128)(2,1)S(1)} %get-tuple-element.197), channel_id=1, source_target_pairs={{0,16},{4,20},{8,24},{12,28},{16,0},{20,4},{24,8},{28,12},{1,17},{... | collective-permute-start | bytes 3538952 | tf_op jit(solution)/shard_map/ppermute | solution.py:330
  233.0 31.1 %collective-permute-start.33 = (bf16[2,4,112,768]{3,2,1,0:T(8,128)(2,1)}, bf16[2,4,112,768]{3,2,1,0:T(8,128)(2,1)}, u32[]{:S(2)}, u32[]{:S(2)}) collective-permute-start(bf16[2,4,112,768]{3,2,1,0:T(8,128)(2,1)} %get-tuple-element.128), channel_id=1, source_target_pairs={{0,4},{4,0},{8,12},{12,8},{16,20},{20,16},{24,28},{28,24},{1,5},{5... | collective-permute-start | bytes 4128776 | tf_op jit(solution)/shard_map/ppermute | solution.py:330
  233.0 31.1 %collective-permute-start.34 = (bf16[2,4,112,768]{3,2,1,0:T(8,128)(2,1)}, bf16[2,4,112,768]{3,2,1,0:T(8,128)(2,1)}, u32[]{:S(2)}, u32[]{:S(2)}) collective-permute-start(bf16[2,4,112,768]{3,2,1,0:T(8,128)(2,1)} %get-tuple-element.129), channel_id=1, source_target_pairs={{0,4},{4,0},{8,12},{12,8},{16,20},{20,16},{24,28},{28,24},{1,5},{5... | collective-permute-start | bytes 4128776 | tf_op jit(solution)/shard_map/ppermute | solution.py:330
  233.5 29.5 %collective-permute-start.29 = (bf16[512,768]{1,0:T(8,128)(2,1)}, bf16[512,768]{1,0:T(8,128)(2,1)}, u32[]{:S(2)}, u32[]{:S(2)}) collective-permute-start(bf16[512,768]{1,0:T(8,128)(2,1)} %get-tuple-element.120.refs_0_), channel_id=1, source_target_pairs={{0,1},{1,2},{2,3},{3,0},{4,5},{5,6},{6,7},{7,4},{8,9},{9,10},{10,1... | collective-permute-start | bytes 2359304 | tf_op jit(solution)/shard_map/ppermute | solution.py:338
  234.9 25.9 %collective-permute-start.44 = (bf16[2,96,768]{2,1,0:T(8,128)(2,1)S(1)}, bf16[2,96,768]{2,1,0:T(8,128)(2,1)}, u32[]{:S(2)}, u32[]{:S(2)}) collective-permute-start(bf16[2,96,768]{2,1,0:T(8,128)(2,1)S(1)} %get-tuple-element.205), channel_id=1, source_target_pairs={{0,1},{1,0},{2,3},{3,2},{4,5},{5,4},{6,7},{7,6},{8,9},{9,8},{10,11... | collective-permute-start | bytes 884744 | tf_op jit(solution)/shard_map/ppermute | solution.py:334
  239.1 29.8 %collective-permute-start.41 = (bf16[4,96,768]{2,1,0:T(8,128)(2,1)}, bf16[4,96,768]{2,1,0:T(8,128)(2,1)}, u32[]{:S(2)}, u32[]{:S(2)}) collective-permute-start(bf16[4,96,768]{2,1,0:T(8,128)(2,1)} %get-tuple-element.193), channel_id=1, source_target_pairs={{0,8},{4,12},{8,0},{12,4},{16,24},{20,28},{24,16},{28,20},{1,9},{5... | collective-permute-start | bytes 1769480 | tf_op jit(solution)/shard_map/ppermute | solution.py:330
  261.7 25.0 %collective-permute-start.45 = (bf16[96,768]{1,0:T(8,128)(2,1)S(1)}, bf16[96,768]{1,0:T(8,128)(2,1)S(1)}, u32[]{:S(2)}, u32[]{:S(2)}) collective-permute-start(bf16[96,768]{1,0:T(8,128)(2,1)S(1)} %fusion.25), channel_id=1, source_target_pairs={{0,2},{1,3},{2,0},{3,1},{4,6},{5,7},{6,4},{7,5},{8,10},{9,11},{10,... | collective-permute-start | bytes 442376 | tf_op jit(solution)/shard_map/ppermute | solution.py:334
  263.0 35.8 %collective-permute-start.31 = (bf16[512,768]{1,0:T(8,128)(2,1)}, bf16[512,768]{1,0:T(8,128)(2,1)S(1)}, u32[]{:S(2)}, u32[]{:S(2)}) collective-permute-start(bf16[512,768]{1,0:T(8,128)(2,1)} %collective-permute-done.29.refs_1_), channel_id=1, source_target_pairs={{0,1},{1,2},{2,3},{3,0},{4,5},{5,6},{6,7},{7,4},{8,9},{9,10},{10,1... | collective-permute-start | bytes 2359304 | tf_op jit(solution)/shard_map/ppermute | solution.py:338
  266.5 29.2 %collective-permute-start.35 = (bf16[4,112,768]{2,1,0:T(8,128)(2,1)S(1)}, bf16[4,112,768]{2,1,0:T(8,128)(2,1)S(1)}, u32[]{:S(2)}, u32[]{:S(2)}) collective-permute-start(bf16[4,112,768]{2,1,0:T(8,128)(2,1)S(1)} %get-tuple-element.192), channel_id=1, source_target_pairs={{0,8},{4,12},{8,0},{12,4},{16,24},{20,28},{24,16},{28,20},{1,9},{5... | collective-permute-start | bytes 2064392 | tf_op jit(solution)/shard_map/ppermute | solution.py:330
  268.0 30.4 %collective-permute-start.36 = (bf16[4,112,768]{2,1,0:T(8,128)(2,1)S(1)}, bf16[4,112,768]{2,1,0:T(8,128)(2,1)S(1)}, u32[]{:S(2)}, u32[]{:S(2)}) collective-permute-start(bf16[4,112,768]{2,1,0:T(8,128)(2,1)S(1)} %get-tuple-element.186), channel_id=1, source_target_pairs={{0,16},{4,20},{8,24},{12,28},{16,0},{20,4},{24,8},{28,12},{1,17},{... | collective-permute-start | bytes 2064392 | tf_op jit(solution)/shard_map/ppermute | solution.py:330
  268.8 29.6 %collective-permute-start.37 = (bf16[4,112,768]{2,1,0:T(8,128)(2,1)S(1)}, bf16[4,112,768]{2,1,0:T(8,128)(2,1)S(1)}, u32[]{:S(2)}, u32[]{:S(2)}) collective-permute-start(bf16[4,112,768]{2,1,0:T(8,128)(2,1)S(1)} %get-tuple-element.185), channel_id=1, source_target_pairs={{0,24},{4,28},{8,16},{12,20},{16,8},{20,12},{24,0},{28,4},{1,25},{... | collective-permute-start | bytes 2064392 | tf_op jit(solution)/shard_map/ppermute | solution.py:330
  298.8 26.1 %collective-permute-start.38 = (bf16[2,112,768]{2,1,0:T(8,128)(2,1)S(1)}, bf16[2,112,768]{2,1,0:T(8,128)(2,1)S(1)}, u32[]{:S(2)}, u32[]{:S(2)}) collective-permute-start(bf16[2,112,768]{2,1,0:T(8,128)(2,1)S(1)} %get-tuple-element.135), channel_id=1, source_target_pairs={{0,1},{1,0},{2,3},{3,2},{4,5},{5,4},{6,7},{7,6},{8,9},{9,8},{10,11... | collective-permute-start | bytes 1032200 | tf_op jit(solution)/shard_map/ppermute | solution.py:334
  300.8 26.7 %collective-permute-start.32 = (bf16[512,768]{1,0:T(8,128)(2,1)S(1)}, bf16[512,768]{1,0:T(8,128)(2,1)S(1)}, u32[]{:S(2)}, u32[]{:S(2)}) collective-permute-start(bf16[512,768]{1,0:T(8,128)(2,1)S(1)} %collective-permute-done.31.refs_2_), channel_id=1, source_target_pairs={{0,1},{1,2},{2,3},{3,0},{4,5},{5,6},{6,7},{7,4},{8,9},{9,10},{10,1... | collective-permute-start | bytes 2359304 | tf_op jit(solution)/shard_map/ppermute | solution.py:338
  (53 other events, 599.1 us)

commit v4 on v3

--- a/solution.py
+++ b/solution.py
@@ -65,7 +65,6 @@
             place = jnp.bitwise_xor(chip, j)
             if x_last:
                 place = 2 * jnp.bitwise_and(place, 1) + jnp.right_shift(place, 1)
-            half, low = jnp.right_shift(place, 1), jnp.bitwise_and(place, 1)
 
             def store(ref, index, slab):
                 ref[index, hop, :DEPTH] = value[DEPTH * slab : DEPTH * (slab + 1)]
@@ -73,8 +72,11 @@
                     ref[index, hop, DEPTH:] = extra
 
             store(near_ref, place, 2 * j + near)
-            for k in (0, 1):
-                pl.when(half == k)(functools.partial(store, far_refs[k], low, 2 * j + far))
+            size = 4 // len(far_refs)
+            for k, ref in enumerate(far_refs):
+                inside = jnp.logical_and(place >= size * k, place < size * (k + 1))
+                index = jnp.clip(place - size * k, 0, size - 1)
+                pl.when(inside)(functools.partial(store, ref, index, 2 * j + far))
 
     pl.when(core == 0)(functools.partial(put, 0, 1))
     pl.when(core == 1)(functools.partial(put, 1, 0))
@@ -199,7 +201,7 @@
     near_ref, *far_refs = refs
 
     def step(g, carry):
-        scatter_slabs(where_ref, g, tn(first_ref[...], dup_ref[g]).astype(bf), near_ref, far_refs)
+        scatter_slabs(where_ref, g, tn(first_ref[...], dup_ref[g]).astype(bf), near_ref, far_refs, x_last=True)
         return carry
 
     lax.fori_loop(0, 4, step, 0)
@@ -353,19 +355,10 @@
     return jnp.stack([shard] + [cross(shard, hop) for hop in (1, 2, 3)])
 
 
-def tensor_stack_doubling(shard):
-    pair = jnp.stack([shard, cross(shard, 1)])
-    return jnp.concatenate([pair, cross(pair, 2)])
-
-
-def gather_direct(own):
-    return with_core([(own, (0, ALL))] + [(flip(own, r), (r, ALL)) for r in (2, 4, 6)])
-
-
-def gather_staged(own, gate):
+def gather_staged(own, gates=()):
     over_x = flip(own, 2)
     over_y = flip(own, 4)
-    half_x, half_y = late([over_x[:2], over_y[2:]], gate)
+    half_x, half_y = late([over_x[:2], over_y[2:]], *gates)
     far_a = flip(half_x, 4)
     far_b = flip(half_y, 2)
     near = [(own, (0, ALL)), (over_x, (2, ALL)), (over_y, (4, ALL))]
@@ -379,31 +372,35 @@
     return total
 
 
-def reduce_core(near, far, gate, cuts=(0, 2)):
-    got = late([flip(half, 1) for half in far], gate)
+def reduce_core(near, far, gates=(), parts=1):
+    got = late([flip(part, 1) for part in far], *gates) if gates else [flip(part, 1) for part in far]
+    size, each = 4 // len(far), len(far) * parts
     return [
-        add(near[2 * k + a : 2 * k + b], got[k][a:b]).astype(bf) for k in (0, 1) for a, b in zip(cuts, cuts[1:])
+        add(near[a : a + 4 // each], got[a // size][a % size : a % size + 4 // each]).astype(bf)
+        for a in range(0, 4, 4 // each)
     ]
 
 
-def reduce_pair(half, axis, gate):
-    (got,) = late([flip(half[1], 2 * axis)], gate)
+def halves(parts):
+    return [jnp.concatenate(parts[:2]), jnp.concatenate(parts[2:])]
+
+
+def reduce_pair(half, axis, gates=()):
+    got = flip(half[1], 2 * axis)
+    if gates:
+        (got,) = late([got], *gates)
     return [add(half[0][k], got[k]).astype(bf) for k in (0, 1)]
 
 
-def reduce_chip(pair, axis, gate):
-    (got,) = late([flip(pair[1], 2 * axis)], gate)
-    return [add(pair[0][:2], got[:2]).astype(bf), add(pair[0][2:], got[2:]).astype(bf)]
-
-
-def reduce_plane(half, gate):
-    half = [h[0] for h in half]
-    got = late([flip(half[r], 2 * r) for r in (1, 2, 3)], gate)
-    return [add(half[0][k : k + 2], *[g[k : k + 2] for g in got]).astype(bf) for k in (0, 2)]
-
-
-def reduce_tensor(plane, gate):
-    (got,) = late([cross(plane[1], 1)], gate)
+def reduce_chip(pair, axis, gates=()):
+    got = flip(pair[1], 2 * axis)
+    if gates:
+        (got,) = late([got], *gates)
+    return [add(pair[0][k : k + 2], got[k : k + 2]).astype(bf) for k in (0, 2)]
+
+
+def reduce_tensor(plane):
+    got = cross(plane[1], 1)
     near, far = add(plane[0][0], got[0]), add(plane[0][1], got[1]).astype(bf)
     return add(near, cross(far, 2))
 
@@ -497,15 +494,16 @@
     row_f, row_b = ((length, width), fl), ((length, width), bf)
     whole = ((4, SLABS, DEPTH, 768), bf)
     attn_whole = ((4, SLABS, DEPTH + EXTRA, 768), bf)
-    grad_shapes = [((n, 4, DEPTH, 768), bf) for n in (4, 2, 2)]
-    attn_grad_shapes = [((n, 4, DEPTH + EXTRA, 768), bf) for n in (4, 2, 2)]
+    down_shapes = [((n, 4, DEPTH, 768), bf) for n in (4, 1, 1, 1, 1)]
+    up_shapes = [((n, 4, DEPTH, 768), bf) for n in (4, 4)]
+    attn_shapes = [((n, 4, DEPTH + EXTRA, 768), bf) for n in (4, 1, 1, 1, 1)]
     thin = ((4, 1, 768), fl)
 
     if fast:
         own = tensor_stack(jnp.concatenate([attn_shard, extra]))
-        attn_pieces = gather_direct(own)
+        attn_pieces = gather_staged(own)
         (ffn_shard,) = late([jnp.concatenate([up_shard, down_shard])], own)
-        ffn_own = tensor_stack_doubling(ffn_shard)
+        ffn_own = tensor_stack(ffn_shard)
         wait = [ffn_own]
     else:
         attn_pieces = gather_plain(attn_shard, extra)
@@ -524,7 +522,7 @@
         where, x, seg, seg_col, *pieces, after=wait,
     )
     if fast:
-        ffn_pieces = gather_staged(ffn_own, vec)
+        ffn_pieces = gather_staged(ffn_own, [vec])
     pieces, plan = split(ffn_pieces)
     out, dr2, act, slope, small_two, up_w, down_w = call(
         functools.partial(ffn_fwd_kernel, plan), "ffn_fwd",
@@ -532,55 +530,54 @@
         where, xhat, first, dy, vec, b_up, *pieces,
     )
     down_near, *down_far = call(
-        down_weights_kernel, "down_weights", grad_shapes, where, dr2, act,
+        down_weights_kernel, "down_weights", down_shapes, where, dr2, act,
     )
     dup, b_up_grad = call(down_bwd_kernel, "down_bwd", [(wide, bf), thin], where, dr2, slope, down_w)
     out_one = next_row(out, b_up_grad)
     wait = [out_one]
     if fast:
-        down_half = reduce_core(down_near, down_far, b_up_grad)
+        down_half = halves(reduce_core(down_near, down_far, [b_up_grad, out_one]))
         wait += down_half
     dr1, dctx, small_one = call(
         up_bwd_kernel, "up_bwd", [row_f, ((4, length, 256), bf), ((3, width), fl)],
         where, dr2, dup, xhat, rstd, vec, up_w, attn_w, after=wait,
     )
     out_two = next_row(out_one, small_one)
-    up_near, *up_far = call(
-        up_weights_kernel, "up_weights", grad_shapes, where, first, dup, after=[small_one, out_two],
-    )
-    wait = [up_near]
-    if fast:
-        down_pair = reduce_pair(down_half, 1, up_near)
-        up_half = reduce_core(up_near, up_far, up_near)
-        wait += down_pair + up_half
     grad_row, dproj, bias_grad = call(
         attn_bwd_kernel, "attn_bwd", [row_b, (wide, bf), thin],
-        where, seg, seg_col, proj, lse, dr1, dctx, attn_w, after=wait,
+        where, seg, seg_col, proj, lse, dr1, dctx, attn_w, after=[out_two],
         scratch=[pltpu.VMEM((length, width), fl)],
     )
     out_three = next_row(out_two, bias_grad)
     wait = [out_three]
     if fast:
-        down_plane = reduce_chip(down_pair, 2, bias_grad)
-        wait += down_plane
+        down_pair = reduce_pair(down_half, 1, [bias_grad])
+        wait += down_pair
     attn_near, *attn_far = call(
-        attn_weights_kernel, "attn_weights", attn_grad_shapes,
+        attn_weights_kernel, "attn_weights", attn_shapes,
         where, x, dproj, ctx, dr1, bias_grad, b_up_grad, small_one, small_two,
         scratch=[pltpu.VMEM((EXTRA, width), fl)], after=wait,
     )
-    in_one = next_row(grad_row, attn_near)
+    up_near, *up_far = call(
+        up_weights_kernel, "up_weights", up_shapes, where, first, dup, after=[bias_grad, attn_near],
+    )
+    in_one = rotate(grad_row)
     in_two = rotate(in_one)
+    in_three = rotate(in_two)
     hidden_out = place_rows([out, out_one, out_two, out_three], spin)
-    grad_in = place_rows([grad_row, in_one, in_two, rotate(in_two)], spin)
+    grad_in = place_rows([grad_row, in_one, in_two, in_three], spin)
     if fast:
-        down_sum = reduce_tensor(down_plane, attn_near)
-        up_plane = reduce_chip(reduce_pair(up_half, 2, attn_near), 1, attn_near)
-        up_sum = reduce_tensor(up_plane, attn_near)
-        attn_plane = reduce_plane(reduce_core(attn_near, attn_far, attn_near, (0, 1, 2)), attn_near)
-        attn_sum = reduce_tensor([attn_plane[0]] + late(attn_plane[1:], in_two), attn_near)
+        attn_half = halves(reduce_core(attn_near, attn_far, [up_near, in_one]))
+        up_far = late(up_far, in_one, *attn_half)
+        down_sum = reduce_tensor(reduce_chip([down_pair[0]] + late(down_pair[1:], in_one), 2))
+        up_pair = reduce_pair(reduce_core(up_near, up_far, parts=2), 1, [in_two])
+        up_plane = reduce_chip(up_pair, 2)
+        attn_plane = reduce_chip(reduce_pair(attn_half, 2), 1, [in_three])
+        attn_sum = reduce_tensor([attn_plane[0]] + late(attn_plane[1:], *up_plane))
+        up_sum = reduce_tensor(up_plane)
     else:
         down_sum = reduce_plain(down_near, down_far, x_last=True)
-        up_sum = reduce_plain(up_near, up_far)
+        up_sum = reduce_plain(up_near, up_far, x_last=True)
         attn_sum = reduce_plain(attn_near, attn_far)
 
     def own_part(value):

time: 341 us -> 348 us (1.021)
  waiting for transfers between devices: 146 us -> 125 us
  starting transfers between devices: 34.9 us -> 52.4 us
  other arithmetic: 24.7 us -> 32.4 us
    ppermute x11 -> x12, waiting for transfers between devices: 101 us -> 47 us  [cross(): return lax.ppermute(value, 'tensor', [(k, k ^ bits) for k in range(4)])]
    ppermute x29 -> x33, waiting for transfers between devices: 28 us -> 69.3 us  [flip(): return lax.ppermute(value, 'dp', [(k, k ^ bits) for k in range(n)])]
    ppermute x6, waiting for transfers between devices: 17.1 us -> 8.43 us  [rotate(): return lax.ppermute(value, 'tensor', [(k, (k + 1) % 4) for k in range(4)])]
    ppermute x11 -> x12, starting transfers between devices: 14.4 us -> 22.9 us  [cross(): return lax.ppermute(value, 'tensor', [(k, k ^ bits) for k in range(4)])]
    ppermute x6, starting transfers between devices: 2.39 us -> 9.06 us  [rotate(): return lax.ppermute(value, 'tensor', [(k, (k + 1) % 4) for k in range(4)])]
    convert_element_type x2 -> x3, other arithmetic: 3.43 us -> 8.67 us  [reduce_pair(): return [add(half[0][k], got[k]).astype(bf) for k in (0, 1)]]
    ppermute x29 -> x33, starting transfers between devices: 18.1 us -> 20.4 us  [flip(): return lax.ppermute(value, 'dp', [(k, k ^ bits) for k in range(n)])]
    convert_element_type x5 -> x6, other arithmetic: 6.79 us -> 8.29 us  [the longest x3 5.02 us: reduce_core(): add(near[a:a + 4 // each], got[a // size][a % size:a % size + 4 // each])]
  transfers between devices with their start and end apart: 46 -> 51, of which waited for: 22 -> 19; matrix products, arithmetic and copies ran while one was open for 9% -> 10% of each run, Pallas kernels for 25% -> 27%
where the time goes in v4:
time: 348 us; the launch traced here: 347 us
  waiting for transfers between devices  125 us (36%)
  Pallas kernels  110 us (32%)
  starting transfers between devices  52.4 us (15%)
  other arithmetic  32.4 us (9%)
  local copies, waits for them, and re-layouts  25.4 us (7%)
    pallas_call x10, Pallas kernels, call(): pl.pallas_call(kernel, name=name, out_shape=[jax.ShapeDtypeStruct(s, d) f...  110 us
    ppermute x33, waiting for transfers between devices, flip(): return lax.ppermute(value, 'dp', [(k, k ^ bits) for k in range(n)])  69.3 us
    ppermute x12, waiting for transfers between devices, cross(): return lax.ppermute(value, 'tensor', [(k, k ^ bits) for k in range(4)])  47 us
    ppermute x12, starting transfers between devices, cross(): return lax.ppermute(value, 'tensor', [(k, k ^ bits) for k in range(4)])  22.9 us
    ppermute x33, starting transfers between devices, flip(): return lax.ppermute(value, 'dp', [(k, k ^ bits) for k in range(n)])  20.4 us
    unnamed x78, local copies, waits for them, and re-layouts  9.48 us
    ppermute x6, starting transfers between devices, rotate(): return lax.ppermute(value, 'tensor', [(k, (k + 1) % 4) for k in range(4)])  9.06 us
    convert_element_type x3, other arithmetic, reduce_pair(): return [add(half[0][k], got[k]).astype(bf) for k in (0, 1)]  8.67 us
  transfers between devices with their start and end apart: 51, of which 19 were waited for; matrix products, arithmetic and copies ran while one was open for 10% of the time, Pallas kernels for 27%

profile of v4, /device:TPU:0, one launch (start us, length us, event | category | flops | bytes accessed | tf_op | source)
XLA Modules:
  0.0 347.4 jit_solution(8830817682621298818)
XLA Ops:
  18.5 7.6 %collective-permute-done.1 = bf16[112,768]{1,0:T(8,128)(2,1)S(1)} collective-permute-done((bf16[112,768]{1,0:T(8,128)(2,1)S(1)}, bf16[112,768]{1,0:T(8,128)(2,1)S(1)}, u32[]{:S(2)}, u32[]{:S(2)}) %collective-permute-start.1) | collective-permute-done | bytes 172064 | tf_op jit(solution)/shard_map/ppermute | solution.py:336
  35.1 7.5 %collective-permute-done.3 = bf16[192,768]{1,0:T(8,128)(2,1)S(1)} collective-permute-done((bf16[192,768]{1,0:T(8,128)(2,1)S(1)}, bf16[192,768]{1,0:T(8,128)(2,1)S(1)}, u32[]{:S(2)}, u32[]{:S(2)}) %collective-permute-start.3) | collective-permute-done | bytes 294944 | tf_op jit(solution)/shard_map/ppermute | solution.py:336
  42.7 13.4 %collective-permute-done.4 = bf16[192,768]{1,0:T(8,128)(2,1)S(1)} collective-permute-done((bf16[192,768]{1,0:T(8,128)(2,1)S(1)}, bf16[192,768]{1,0:T(8,128)(2,1)S(1)}, u32[]{:S(2)}, u32[]{:S(2)}) %collective-permute-start.4) | collective-permute-done | bytes 294944 | tf_op jit(solution)/shard_map/ppermute | solution.py:336
  63.4 23.9 %collective-permute-done.8.refs_3_ = bf16[2,112,768]{2,1,0:T(8,128)(2,1)S(1)} collective-permute-done((bf16[2,112,768]{2,1,0:T(8,128)(2,1)S(1)}, bf16[2,112,768]{2,1,0:T(8,128)(2,1)S(1)}, u32[]{:S(2)}, u32[]{:S(2)}) %collective-permute-start.8) | collective-permute-done | bytes 344096 | tf_op jit(solution)/shard_map/ppermute | solution.py:332
  93.7 15.5 %attn_fwd.1 = (bf16[4,512,768]{2,1,0:T(8,128)(2,1)}, bf16[4,512,256]{2,1,0:T(8,128)(2,1)}, f32[4,3,1,512]{3,2,1,0:T(1,128)}, bf16[4,8,112,768]{3,2,1,0:T(8,128)(...) custom-call(s32[2]{0:T(128)} %pad_add_fusion.1.where_ref, ...), custom_call_target="tpu_custom_call" | custom-call | flops 1000 | bytes 1000 | tf_op jit(solution)/shard_map/attn_fwd/pallas_call | solution.py:315
  113.9 12.8 %collective-permute-done.17.refs_3_ = bf16[2,192,768]{2,1,0:T(8,128)(2,1)S(1)} collective-permute-done((bf16[2,192,768]{2,1,0:T(8,128)(2,1)S(1)}, bf16[2,192,768]{2,1,0:T(8,128)(2,1)S(1)}, u32[]{:S(2)}, u32[]{:S(2)}) %collective-permute-start.17) | collective-permute-done | bytes 589856 | tf_op jit(solution)/shard_map/ppermute | solution.py:332
  132.4 17.7 %ffn_fwd.1 = (bf16[512,768]{1,0:T(8,128)(2,1)}, f32[512,768]{1,0:T(8,128)}, bf16[4,512,768]{2,1,0:T(8,128)(2,1)}, f32[4,512,768]{2,1,0:T(8,128)}, f32[3,768]{1,0...) custom-call(s32[2]{0:T(128)} %pad_add_fusion.1.where_ref, ...), custom_call_target="tpu_custom_call" | custom-call | flops 1000 | bytes 1000 | tf_op jit(solution)/shard_map/ffn_fwd/pallas_call | solution.py:315
  150.1 6.9 %collective-permute-start.24 = (bf16[512,768]{1,0:T(8,128)(2,1)}, bf16[512,768]{1,0:T(8,128)(2,1)S(1)}, u32[]{:S(2)}, u32[]{:S(2)}) collective-permute-start(bf16[512,768]{1,0:T(8,128)(2,1)} %get-tuple-element.90.refs_0_), channel_id=1, source_target_pairs={{0,1},{1,2},{2,3},{3,0},{4,5},{5,6},{6,7},{7,4},{8,9},{9,10},{10,1... | collective-permute-start | bytes 2359304 | tf_op jit(solution)/shard_map/ppermute | solution.py:340
  157.0 8.6 %down_weights.1 = (bf16[4,4,96,768]{3,2,1,0:T(8,128)(2,1)}, bf16[1,4,96,768]{3,2,1,0:T(8,128)(2,1)}, bf16[1,4,96,768]{3,2,1,0:T(8,128)(2,1)}, bf16[1,4,96,768]{3,2,1,0:T(8,128)(2,1)}, bf16[1,4,96,768]{3,2,1,0:T(8,128)(2,1)}) custom-call(s32[2]{0:T(128)} %pad_add_fusion.1.where_ref, f32[512,768]{1,0:T(8,128)} %get-tuple-element.91.dr2_ref, ...), custom_call_target="tpu_custom_call" | custom-call | flops 1000 | bytes 1000 | tf_op jit(solution)/shard_map/down_weights/pallas_call | solution.py:315
  166.6 9.6 %down_bwd.1 = (bf16[4,512,768]{2,1,0:T(8,128)(2,1)}, f32[4,1,768]{2,1,0:T(1,128)}) custom-call(s32[2]{0:T(128)} %pad_add_fusion.1.where_ref, f32[512,768]{1,0:T(8,128)} %get-tuple-element.91.dr2_ref, f32[4,512,768]{2,1,0:T(8,128)} %get-tuple-element.92.slope_ref, bf16[4,8,96,768]{3,2,1,0:T(8,128)(2,1)} %get-tuple-element.93.weight_ref), custom_call_target="tpu_custom_call" | custom-call | flops 1000 | bytes 1000 | tf_op jit(solution)/shard_map/down_bwd/pallas_call | solution.py:315
  182.6 12.2 %up_bwd.1 = (f32[512,768]{1,0:T(8,128)}, bf16[4,512,256]{2,1,0:T(8,128)(2,1)}, f32[3,768]{1,0:T(4,128)}) custom-call(s32[2]{0:T(128)} %pad_add_fusion.1.where_ref, f32[512,768]{1,0:T(8,128)} %get-tuple-element.91.dr2_ref, bf16[4,512,768]{2,1,0:T(8,128)(2,1)} %get-tuple-element.105.dup_ref, f32[512,768]{1,0:T(8,128)} %get-tuple-element.84.xhat_ref, ...), custom_call_target="tpu_custom_call" | custom-call | flops 1000 | bytes 1000 | tf_op jit(solution)/shard_map/up_bwd/pallas_call | solution.py:315
  197.7 20.6 %attn_bwd.1 = (bf16[512,768]{1,0:T(8,128)(2,1)}, bf16[4,512,768]{2,1,0:T(8,128)(2,1)}, f32[4,1,768]{2,1,0:T(1,128)}) custom-call(s32[2]{0:T(128)} %pad_add_fusion.1.where_ref, s32[1,512]{1,0:T(1,128)} %constant_dynamic-slice_fusion.2.seg_row_ref, s32[512,1]{1,0:T(8,128)} %copy.38.seg_col_ref, bf16[4,512,768]{2,1,0:T(8,128)(2,1)} %get-tuple-element.112.proj_ref, ...), custom_call_target="tpu_custom_call" | custom-call | flops 1000 | bytes 1000 | tf_op jit(solution)/shard_map/attn_bwd/pallas_call | solution.py:315
  221.2 10.4 %attn_weights.1 = (bf16[4,4,112,768]{3,2,1,0:T(8,128)(2,1)}, bf16[1,4,112,768]{3,2,1,0:T(8,128)(2,1)}, bf16[1,4,112,768]{3,2,1,0:T(8,128)(2,1)}, bf16[1,4,112,76...) custom-call(s32[2]{0:T(128)} %pad_add_fusion.1.where_ref, bf16[512,768]{1,0:T(8,128)(2,1)} %dynamic-slice_bitcast_fusion.1.x_ref, ...), custom_call_target="tpu_custom_call" | custom-call | flops 1000 | bytes 1000 | tf_op jit(solution)/shard_map/attn_weights/pallas_call | solution.py:315
  232.7 8.2 %up_weights.1 = (bf16[4,4,96,768]{3,2,1,0:T(8,128)(2,1)}, bf16[4,4,96,768]{3,2,1,0:T(8,128)(2,1)}) custom-call(s32[2]{0:T(128)} %pad_add_fusion.1.where_ref, bf16[512,768]{1,0:T(8,128)(2,1)} %get-tuple-element.85.first_ref, bf16[4,512,768]{2,1,0:T(8,128)(2,1)} %get-tuple-element.105.dup_ref), custom_call_target="tpu_custom_call" | custom-call | flops 1000 | bytes 1000 | tf_op jit(solution)/shard_map/up_weights/pallas_call | solution.py:315
  250.5 8.9 %collective-permute-done.48 = bf16[4,96,768]{2,1,0:T(8,128)(2,1)S(1)} collective-permute-done((bf16[4,96,768]{2,1,0:T(8,128)(2,1)S(1)}, bf16[4,96,768]{2,1,0:T(8,128)(2,1)S(1)}, u32[]{:S(2)}, u32[]{:S(2)}) %collective-permute-start.48) | collective-permute-done | bytes 589856 | tf_op jit(solution)/shard_map/ppermute | solution.py:332
  262.1 5.5 %collective-permute-done.32.refs_2_ = bf16[512,768]{1,0:T(8,128)(2,1)} collective-permute-done((bf16[512,768]{1,0:T(8,128)(2,1)}, bf16[512,768]{1,0:T(8,128)(2,1)}, u32[]{:S(2)}, u32[]{:S(2)}) %collective-permute-start.32) | collective-permute-done | bytes 786464 | tf_op jit(solution)/shard_map/ppermute | solution.py:340
  267.7 6.4 %collective-permute-done.49 = bf16[2,96,768]{2,1,0:T(8,128)(2,1)S(1)} collective-permute-done((bf16[2,96,768]{2,1,0:T(8,128)(2,1)}, bf16[2,96,768]{2,1,0:T(8,128)(2,1)S(1)}, u32[]{:S(2)}, u32[]{:S(2)}) %collective-permute-start.49) | collective-permute-done | bytes 294944 | tf_op jit(solution)/shard_map/ppermute | solution.py:336
  274.7 13.7 %collective-permute-done.39 = bf16[2,4,112,768]{3,2,1,0:T(8,128)(2,1)} collective-permute-done((bf16[2,4,112,768]{3,2,1,0:T(8,128)(2,1)S(1)}, bf16[2,4,112,768]{3,2,1,0:T(8,128)(2,1)}, u32[]{:S(2)}, u32[]{:S(2)}) %collective-permute-start.39) | collective-permute-done | bytes 1376288 | tf_op jit(solution)/shard_map/ppermute | solution.py:332
  297.6 3.8 %place_rows.2 = bf16[4,512,768]{2,1,0:T(8,128)(2,1)} custom-call(s32[2]{0:T(128)} %pad_add_fusion.where_ref, bf16[512,768]{1,0:T(8,128)(2,1)} %get-tuple-element.90.refs_0_, bf16[512,768]{1,0:T(8,128)(2,1)} %copy-done.10, bf16[512,768]{1,0:T(8,128)(2,1)} %collective-permute-done.25.refs_2_, bf16[512,768]{1,0:T(8,128)(2,1)} %copy-done.11), custom_call_target="tpu_custom_call" | custom-call | flops 1000 | bytes 1000 | tf_op jit(solution)/shard_map/place_rows/pallas_call | solution.py:315
  303.6 5.5 %collective-permute-done.40 = bf16[4,112,768]{2,1,0:T(8,128)(2,1)} collective-permute-done((bf16[4,112,768]{2,1,0:T(8,128)(2,1)}, bf16[4,112,768]{2,1,0:T(8,128)(2,1)}, u32[]{:S(2)}, u32[]{:S(2)}) %collective-permute-start.40) | collective-permute-done | bytes 688160 | tf_op jit(solution)/shard_map/ppermute | solution.py:332
  316.4 3.8 %place_rows.3 = bf16[4,512,768]{2,1,0:T(8,128)(2,1)} custom-call(s32[2]{0:T(128)} %pad_add_fusion.where_ref, bf16[512,768]{1,0:T(8,128)(2,1)} %get-tuple-element.118.refs_0_, bf16[512,768]{1,0:T(8,128)(2,1)} %collective-permute-done.31.refs_1_, bf16[512,768]{1,0:T(8,128)(2,1)} %collective-permute-done.32.refs_2_, ...), custom_call_target="tpu_custom_call" | custom-call | flops 1000 | bytes 1000 | tf_op jit(solution)/shard_map/place_rows/pallas_call | solution.py:315
  323.1 3.8 %collective-permute-start.47 = (bf16[96,768]{1,0:T(8,128)(2,1)S(1)}, bf16[96,768]{1,0:T(8,128)(2,1)S(1)}, u32[]{:S(2)}, u32[]{:S(2)}) collective-permute-start(bf16[96,768]{1,0:T(8,128)(2,1)S(1)} %fusion.18), channel_id=1, source_target_pairs={{0,2},{1,3},{2,0},{3,1},{4,6},{5,7},{6,4},{7,5},{8,10},{9,11},{10,... | collective-permute-start | bytes 442376 | tf_op jit(solution)/shard_map/ppermute | solution.py:336
  328.7 4.6 %collective-permute-start.45 = (bf16[112,768]{1,0:T(8,128)(2,1)S(1)}, bf16[112,768]{1,0:T(8,128)(2,1)S(1)}, u32[]{:S(2)}, u32[]{:S(2)}) collective-permute-start(bf16[112,768]{1,0:T(8,128)(2,1)S(1)} %fusion.17), channel_id=1, source_target_pairs={{0,2},{1,3},{2,0},{3,1},{4,6},{5,7},{6,4},{7,5},{8,10},{9,11},{10,... | collective-permute-start | bytes 516104 | tf_op jit(solution)/shard_map/ppermute | solution.py:336
  333.3 4.1 %collective-permute-done.47 = bf16[96,768]{1,0:T(8,128)(2,1)S(1)} collective-permute-done((bf16[96,768]{1,0:T(8,128)(2,1)S(1)}, bf16[96,768]{1,0:T(8,128)(2,1)S(1)}, u32[]{:S(2)}, u32[]{:S(2)}) %collective-permute-start.47) | collective-permute-done | bytes 147488 | tf_op jit(solution)/shard_map/ppermute | solution.py:336
  (263 shorter events, 110.3 us)
Async XLA Ops:
  26.2 32.2 %collective-permute-start.6 = (bf16[4,112,768]{2,1,0:T(8,128)(2,1)S(1)}, bf16[4,112,768]{2,1,0:T(8,128)(2,1)}, u32[]{:S(2)}, u32[]{:S(2)}) collective-permute-start(bf16[4,112,768]{2,1,0:T(8,128)(2,1)S(1)} %pad_maximum_fusion.3.refs_0_), channel_id=1, source_target_pairs={{0,8},{4,12},{8,0},{12,4},{16,24},{20,28},{24,16},{28,20},{1,9},{5... | collective-permute-start | bytes 2064392 | tf_op jit(solution)/shard_map/ppermute | solution.py:332
  28.2 31.2 %collective-permute-start.7 = (bf16[4,112,768]{2,1,0:T(8,128)(2,1)S(1)}, bf16[4,112,768]{2,1,0:T(8,128)(2,1)}, u32[]{:S(2)}, u32[]{:S(2)}) collective-permute-start(bf16[4,112,768]{2,1,0:T(8,128)(2,1)S(1)} %pad_maximum_fusion.3.refs_0_), channel_id=1, source_target_pairs={{0,16},{4,20},{8,24},{12,28},{16,0},{20,4},{24,8},{28,12},{1,17},{... | collective-permute-start | bytes 2064392 | tf_op jit(solution)/shard_map/ppermute | solution.py:332
  32.6 23.4 %collective-permute-start.4 = (bf16[192,768]{1,0:T(8,128)(2,1)S(1)}, bf16[192,768]{1,0:T(8,128)(2,1)S(1)}, u32[]{:S(2)}, u32[]{:S(2)}) collective-permute-start(bf16[192,768]{1,0:T(8,128)(2,1)S(1)} %pad_maximum_fusion.7), channel_id=1, source_target_pairs={{0,2},{1,3},{2,0},{3,1},{4,6},{5,7},{6,4},{7,5},{8,10},{9,11},{10,... | collective-permute-start | bytes 884744 | tf_op jit(solution)/shard_map/ppermute | solution.py:336
  33.7 22.3 %collective-permute-start.5 = (bf16[192,768]{1,0:T(8,128)(2,1)S(1)}, bf16[192,768]{1,0:T(8,128)(2,1)S(1)}, u32[]{:S(2)}, u32[]{:S(2)}) collective-permute-start(bf16[192,768]{1,0:T(8,128)(2,1)S(1)} %pad_maximum_fusion.7), channel_id=1, source_target_pairs={{0,3},{1,2},{2,1},{3,0},{4,7},{5,6},{6,5},{7,4},{8,11},{9,10},{10,... | collective-permute-start | bytes 884744 | tf_op jit(solution)/shard_map/ppermute | solution.py:336
  42.7 44.7 %collective-permute-start.10 = (bf16[4,112,768]{2,1,0:T(8,128)(2,1)S(1)}, bf16[4,112,768]{2,1,0:T(8,128)(2,1)S(1)}, u32[]{:S(2)}, u32[]{:S(2)}) collective-permute-start(bf16[4,112,768]{2,1,0:T(8,128)(2,1)S(1)} %pad_maximum_fusion.3.refs_0_), channel_id=1, source_target_pairs={{0,4},{4,0},{8,12},{12,8},{16,20},{20,16},{24,28},{28,24},{1,5},{5... | collective-permute-start | bytes 2064392 | tf_op jit(solution)/shard_map/ppermute | solution.py:332
  57.3 51.8 %collective-permute-start.15 = (bf16[4,192,768]{2,1,0:T(8,128)(2,1)}, bf16[4,192,768]{2,1,0:T(8,128)(2,1)}, u32[]{:S(2)}, u32[]{:S(2)}) collective-permute-start(bf16[4,192,768]{2,1,0:T(8,128)(2,1)} %pad_maximum_fusion.1.refs_0_), channel_id=1, source_target_pairs={{0,8},{4,12},{8,0},{12,4},{16,24},{20,28},{24,16},{28,20},{1,9},{5... | collective-permute-start | bytes 3538952 | tf_op jit(solution)/shard_map/ppermute | solution.py:332
  57.8 52.4 %collective-permute-start.16 = (bf16[4,192,768]{2,1,0:T(8,128)(2,1)}, bf16[4,192,768]{2,1,0:T(8,128)(2,1)}, u32[]{:S(2)}, u32[]{:S(2)}) collective-permute-start(bf16[4,192,768]{2,1,0:T(8,128)(2,1)} %pad_maximum_fusion.1.refs_0_), channel_id=1, source_target_pairs={{0,16},{4,20},{8,24},{12,28},{16,0},{20,4},{24,8},{28,12},{1,17},{... | collective-permute-start | bytes 3538952 | tf_op jit(solution)/shard_map/ppermute | solution.py:332
  60.4 27.0 %collective-permute-start.8 = (bf16[2,112,768]{2,1,0:T(8,128)(2,1)S(1)}, bf16[2,112,768]{2,1,0:T(8,128)(2,1)S(1)}, u32[]{:S(2)}, u32[]{:S(2)}) collective-permute-start(bf16[2,112,768]{2,1,0:T(8,128)(2,1)S(1)} %slice.459), channel_id=1, source_target_pairs={{0,16},{4,20},{8,24},{12,28},{16,0},{20,4},{24,8},{28,12},{1,17},{... | collective-permute-start | bytes 1032200 | tf_op jit(solution)/shard_map/ppermute | solution.py:332
  61.9 26.8 %collective-permute-start.9 = (bf16[2,112,768]{2,1,0:T(8,128)(2,1)S(1)}, bf16[2,112,768]{2,1,0:T(8,128)(2,1)S(1)}, u32[]{:S(2)}, u32[]{:S(2)}) collective-permute-start(bf16[2,112,768]{2,1,0:T(8,128)(2,1)S(1)} %slice.460), channel_id=1, source_target_pairs={{0,8},{4,12},{8,0},{12,4},{16,24},{20,28},{24,16},{28,20},{1,9},{5... | collective-permute-start | bytes 1032200 | tf_op jit(solution)/shard_map/ppermute | solution.py:332
  92.9 37.7 %collective-permute-start.19 = (bf16[4,192,768]{2,1,0:T(8,128)(2,1)}, bf16[4,192,768]{2,1,0:T(8,128)(2,1)S(1)}, u32[]{:S(2)}, u32[]{:S(2)}) collective-permute-start(bf16[4,192,768]{2,1,0:T(8,128)(2,1)} %pad_maximum_fusion.1.refs_0_), channel_id=1, source_target_pairs={{0,4},{4,0},{8,12},{12,8},{16,20},{20,16},{24,28},{28,24},{1,5},{5... | collective-permute-start | bytes 3538952 | tf_op jit(solution)/shard_map/ppermute | solution.py:332
  112.6 18.1 %collective-permute-start.20 = (bf16[4,192,768]{2,1,0:T(8,128)(2,1)}, bf16[4,192,768]{2,1,0:T(8,128)(2,1)S(1)}, u32[]{:S(2)}, u32[]{:S(2)}) collective-permute-start(bf16[4,192,768]{2,1,0:T(8,128)(2,1)} %collective-permute-done.15.refs_1_), channel_id=1, source_target_pairs={{0,4},{4,0},{8,12},{12,8},{16,20},{20,16},{24,28},{28,24},{1,5},{5... | collective-permute-start | bytes 3538952 | tf_op jit(solution)/shard_map/ppermute | solution.py:332
  112.6 18.1 %collective-permute-start.21 = (bf16[4,192,768]{2,1,0:T(8,128)(2,1)}, bf16[4,192,768]{2,1,0:T(8,128)(2,1)}, u32[]{:S(2)}, u32[]{:S(2)}) collective-permute-start(bf16[4,192,768]{2,1,0:T(8,128)(2,1)} %collective-permute-done.16.refs_2_), channel_id=1, source_target_pairs={{0,4},{4,0},{8,12},{12,8},{16,20},{20,16},{24,28},{28,24},{1,5},{5... | collective-permute-start | bytes 3538952 | tf_op jit(solution)/shard_map/ppermute | solution.py:332
  150.1 26.1 %collective-permute-start.24 = (bf16[512,768]{1,0:T(8,128)(2,1)}, bf16[512,768]{1,0:T(8,128)(2,1)S(1)}, u32[]{:S(2)}, u32[]{:S(2)}) collective-permute-start(bf16[512,768]{1,0:T(8,128)(2,1)} %get-tuple-element.90.refs_0_), channel_id=1, source_target_pairs={{0,1},{1,2},{2,3},{3,0},{4,5},{5,6},{6,7},{7,4},{8,9},{9,10},{10,1... | collective-permute-start | bytes 2359304 | tf_op jit(solution)/shard_map/ppermute | solution.py:340
  176.3 21.4 %collective-permute-start.25 = (bf16[512,768]{1,0:T(8,128)(2,1)S(1)}, bf16[512,768]{1,0:T(8,128)(2,1)}, u32[]{:S(2)}, u32[]{:S(2)}) collective-permute-start(bf16[512,768]{1,0:T(8,128)(2,1)S(1)} %collective-permute-done.24.refs_1_), channel_id=1, source_target_pairs={{0,1},{1,2},{2,3},{3,0},{4,5},{5,6},{6,7},{7,4},{8,9},{9,10},{10,1... | collective-permute-start | bytes 2359304 | tf_op jit(solution)/shard_map/ppermute | solution.py:340
  181.4 37.0 %collective-permute-start.34 = (bf16[2,4,96,768]{3,2,1,0:T(8,128)(2,1)}, bf16[2,4,96,768]{3,2,1,0:T(8,128)(2,1)}, u32[]{:S(2)}, u32[]{:S(2)}) collective-permute-start(bf16[2,4,96,768]{3,2,1,0:T(8,128)(2,1)} %pad_maximum_fusion.2), channel_id=1, source_target_pairs={{0,8},{4,12},{8,0},{12,4},{16,24},{20,28},{24,16},{28,20},{1,9},{5... | collective-permute-start | bytes 3538952 | tf_op jit(solution)/shard_map/ppermute | solution.py:332
  197.7 23.5 %collective-permute-start.30 = (bf16[512,768]{1,0:T(8,128)(2,1)}, bf16[512,768]{1,0:T(8,128)(2,1)S(1)}, u32[]{:S(2)}, u32[]{:S(2)}) collective-permute-start(bf16[512,768]{1,0:T(8,128)(2,1)} %collective-permute-done.25.refs_2_), channel_id=1, source_target_pairs={{0,1},{1,2},{2,3},{3,0},{4,5},{5,6},{6,7},{7,4},{8,9},{9,10},{10,1... | collective-permute-start | bytes 2359304 | tf_op jit(solution)/shard_map/ppermute | solution.py:340
  218.3 22.6 %collective-permute-start.31 = (bf16[512,768]{1,0:T(8,128)(2,1)}, bf16[512,768]{1,0:T(8,128)(2,1)}, u32[]{:S(2)}, u32[]{:S(2)}) collective-permute-start(bf16[512,768]{1,0:T(8,128)(2,1)} %get-tuple-element.118.refs_0_), channel_id=1, source_target_pairs={{0,1},{1,2},{2,3},{3,0},{4,5},{5,6},{6,7},{7,4},{8,9},{9,10},{10,1... | collective-permute-start | bytes 2359304 | tf_op jit(solution)/shard_map/ppermute | solution.py:340
  243.2 16.2 %collective-permute-start.48 = (bf16[4,96,768]{2,1,0:T(8,128)(2,1)S(1)}, bf16[4,96,768]{2,1,0:T(8,128)(2,1)S(1)}, u32[]{:S(2)}, u32[]{:S(2)}) collective-permute-start(bf16[4,96,768]{2,1,0:T(8,128)(2,1)S(1)} %copy-done.14), channel_id=1, source_target_pairs={{0,16},{4,20},{8,24},{12,28},{16,0},{20,4},{24,8},{28,12},{1,17},{... | collective-permute-start | bytes 1769480 | tf_op jit(solution)/shard_map/ppermute | solution.py:332
  244.3 44.1 %collective-permute-start.39 = (bf16[2,4,112,768]{3,2,1,0:T(8,128)(2,1)S(1)}, bf16[2,4,112,768]{3,2,1,0:T(8,128)(2,1)}, u32[]{:S(2)}, u32[]{:S(2)}) collective-permute-start(bf16[2,4,112,768]{3,2,1,0:T(8,128)(2,1)S(1)} %pad_maximum_fusion), channel_id=1, source_target_pairs={{0,16},{4,20},{8,24},{12,28},{16,0},{20,4},{24,8},{28,12},{1,17},{... | collective-permute-start | bytes 4128776 | tf_op jit(solution)/shard_map/ppermute | solution.py:332
  245.2 22.5 %collective-permute-start.32 = (bf16[512,768]{1,0:T(8,128)(2,1)}, bf16[512,768]{1,0:T(8,128)(2,1)}, u32[]{:S(2)}, u32[]{:S(2)}) collective-permute-start(bf16[512,768]{1,0:T(8,128)(2,1)} %collective-permute-done.31.refs_1_), channel_id=1, source_target_pairs={{0,1},{1,2},{2,3},{3,0},{4,5},{5,6},{6,7},{7,4},{8,9},{9,10},{10,1... | collective-permute-start | bytes 2359304 | tf_op jit(solution)/shard_map/ppermute | solution.py:340
  249.3 43.8 %collective-permute-start.42 = (bf16[2,4,96,768]{3,2,1,0:T(8,128)(2,1)}, bf16[2,4,96,768]{3,2,1,0:T(8,128)(2,1)}, u32[]{:S(2)}, u32[]{:S(2)}) collective-permute-start(bf16[2,4,96,768]{3,2,1,0:T(8,128)(2,1)} %get-tuple-element.187), channel_id=1, source_target_pairs={{0,8},{4,12},{8,0},{12,4},{16,24},{20,28},{24,16},{28,20},{1,9},{5... | collective-permute-start | bytes 3538952 | tf_op jit(solution)/shard_map/ppermute | solution.py:332
  267.7 35.9 %collective-permute-start.33 = (bf16[512,768]{1,0:T(8,128)(2,1)}, bf16[512,768]{1,0:T(8,128)(2,1)}, u32[]{:S(2)}, u32[]{:S(2)}) collective-permute-start(bf16[512,768]{1,0:T(8,128)(2,1)} %collective-permute-done.32.refs_2_), channel_id=1, source_target_pairs={{0,1},{1,2},{2,3},{3,0},{4,5},{5,6},{6,7},{7,4},{8,9},{9,10},{10,1... | collective-permute-start | bytes 2359304 | tf_op jit(solution)/shard_map/ppermute | solution.py:340
  274.1 27.3 %collective-permute-start.50 = (bf16[96,768]{1,0:T(8,128)(2,1)S(1)}, bf16[96,768]{1,0:T(8,128)(2,1)}, u32[]{:S(2)}, u32[]{:S(2)}) collective-permute-start(bf16[96,768]{1,0:T(8,128)(2,1)S(1)} %fusion.19), channel_id=1, source_target_pairs={{0,2},{1,3},{2,0},{3,1},{4,6},{5,7},{6,4},{7,5},{8,10},{9,11},{10,... | collective-permute-start | bytes 442376 | tf_op jit(solution)/shard_map/ppermute | solution.py:336
  291.9 17.2 %collective-permute-start.40 = (bf16[4,112,768]{2,1,0:T(8,128)(2,1)}, bf16[4,112,768]{2,1,0:T(8,128)(2,1)}, u32[]{:S(2)}, u32[]{:S(2)}) collective-permute-start(bf16[4,112,768]{2,1,0:T(8,128)(2,1)} %get-tuple-element.189), channel_id=1, source_target_pairs={{0,8},{4,12},{8,0},{12,4},{16,24},{20,28},{24,16},{28,20},{1,9},{5... | collective-permute-start | bytes 2064392 | tf_op jit(solution)/shard_map/ppermute | solution.py:332
  (62 other events, 585.4 us)

commit v5 on v4

--- a/solution.py
+++ b/solution.py
@@ -351,8 +351,8 @@
 ALL = (0, 1, 2, 3)
 
 
-def tensor_stack(shard):
-    return jnp.stack([shard] + [cross(shard, hop) for hop in (1, 2, 3)])
+def over_tensor(shard):
+    return [shard] + [cross(shard, hop) for hop in (1, 2, 3)]
 
 
 def gather_staged(own, gates=()):
@@ -500,10 +500,10 @@
     thin = ((4, 1, 768), fl)
 
     if fast:
-        own = tensor_stack(jnp.concatenate([attn_shard, extra]))
-        attn_pieces = gather_staged(own)
-        (ffn_shard,) = late([jnp.concatenate([up_shard, down_shard])], own)
-        ffn_own = tensor_stack(ffn_shard)
+        own = jnp.stack(over_tensor(jnp.concatenate([attn_shard, extra])))
+        ffn_slabs = over_tensor(late([jnp.concatenate([up_shard, down_shard])], own)[0])
+        attn_pieces = gather_staged(own, ffn_slabs[1:3])
+        ffn_own = jnp.stack(late(ffn_slabs, attn_pieces[3][0], attn_pieces[4][0]))
         wait = [ffn_own]
     else:
         attn_pieces = gather_plain(attn_shard, extra)
@@ -567,9 +567,11 @@
     hidden_out = place_rows([out, out_one, out_two, out_three], spin)
     grad_in = place_rows([grad_row, in_one, in_two, in_three], spin)
     if fast:
+        down_plane = reduce_chip(down_pair, 2)
+        attn_far = late(attn_far, *down_plane)
         attn_half = halves(reduce_core(attn_near, attn_far, [up_near, in_one]))
         up_far = late(up_far, in_one, *attn_half)
-        down_sum = reduce_tensor(reduce_chip([down_pair[0]] + late(down_pair[1:], in_one), 2))
+        down_sum = reduce_tensor(down_plane)
         up_pair = reduce_pair(reduce_core(up_near, up_far, parts=2), 1, [in_two])
         up_plane = reduce_chip(up_pair, 2)
         attn_plane = reduce_chip(reduce_pair(attn_half, 2), 1, [in_three])

time: 348 us -> 323 us (0.928)
  waiting for transfers between devices: 125 us -> 109 us
  starting transfers between devices: 52.4 us -> 43.9 us
    ppermute x33, waiting for transfers between devices: 69.3 us -> 25.8 us  [flip(): return lax.ppermute(value, 'dp', [(k, k ^ bits) for k in range(n)])]
    ppermute x12, waiting for transfers between devices: 47 us -> 74.7 us  [cross(): return lax.ppermute(value, 'tensor', [(k, k ^ bits) for k in range(4)])]
    ppermute x12, starting transfers between devices: 22.9 us -> 16.4 us  [cross(): return lax.ppermute(value, 'tensor', [(k, k ^ bits) for k in range(4)])]
    ppermute x6, starting transfers between devices: 9.06 us -> 4.37 us  [rotate(): return lax.ppermute(value, 'tensor', [(k, (k + 1) % 4) for k in range(4)])]
    unnamed x78 -> x76, local copies, waits for them, and re-layouts: 9.48 us -> 10.1 us
  transfers between devices with their start and end apart: 51 -> 51, of which waited for: 19 -> 18; matrix products, arithmetic and copies ran while one was open for 10% -> 10% of each run, Pallas kernels for 27% -> 29%
where the time goes in v5:
time: 323 us
  Pallas kernels  110 us (34%)
  waiting for transfers between devices  109 us (34%)
  starting transfers between devices  43.9 us (14%)
  other arithmetic  32.3 us (10%)
  local copies, waits for them, and re-layouts  25.8 us (8%)
    pallas_call x10, Pallas kernels, call(): pl.pallas_call(kernel, name=name, out_shape=[jax.ShapeDtypeStruct(s, d) f...  110 us
    ppermute x12, waiting for transfers between devices, cross(): return lax.ppermute(value, 'tensor', [(k, k ^ bits) for k in range(4)])  74.7 us
    ppermute x33, waiting for transfers between devices, flip(): return lax.ppermute(value, 'dp', [(k, k ^ bits) for k in range(n)])  25.8 us
    ppermute x33, starting transfers between devices, flip(): return lax.ppermute(value, 'dp', [(k, k ^ bits) for k in range(n)])  23.1 us
    ppermute x12, starting transfers between devices, cross(): return lax.ppermute(value, 'tensor', [(k, k ^ bits) for k in range(4)])  16.4 us
    unnamed x76, local copies, waits for them, and re-layouts  10.1 us
    convert_element_type x3, other arithmetic, reduce_pair(): return [add(half[0][k], got[k]).astype(bf) for k in (0, 1)]  8.75 us
    ppermute x6, waiting for transfers between devices, rotate(): return lax.ppermute(value, 'tensor', [(k, (k + 1) % 4) for k in range(4)])  8.05 us
  transfers between devices with their start and end apart: 51, of which 18 were waited for; matrix products, arithmetic and copies ran while one was open for 10% of the time, Pallas kernels for 29%

profile of v5, /device:TPU:0, one launch (start us, length us, event | category | flops | bytes accessed | tf_op | source)
XLA Modules:
  0.0 322.7 jit_solution(17491308067138735489)
XLA Ops:
  7.4 3.1 collective-permute-start
  13.1 5.4 %collective-permute-done = bf16[112,768]{1,0:T(8,128)(2,1)S(1)} collective-permute-done((bf16[112,768]{1,0:T(8,128)(2,1)S(1)}, bf16[112,768]{1,0:T(8,128)(2,1)S(1)}, u32[]{:S(2)}, u32[]{:S(2)}) %collective-permute-start) | collective-permute-done | bytes 172064 | tf_op jit(solution)/shard_map/ppermute | solution.py:336
  18.5 7.6 %collective-permute-done.1 = bf16[112,768]{1,0:T(8,128)(2,1)S(1)} collective-permute-done((bf16[112,768]{1,0:T(8,128)(2,1)S(1)}, bf16[112,768]{1,0:T(8,128)(2,1)S(1)}, u32[]{:S(2)}, u32[]{:S(2)}) %collective-permute-start.1) | collective-permute-done | bytes 172064 | tf_op jit(solution)/shard_map/ppermute | solution.py:336
  35.7 6.3 %collective-permute-done.6.refs_1_ = bf16[4,112,768]{2,1,0:T(8,128)(2,1)} collective-permute-done((bf16[4,112,768]{2,1,0:T(8,128)(2,1)S(1)}, bf16[4,112,768]{2,1,0:T(8,128)(2,1)}, u32[]{:S(2)}, u32[]{:S(2)}) %collective-permute-start.6) | collective-permute-done | bytes 688160 | tf_op jit(solution)/shard_map/ppermute | solution.py:332
  49.2 3.4 %collective-permute-start.9 = (bf16[2,112,768]{2,1,0:T(8,128)(2,1)S(1)}, bf16[2,112,768]{2,1,0:T(8,128)(2,1)S(1)}, u32[]{:S(2)}, u32[]{:S(2)}) collective-permute-start(bf16[2,112,768]{2,1,0:T(8,128)(2,1)S(1)} %slice.460), channel_id=1, source_target_pairs={{0,8},{4,12},{8,0},{12,4},{16,24},{20,28},{24,16},{28,20},{1,9},{5... | collective-permute-start | bytes 1032200 | tf_op jit(solution)/shard_map/ppermute | solution.py:332
  52.7 8.6 %collective-permute-done.5 = bf16[192,768]{1,0:T(8,128)(2,1)S(1)} collective-permute-done((bf16[192,768]{1,0:T(8,128)(2,1)S(1)}, bf16[192,768]{1,0:T(8,128)(2,1)S(1)}, u32[]{:S(2)}, u32[]{:S(2)}) %collective-permute-start.5) | collective-permute-done | bytes 294944 | tf_op jit(solution)/shard_map/ppermute | solution.py:336
  70.8 15.5 %attn_fwd.1 = (bf16[4,512,768]{2,1,0:T(8,128)(2,1)}, bf16[4,512,256]{2,1,0:T(8,128)(2,1)}, f32[4,3,1,512]{3,2,1,0:T(1,128)}, bf16[4,8,112,768]{3,2,1,0:T(8,128)(...) custom-call(s32[2]{0:T(128)} %pad_add_fusion.1.where_ref, ...), custom_call_target="tpu_custom_call" | custom-call | flops 1000 | bytes 1000 | tf_op jit(solution)/shard_map/attn_fwd/pallas_call | solution.py:315
  91.1 12.7 %collective-permute-done.17.refs_3_ = bf16[2,192,768]{2,1,0:T(8,128)(2,1)S(1)} collective-permute-done((bf16[2,192,768]{2,1,0:T(8,128)(2,1)S(1)}, bf16[2,192,768]{2,1,0:T(8,128)(2,1)S(1)}, u32[]{:S(2)}, u32[]{:S(2)}) %collective-permute-start.17) | collective-permute-done | bytes 589856 | tf_op jit(solution)/shard_map/ppermute | solution.py:332
  108.3 17.7 %ffn_fwd.1 = (bf16[512,768]{1,0:T(8,128)(2,1)}, f32[512,768]{1,0:T(8,128)}, bf16[4,512,768]{2,1,0:T(8,128)(2,1)}, f32[4,512,768]{2,1,0:T(8,128)}, f32[3,768]{1,0...) custom-call(s32[2]{0:T(128)} %pad_add_fusion.1.where_ref, ...), custom_call_target="tpu_custom_call" | custom-call | flops 1000 | bytes 1000 | tf_op jit(solution)/shard_map/ffn_fwd/pallas_call | solution.py:315
  127.2 8.6 %down_weights.1 = (bf16[4,4,96,768]{3,2,1,0:T(8,128)(2,1)}, bf16[1,4,96,768]{3,2,1,0:T(8,128)(2,1)}, bf16[1,4,96,768]{3,2,1,0:T(8,128)(2,1)}, bf16[1,4,96,768]{3,2,1,0:T(8,128)(2,1)}, bf16[1,4,96,768]{3,2,1,0:T(8,128)(2,1)}) custom-call(s32[2]{0:T(128)} %pad_add_fusion.1.where_ref, f32[512,768]{1,0:T(8,128)} %get-tuple-element.102.dr2_ref, ...), custom_call_target="tpu_custom_call" | custom-call | flops 1000 | bytes 1000 | tf_op jit(solution)/shard_map/down_weights/pallas_call | solution.py:315
  136.8 9.6 %down_bwd.1 = (bf16[4,512,768]{2,1,0:T(8,128)(2,1)}, f32[4,1,768]{2,1,0:T(1,128)}) custom-call(s32[2]{0:T(128)} %pad_add_fusion.1.where_ref, f32[512,768]{1,0:T(8,128)} %get-tuple-element.102.dr2_ref, f32[4,512,768]{2,1,0:T(8,128)} %get-tuple-element.103.slope_ref, bf16[4,8,96,768]{3,2,1,0:T(8,128)(2,1)} %get-tuple-element.104.weight_ref), custom_call_target="tpu_custom_call" | custom-call | flops 1000 | bytes 1000 | tf_op jit(solution)/shard_map/down_bwd/pallas_call | solution.py:315
  154.7 12.2 %up_bwd.1 = (f32[512,768]{1,0:T(8,128)}, bf16[4,512,256]{2,1,0:T(8,128)(2,1)}, f32[3,768]{1,0:T(4,128)}) custom-call(s32[2]{0:T(128)} %pad_add_fusion.1.where_ref, f32[512,768]{1,0:T(8,128)} %get-tuple-element.102.dr2_ref, bf16[4,512,768]{2,1,0:T(8,128)(2,1)} %get-tuple-element.116.dup_ref, f32[512,768]{1,0:T(8,128)} %get-tuple-element.95.xhat_ref, ...), custom_call_target="tpu_custom_call" | custom-call | flops 1000 | bytes 1000 | tf_op jit(solution)/shard_map/up_bwd/pallas_call | solution.py:315
  166.9 6.7 %collective-permute-done.25.refs_2_ = bf16[512,768]{1,0:T(8,128)(2,1)} collective-permute-done((bf16[512,768]{1,0:T(8,128)(2,1)S(1)}, bf16[512,768]{1,0:T(8,128)(2,1)}, u32[]{:S(2)}, u32[]{:S(2)}) %collective-permute-start.25) | collective-permute-done | bytes 786464 | tf_op jit(solution)/shard_map/ppermute | solution.py:340
  174.0 20.5 %attn_bwd.1 = (bf16[512,768]{1,0:T(8,128)(2,1)}, bf16[4,512,768]{2,1,0:T(8,128)(2,1)}, f32[4,1,768]{2,1,0:T(1,128)}) custom-call(s32[2]{0:T(128)} %pad_add_fusion.1.where_ref, s32[1,512]{1,0:T(1,128)} %constant_dynamic-slice_fusion.2.seg_row_ref, s32[512,1]{1,0:T(8,128)} %copy.38.seg_col_ref, bf16[4,512,768]{2,1,0:T(8,128)(2,1)} %get-tuple-element.123.proj_ref, ...), custom_call_target="tpu_custom_call" | custom-call | flops 1000 | bytes 1000 | tf_op jit(solution)/shard_map/attn_bwd/pallas_call | solution.py:315
  198.7 10.1 %attn_weights.1 = (bf16[4,4,112,768]{3,2,1,0:T(8,128)(2,1)}, bf16[1,4,112,768]{3,2,1,0:T(8,128)(2,1)}, bf16[1,4,112,768]{3,2,1,0:T(8,128)(2,1)}, bf16[1,4,112,76...) custom-call(s32[2]{0:T(128)} %pad_add_fusion.1.where_ref, bf16[512,768]{1,0:T(8,128)(2,1)} %dynamic-slice_bitcast_fusion.1.x_ref, ...), custom_call_target="tpu_custom_call" | custom-call | flops 1000 | bytes 1000 | tf_op jit(solution)/shard_map/attn_weights/pallas_call | solution.py:315
  213.4 8.2 %up_weights.1 = (bf16[4,4,96,768]{3,2,1,0:T(8,128)(2,1)}, bf16[4,4,96,768]{3,2,1,0:T(8,128)(2,1)}) custom-call(s32[2]{0:T(128)} %pad_add_fusion.1.where_ref, bf16[512,768]{1,0:T(8,128)(2,1)} %get-tuple-element.96.first_ref, bf16[4,512,768]{2,1,0:T(8,128)(2,1)} %get-tuple-element.116.dup_ref), custom_call_target="tpu_custom_call" | custom-call | flops 1000 | bytes 1000 | tf_op jit(solution)/shard_map/up_weights/pallas_call | solution.py:315
  224.7 3.6 %collective-permute-done.42 = bf16[4,4,96,768]{3,2,1,0:T(8,128)(2,1)S(1)} collective-permute-done((bf16[4,4,96,768]{3,2,1,0:T(8,128)(2,1)S(1)}, bf16[4,4,96,768]{3,2,1,0:T(8,128)(2,1)S(1)}, u32[]{:S(2)}, u32[]{:S(2)}) %collective-permute-start.42) | collective-permute-done | bytes 2359328 | tf_op jit(solution)/shard_map/ppermute | solution.py:332
  234.0 22.3 %collective-permute-done.49 = bf16[2,96,768]{2,1,0:T(8,128)(2,1)} collective-permute-done((bf16[2,96,768]{2,1,0:T(8,128)(2,1)S(1)}, bf16[2,96,768]{2,1,0:T(8,128)(2,1)}, u32[]{:S(2)}, u32[]{:S(2)}) %collective-permute-start.49) | collective-permute-done | bytes 294944 | tf_op jit(solution)/shard_map/ppermute | solution.py:336
  260.7 3.5 %fusion = (bf16[4,112,768]{2,1,0:T(8,128)(2,1)}, bf16[1,4,112,768]{3,2,1,0:T(8,128)(2,1)S(1)}) fusion(bf16[1,4,112,768]{3,2,1,0:T(8,128)(2,1)} %collective-permute-done.37, bf16[2,4,112,768]{3,2,1,0:T(8,128)(2,1)} %collective-permute-done.40, bf16[4,4,112,768]{3,2,1,0:T(8,128)(2,1)} %get-tuple-element.136, bf16[1,4,112,768]{3,2,1,0:T(8,128)(2,1)} %collective-permute-done.36), kind=kLoop, calls=%fused_computation.21 | loop fusion | flops 5505024 | bytes 5505024 | tf_op jit(solution)/shard_map/convert_element_type | solution.py:392
  271.2 3.7 %place_rows.2 = bf16[4,512,768]{2,1,0:T(8,128)(2,1)} custom-call(s32[2]{0:T(128)} %pad_add_fusion.where_ref, bf16[512,768]{1,0:T(8,128)(2,1)} %get-tuple-element.101.refs_0_, bf16[512,768]{1,0:T(8,128)(2,1)} %copy-done.10, bf16[512,768]{1,0:T(8,128)(2,1)} %collective-permute-done.25.refs_2_, bf16[512,768]{1,0:T(8,128)(2,1)} %collective-permute-done.30.refs_3_), custom_call_target="tpu_custom_call" | custom-call | flops 1000 | bytes 1000 | tf_op jit(solution)/shard_map/place_rows/pallas_call | solution.py:315
  274.9 8.1 %collective-permute-done.50 = bf16[96,768]{1,0:T(8,128)(2,1)} collective-permute-done((bf16[96,768]{1,0:T(8,128)(2,1)S(1)}, bf16[96,768]{1,0:T(8,128)(2,1)}, u32[]{:S(2)}, u32[]{:S(2)}) %collective-permute-start.50) | collective-permute-done | bytes 147488 | tf_op jit(solution)/shard_map/ppermute | solution.py:336
  292.2 3.8 %place_rows.3 = bf16[4,512,768]{2,1,0:T(8,128)(2,1)} custom-call(s32[2]{0:T(128)} %pad_add_fusion.where_ref, bf16[512,768]{1,0:T(8,128)(2,1)} %get-tuple-element.129.refs_0_, bf16[512,768]{1,0:T(8,128)(2,1)} %collective-permute-done.31.refs_1_, bf16[512,768]{1,0:T(8,128)(2,1)} %collective-permute-done.32.refs_2_, ...), custom_call_target="tpu_custom_call" | custom-call | flops 1000 | bytes 1000 | tf_op jit(solution)/shard_map/place_rows/pallas_call | solution.py:315
  298.2 9.1 %collective-permute-done.45 = bf16[2,112,768]{2,1,0:T(8,128)(2,1)S(1)} collective-permute-done((bf16[2,112,768]{2,1,0:T(8,128)(2,1)S(1)}, bf16[2,112,768]{2,1,0:T(8,128)(2,1)S(1)}, u32[]{:S(2)}, u32[]{:S(2)}) %collective-permute-start.45) | collective-permute-done | bytes 344096 | tf_op jit(solution)/shard_map/ppermute | solution.py:336
  308.6 7.0 %collective-permute-done.46 = bf16[112,768]{1,0:T(8,128)(2,1)S(1)} collective-permute-done((bf16[112,768]{1,0:T(8,128)(2,1)S(1)}, bf16[112,768]{1,0:T(8,128)(2,1)S(1)}, u32[]{:S(2)}, u32[]{:S(2)}) %collective-permute-start.46) | collective-permute-done | bytes 172064 | tf_op jit(solution)/shard_map/ppermute | solution.py:336
  (261 shorter events, 103.3 us)
Async XLA Ops:
  10.5 15.6 %collective-permute-start.1 = (bf16[112,768]{1,0:T(8,128)(2,1)S(1)}, bf16[112,768]{1,0:T(8,128)(2,1)S(1)}, u32[]{:S(2)}, u32[]{:S(2)}) collective-permute-start(bf16[112,768]{1,0:T(8,128)(2,1)S(1)} %concatenate.66), channel_id=1, source_target_pairs={{0,2},{1,3},{2,0},{3,1},{4,6},{5,7},{6,4},{7,5},{8,10},{9,11},{10,... | collective-permute-start | bytes 516104 | tf_op jit(solution)/shard_map/ppermute | solution.py:336
  26.2 15.9 %collective-permute-start.6 = (bf16[4,112,768]{2,1,0:T(8,128)(2,1)S(1)}, bf16[4,112,768]{2,1,0:T(8,128)(2,1)}, u32[]{:S(2)}, u32[]{:S(2)}) collective-permute-start(bf16[4,112,768]{2,1,0:T(8,128)(2,1)S(1)} %pad_maximum_fusion.3.refs_0_), channel_id=1, source_target_pairs={{0,8},{4,12},{8,0},{12,4},{16,24},{20,28},{24,16},{28,20},{1,9},{5... | collective-permute-start | bytes 2064392 | tf_op jit(solution)/shard_map/ppermute | solution.py:332
  28.2 14.9 %collective-permute-start.7 = (bf16[4,112,768]{2,1,0:T(8,128)(2,1)S(1)}, bf16[4,112,768]{2,1,0:T(8,128)(2,1)}, u32[]{:S(2)}, u32[]{:S(2)}) collective-permute-start(bf16[4,112,768]{2,1,0:T(8,128)(2,1)S(1)} %pad_maximum_fusion.3.refs_0_), channel_id=1, source_target_pairs={{0,16},{4,20},{8,24},{12,28},{16,0},{20,4},{24,8},{28,12},{1,17},{... | collective-permute-start | bytes 2064392 | tf_op jit(solution)/shard_map/ppermute | solution.py:332
  63.2 23.1 %collective-permute-start.15 = (bf16[4,192,768]{2,1,0:T(8,128)(2,1)}, bf16[4,192,768]{2,1,0:T(8,128)(2,1)}, u32[]{:S(2)}, u32[]{:S(2)}) collective-permute-start(bf16[4,192,768]{2,1,0:T(8,128)(2,1)} %pad_maximum_fusion.1.refs_0_), channel_id=1, source_target_pairs={{0,8},{4,12},{8,0},{12,4},{16,24},{20,28},{24,16},{28,20},{1,9},{5... | collective-permute-start | bytes 3538952 | tf_op jit(solution)/shard_map/ppermute | solution.py:332
  63.2 24.2 %collective-permute-start.16 = (bf16[4,192,768]{2,1,0:T(8,128)(2,1)}, bf16[4,192,768]{2,1,0:T(8,128)(2,1)}, u32[]{:S(2)}, u32[]{:S(2)}) collective-permute-start(bf16[4,192,768]{2,1,0:T(8,128)(2,1)} %pad_maximum_fusion.1.refs_0_), channel_id=1, source_target_pairs={{0,16},{4,20},{8,24},{12,28},{16,0},{20,4},{24,8},{28,12},{1,17},{... | collective-permute-start | bytes 3538952 | tf_op jit(solution)/shard_map/ppermute | solution.py:332
  70.1 36.3 %collective-permute-start.19 = (bf16[4,192,768]{2,1,0:T(8,128)(2,1)}, bf16[4,192,768]{2,1,0:T(8,128)(2,1)S(1)}, u32[]{:S(2)}, u32[]{:S(2)}) collective-permute-start(bf16[4,192,768]{2,1,0:T(8,128)(2,1)} %pad_maximum_fusion.1.refs_0_), channel_id=1, source_target_pairs={{0,4},{4,0},{8,12},{12,8},{16,20},{20,16},{24,28},{28,24},{1,5},{5... | collective-permute-start | bytes 3538952 | tf_op jit(solution)/shard_map/ppermute | solution.py:332
  88.5 15.3 %collective-permute-start.17 = (bf16[2,192,768]{2,1,0:T(8,128)(2,1)S(1)}, bf16[2,192,768]{2,1,0:T(8,128)(2,1)S(1)}, u32[]{:S(2)}, u32[]{:S(2)}) collective-permute-start(bf16[2,192,768]{2,1,0:T(8,128)(2,1)S(1)} %slice.461), channel_id=1, source_target_pairs={{0,16},{4,20},{8,24},{12,28},{16,0},{20,4},{24,8},{28,12},{1,17},{... | collective-permute-start | bytes 1769480 | tf_op jit(solution)/shard_map/ppermute | solution.py:332
  88.6 15.5 %collective-permute-start.18 = (bf16[2,192,768]{2,1,0:T(8,128)(2,1)S(1)}, bf16[2,192,768]{2,1,0:T(8,128)(2,1)S(1)}, u32[]{:S(2)}, u32[]{:S(2)}) collective-permute-start(bf16[2,192,768]{2,1,0:T(8,128)(2,1)S(1)} %slice.462), channel_id=1, source_target_pairs={{0,8},{4,12},{8,0},{12,4},{16,24},{20,28},{24,16},{28,20},{1,9},{5... | collective-permute-start | bytes 1769480 | tf_op jit(solution)/shard_map/ppermute | solution.py:332
  90.6 16.1 %collective-permute-start.20 = (bf16[4,192,768]{2,1,0:T(8,128)(2,1)}, bf16[4,192,768]{2,1,0:T(8,128)(2,1)S(1)}, u32[]{:S(2)}, u32[]{:S(2)}) collective-permute-start(bf16[4,192,768]{2,1,0:T(8,128)(2,1)} %collective-permute-done.15.refs_1_), channel_id=1, source_target_pairs={{0,4},{4,0},{8,12},{12,8},{16,20},{20,16},{24,28},{28,24},{1,5},{5... | collective-permute-start | bytes 3538952 | tf_op jit(solution)/shard_map/ppermute | solution.py:332
  90.6 16.7 %collective-permute-start.21 = (bf16[4,192,768]{2,1,0:T(8,128)(2,1)}, bf16[4,192,768]{2,1,0:T(8,128)(2,1)}, u32[]{:S(2)}, u32[]{:S(2)}) collective-permute-start(bf16[4,192,768]{2,1,0:T(8,128)(2,1)} %collective-permute-done.16.refs_2_), channel_id=1, source_target_pairs={{0,4},{4,0},{8,12},{12,8},{16,20},{20,16},{24,28},{28,24},{1,5},{5... | collective-permute-start | bytes 3538952 | tf_op jit(solution)/shard_map/ppermute | solution.py:332
  126.0 21.8 %collective-permute-start.24 = (bf16[512,768]{1,0:T(8,128)(2,1)}, bf16[512,768]{1,0:T(8,128)(2,1)S(1)}, u32[]{:S(2)}, u32[]{:S(2)}) collective-permute-start(bf16[512,768]{1,0:T(8,128)(2,1)} %get-tuple-element.101.refs_0_), channel_id=1, source_target_pairs={{0,1},{1,2},{2,3},{3,0},{4,5},{5,6},{6,7},{7,4},{8,9},{9,10},{10,1... | collective-permute-start | bytes 2359304 | tf_op jit(solution)/shard_map/ppermute | solution.py:340
  151.3 43.2 %collective-permute-start.34 = (bf16[2,4,96,768]{3,2,1,0:T(8,128)(2,1)}, bf16[2,4,96,768]{3,2,1,0:T(8,128)(2,1)}, u32[]{:S(2)}, u32[]{:S(2)}) collective-permute-start(bf16[2,4,96,768]{3,2,1,0:T(8,128)(2,1)} %pad_maximum_fusion.2), channel_id=1, source_target_pairs={{0,8},{4,12},{8,0},{12,4},{16,24},{20,28},{24,16},{28,20},{1,9},{5... | collective-permute-start | bytes 3538952 | tf_op jit(solution)/shard_map/ppermute | solution.py:332
  153.2 20.4 %collective-permute-start.25 = (bf16[512,768]{1,0:T(8,128)(2,1)S(1)}, bf16[512,768]{1,0:T(8,128)(2,1)}, u32[]{:S(2)}, u32[]{:S(2)}) collective-permute-start(bf16[512,768]{1,0:T(8,128)(2,1)S(1)} %collective-permute-done.24.refs_1_), channel_id=1, source_target_pairs={{0,1},{1,2},{2,3},{3,0},{4,5},{5,6},{6,7},{7,4},{8,9},{9,10},{10,1... | collective-permute-start | bytes 2359304 | tf_op jit(solution)/shard_map/ppermute | solution.py:340
  173.6 25.1 %collective-permute-start.30 = (bf16[512,768]{1,0:T(8,128)(2,1)}, bf16[512,768]{1,0:T(8,128)(2,1)}, u32[]{:S(2)}, u32[]{:S(2)}) collective-permute-start(bf16[512,768]{1,0:T(8,128)(2,1)} %collective-permute-done.25.refs_2_), channel_id=1, source_target_pairs={{0,1},{1,2},{2,3},{3,0},{4,5},{5,6},{6,7},{7,4},{8,9},{9,10},{10,1... | collective-permute-start | bytes 2359304 | tf_op jit(solution)/shard_map/ppermute | solution.py:340
  198.7 23.0 %collective-permute-start.31 = (bf16[512,768]{1,0:T(8,128)(2,1)S(1)}, bf16[512,768]{1,0:T(8,128)(2,1)}, u32[]{:S(2)}, u32[]{:S(2)}) collective-permute-start(bf16[512,768]{1,0:T(8,128)(2,1)S(1)} %copy-done.11), channel_id=1, source_target_pairs={{0,1},{1,2},{2,3},{3,0},{4,5},{5,6},{6,7},{7,4},{8,9},{9,10},{10,1... | collective-permute-start | bytes 2359304 | tf_op jit(solution)/shard_map/ppermute | solution.py:340
  223.8 37.0 %collective-permute-start.40 = (bf16[2,4,112,768]{3,2,1,0:T(8,128)(2,1)S(1)}, bf16[2,4,112,768]{3,2,1,0:T(8,128)(2,1)}, u32[]{:S(2)}, u32[]{:S(2)}) collective-permute-start(bf16[2,4,112,768]{3,2,1,0:T(8,128)(2,1)S(1)} %pad_maximum_fusion), channel_id=1, source_target_pairs={{0,16},{4,20},{8,24},{12,28},{16,0},{20,4},{24,8},{28,12},{1,17},{... | collective-permute-start | bytes 4128776 | tf_op jit(solution)/shard_map/ppermute | solution.py:332
  230.0 35.8 %collective-permute-start.43 = (bf16[2,4,96,768]{3,2,1,0:T(8,128)(2,1)}, bf16[2,4,96,768]{3,2,1,0:T(8,128)(2,1)}, u32[]{:S(2)}, u32[]{:S(2)}) collective-permute-start(bf16[2,4,96,768]{3,2,1,0:T(8,128)(2,1)} %get-tuple-element.201), channel_id=1, source_target_pairs={{0,8},{4,12},{8,0},{12,4},{16,24},{20,28},{24,16},{28,20},{1,9},{5... | collective-permute-start | bytes 3538952 | tf_op jit(solution)/shard_map/ppermute | solution.py:332
  230.4 29.3 %collective-permute-start.32 = (bf16[512,768]{1,0:T(8,128)(2,1)}, bf16[512,768]{1,0:T(8,128)(2,1)}, u32[]{:S(2)}, u32[]{:S(2)}) collective-permute-start(bf16[512,768]{1,0:T(8,128)(2,1)} %collective-permute-done.31.refs_1_), channel_id=1, source_target_pairs={{0,1},{1,2},{2,3},{3,0},{4,5},{5,6},{6,7},{7,4},{8,9},{9,10},{10,1... | collective-permute-start | bytes 2359304 | tf_op jit(solution)/shard_map/ppermute | solution.py:340
  230.6 25.6 %collective-permute-start.49 = (bf16[2,96,768]{2,1,0:T(8,128)(2,1)S(1)}, bf16[2,96,768]{2,1,0:T(8,128)(2,1)}, u32[]{:S(2)}, u32[]{:S(2)}) collective-permute-start(bf16[2,96,768]{2,1,0:T(8,128)(2,1)S(1)} %copy-done.24), channel_id=1, source_target_pairs={{0,1},{1,0},{2,3},{3,2},{4,5},{5,4},{6,7},{7,6},{8,9},{9,8},{10,11... | collective-permute-start | bytes 884744 | tf_op jit(solution)/shard_map/ppermute | solution.py:336
  257.2 25.7 %collective-permute-start.50 = (bf16[96,768]{1,0:T(8,128)(2,1)S(1)}, bf16[96,768]{1,0:T(8,128)(2,1)}, u32[]{:S(2)}, u32[]{:S(2)}) collective-permute-start(bf16[96,768]{1,0:T(8,128)(2,1)S(1)} %fusion.19), channel_id=1, source_target_pairs={{0,2},{1,3},{2,0},{3,1},{4,6},{5,7},{6,4},{7,5},{8,10},{9,11},{10,... | collective-permute-start | bytes 442376 | tf_op jit(solution)/shard_map/ppermute | solution.py:336
  259.7 25.6 %collective-permute-start.33 = (bf16[512,768]{1,0:T(8,128)(2,1)}, bf16[512,768]{1,0:T(8,128)(2,1)}, u32[]{:S(2)}, u32[]{:S(2)}) collective-permute-start(bf16[512,768]{1,0:T(8,128)(2,1)} %collective-permute-done.32.refs_2_), channel_id=1, source_target_pairs={{0,1},{1,2},{2,3},{3,0},{4,5},{5,6},{6,7},{7,4},{8,9},{9,10},{10,1... | collective-permute-start | bytes 2359304 | tf_op jit(solution)/shard_map/ppermute | solution.py:340
  264.2 21.1 %collective-permute-start.41 = (bf16[4,112,768]{2,1,0:T(8,128)(2,1)}, bf16[4,112,768]{2,1,0:T(8,128)(2,1)}, u32[]{:S(2)}, u32[]{:S(2)}) collective-permute-start(bf16[4,112,768]{2,1,0:T(8,128)(2,1)} %get-tuple-element.203), channel_id=1, source_target_pairs={{0,8},{4,12},{8,0},{12,4},{16,24},{20,28},{24,16},{28,20},{1,9},{5... | collective-permute-start | bytes 2064392 | tf_op jit(solution)/shard_map/ppermute | solution.py:332
  268.2 17.1 %collective-permute-start.44 = (bf16[4,96,768]{2,1,0:T(8,128)(2,1)}, bf16[4,96,768]{2,1,0:T(8,128)(2,1)S(1)}, u32[]{:S(2)}, u32[]{:S(2)}) collective-permute-start(bf16[4,96,768]{2,1,0:T(8,128)(2,1)} %get-tuple-element.210), channel_id=1, source_target_pairs={{0,16},{4,20},{8,24},{12,28},{16,0},{20,4},{24,8},{28,12},{1,17},{... | collective-permute-start | bytes 1769480 | tf_op jit(solution)/shard_map/ppermute | solution.py:332
  289.3 18.1 %collective-permute-start.45 = (bf16[2,112,768]{2,1,0:T(8,128)(2,1)S(1)}, bf16[2,112,768]{2,1,0:T(8,128)(2,1)S(1)}, u32[]{:S(2)}, u32[]{:S(2)}) collective-permute-start(bf16[2,112,768]{2,1,0:T(8,128)(2,1)S(1)} %get-tuple-element.156), channel_id=1, source_target_pairs={{0,1},{1,0},{2,3},{3,2},{4,5},{5,4},{6,7},{7,6},{8,9},{9,8},{10,11... | collective-permute-start | bytes 1032200 | tf_op jit(solution)/shard_map/ppermute | solution.py:336
  (61 other events, 525.7 us)

commit v6 on v5

--- a/solution.py
+++ b/solution.py
@@ -54,9 +54,7 @@
                 first = last
 
 
-def scatter_slabs(where_ref, group, value, near_ref, far_refs, extra=None, x_last=False):
-    hop = jnp.bitwise_xor(group, where_ref[1])
-    hop = 2 * jnp.bitwise_and(hop, 1) + jnp.right_shift(hop, 1)
+def scatter_slabs(where_ref, value, near_ref, far_refs, extra=None, x_last=False):
     chip = jnp.right_shift(where_ref[0], 1)
     core = jnp.bitwise_and(where_ref[0], 1)
 
@@ -67,9 +65,9 @@
                 place = 2 * jnp.bitwise_and(place, 1) + jnp.right_shift(place, 1)
 
             def store(ref, index, slab):
-                ref[index, hop, :DEPTH] = value[DEPTH * slab : DEPTH * (slab + 1)]
+                ref[index, 0, :DEPTH] = value[DEPTH * slab : DEPTH * (slab + 1)]
                 if extra is not None:
-                    ref[index, hop, DEPTH:] = extra
+                    ref[index, 0, DEPTH:] = extra
 
             store(near_ref, place, 2 * j + near)
             size = 4 // len(far_refs)
@@ -177,34 +175,30 @@
     small_ref[2:3] = jnp.sum(dr2, axis=0, keepdims=True)
 
 
-def down_weights_kernel(where_ref, dr2_ref, act_ref, near_ref, *far_refs):
-    def step(g, carry):
-        dffn = dr2_ref[...].astype(bf)
-        scatter_slabs(where_ref, g, tn(dffn, act_ref[g]).astype(bf), near_ref, far_refs, x_last=True)
-        return carry
-
-    lax.fori_loop(0, 4, step, 0)
+def down_weights_kernel(where_ref, dr2_ref, act_ref, near_ref, *refs):
+    *far_refs, turned_ref = refs
+
+    @pl.when(pl.program_id(0) == 0)
+    def _():
+        turned_ref[...] = dr2_ref[...].astype(bf).T
+
+    scatter_slabs(where_ref, nn(turned_ref[...], act_ref[0]).astype(bf), near_ref, far_refs, x_last=True)
 
 
 def down_bwd_kernel(where_ref, dr2_ref, slope_ref, weight_ref, dup_ref, b_up_ref):
-    def step(g, carry):
-        dffn = dr2_ref[...].astype(bf)
-        dup = (nn(dffn, matrix(weight_ref, g)) * slope_ref[g]).astype(bf)
-        dup_ref[g] = dup
-        b_up_ref[g] = jnp.sum(dup.astype(fl), axis=0, keepdims=True)
-        return carry
-
-    lax.fori_loop(0, 4, step, 0)
-
-
-def up_weights_kernel(where_ref, first_ref, dup_ref, *refs):
-    near_ref, *far_refs = refs
-
-    def step(g, carry):
-        scatter_slabs(where_ref, g, tn(first_ref[...], dup_ref[g]).astype(bf), near_ref, far_refs, x_last=True)
-        return carry
-
-    lax.fori_loop(0, 4, step, 0)
+    dup = (nn(dr2_ref[...].astype(bf), matrix(weight_ref, 0)) * slope_ref[0]).astype(bf)
+    dup_ref[0] = dup
+    b_up_ref[0] = jnp.sum(dup.astype(fl), axis=0, keepdims=True)
+
+
+def up_weights_kernel(where_ref, first_ref, dup_ref, near_ref, *refs):
+    *far_refs, turned_ref = refs
+
+    @pl.when(pl.program_id(0) == 0)
+    def _():
+        turned_ref[...] = first_ref[...].T
+
+    scatter_slabs(where_ref, nn(turned_ref[...], dup_ref[0]).astype(bf), near_ref, far_refs, x_last=True)
 
 
 def up_bwd_kernel(where_ref, dr2_ref, dup_ref, xhat_ref, rstd_ref, vec_ref, weight_ref, attn_weight_ref, *refs):
@@ -279,24 +273,26 @@
     grad_in_ref[...] = (dr1 + back_ref[...].astype(bf).astype(fl)).astype(bf)
 
 
-def attn_weights_kernel(where_ref, x_ref, dproj_ref, ctx_ref, dr1_ref, bias_ref, b_up_ref, one_ref, two_ref, *refs):
-    near_ref, *far_refs, small_ref = refs
-    small_ref[...] = jnp.zeros_like(small_ref)
-    small_ref[0:2] = one_ref[0:2]
-    small_ref[2:4] = two_ref[0:2]
-    small_ref[4:5] = one_ref[2:3]
-    small_ref[5:6] = two_ref[2:3]
-
-    def grads(g, carry):
-        small_ref[6:7] = bias_ref[g]
-        small_ref[7:8] = b_up_ref[g]
-        main = tn(x_ref[...], dproj_ref[g])
-        side = tn(dr1_ref[...].astype(bf), ctx_ref[g])
-        whole = jnp.concatenate([main[:, :512], main[:, 512:] + side], axis=1).astype(bf)
-        scatter_slabs(where_ref, g, whole, near_ref, far_refs, small_ref[...].astype(bf))
-        return carry
-
-    lax.fori_loop(0, 4, grads, 0)
+def attn_weights_kernel(where_ref, x_ref, dproj_ref, ctx_ref, dr1_ref, bias_ref, b_up_ref, one_ref, two_ref,
+                        near_ref, *refs):
+    *far_refs, small_ref, x_turned_ref, dr1_turned_ref = refs
+
+    @pl.when(pl.program_id(0) == 0)
+    def _():
+        small_ref[...] = jnp.zeros_like(small_ref)
+        small_ref[0:2] = one_ref[0:2]
+        small_ref[2:4] = two_ref[0:2]
+        small_ref[4:5] = one_ref[2:3]
+        small_ref[5:6] = two_ref[2:3]
+        x_turned_ref[...] = x_ref[...].T
+        dr1_turned_ref[...] = dr1_ref[...].astype(bf).T
+
+    small_ref[6:7] = bias_ref[0]
+    small_ref[7:8] = b_up_ref[0]
+    main = nn(x_turned_ref[...], dproj_ref[0])
+    side = nn(dr1_turned_ref[...], ctx_ref[0])
+    whole = jnp.concatenate([main[:, :512], main[:, 512:] + side], axis=1).astype(bf)
+    scatter_slabs(where_ref, whole, near_ref, far_refs, small_ref[...].astype(bf))
 
 
 def place_kernel(where_ref, *refs):
@@ -327,6 +323,43 @@
 COST = 1000
 
 
+def whole_block(shape):
+    return pl.BlockSpec(shape, lambda g, where: (0,) * len(shape))
+
+
+def group_block(shape):
+    return pl.BlockSpec((1, *shape[1:]), lambda g, where: (g,) + (0,) * (len(shape) - 1))
+
+
+def slab_block(shape):
+    def index(g, where):
+        hop = jnp.bitwise_xor(g, where[1])
+        return (0, 2 * jnp.bitwise_and(hop, 1) + jnp.right_shift(hop, 1), 0, 0)
+
+    return pl.BlockSpec((shape[0], 1, *shape[2:]), index)
+
+
+def call_groups(kernel, name, outs, where, *args, scratch=(), after=()):
+    if after:
+        (where,) = late([where], *after)
+    return pl.pallas_call(
+        kernel,
+        name=name,
+        out_shape=[jax.ShapeDtypeStruct(s, d) for (s, d), _ in outs],
+        grid_spec=pltpu.PrefetchScalarGridSpec(
+            num_scalar_prefetch=1,
+            grid=(4,),
+            in_specs=[block(a.shape) for a, block in args],
+            out_specs=[block(s) for (s, _), block in outs],
+            scratch_shapes=list(scratch),
+        ),
+        compiler_params=pltpu.CompilerParams(
+            vmem_limit_bytes=VMEM_LIMIT, dimension_semantics=("arbitrary",)
+        ),
+        cost_estimate=pl.CostEstimate(flops=COST, bytes_accessed=COST, transcendentals=0),
+    )(where, *[a for a, _ in args])
+
+
 def flip(value, bits):
     n = lax.axis_size("dp")
     return lax.ppermute(value, "dp", [(k, k ^ bits) for k in range(n)])
@@ -399,8 +432,10 @@
     return [add(pair[0][k : k + 2], got[k : k + 2]).astype(bf) for k in (0, 2)]
 
 
-def reduce_tensor(plane):
+def reduce_tensor(plane, gates=()):
     got = cross(plane[1], 1)
+    if gates:
+        (got,) = late([got], *gates)
     near, far = add(plane[0][0], got[0]), add(plane[0][1], got[1]).astype(bf)
     return add(near, cross(far, 2))
 
@@ -433,8 +468,8 @@
     return row
 
 
-def place_rows(rows, where):
-    return call(place_kernel, "place_rows", [((4,) + rows[0].shape, rows[0].dtype)], where, *rows)[0]
+def place_rows(rows, where, after=()):
+    return call(place_kernel, "place_rows", [((4,) + rows[0].shape, rows[0].dtype)], where, *rows, after=after)[0]
 
 
 def moment_update(state, grad):
@@ -494,9 +529,9 @@
     row_f, row_b = ((length, width), fl), ((length, width), bf)
     whole = ((4, SLABS, DEPTH, 768), bf)
     attn_whole = ((4, SLABS, DEPTH + EXTRA, 768), bf)
-    down_shapes = [((n, 4, DEPTH, 768), bf) for n in (4, 1, 1, 1, 1)]
-    up_shapes = [((n, 4, DEPTH, 768), bf) for n in (4, 4)]
-    attn_shapes = [((n, 4, DEPTH + EXTRA, 768), bf) for n in (4, 1, 1, 1, 1)]
+    down_outs = [(((n, 4, DEPTH, 768), bf), slab_block) for n in (4, 1, 1, 1, 1)]
+    up_outs = [(((n, 4, DEPTH, 768), bf), slab_block) for n in (4, 4)]
+    attn_outs = [(((n, 4, DEPTH + EXTRA, 768), bf), slab_block) for n in (4, 1, 1, 1, 1)]
     thin = ((4, 1, 768), fl)
 
     if fast:
@@ -529,10 +564,15 @@
         [row_b, row_f, (wide, bf), (wide, fl), ((3, width), fl), whole, whole],
         where, xhat, first, dy, vec, b_up, *pieces,
     )
-    down_near, *down_far = call(
-        down_weights_kernel, "down_weights", down_shapes, where, dr2, act,
-    )
-    dup, b_up_grad = call(down_bwd_kernel, "down_bwd", [(wide, bf), thin], where, dr2, slope, down_w)
+    turned = pltpu.VMEM((width, length), bf)
+    down_near, *down_far = call_groups(
+        down_weights_kernel, "down_weights", down_outs, where, (dr2, whole_block), (act, group_block),
+        scratch=[turned],
+    )
+    dup, b_up_grad = call_groups(
+        down_bwd_kernel, "down_bwd", [((wide, bf), group_block), (thin, group_block)],
+        where, (dr2, whole_block), (slope, group_block), (down_w, group_block),
+    )
     out_one = next_row(out, b_up_grad)
     wait = [out_one]
     if fast:
@@ -553,34 +593,40 @@
     if fast:
         down_pair = reduce_pair(down_half, 1, [bias_grad])
         wait += down_pair
-    attn_near, *attn_far = call(
-        attn_weights_kernel, "attn_weights", attn_shapes,
-        where, x, dproj, ctx, dr1, bias_grad, b_up_grad, small_one, small_two,
-        scratch=[pltpu.VMEM((EXTRA, width), fl)], after=wait,
-    )
-    up_near, *up_far = call(
-        up_weights_kernel, "up_weights", up_shapes, where, first, dup, after=[bias_grad, attn_near],
+    attn_near, *attn_far = call_groups(
+        attn_weights_kernel, "attn_weights", attn_outs,
+        where, (x, whole_block), (dproj, group_block), (ctx, group_block), (dr1, whole_block),
+        (bias_grad, group_block), (b_up_grad, group_block), (small_one, whole_block), (small_two, whole_block),
+        scratch=[pltpu.VMEM((EXTRA, width), fl), turned, turned], after=wait,
+    )
+    up_near, *up_far = call_groups(
+        up_weights_kernel, "up_weights", up_outs, where, (first, whole_block), (dup, group_block),
+        scratch=[turned], after=[bias_grad, attn_near],
     )
     in_one = rotate(grad_row)
     in_two = rotate(in_one)
     in_three = rotate(in_two)
     hidden_out = place_rows([out, out_one, out_two, out_three], spin)
-    grad_in = place_rows([grad_row, in_one, in_two, in_three], spin)
+    wait = []
     if fast:
         down_plane = reduce_chip(down_pair, 2)
         attn_far = late(attn_far, *down_plane)
         attn_half = halves(reduce_core(attn_near, attn_far, [up_near, in_one]))
         up_far = late(up_far, in_one, *attn_half)
-        down_sum = reduce_tensor(down_plane)
         up_pair = reduce_pair(reduce_core(up_near, up_far, parts=2), 1, [in_two])
         up_plane = reduce_chip(up_pair, 2)
-        attn_plane = reduce_chip(reduce_pair(attn_half, 2), 1, [in_three])
+        attn_pair = reduce_pair(attn_half, 2)
+        attn_plane = reduce_chip(attn_pair, 1, [in_three, *up_pair])
+        down_sum = reduce_tensor(down_plane, [*up_pair, *attn_pair])
         attn_sum = reduce_tensor([attn_plane[0]] + late(attn_plane[1:], *up_plane))
         up_sum = reduce_tensor(up_plane)
+        wait = up_plane + attn_plane
     else:
         down_sum = reduce_plain(down_near, down_far, x_last=True)
         up_sum = reduce_plain(up_near, up_far, x_last=True)
         attn_sum = reduce_plain(attn_near, attn_far)
+
+    grad_in = place_rows([grad_row, in_one, in_two, in_three], spin, wait)
 
     def own_part(value):
         size = value.shape[-1] // n_dp

time: 323 us -> 322 us (level)
  waiting for transfers between devices: 109 us -> 116 us
  other arithmetic: 32.3 us -> 28.4 us
  starting transfers between devices: 43.9 us -> 40.5 us
    pallas_call x10 -> x6, Pallas kernels: 110 us -> 73.4 us  [call(): pl.pallas_call(kernel, name=name, out_shape=[jax.ShapeDtypeStruct(s, d) f...]
    pallas_call x0 -> x4, Pallas kernels: none -> 35.1 us  [call_groups(): pl.pallas_call(kernel, name=name, out_shape=[jax.ShapeDtypeStruct(s, d) f...]
    ppermute x12, waiting for transfers between devices: 74.7 us -> 55.5 us  [cross(): return lax.ppermute(value, 'tensor', [(k, k ^ bits) for k in range(4)])]
    ppermute x6, waiting for transfers between devices: 8.05 us -> 25.5 us  [rotate(): return lax.ppermute(value, 'tensor', [(k, (k + 1) % 4) for k in range(4)])]
    ppermute x33, waiting for transfers between devices: 25.8 us -> 35.1 us  [flip(): return lax.ppermute(value, 'dp', [(k, k ^ bits) for k in range(n)])]
    unnamed x76 -> x78, local copies, waits for them, and re-layouts: 10.1 us -> 9.27 us
  transfers between devices with their start and end apart: 51 -> 51, of which waited for: 18 -> 21; matrix products, arithmetic and copies ran while one was open for 10% -> 9% of each run, Pallas kernels for 29% -> 28%
where the time goes in v6:
time: 322 us; the launch traced here: 321 us
  waiting for transfers between devices  116 us (36%)
  Pallas kernels  109 us (34%)
  starting transfers between devices  40.5 us (13%)
  other arithmetic  28.4 us (9%)
  local copies, waits for them, and re-layouts  25 us (8%)
    pallas_call x6, Pallas kernels, call(): pl.pallas_call(kernel, name=name, out_shape=[jax.ShapeDtypeStruct(s, d) f...  73.4 us
    ppermute x12, waiting for transfers between devices, cross(): return lax.ppermute(value, 'tensor', [(k, k ^ bits) for k in range(4)])  55.5 us
    ppermute x33, waiting for transfers between devices, flip(): return lax.ppermute(value, 'dp', [(k, k ^ bits) for k in range(n)])  35.1 us
    pallas_call x4, Pallas kernels, call_groups(): pl.pallas_call(kernel, name=name, out_shape=[jax.ShapeDtypeStruct(s, d) f...  35.1 us
    ppermute x6, waiting for transfers between devices, rotate(): return lax.ppermute(value, 'tensor', [(k, (k + 1) % 4) for k in range(4)])  25.5 us
    ppermute x33, starting transfers between devices, flip(): return lax.ppermute(value, 'dp', [(k, k ^ bits) for k in range(n)])  22.7 us
    ppermute x12, starting transfers between devices, cross(): return lax.ppermute(value, 'tensor', [(k, k ^ bits) for k in range(4)])  15.9 us
    unnamed x78, local copies, waits for them, and re-layouts  9.27 us
  transfers between devices with their start and end apart: 51, of which 21 were waited for; matrix products, arithmetic and copies ran while one was open for 9% of the time, Pallas kernels for 28%

profile of v6, /device:TPU:0, one launch (start us, length us, event | category | flops | bytes accessed | tf_op | source)
XLA Modules:
  0.0 320.7 jit_solution(10925241279568545512)
XLA Ops:
  7.4 3.1 collective-permute-start
  13.1 5.4 %collective-permute-done = bf16[112,768]{1,0:T(8,128)(2,1)S(1)} collective-permute-done((bf16[112,768]{1,0:T(8,128)(2,1)S(1)}, bf16[112,768]{1,0:T(8,128)(2,1)S(1)}, u32[]{:S(2)}, u32[]{:S(2)}) %collective-permute-start) | collective-permute-done | bytes 172064 | tf_op jit(solution)/shard_map/ppermute | solution.py:369
  18.5 7.6 %collective-permute-done.1 = bf16[112,768]{1,0:T(8,128)(2,1)S(1)} collective-permute-done((bf16[112,768]{1,0:T(8,128)(2,1)S(1)}, bf16[112,768]{1,0:T(8,128)(2,1)S(1)}, u32[]{:S(2)}, u32[]{:S(2)}) %collective-permute-start.1) | collective-permute-done | bytes 172064 | tf_op jit(solution)/shard_map/ppermute | solution.py:369
  35.7 6.3 %collective-permute-done.6.refs_1_ = bf16[4,112,768]{2,1,0:T(8,128)(2,1)} collective-permute-done((bf16[4,112,768]{2,1,0:T(8,128)(2,1)S(1)}, bf16[4,112,768]{2,1,0:T(8,128)(2,1)}, u32[]{:S(2)}, u32[]{:S(2)}) %collective-permute-start.6) | collective-permute-done | bytes 688160 | tf_op jit(solution)/shard_map/ppermute | solution.py:365
  49.2 3.4 %collective-permute-start.9 = (bf16[2,112,768]{2,1,0:T(8,128)(2,1)S(1)}, bf16[2,112,768]{2,1,0:T(8,128)(2,1)S(1)}, u32[]{:S(2)}, u32[]{:S(2)}) collective-permute-start(bf16[2,112,768]{2,1,0:T(8,128)(2,1)S(1)} %slice.460), channel_id=1, source_target_pairs={{0,8},{4,12},{8,0},{12,4},{16,24},{20,28},{24,16},{28,20},{1,9},{5... | collective-permute-start | bytes 1032200 | tf_op jit(solution)/shard_map/ppermute | solution.py:365
  52.7 8.6 %collective-permute-done.5 = bf16[192,768]{1,0:T(8,128)(2,1)S(1)} collective-permute-done((bf16[192,768]{1,0:T(8,128)(2,1)S(1)}, bf16[192,768]{1,0:T(8,128)(2,1)S(1)}, u32[]{:S(2)}, u32[]{:S(2)}) %collective-permute-start.5) | collective-permute-done | bytes 294944 | tf_op jit(solution)/shard_map/ppermute | solution.py:369
  70.8 15.5 %attn_fwd.1 = (bf16[4,512,768]{2,1,0:T(8,128)(2,1)}, bf16[4,512,256]{2,1,0:T(8,128)(2,1)}, f32[4,3,1,512]{3,2,1,0:T(1,128)}, bf16[4,8,112,768]{3,2,1,0:T(8,128)(...) custom-call(s32[2]{0:T(128)} %pad_add_fusion.1.where_ref, ...), custom_call_target="tpu_custom_call" | custom-call | flops 1000 | bytes 1000 | tf_op jit(solution)/shard_map/attn_fwd/pallas_call | solution.py:311
  91.2 12.7 %collective-permute-done.17.refs_3_ = bf16[2,192,768]{2,1,0:T(8,128)(2,1)S(1)} collective-permute-done((bf16[2,192,768]{2,1,0:T(8,128)(2,1)S(1)}, bf16[2,192,768]{2,1,0:T(8,128)(2,1)S(1)}, u32[]{:S(2)}, u32[]{:S(2)}) %collective-permute-start.17) | collective-permute-done | bytes 589856 | tf_op jit(solution)/shard_map/ppermute | solution.py:365
  108.3 17.7 %ffn_fwd.1 = (bf16[512,768]{1,0:T(8,128)(2,1)}, f32[512,768]{1,0:T(8,128)}, bf16[4,512,768]{2,1,0:T(8,128)(2,1)}, f32[4,512,768]{2,1,0:T(8,128)}, f32[3,768]{1,0...) custom-call(s32[2]{0:T(128)} %pad_add_fusion.1.where_ref, ...), custom_call_target="tpu_custom_call" | custom-call | flops 1000 | bytes 1000 | tf_op jit(solution)/shard_map/ffn_fwd/pallas_call | solution.py:311
  127.2 8.2 %down_weights.1 = (bf16[4,4,96,768]{3,2,1,0:T(8,128)(2,1)}, bf16[1,4,96,768]{3,2,1,0:T(8,128)(2,1)}, bf16[1,4,96,768]{3,2,1,0:T(8,128)(2,1)}, bf16[1,4,96,768]{3,2,1,0:T(8,128)(2,1)}, bf16[1,4,96,768]{3,2,1,0:T(8,128)(2,1)}) custom-call(s32[2]{0:T(128)} %pad_add_fusion.1.where_ref, f32[512,768]{1,0:T(8,128)} %get-tuple-element.104.dr2_ref, ...), custom_call_target="tpu_custom_call" | custom-call | flops 1000 | bytes 1000 | tf_op jit(solution)/shard_map/down_weights/pallas_call | solution.py:345
  136.4 9.3 %down_bwd.1 = (bf16[4,512,768]{2,1,0:T(8,128)(2,1)}, f32[4,1,768]{2,1,0:T(1,128)}) custom-call(s32[2]{0:T(128)} %pad_add_fusion.1.where_ref, f32[512,768]{1,0:T(8,128)} %get-tuple-element.104.dr2_ref, f32[4,512,768]{2,1,0:T(8,128)} %get-tuple-element.105.slope_ref, bf16[4,8,96,768]{3,2,1,0:T(8,128)(2,1)} %get-tuple-element.106.weight_ref), custom_call_target="tpu_custom_call" | custom-call | flops 1000 | bytes 1000 | tf_op jit(solution)/shard_map/down_bwd/pallas_call | solution.py:345
  154.0 12.2 %up_bwd.1 = (f32[512,768]{1,0:T(8,128)}, bf16[4,512,256]{2,1,0:T(8,128)(2,1)}, f32[3,768]{1,0:T(4,128)}) custom-call(s32[2]{0:T(128)} %pad_add_fusion.1.where_ref, f32[512,768]{1,0:T(8,128)} %get-tuple-element.104.dr2_ref, bf16[4,512,768]{2,1,0:T(8,128)(2,1)} %get-tuple-element.118.dup_ref, f32[512,768]{1,0:T(8,128)} %get-tuple-element.97.xhat_ref, ...), custom_call_target="tpu_custom_call" | custom-call | flops 1000 | bytes 1000 | tf_op jit(solution)/shard_map/up_bwd/pallas_call | solution.py:311
  166.2 7.4 %collective-permute-done.25.refs_2_ = bf16[512,768]{1,0:T(8,128)(2,1)} collective-permute-done((bf16[512,768]{1,0:T(8,128)(2,1)S(1)}, bf16[512,768]{1,0:T(8,128)(2,1)}, u32[]{:S(2)}, u32[]{:S(2)}) %collective-permute-start.25) | collective-permute-done | bytes 786464 | tf_op jit(solution)/shard_map/ppermute | solution.py:373
  173.7 20.5 %attn_bwd.1 = (bf16[512,768]{1,0:T(8,128)(2,1)}, bf16[4,512,768]{2,1,0:T(8,128)(2,1)}, f32[4,1,768]{2,1,0:T(1,128)}) custom-call(s32[2]{0:T(128)} %pad_add_fusion.1.where_ref, s32[1,512]{1,0:T(1,128)} %constant_dynamic-slice_fusion.2.seg_row_ref, s32[512,1]{1,0:T(8,128)} %copy.38.seg_col_ref, bf16[4,512,768]{2,1,0:T(8,128)(2,1)} %get-tuple-element.125.proj_ref, ...), custom_call_target="tpu_custom_call" | custom-call | flops 1000 | bytes 1000 | tf_op jit(solution)/shard_map/attn_bwd/pallas_call | solution.py:311
  198.7 9.7 %attn_weights.1 = (bf16[4,4,112,768]{3,2,1,0:T(8,128)(2,1)}, bf16[1,4,112,768]{3,2,1,0:T(8,128)(2,1)}, bf16[1,4,112,768]{3,2,1,0:T(8,128)(2,1)}, bf16[1,4,112,76...) custom-call(s32[2]{0:T(128)} %pad_add_fusion.1.where_ref, bf16[512,768]{1,0:T(8,128)(2,1)} %dynamic-slice_bitcast_fusion.1.x_ref, ...), custom_call_target="tpu_custom_call" | custom-call | flops 1000 | bytes 1000 | tf_op jit(solution)/shard_map/attn_weights/pallas_call | solution.py:345
  212.7 7.9 %up_weights.1 = (bf16[4,4,96,768]{3,2,1,0:T(8,128)(2,1)}, bf16[4,4,96,768]{3,2,1,0:T(8,128)(2,1)}) custom-call(s32[2]{0:T(128)} %pad_add_fusion.1.where_ref, bf16[512,768]{1,0:T(8,128)(2,1)} %get-tuple-element.98.first_ref, bf16[4,512,768]{2,1,0:T(8,128)(2,1)} %get-tuple-element.118.dup_ref), custom_call_target="tpu_custom_call" | custom-call | flops 1000 | bytes 1000 | tf_op jit(solution)/shard_map/up_weights/pallas_call | solution.py:345
  230.2 16.0 %collective-permute-done.40.refs_2_ = bf16[512,768]{1,0:T(8,128)(2,1)} collective-permute-done((bf16[512,768]{1,0:T(8,128)(2,1)}, bf16[512,768]{1,0:T(8,128)(2,1)}, u32[]{:S(2)}, u32[]{:S(2)}) %collective-permute-start.40) | collective-permute-done | bytes 786464 | tf_op jit(solution)/shard_map/ppermute | solution.py:373
  246.2 9.2 %collective-permute-done.42 = bf16[2,4,112,768]{3,2,1,0:T(8,128)(2,1)S(1)} collective-permute-done((bf16[2,4,112,768]{3,2,1,0:T(8,128)(2,1)S(1)}, bf16[2,4,112,768]{3,2,1,0:T(8,128)(2,1)S(1)}, u32[]{:S(2)}, u32[]{:S(2)}) %collective-permute-start.42) | collective-permute-done | bytes 1376288 | tf_op jit(solution)/shard_map/ppermute | solution.py:365
  260.6 3.7 %place_rows.2 = bf16[4,512,768]{2,1,0:T(8,128)(2,1)} custom-call(s32[2]{0:T(128)} %pad_add_fusion.where_ref, bf16[512,768]{1,0:T(8,128)(2,1)} %get-tuple-element.103.refs_0_, bf16[512,768]{1,0:T(8,128)(2,1)} %copy-done.11, bf16[512,768]{1,0:T(8,128)(2,1)} %collective-permute-done.25.refs_2_, bf16[512,768]{1,0:T(8,128)(2,1)} %collective-permute-done.30.refs_3_), custom_call_target="tpu_custom_call" | custom-call | flops 1000 | bytes 1000 | tf_op jit(solution)/shard_map/place_rows/pallas_call | solution.py:311
  267.2 6.2 %collective-permute-done.49 = bf16[2,96,768]{2,1,0:T(8,128)(2,1)} collective-permute-done((bf16[2,96,768]{2,1,0:T(8,128)(2,1)S(1)}, bf16[2,96,768]{2,1,0:T(8,128)(2,1)}, u32[]{:S(2)}, u32[]{:S(2)}) %collective-permute-start.49) | collective-permute-done | bytes 294944 | tf_op jit(solution)/shard_map/ppermute | solution.py:369
  279.2 5.0 %collective-permute-done.50 = bf16[96,768]{1,0:T(8,128)(2,1)S(1)} collective-permute-done((bf16[96,768]{1,0:T(8,128)(2,1)S(1)}, bf16[96,768]{1,0:T(8,128)(2,1)S(1)}, u32[]{:S(2)}, u32[]{:S(2)}) %collective-permute-start.50) | collective-permute-done | bytes 147488 | tf_op jit(solution)/shard_map/ppermute | solution.py:369
  288.5 3.8 %place_rows.3 = bf16[4,512,768]{2,1,0:T(8,128)(2,1)} custom-call(s32[2]{0:T(128)} %pad_add_fusion.where_ref, bf16[512,768]{1,0:T(8,128)(2,1)} %get-tuple-element.141.refs_0_, bf16[512,768]{1,0:T(8,128)(2,1)} %collective-permute-done.32.refs_1_, bf16[512,768]{1,0:T(8,128)(2,1)} %collective-permute-done.40.refs_2_, ...), custom_call_target="tpu_custom_call" | custom-call | flops 1000 | bytes 1000 | tf_op jit(solution)/shard_map/place_rows/pallas_call | solution.py:311
  296.6 7.7 %collective-permute-done.45 = bf16[2,112,768]{2,1,0:T(8,128)(2,1)S(1)} collective-permute-done((bf16[2,112,768]{2,1,0:T(8,128)(2,1)}, bf16[2,112,768]{2,1,0:T(8,128)(2,1)S(1)}, u32[]{:S(2)}, u32[]{:S(2)}) %collective-permute-start.45) | collective-permute-done | bytes 344096 | tf_op jit(solution)/shard_map/ppermute | solution.py:369
  306.0 7.4 %collective-permute-done.46 = bf16[112,768]{1,0:T(8,128)(2,1)S(1)} collective-permute-done((bf16[112,768]{1,0:T(8,128)(2,1)S(1)}, bf16[112,768]{1,0:T(8,128)(2,1)S(1)}, u32[]{:S(2)}, u32[]{:S(2)}) %collective-permute-start.46) | collective-permute-done | bytes 172064 | tf_op jit(solution)/shard_map/ppermute | solution.py:369
  (263 shorter events, 104.1 us)
Async XLA Ops:
  10.5 15.6 %collective-permute-start.1 = (bf16[112,768]{1,0:T(8,128)(2,1)S(1)}, bf16[112,768]{1,0:T(8,128)(2,1)S(1)}, u32[]{:S(2)}, u32[]{:S(2)}) collective-permute-start(bf16[112,768]{1,0:T(8,128)(2,1)S(1)} %concatenate.66), channel_id=1, source_target_pairs={{0,2},{1,3},{2,0},{3,1},{4,6},{5,7},{6,4},{7,5},{8,10},{9,11},{10,... | collective-permute-start | bytes 516104 | tf_op jit(solution)/shard_map/ppermute | solution.py:369
  26.2 15.9 %collective-permute-start.6 = (bf16[4,112,768]{2,1,0:T(8,128)(2,1)S(1)}, bf16[4,112,768]{2,1,0:T(8,128)(2,1)}, u32[]{:S(2)}, u32[]{:S(2)}) collective-permute-start(bf16[4,112,768]{2,1,0:T(8,128)(2,1)S(1)} %pad_maximum_fusion.3.refs_0_), channel_id=1, source_target_pairs={{0,8},{4,12},{8,0},{12,4},{16,24},{20,28},{24,16},{28,20},{1,9},{5... | collective-permute-start | bytes 2064392 | tf_op jit(solution)/shard_map/ppermute | solution.py:365
  28.2 14.9 %collective-permute-start.7 = (bf16[4,112,768]{2,1,0:T(8,128)(2,1)S(1)}, bf16[4,112,768]{2,1,0:T(8,128)(2,1)}, u32[]{:S(2)}, u32[]{:S(2)}) collective-permute-start(bf16[4,112,768]{2,1,0:T(8,128)(2,1)S(1)} %pad_maximum_fusion.3.refs_0_), channel_id=1, source_target_pairs={{0,16},{4,20},{8,24},{12,28},{16,0},{20,4},{24,8},{28,12},{1,17},{... | collective-permute-start | bytes 2064392 | tf_op jit(solution)/shard_map/ppermute | solution.py:365
  31.7 14.6 %collective-permute-start.3 = (bf16[192,768]{1,0:T(8,128)(2,1)S(1)}, bf16[192,768]{1,0:T(8,128)(2,1)S(1)}, u32[]{:S(2)}, u32[]{:S(2)}) collective-permute-start(bf16[192,768]{1,0:T(8,128)(2,1)S(1)} %pad_maximum_fusion.7), channel_id=1, source_target_pairs={{0,1},{1,0},{2,3},{3,2},{4,5},{5,4},{6,7},{7,6},{8,9},{9,8},{10,11... | collective-permute-start | bytes 884744 | tf_op jit(solution)/shard_map/ppermute | solution.py:369
  63.2 23.1 %collective-permute-start.15 = (bf16[4,192,768]{2,1,0:T(8,128)(2,1)}, bf16[4,192,768]{2,1,0:T(8,128)(2,1)}, u32[]{:S(2)}, u32[]{:S(2)}) collective-permute-start(bf16[4,192,768]{2,1,0:T(8,128)(2,1)} %pad_maximum_fusion.1.refs_0_), channel_id=1, source_target_pairs={{0,8},{4,12},{8,0},{12,4},{16,24},{20,28},{24,16},{28,20},{1,9},{5... | collective-permute-start | bytes 3538952 | tf_op jit(solution)/shard_map/ppermute | solution.py:365
  63.2 24.2 %collective-permute-start.16 = (bf16[4,192,768]{2,1,0:T(8,128)(2,1)}, bf16[4,192,768]{2,1,0:T(8,128)(2,1)}, u32[]{:S(2)}, u32[]{:S(2)}) collective-permute-start(bf16[4,192,768]{2,1,0:T(8,128)(2,1)} %pad_maximum_fusion.1.refs_0_), channel_id=1, source_target_pairs={{0,16},{4,20},{8,24},{12,28},{16,0},{20,4},{24,8},{28,12},{1,17},{... | collective-permute-start | bytes 3538952 | tf_op jit(solution)/shard_map/ppermute | solution.py:365
  70.1 36.4 %collective-permute-start.19 = (bf16[4,192,768]{2,1,0:T(8,128)(2,1)}, bf16[4,192,768]{2,1,0:T(8,128)(2,1)S(1)}, u32[]{:S(2)}, u32[]{:S(2)}) collective-permute-start(bf16[4,192,768]{2,1,0:T(8,128)(2,1)} %pad_maximum_fusion.1.refs_0_), channel_id=1, source_target_pairs={{0,4},{4,0},{8,12},{12,8},{16,20},{20,16},{24,28},{28,24},{1,5},{5... | collective-permute-start | bytes 3538952 | tf_op jit(solution)/shard_map/ppermute | solution.py:365
  88.5 15.3 %collective-permute-start.17 = (bf16[2,192,768]{2,1,0:T(8,128)(2,1)S(1)}, bf16[2,192,768]{2,1,0:T(8,128)(2,1)S(1)}, u32[]{:S(2)}, u32[]{:S(2)}) collective-permute-start(bf16[2,192,768]{2,1,0:T(8,128)(2,1)S(1)} %slice.461), channel_id=1, source_target_pairs={{0,16},{4,20},{8,24},{12,28},{16,0},{20,4},{24,8},{28,12},{1,17},{... | collective-permute-start | bytes 1769480 | tf_op jit(solution)/shard_map/ppermute | solution.py:365
  88.6 15.5 %collective-permute-start.18 = (bf16[2,192,768]{2,1,0:T(8,128)(2,1)S(1)}, bf16[2,192,768]{2,1,0:T(8,128)(2,1)S(1)}, u32[]{:S(2)}, u32[]{:S(2)}) collective-permute-start(bf16[2,192,768]{2,1,0:T(8,128)(2,1)S(1)} %slice.462), channel_id=1, source_target_pairs={{0,8},{4,12},{8,0},{12,4},{16,24},{20,28},{24,16},{28,20},{1,9},{5... | collective-permute-start | bytes 1769480 | tf_op jit(solution)/shard_map/ppermute | solution.py:365
  90.6 16.1 %collective-permute-start.20 = (bf16[4,192,768]{2,1,0:T(8,128)(2,1)}, bf16[4,192,768]{2,1,0:T(8,128)(2,1)S(1)}, u32[]{:S(2)}, u32[]{:S(2)}) collective-permute-start(bf16[4,192,768]{2,1,0:T(8,128)(2,1)} %collective-permute-done.15.refs_1_), channel_id=1, source_target_pairs={{0,4},{4,0},{8,12},{12,8},{16,20},{20,16},{24,28},{28,24},{1,5},{5... | collective-permute-start | bytes 3538952 | tf_op jit(solution)/shard_map/ppermute | solution.py:365
  90.6 16.7 %collective-permute-start.21 = (bf16[4,192,768]{2,1,0:T(8,128)(2,1)}, bf16[4,192,768]{2,1,0:T(8,128)(2,1)}, u32[]{:S(2)}, u32[]{:S(2)}) collective-permute-start(bf16[4,192,768]{2,1,0:T(8,128)(2,1)} %collective-permute-done.16.refs_2_), channel_id=1, source_target_pairs={{0,4},{4,0},{8,12},{12,8},{16,20},{20,16},{24,28},{28,24},{1,5},{5... | collective-permute-start | bytes 3538952 | tf_op jit(solution)/shard_map/ppermute | solution.py:365
  126.0 21.8 %collective-permute-start.24 = (bf16[512,768]{1,0:T(8,128)(2,1)}, bf16[512,768]{1,0:T(8,128)(2,1)S(1)}, u32[]{:S(2)}, u32[]{:S(2)}) collective-permute-start(bf16[512,768]{1,0:T(8,128)(2,1)} %get-tuple-element.103.refs_0_), channel_id=1, source_target_pairs={{0,1},{1,2},{2,3},{3,0},{4,5},{5,6},{6,7},{7,4},{8,9},{9,10},{10,1... | collective-permute-start | bytes 2359304 | tf_op jit(solution)/shard_map/ppermute | solution.py:373
  151.3 42.9 %collective-permute-start.31 = (bf16[2,4,96,768]{3,2,1,0:T(8,128)(2,1)}, bf16[2,4,96,768]{3,2,1,0:T(8,128)(2,1)}, u32[]{:S(2)}, u32[]{:S(2)}) collective-permute-start(bf16[2,4,96,768]{3,2,1,0:T(8,128)(2,1)} %pad_maximum_fusion.2), channel_id=1, source_target_pairs={{0,8},{4,12},{8,0},{12,4},{16,24},{20,28},{24,16},{28,20},{1,9},{5... | collective-permute-start | bytes 3538952 | tf_op jit(solution)/shard_map/ppermute | solution.py:365
  153.2 20.4 %collective-permute-start.25 = (bf16[512,768]{1,0:T(8,128)(2,1)S(1)}, bf16[512,768]{1,0:T(8,128)(2,1)}, u32[]{:S(2)}, u32[]{:S(2)}) collective-permute-start(bf16[512,768]{1,0:T(8,128)(2,1)S(1)} %collective-permute-done.24.refs_1_), channel_id=1, source_target_pairs={{0,1},{1,2},{2,3},{3,0},{4,5},{5,6},{6,7},{7,4},{8,9},{9,10},{10,1... | collective-permute-start | bytes 2359304 | tf_op jit(solution)/shard_map/ppermute | solution.py:373
  173.7 25.0 %collective-permute-start.30 = (bf16[512,768]{1,0:T(8,128)(2,1)}, bf16[512,768]{1,0:T(8,128)(2,1)}, u32[]{:S(2)}, u32[]{:S(2)}) collective-permute-start(bf16[512,768]{1,0:T(8,128)(2,1)} %collective-permute-done.25.refs_2_), channel_id=1, source_target_pairs={{0,1},{1,2},{2,3},{3,0},{4,5},{5,6},{6,7},{7,4},{8,9},{9,10},{10,1... | collective-permute-start | bytes 2359304 | tf_op jit(solution)/shard_map/ppermute | solution.py:373
  198.7 21.9 %collective-permute-start.32 = (bf16[512,768]{1,0:T(8,128)(2,1)S(1)}, bf16[512,768]{1,0:T(8,128)(2,1)}, u32[]{:S(2)}, u32[]{:S(2)}) collective-permute-start(bf16[512,768]{1,0:T(8,128)(2,1)S(1)} %copy-done.12), channel_id=1, source_target_pairs={{0,1},{1,2},{2,3},{3,0},{4,5},{5,6},{6,7},{7,4},{8,9},{9,10},{10,1... | collective-permute-start | bytes 2359304 | tf_op jit(solution)/shard_map/ppermute | solution.py:373
  222.8 32.6 %collective-permute-start.42 = (bf16[2,4,112,768]{3,2,1,0:T(8,128)(2,1)S(1)}, bf16[2,4,112,768]{3,2,1,0:T(8,128)(2,1)S(1)}, u32[]{:S(2)}, u32[]{:S(2)}) collective-permute-start(bf16[2,4,112,768]{3,2,1,0:T(8,128)(2,1)S(1)} %pad_maximum_fusion), channel_id=1, source_target_pairs={{0,16},{4,20},{8,24},{12,28},{16,0},{20,4},{24,8},{28,12},{1,17},{... | collective-permute-start | bytes 4128776 | tf_op jit(solution)/shard_map/ppermute | solution.py:365
  224.4 21.8 %collective-permute-start.40 = (bf16[512,768]{1,0:T(8,128)(2,1)}, bf16[512,768]{1,0:T(8,128)(2,1)}, u32[]{:S(2)}, u32[]{:S(2)}) collective-permute-start(bf16[512,768]{1,0:T(8,128)(2,1)} %collective-permute-done.32.refs_1_), channel_id=1, source_target_pairs={{0,1},{1,2},{2,3},{3,0},{4,5},{5,6},{6,7},{7,4},{8,9},{9,10},{10,1... | collective-permute-start | bytes 2359304 | tf_op jit(solution)/shard_map/ppermute | solution.py:373
  229.0 35.3 %collective-permute-start.39 = (bf16[2,4,96,768]{3,2,1,0:T(8,128)(2,1)}, bf16[2,4,96,768]{3,2,1,0:T(8,128)(2,1)}, u32[]{:S(2)}, u32[]{:S(2)}) collective-permute-start(bf16[2,4,96,768]{3,2,1,0:T(8,128)(2,1)} %get-tuple-element.205), channel_id=1, source_target_pairs={{0,8},{4,12},{8,0},{12,4},{16,24},{20,28},{24,16},{28,20},{1,9},{5... | collective-permute-start | bytes 3538952 | tf_op jit(solution)/shard_map/ppermute | solution.py:365
  246.2 28.2 %collective-permute-start.44 = (bf16[512,768]{1,0:T(8,128)(2,1)}, bf16[512,768]{1,0:T(8,128)(2,1)}, u32[]{:S(2)}, u32[]{:S(2)}) collective-permute-start(bf16[512,768]{1,0:T(8,128)(2,1)} %collective-permute-done.40.refs_2_), channel_id=1, source_target_pairs={{0,1},{1,2},{2,3},{3,0},{4,5},{5,6},{6,7},{7,4},{8,9},{9,10},{10,1... | collective-permute-start | bytes 2359304 | tf_op jit(solution)/shard_map/ppermute | solution.py:373
  258.0 17.4 %collective-permute-start.43 = (bf16[4,112,768]{2,1,0:T(8,128)(2,1)}, bf16[4,112,768]{2,1,0:T(8,128)(2,1)}, u32[]{:S(2)}, u32[]{:S(2)}) collective-permute-start(bf16[4,112,768]{2,1,0:T(8,128)(2,1)} %get-tuple-element.207), channel_id=1, source_target_pairs={{0,8},{4,12},{8,0},{12,4},{16,24},{20,28},{24,16},{28,20},{1,9},{5... | collective-permute-start | bytes 2064392 | tf_op jit(solution)/shard_map/ppermute | solution.py:365
  259.0 14.4 %collective-permute-start.49 = (bf16[2,96,768]{2,1,0:T(8,128)(2,1)S(1)}, bf16[2,96,768]{2,1,0:T(8,128)(2,1)}, u32[]{:S(2)}, u32[]{:S(2)}) collective-permute-start(bf16[2,96,768]{2,1,0:T(8,128)(2,1)S(1)} %copy-done.25), channel_id=1, source_target_pairs={{0,1},{1,0},{2,3},{3,2},{4,5},{5,4},{6,7},{7,6},{8,9},{9,8},{10,11... | collective-permute-start | bytes 884744 | tf_op jit(solution)/shard_map/ppermute | solution.py:369
  265.9 19.4 %collective-permute-start.41 = (bf16[4,96,768]{2,1,0:T(8,128)(2,1)S(1)}, bf16[4,96,768]{2,1,0:T(8,128)(2,1)S(1)}, u32[]{:S(2)}, u32[]{:S(2)}) collective-permute-start(bf16[4,96,768]{2,1,0:T(8,128)(2,1)S(1)} %get-tuple-element.214), channel_id=1, source_target_pairs={{0,16},{4,20},{8,24},{12,28},{16,0},{20,4},{24,8},{28,12},{1,17},{... | collective-permute-start | bytes 1769480 | tf_op jit(solution)/shard_map/ppermute | solution.py:365
  285.6 18.7 %collective-permute-start.45 = (bf16[2,112,768]{2,1,0:T(8,128)(2,1)}, bf16[2,112,768]{2,1,0:T(8,128)(2,1)S(1)}, u32[]{:S(2)}, u32[]{:S(2)}) collective-permute-start(bf16[2,112,768]{2,1,0:T(8,128)(2,1)} %get-tuple-element.159), channel_id=1, source_target_pairs={{0,1},{1,0},{2,3},{3,2},{4,5},{5,4},{6,7},{7,6},{8,9},{9,8},{10,11... | collective-permute-start | bytes 1032200 | tf_op jit(solution)/shard_map/ppermute | solution.py:369
  (62 other events, 593.3 us)

commit v7 on v6

--- a/solution.py
+++ b/solution.py
@@ -106,11 +106,12 @@
         low = low_lanes((length, LANES))
         none = jnp.zeros((length, LANES), bf)
         parts = [proj[:, LANES * k : LANES * (k + 1)] for k in range(6)]
+        turned = [parts[2].T, parts[3].T]
         outs = []
         for head in range(3):
             query = parts[0] if head < 2 else parts[3]
             keys = parts[1] if head < 2 else parts[5]
-            value = parts[2] if head < 2 else parts[3]
+            value = turned[0][:HD] if head == 0 else turned[head // 2][HD:]
             query = jnp.where(low, none, query) if head == 1 else jnp.where(low, query, none)
             scores = jnp.where(same, nt(keys, query) * scale, -1e30)
             top = jnp.max(scores, axis=0, keepdims=True)
@@ -118,10 +119,10 @@
             denom = jnp.sum(expd, axis=0, keepdims=True)
             lse_ref[g, head] = top + jnp.log(denom)
             probs = (expd / denom).astype(bf)
-            outs.append(tn(probs, value).astype(bf))
-        ctx_ref[g] = jnp.concatenate(
-            [jnp.where(low, outs[0], outs[1]), jnp.where(low, none, outs[2])], axis=1
-        )
+            outs.append(nn(value, probs))
+        outs.insert(2, jnp.zeros_like(outs[2]))
+        ctx_ref[g, :, :LANES] = jnp.concatenate(outs[:2]).T.astype(bf)
+        ctx_ref[g, :, LANES:] = jnp.concatenate(outs[2:]).T.astype(bf)
         return carry
 
     lax.fori_loop(0, 4, group_step, 0)
@@ -236,6 +237,7 @@
         none = jnp.zeros((length, LANES), bf)
         parts = [proj_ref[g, :, LANES * k : LANES * (k + 1)] for k in range(6)]
         dctx = [dctx_ref[g, :, :LANES], dctx_ref[g, :, LANES:]]
+        turned = [parts[1].T, parts[5].T]
         dq, dk, dv = [], [], []
         for head in range(3):
             query = parts[0] if head < 2 else parts[3]
@@ -250,14 +252,17 @@
             dv.append(nn(probs.astype(bf), dout))
             row_dot = jnp.sum(probs * dprobs, axis=0, keepdims=True)
             dscores = (probs * (dprobs - row_dot)).astype(bf)
-            dq.append(tn(dscores, keys) * scale)
+            keys_turned = turned[0][HD:] if head == 1 else turned[head // 2][:HD]
+            dq.append(nn(keys_turned, dscores) * scale)
             dk.append(nn(dscores, query) * scale)
+        dq.append(jnp.zeros_like(dq[2]))
+        dq_near, dq_far = jnp.concatenate(dq[:2]).T, jnp.concatenate(dq[2:]).T
         dproj = jnp.concatenate(
             [
-                jnp.where(low, dq[0], dq[1]).astype(bf),
+                dq_near.astype(bf),
                 jnp.where(low, dk[0], dk[1]).astype(bf),
                 jnp.where(low, dv[0], dv[1]).astype(bf),
-                jnp.where(low, dq[2], dv[2]).astype(bf),
+                jnp.where(low, dq_far, dv[2]).astype(bf),
                 none,
                 jnp.where(low, dk[2].astype(bf), none),
             ],
@@ -436,8 +441,14 @@
     got = cross(plane[1], 1)
     if gates:
         (got,) = late([got], *gates)
-    near, far = add(plane[0][0], got[0]), add(plane[0][1], got[1]).astype(bf)
-    return add(near, cross(far, 2))
+    return add(plane[0][0], got[0]), add(plane[0][1], got[1]).astype(bf)
+
+
+def reduce_last(pair, gates=()):
+    got = cross(pair[1], 2)
+    if gates:
+        (got,) = late([got], *gates)
+    return add(pair[0], got)
 
 
 def gather_plain(shard, extra=None):
@@ -617,9 +628,12 @@
         up_plane = reduce_chip(up_pair, 2)
         attn_pair = reduce_pair(attn_half, 2)
         attn_plane = reduce_chip(attn_pair, 1, [in_three, *up_pair])
-        down_sum = reduce_tensor(down_plane, [*up_pair, *attn_pair])
-        attn_sum = reduce_tensor([attn_plane[0]] + late(attn_plane[1:], *up_plane))
-        up_sum = reduce_tensor(up_plane)
+        down_last = reduce_tensor(down_plane, [*up_pair, *attn_pair])
+        attn_last = reduce_tensor([attn_plane[0]] + late(attn_plane[1:], *up_plane))
+        up_last = reduce_tensor(up_plane)
+        down_sum = reduce_last(down_last, [attn_last[1], up_last[1]])
+        attn_sum = reduce_last(attn_last)
+        up_sum = reduce_last(up_last)
         wait = up_plane + attn_plane
     else:
         down_sum = reduce_plain(down_near, down_far, x_last=True)

time: 322 us -> 314 us (0.975)
  other arithmetic: 28.4 us -> 22.5 us
    ppermute x6, waiting for transfers between devices: 25.5 us -> 35.6 us  [rotate(): return lax.ppermute(value, 'tensor', [(k, (k + 1) % 4) for k in range(4)])]
    ppermute x12, waiting for transfers between devices: 55.5 us -> 45.6 us  [cross(): return lax.ppermute(value, 'tensor', [(k, k ^ bits) for k in range(4)])]
    unnamed x78 -> x88, local copies, waits for them, and re-layouts: 9.27 us -> 8.96 us
  transfers between devices with their start and end apart: 51 -> 51, of which waited for: 21 -> 22; matrix products, arithmetic and copies ran while one was open for 9% -> 8% of each run, Pallas kernels for 28% -> 29%
where the time goes in v7:
time: 314 us; the launch traced here: 313 us
  waiting for transfers between devices  116 us (37%)
  Pallas kernels  108 us (34%)
  starting transfers between devices  39.9 us (13%)
  local copies, waits for them, and re-layouts  24.7 us (8%)
  other arithmetic  22.5 us (7%)
    pallas_call x6, Pallas kernels, call(): pl.pallas_call(kernel, name=name, out_shape=[jax.ShapeDtypeStruct(s, d) f...  72.7 us
    ppermute x12, waiting for transfers between devices, cross(): return lax.ppermute(value, 'tensor', [(k, k ^ bits) for k in range(4)])  45.6 us
    ppermute x6, waiting for transfers between devices, rotate(): return lax.ppermute(value, 'tensor', [(k, (k + 1) % 4) for k in range(4)])  35.6 us
    pallas_call x4, Pallas kernels, call_groups(): pl.pallas_call(kernel, name=name, out_shape=[jax.ShapeDtypeStruct(s, d) f...  35.1 us
    ppermute x33, waiting for transfers between devices, flip(): return lax.ppermute(value, 'dp', [(k, k ^ bits) for k in range(n)])  34.6 us
    ppermute x33, starting transfers between devices, flip(): return lax.ppermute(value, 'dp', [(k, k ^ bits) for k in range(n)])  23.5 us
    ppermute x12, starting transfers between devices, cross(): return lax.ppermute(value, 'tensor', [(k, k ^ bits) for k in range(4)])  15.6 us
    unnamed x88, local copies, waits for them, and re-layouts  8.96 us
  transfers between devices with their start and end apart: 51, of which 22 were waited for; matrix products, arithmetic and copies ran while one was open for 8% of the time, Pallas kernels for 29%

profile of v7, /device:TPU:0, one launch (start us, length us, event | category | flops | bytes accessed | tf_op | source)
XLA Modules:
  0.0 312.7 jit_solution(4772222434887965236)
XLA Ops:
  13.1 5.4 %collective-permute-done = bf16[112,768]{1,0:T(8,128)(2,1)S(1)} collective-permute-done((bf16[112,768]{1,0:T(8,128)(2,1)S(1)}, bf16[112,768]{1,0:T(8,128)(2,1)S(1)}, u32[]{:S(2)}, u32[]{:S(2)}) %collective-permute-start) | collective-permute-done | bytes 172064 | tf_op jit(solution)/shard_map/ppermute | solution.py:374
  18.5 7.6 %collective-permute-done.1 = bf16[112,768]{1,0:T(8,128)(2,1)S(1)} collective-permute-done((bf16[112,768]{1,0:T(8,128)(2,1)S(1)}, bf16[112,768]{1,0:T(8,128)(2,1)S(1)}, u32[]{:S(2)}, u32[]{:S(2)}) %collective-permute-start.1) | collective-permute-done | bytes 172064 | tf_op jit(solution)/shard_map/ppermute | solution.py:374
  35.7 6.3 %collective-permute-done.6.refs_1_ = bf16[4,112,768]{2,1,0:T(8,128)(2,1)} collective-permute-done((bf16[4,112,768]{2,1,0:T(8,128)(2,1)S(1)}, bf16[4,112,768]{2,1,0:T(8,128)(2,1)}, u32[]{:S(2)}, u32[]{:S(2)}) %collective-permute-start.6) | collective-permute-done | bytes 688160 | tf_op jit(solution)/shard_map/ppermute | solution.py:370
  49.2 3.4 %collective-permute-start.9 = (bf16[2,112,768]{2,1,0:T(8,128)(2,1)S(1)}, bf16[2,112,768]{2,1,0:T(8,128)(2,1)S(1)}, u32[]{:S(2)}, u32[]{:S(2)}) collective-permute-start(bf16[2,112,768]{2,1,0:T(8,128)(2,1)S(1)} %slice.460), channel_id=1, source_target_pairs={{0,8},{4,12},{8,0},{12,4},{16,24},{20,28},{24,16},{28,20},{1,9},{5... | collective-permute-start | bytes 1032200 | tf_op jit(solution)/shard_map/ppermute | solution.py:370
  52.7 8.6 %collective-permute-done.5 = bf16[192,768]{1,0:T(8,128)(2,1)S(1)} collective-permute-done((bf16[192,768]{1,0:T(8,128)(2,1)S(1)}, bf16[192,768]{1,0:T(8,128)(2,1)S(1)}, u32[]{:S(2)}, u32[]{:S(2)}) %collective-permute-start.5) | collective-permute-done | bytes 294944 | tf_op jit(solution)/shard_map/ppermute | solution.py:374
  70.8 15.7 %attn_fwd.1 = (bf16[4,512,768]{2,1,0:T(8,128)(2,1)}, bf16[4,512,256]{2,1,0:T(8,128)(2,1)}, f32[4,3,1,512]{3,2,1,0:T(1,128)}, bf16[4,8,112,768]{3,2,1,0:T(8,128)(...) custom-call(s32[2]{0:T(128)} %pad_add_fusion.1.where_ref, ...), custom_call_target="tpu_custom_call" | custom-call | flops 1000 | bytes 1000 | tf_op jit(solution)/shard_map/attn_fwd/pallas_call | solution.py:316
  91.3 13.2 %collective-permute-done.17.refs_3_ = bf16[2,192,768]{2,1,0:T(8,128)(2,1)S(1)} collective-permute-done((bf16[2,192,768]{2,1,0:T(8,128)(2,1)S(1)}, bf16[2,192,768]{2,1,0:T(8,128)(2,1)S(1)}, u32[]{:S(2)}, u32[]{:S(2)}) %collective-permute-start.17) | collective-permute-done | bytes 589856 | tf_op jit(solution)/shard_map/ppermute | solution.py:370
  109.4 17.7 %ffn_fwd.1 = (bf16[512,768]{1,0:T(8,128)(2,1)}, f32[512,768]{1,0:T(8,128)}, bf16[4,512,768]{2,1,0:T(8,128)(2,1)}, f32[4,512,768]{2,1,0:T(8,128)}, f32[3,768]{1,0...) custom-call(s32[2]{0:T(128)} %pad_add_fusion.1.where_ref, ...), custom_call_target="tpu_custom_call" | custom-call | flops 1000 | bytes 1000 | tf_op jit(solution)/shard_map/ffn_fwd/pallas_call | solution.py:316
  127.8 8.2 %down_weights.1 = (bf16[4,4,96,768]{3,2,1,0:T(8,128)(2,1)}, bf16[1,4,96,768]{3,2,1,0:T(8,128)(2,1)}, bf16[1,4,96,768]{3,2,1,0:T(8,128)(2,1)}, bf16[1,4,96,768]{3,2,1,0:T(8,128)(2,1)}, bf16[1,4,96,768]{3,2,1,0:T(8,128)(2,1)}) custom-call(s32[2]{0:T(128)} %pad_add_fusion.1.where_ref, f32[512,768]{1,0:T(8,128)} %get-tuple-element.105.dr2_ref, ...), custom_call_target="tpu_custom_call" | custom-call | flops 1000 | bytes 1000 | tf_op jit(solution)/shard_map/down_weights/pallas_call | solution.py:350
  137.1 9.3 %down_bwd.1 = (bf16[4,512,768]{2,1,0:T(8,128)(2,1)}, f32[4,1,768]{2,1,0:T(1,128)}) custom-call(s32[2]{0:T(128)} %pad_add_fusion.1.where_ref, f32[512,768]{1,0:T(8,128)} %get-tuple-element.105.dr2_ref, f32[4,512,768]{2,1,0:T(8,128)} %get-tuple-element.106.slope_ref, bf16[4,8,96,768]{3,2,1,0:T(8,128)(2,1)} %get-tuple-element.107.weight_ref), custom_call_target="tpu_custom_call" | custom-call | flops 1000 | bytes 1000 | tf_op jit(solution)/shard_map/down_bwd/pallas_call | solution.py:350
  152.8 12.2 %up_bwd.1 = (f32[512,768]{1,0:T(8,128)}, bf16[4,512,256]{2,1,0:T(8,128)(2,1)}, f32[3,768]{1,0:T(4,128)}) custom-call(s32[2]{0:T(128)} %pad_add_fusion.1.where_ref, f32[512,768]{1,0:T(8,128)} %get-tuple-element.105.dr2_ref, bf16[4,512,768]{2,1,0:T(8,128)(2,1)} %get-tuple-element.119.dup_ref, f32[512,768]{1,0:T(8,128)} %get-tuple-element.98.xhat_ref, ...), custom_call_target="tpu_custom_call" | custom-call | flops 1000 | bytes 1000 | tf_op jit(solution)/shard_map/up_bwd/pallas_call | solution.py:316
  165.0 8.4 %collective-permute-done.25.refs_2_ = bf16[512,768]{1,0:T(8,128)(2,1)} collective-permute-done((bf16[512,768]{1,0:T(8,128)(2,1)}, bf16[512,768]{1,0:T(8,128)(2,1)}, u32[]{:S(2)}, u32[]{:S(2)}) %collective-permute-start.25) | collective-permute-done | bytes 786464 | tf_op jit(solution)/shard_map/ppermute | solution.py:378
  173.4 19.5 %attn_bwd.1 = (bf16[512,768]{1,0:T(8,128)(2,1)}, bf16[4,512,768]{2,1,0:T(8,128)(2,1)}, f32[4,1,768]{2,1,0:T(1,128)}) custom-call(s32[2]{0:T(128)} %pad_add_fusion.1.where_ref, s32[1,512]{1,0:T(1,128)} %constant_dynamic-slice_fusion.2.seg_row_ref, s32[512,1]{1,0:T(8,128)} %copy.38.seg_col_ref, bf16[4,512,768]{2,1,0:T(8,128)(2,1)} %get-tuple-element.126.proj_ref, ...), custom_call_target="tpu_custom_call" | custom-call | flops 1000 | bytes 1000 | tf_op jit(solution)/shard_map/attn_bwd/pallas_call | solution.py:316
  196.7 9.7 %attn_weights.1 = (bf16[4,4,112,768]{3,2,1,0:T(8,128)(2,1)}, bf16[1,4,112,768]{3,2,1,0:T(8,128)(2,1)}, bf16[1,4,112,768]{3,2,1,0:T(8,128)(2,1)}, bf16[1,4,112,76...) custom-call(s32[2]{0:T(128)} %pad_add_fusion.1.where_ref, bf16[512,768]{1,0:T(8,128)(2,1)} %dynamic-slice_bitcast_fusion.1.x_ref, ...), custom_call_target="tpu_custom_call" | custom-call | flops 1000 | bytes 1000 | tf_op jit(solution)/shard_map/attn_weights/pallas_call | solution.py:350
  209.8 7.9 %up_weights.1 = (bf16[4,4,96,768]{3,2,1,0:T(8,128)(2,1)}, bf16[4,4,96,768]{3,2,1,0:T(8,128)(2,1)}) custom-call(s32[2]{0:T(128)} %pad_add_fusion.1.where_ref, bf16[512,768]{1,0:T(8,128)(2,1)} %get-tuple-element.99.first_ref, bf16[4,512,768]{2,1,0:T(8,128)(2,1)} %get-tuple-element.119.dup_ref), custom_call_target="tpu_custom_call" | custom-call | flops 1000 | bytes 1000 | tf_op jit(solution)/shard_map/up_weights/pallas_call | solution.py:350
  225.9 21.4 %collective-permute-done.40.refs_2_ = bf16[512,768]{1,0:T(8,128)(2,1)} collective-permute-done((bf16[512,768]{1,0:T(8,128)(2,1)}, bf16[512,768]{1,0:T(8,128)(2,1)}, u32[]{:S(2)}, u32[]{:S(2)}) %collective-permute-start.40) | collective-permute-done | bytes 786464 | tf_op jit(solution)/shard_map/ppermute | solution.py:378
  247.3 5.3 %collective-permute-done.42 = bf16[2,4,112,768]{3,2,1,0:T(8,128)(2,1)S(1)} collective-permute-done((bf16[2,4,112,768]{3,2,1,0:T(8,128)(2,1)S(1)}, bf16[2,4,112,768]{3,2,1,0:T(8,128)(2,1)S(1)}, u32[]{:S(2)}, u32[]{:S(2)}) %collective-permute-start.42) | collective-permute-done | bytes 1376288 | tf_op jit(solution)/shard_map/ppermute | solution.py:370
  261.0 3.7 %place_rows.2 = bf16[4,512,768]{2,1,0:T(8,128)(2,1)} custom-call(s32[2]{0:T(128)} %pad_add_fusion.where_ref, bf16[512,768]{1,0:T(8,128)(2,1)} %get-tuple-element.104.refs_0_, bf16[512,768]{1,0:T(8,128)(2,1)} %collective-permute-done.24.refs_1_, bf16[512,768]{1,0:T(8,128)(2,1)} %collective-permute-done.25.refs_2_, ...), custom_call_target="tpu_custom_call" | custom-call | flops 1000 | bytes 1000 | tf_op jit(solution)/shard_map/place_rows/pallas_call | solution.py:316
  264.7 3.2 %collective-permute-done.44.refs_3_ = bf16[512,768]{1,0:T(8,128)(2,1)} collective-permute-done((bf16[512,768]{1,0:T(8,128)(2,1)}, bf16[512,768]{1,0:T(8,128)(2,1)}, u32[]{:S(2)}, u32[]{:S(2)}) %collective-permute-start.44) | collective-permute-done | bytes 786464 | tf_op jit(solution)/shard_map/ppermute | solution.py:378
  268.0 4.2 %collective-permute-done.43 = bf16[4,112,768]{2,1,0:T(8,128)(2,1)S(1)} collective-permute-done((bf16[4,112,768]{2,1,0:T(8,128)(2,1)}, bf16[4,112,768]{2,1,0:T(8,128)(2,1)S(1)}, u32[]{:S(2)}, u32[]{:S(2)}) %collective-permute-start.43) | collective-permute-done | bytes 688160 | tf_op jit(solution)/shard_map/ppermute | solution.py:370
  277.8 3.8 %place_rows.3 = bf16[4,512,768]{2,1,0:T(8,128)(2,1)} custom-call(s32[2]{0:T(128)} %pad_add_fusion.where_ref, bf16[512,768]{1,0:T(8,128)(2,1)} %get-tuple-element.142.refs_0_, bf16[512,768]{1,0:T(8,128)(2,1)} %collective-permute-done.32.refs_1_, bf16[512,768]{1,0:T(8,128)(2,1)} %collective-permute-done.40.refs_2_, ...), custom_call_target="tpu_custom_call" | custom-call | flops 1000 | bytes 1000 | tf_op jit(solution)/shard_map/place_rows/pallas_call | solution.py:316
  281.6 6.3 %collective-permute-done.47 = bf16[2,96,768]{2,1,0:T(8,128)(2,1)S(1)} collective-permute-done((bf16[2,96,768]{2,1,0:T(8,128)(2,1)}, bf16[2,96,768]{2,1,0:T(8,128)(2,1)S(1)}, u32[]{:S(2)}, u32[]{:S(2)}) %collective-permute-start.47) | collective-permute-done | bytes 294944 | tf_op jit(solution)/shard_map/ppermute | solution.py:374
  288.3 4.8 %collective-permute-done.45 = bf16[2,112,768]{2,1,0:T(8,128)(2,1)S(1)} collective-permute-done((bf16[2,112,768]{2,1,0:T(8,128)(2,1)S(1)}, bf16[2,112,768]{2,1,0:T(8,128)(2,1)S(1)}, u32[]{:S(2)}, u32[]{:S(2)}) %collective-permute-start.45) | collective-permute-done | bytes 344096 | tf_op jit(solution)/shard_map/ppermute | solution.py:374
  297.0 6.4 %collective-permute-done.48 = bf16[96,768]{1,0:T(8,128)(2,1)S(1)} collective-permute-done((bf16[96,768]{1,0:T(8,128)(2,1)S(1)}, bf16[96,768]{1,0:T(8,128)(2,1)S(1)}, u32[]{:S(2)}, u32[]{:S(2)}) %collective-permute-start.48) | collective-permute-done | bytes 147488 | tf_op jit(solution)/shard_map/ppermute | solution.py:374
  (273 shorter events, 98.3 us)
Async XLA Ops:
  10.5 15.6 %collective-permute-start.1 = (bf16[112,768]{1,0:T(8,128)(2,1)S(1)}, bf16[112,768]{1,0:T(8,128)(2,1)S(1)}, u32[]{:S(2)}, u32[]{:S(2)}) collective-permute-start(bf16[112,768]{1,0:T(8,128)(2,1)S(1)} %concatenate.66), channel_id=1, source_target_pairs={{0,2},{1,3},{2,0},{3,1},{4,6},{5,7},{6,4},{7,5},{8,10},{9,11},{10,... | collective-permute-start | bytes 516104 | tf_op jit(solution)/shard_map/ppermute | solution.py:374
  26.2 15.9 %collective-permute-start.6 = (bf16[4,112,768]{2,1,0:T(8,128)(2,1)S(1)}, bf16[4,112,768]{2,1,0:T(8,128)(2,1)}, u32[]{:S(2)}, u32[]{:S(2)}) collective-permute-start(bf16[4,112,768]{2,1,0:T(8,128)(2,1)S(1)} %pad_maximum_fusion.3.refs_0_), channel_id=1, source_target_pairs={{0,8},{4,12},{8,0},{12,4},{16,24},{20,28},{24,16},{28,20},{1,9},{5... | collective-permute-start | bytes 2064392 | tf_op jit(solution)/shard_map/ppermute | solution.py:370
  28.2 14.9 %collective-permute-start.7 = (bf16[4,112,768]{2,1,0:T(8,128)(2,1)S(1)}, bf16[4,112,768]{2,1,0:T(8,128)(2,1)}, u32[]{:S(2)}, u32[]{:S(2)}) collective-permute-start(bf16[4,112,768]{2,1,0:T(8,128)(2,1)S(1)} %pad_maximum_fusion.3.refs_0_), channel_id=1, source_target_pairs={{0,16},{4,20},{8,24},{12,28},{16,0},{20,4},{24,8},{28,12},{1,17},{... | collective-permute-start | bytes 2064392 | tf_op jit(solution)/shard_map/ppermute | solution.py:370
  63.2 23.3 %collective-permute-start.15 = (bf16[4,192,768]{2,1,0:T(8,128)(2,1)}, bf16[4,192,768]{2,1,0:T(8,128)(2,1)}, u32[]{:S(2)}, u32[]{:S(2)}) collective-permute-start(bf16[4,192,768]{2,1,0:T(8,128)(2,1)} %pad_maximum_fusion.1.refs_0_), channel_id=1, source_target_pairs={{0,8},{4,12},{8,0},{12,4},{16,24},{20,28},{24,16},{28,20},{1,9},{5... | collective-permute-start | bytes 3538952 | tf_op jit(solution)/shard_map/ppermute | solution.py:370
  63.2 24.4 %collective-permute-start.16 = (bf16[4,192,768]{2,1,0:T(8,128)(2,1)}, bf16[4,192,768]{2,1,0:T(8,128)(2,1)}, u32[]{:S(2)}, u32[]{:S(2)}) collective-permute-start(bf16[4,192,768]{2,1,0:T(8,128)(2,1)} %pad_maximum_fusion.1.refs_0_), channel_id=1, source_target_pairs={{0,16},{4,20},{8,24},{12,28},{16,0},{20,4},{24,8},{28,12},{1,17},{... | collective-permute-start | bytes 3538952 | tf_op jit(solution)/shard_map/ppermute | solution.py:370
  70.8 36.4 %collective-permute-start.19 = (bf16[4,192,768]{2,1,0:T(8,128)(2,1)}, bf16[4,192,768]{2,1,0:T(8,128)(2,1)S(1)}, u32[]{:S(2)}, u32[]{:S(2)}) collective-permute-start(bf16[4,192,768]{2,1,0:T(8,128)(2,1)} %pad_maximum_fusion.1.refs_0_), channel_id=1, source_target_pairs={{0,4},{4,0},{8,12},{12,8},{16,20},{20,16},{24,28},{28,24},{1,5},{5... | collective-permute-start | bytes 3538952 | tf_op jit(solution)/shard_map/ppermute | solution.py:370
  88.7 15.8 %collective-permute-start.17 = (bf16[2,192,768]{2,1,0:T(8,128)(2,1)S(1)}, bf16[2,192,768]{2,1,0:T(8,128)(2,1)S(1)}, u32[]{:S(2)}, u32[]{:S(2)}) collective-permute-start(bf16[2,192,768]{2,1,0:T(8,128)(2,1)S(1)} %slice.461), channel_id=1, source_target_pairs={{0,16},{4,20},{8,24},{12,28},{16,0},{20,4},{24,8},{28,12},{1,17},{... | collective-permute-start | bytes 1769480 | tf_op jit(solution)/shard_map/ppermute | solution.py:370
  88.8 15.9 %collective-permute-start.18 = (bf16[2,192,768]{2,1,0:T(8,128)(2,1)S(1)}, bf16[2,192,768]{2,1,0:T(8,128)(2,1)S(1)}, u32[]{:S(2)}, u32[]{:S(2)}) collective-permute-start(bf16[2,192,768]{2,1,0:T(8,128)(2,1)S(1)} %slice.462), channel_id=1, source_target_pairs={{0,8},{4,12},{8,0},{12,4},{16,24},{20,28},{24,16},{28,20},{1,9},{5... | collective-permute-start | bytes 1769480 | tf_op jit(solution)/shard_map/ppermute | solution.py:370
  90.8 16.6 %collective-permute-start.20 = (bf16[4,192,768]{2,1,0:T(8,128)(2,1)}, bf16[4,192,768]{2,1,0:T(8,128)(2,1)S(1)}, u32[]{:S(2)}, u32[]{:S(2)}) collective-permute-start(bf16[4,192,768]{2,1,0:T(8,128)(2,1)} %collective-permute-done.15.refs_1_), channel_id=1, source_target_pairs={{0,4},{4,0},{8,12},{12,8},{16,20},{20,16},{24,28},{28,24},{1,5},{5... | collective-permute-start | bytes 3538952 | tf_op jit(solution)/shard_map/ppermute | solution.py:370
  91.0 16.4 %collective-permute-start.21 = (bf16[4,192,768]{2,1,0:T(8,128)(2,1)}, bf16[4,192,768]{2,1,0:T(8,128)(2,1)S(1)}, u32[]{:S(2)}, u32[]{:S(2)}) collective-permute-start(bf16[4,192,768]{2,1,0:T(8,128)(2,1)} %collective-permute-done.16.refs_2_), channel_id=1, source_target_pairs={{0,4},{4,0},{8,12},{12,8},{16,20},{20,16},{24,28},{28,24},{1,5},{5... | collective-permute-start | bytes 3538952 | tf_op jit(solution)/shard_map/ppermute | solution.py:370
  127.0 21.9 %collective-permute-start.24 = (bf16[512,768]{1,0:T(8,128)(2,1)}, bf16[512,768]{1,0:T(8,128)(2,1)}, u32[]{:S(2)}, u32[]{:S(2)}) collective-permute-start(bf16[512,768]{1,0:T(8,128)(2,1)} %get-tuple-element.104.refs_0_), channel_id=1, source_target_pairs={{0,1},{1,2},{2,3},{3,0},{4,5},{5,6},{6,7},{7,4},{8,9},{9,10},{10,1... | collective-permute-start | bytes 2359304 | tf_op jit(solution)/shard_map/ppermute | solution.py:378
  150.8 42.1 %collective-permute-start.31 = (bf16[2,4,96,768]{3,2,1,0:T(8,128)(2,1)S(1)}, bf16[2,4,96,768]{3,2,1,0:T(8,128)(2,1)}, u32[]{:S(2)}, u32[]{:S(2)}) collective-permute-start(bf16[2,4,96,768]{3,2,1,0:T(8,128)(2,1)S(1)} %pad_maximum_fusion.2), channel_id=1, source_target_pairs={{0,8},{4,12},{8,0},{12,4},{16,24},{20,28},{24,16},{28,20},{1,9},{5... | collective-permute-start | bytes 3538952 | tf_op jit(solution)/shard_map/ppermute | solution.py:370
  152.8 20.6 %collective-permute-start.25 = (bf16[512,768]{1,0:T(8,128)(2,1)}, bf16[512,768]{1,0:T(8,128)(2,1)}, u32[]{:S(2)}, u32[]{:S(2)}) collective-permute-start(bf16[512,768]{1,0:T(8,128)(2,1)} %collective-permute-done.24.refs_1_), channel_id=1, source_target_pairs={{0,1},{1,2},{2,3},{3,0},{4,5},{5,6},{6,7},{7,4},{8,9},{9,10},{10,1... | collective-permute-start | bytes 2359304 | tf_op jit(solution)/shard_map/ppermute | solution.py:378
  173.4 23.3 %collective-permute-start.30 = (bf16[512,768]{1,0:T(8,128)(2,1)}, bf16[512,768]{1,0:T(8,128)(2,1)}, u32[]{:S(2)}, u32[]{:S(2)}) collective-permute-start(bf16[512,768]{1,0:T(8,128)(2,1)} %collective-permute-done.25.refs_2_), channel_id=1, source_target_pairs={{0,1},{1,2},{2,3},{3,0},{4,5},{5,6},{6,7},{7,4},{8,9},{9,10},{10,1... | collective-permute-start | bytes 2359304 | tf_op jit(solution)/shard_map/ppermute | solution.py:378
  196.7 21.0 %collective-permute-start.32 = (bf16[512,768]{1,0:T(8,128)(2,1)}, bf16[512,768]{1,0:T(8,128)(2,1)}, u32[]{:S(2)}, u32[]{:S(2)}) collective-permute-start(bf16[512,768]{1,0:T(8,128)(2,1)} %get-tuple-element.142.refs_0_), channel_id=1, source_target_pairs={{0,1},{1,2},{2,3},{3,0},{4,5},{5,6},{6,7},{7,4},{8,9},{9,10},{10,1... | collective-permute-start | bytes 2359304 | tf_op jit(solution)/shard_map/ppermute | solution.py:378
  220.1 32.5 %collective-permute-start.42 = (bf16[2,4,112,768]{3,2,1,0:T(8,128)(2,1)S(1)}, bf16[2,4,112,768]{3,2,1,0:T(8,128)(2,1)S(1)}, u32[]{:S(2)}, u32[]{:S(2)}) collective-permute-start(bf16[2,4,112,768]{3,2,1,0:T(8,128)(2,1)S(1)} %pad_maximum_fusion), channel_id=1, source_target_pairs={{0,16},{4,20},{8,24},{12,28},{16,0},{20,4},{24,8},{28,12},{1,17},{... | collective-permute-start | bytes 4128776 | tf_op jit(solution)/shard_map/ppermute | solution.py:370
  225.3 30.4 %collective-permute-start.39 = (bf16[2,4,96,768]{3,2,1,0:T(8,128)(2,1)S(1)}, bf16[2,4,96,768]{3,2,1,0:T(8,128)(2,1)S(1)}, u32[]{:S(2)}, u32[]{:S(2)}) collective-permute-start(bf16[2,4,96,768]{3,2,1,0:T(8,128)(2,1)S(1)} %get-tuple-element.207), channel_id=1, source_target_pairs={{0,8},{4,12},{8,0},{12,4},{16,24},{20,28},{24,16},{28,20},{1,9},{5... | collective-permute-start | bytes 3538952 | tf_op jit(solution)/shard_map/ppermute | solution.py:370
  225.9 21.4 %collective-permute-start.40 = (bf16[512,768]{1,0:T(8,128)(2,1)}, bf16[512,768]{1,0:T(8,128)(2,1)}, u32[]{:S(2)}, u32[]{:S(2)}) collective-permute-start(bf16[512,768]{1,0:T(8,128)(2,1)} %collective-permute-done.32.refs_1_), channel_id=1, source_target_pairs={{0,1},{1,2},{2,3},{3,0},{4,5},{5,6},{6,7},{7,4},{8,9},{9,10},{10,1... | collective-permute-start | bytes 2359304 | tf_op jit(solution)/shard_map/ppermute | solution.py:378
  247.3 20.7 %collective-permute-start.44 = (bf16[512,768]{1,0:T(8,128)(2,1)}, bf16[512,768]{1,0:T(8,128)(2,1)}, u32[]{:S(2)}, u32[]{:S(2)}) collective-permute-start(bf16[512,768]{1,0:T(8,128)(2,1)} %collective-permute-done.40.refs_2_), channel_id=1, source_target_pairs={{0,1},{1,2},{2,3},{3,0},{4,5},{5,6},{6,7},{7,4},{8,9},{9,10},{10,1... | collective-permute-start | bytes 2359304 | tf_op jit(solution)/shard_map/ppermute | solution.py:378
  255.1 17.1 %collective-permute-start.43 = (bf16[4,112,768]{2,1,0:T(8,128)(2,1)}, bf16[4,112,768]{2,1,0:T(8,128)(2,1)S(1)}, u32[]{:S(2)}, u32[]{:S(2)}) collective-permute-start(bf16[4,112,768]{2,1,0:T(8,128)(2,1)} %get-tuple-element.209), channel_id=1, source_target_pairs={{0,8},{4,12},{8,0},{12,4},{16,24},{20,28},{24,16},{28,20},{1,9},{5... | collective-permute-start | bytes 2064392 | tf_op jit(solution)/shard_map/ppermute | solution.py:370
  256.7 15.5 %collective-permute-start.41 = (bf16[4,96,768]{2,1,0:T(8,128)(2,1)}, bf16[4,96,768]{2,1,0:T(8,128)(2,1)S(1)}, u32[]{:S(2)}, u32[]{:S(2)}) collective-permute-start(bf16[4,96,768]{2,1,0:T(8,128)(2,1)} %get-tuple-element.216), channel_id=1, source_target_pairs={{0,16},{4,20},{8,24},{12,28},{16,0},{20,4},{24,8},{28,12},{1,17},{... | collective-permute-start | bytes 1769480 | tf_op jit(solution)/shard_map/ppermute | solution.py:370
  274.1 19.0 %collective-permute-start.45 = (bf16[2,112,768]{2,1,0:T(8,128)(2,1)S(1)}, bf16[2,112,768]{2,1,0:T(8,128)(2,1)S(1)}, u32[]{:S(2)}, u32[]{:S(2)}) collective-permute-start(bf16[2,112,768]{2,1,0:T(8,128)(2,1)S(1)} %get-tuple-element.160), channel_id=1, source_target_pairs={{0,1},{1,0},{2,3},{3,2},{4,5},{5,4},{6,7},{7,6},{8,9},{9,8},{10,11... | collective-permute-start | bytes 1032200 | tf_op jit(solution)/shard_map/ppermute | solution.py:374
  275.4 19.6 %collective-permute-start.50 = (bf16[96,768]{1,0:T(8,128)(2,1)S(1)}, bf16[96,768]{1,0:T(8,128)(2,1)S(1)}, u32[]{:S(2)}, u32[]{:S(2)}) collective-permute-start(bf16[96,768]{1,0:T(8,128)(2,1)S(1)} %fusion.19), channel_id=1, source_target_pairs={{0,2},{1,3},{2,0},{3,1},{4,6},{5,7},{6,4},{7,5},{8,10},{9,11},{10,... | collective-permute-start | bytes 442376 | tf_op jit(solution)/shard_map/ppermute | solution.py:374
  287.9 15.4 %collective-permute-start.48 = (bf16[96,768]{1,0:T(8,128)(2,1)S(1)}, bf16[96,768]{1,0:T(8,128)(2,1)S(1)}, u32[]{:S(2)}, u32[]{:S(2)}) collective-permute-start(bf16[96,768]{1,0:T(8,128)(2,1)S(1)} %fusion.18), channel_id=1, source_target_pairs={{0,2},{1,3},{2,0},{3,1},{4,6},{5,7},{6,4},{7,5},{8,10},{9,11},{10,... | collective-permute-start | bytes 442376 | tf_op jit(solution)/shard_map/ppermute | solution.py:374
  (67 other events, 587.6 us)

commit v8 on v7

--- a/solution.py
+++ b/solution.py
@@ -437,6 +437,20 @@
     return [add(pair[0][k : k + 2], got[k : k + 2]).astype(bf) for k in (0, 2)]
 
 
+def reduce_some(sums, gates):
+    one, two, three, four = [part[0] for part in sums]
+    over_x = flip(jnp.stack([two[:2], four[:2]]), 2)
+    over_y = flip(jnp.stack([three[2:], four[2:]]), 4)
+    over_x, over_y = late([over_x, over_y], *gates)
+    pairs = ((one[:2], over_x[0]), (three[:2], over_x[1]), (one[2:], over_y[0]), (two[2:], over_y[1]))
+    return [add(*pair).astype(bf) for pair in pairs]
+
+
+def reduce_rest(some, gates):
+    over_y, over_x = late([flip(some[1], 4), flip(some[3], 2)], *gates)
+    return [add(some[0], over_y).astype(bf), add(some[2], over_x).astype(bf)]
+
+
 def reduce_tensor(plane, gates=()):
     got = cross(plane[1], 1)
     if gates:
@@ -542,7 +556,7 @@
     attn_whole = ((4, SLABS, DEPTH + EXTRA, 768), bf)
     down_outs = [(((n, 4, DEPTH, 768), bf), slab_block) for n in (4, 1, 1, 1, 1)]
     up_outs = [(((n, 4, DEPTH, 768), bf), slab_block) for n in (4, 4)]
-    attn_outs = [(((n, 4, DEPTH + EXTRA, 768), bf), slab_block) for n in (4, 1, 1, 1, 1)]
+    attn_outs = [(((n, 4, DEPTH + EXTRA, 768), bf), slab_block) for n in (4, 4)]
     thin = ((4, 1, 768), fl)
 
     if fast:
@@ -593,10 +607,14 @@
         up_bwd_kernel, "up_bwd", [row_f, ((4, length, 256), bf), ((3, width), fl)],
         where, dr2, dup, xhat, rstd, vec, up_w, attn_w, after=wait,
     )
-    out_two = next_row(out_one, small_one)
+    up_near, *up_far = call_groups(
+        up_weights_kernel, "up_weights", up_outs, where, (first, whole_block), (dup, group_block),
+        scratch=[turned], after=[small_one],
+    )
+    out_two = next_row(out_one, up_near)
     grad_row, dproj, bias_grad = call(
         attn_bwd_kernel, "attn_bwd", [row_b, (wide, bf), thin],
-        where, seg, seg_col, proj, lse, dr1, dctx, attn_w, after=[out_two],
+        where, seg, seg_col, proj, lse, dr1, dctx, attn_w, after=[out_two, up_near],
         scratch=[pltpu.VMEM((length, width), fl)],
     )
     out_three = next_row(out_two, bias_grad)
@@ -610,25 +628,21 @@
         (bias_grad, group_block), (b_up_grad, group_block), (small_one, whole_block), (small_two, whole_block),
         scratch=[pltpu.VMEM((EXTRA, width), fl), turned, turned], after=wait,
     )
-    up_near, *up_far = call_groups(
-        up_weights_kernel, "up_weights", up_outs, where, (first, whole_block), (dup, group_block),
-        scratch=[turned], after=[bias_grad, attn_near],
-    )
     in_one = rotate(grad_row)
     in_two = rotate(in_one)
     in_three = rotate(in_two)
     hidden_out = place_rows([out, out_one, out_two, out_three], spin)
     wait = []
     if fast:
-        down_plane = reduce_chip(down_pair, 2)
-        attn_far = late(attn_far, *down_plane)
-        attn_half = halves(reduce_core(attn_near, attn_far, [up_near, in_one]))
-        up_far = late(up_far, in_one, *attn_half)
-        up_pair = reduce_pair(reduce_core(up_near, up_far, parts=2), 1, [in_two])
-        up_plane = reduce_chip(up_pair, 2)
-        attn_pair = reduce_pair(attn_half, 2)
-        attn_plane = reduce_chip(attn_pair, 1, [in_three, *up_pair])
-        down_last = reduce_tensor(down_plane, [*up_pair, *attn_pair])
+        down_plane = reduce_chip(down_pair, 2, [attn_near])
+        attn_far = late(attn_far, in_one, *down_plane)
+        up_half = reduce_core(up_near, late(up_far, in_one), parts=2)
+        attn_sums = reduce_core(attn_near, attn_far, parts=4)
+        up_pair = reduce_pair(up_half, 1, attn_sums)
+        attn_some = reduce_some(attn_sums, [in_two])
+        up_plane = reduce_chip(up_pair, 2, attn_some)
+        attn_plane = reduce_rest(attn_some, [in_three])
+        down_last = reduce_tensor(down_plane, [*up_pair, *attn_some])
         attn_last = reduce_tensor([attn_plane[0]] + late(attn_plane[1:], *up_plane))
         up_last = reduce_tensor(up_plane)
         down_sum = reduce_last(down_last, [attn_last[1], up_last[1]])

time: 314 us -> 323 us (1.029)
    ppermute x33 -> x32, waiting for transfers between devices: 34.6 us -> 64.7 us  [flip(): return lax.ppermute(value, 'dp', [(k, k ^ bits) for k in range(n)])]
    ppermute x6, waiting for transfers between devices: 35.6 us -> 15.2 us  [rotate(): return lax.ppermute(value, 'tensor', [(k, (k + 1) % 4) for k in range(4)])]
    ppermute x12, waiting for transfers between devices: 45.6 us -> 39.6 us  [cross(): return lax.ppermute(value, 'tensor', [(k, k ^ bits) for k in range(4)])]
    unnamed x88 -> x78, local copies, waits for them, and re-layouts: 8.96 us -> 8.36 us
    ppermute x33 -> x32, starting transfers between devices: 23.5 us -> 24 us  [flip(): return lax.ppermute(value, 'dp', [(k, k ^ bits) for k in range(n)])]
  transfers between devices with their start and end apart: 51 -> 50, of which waited for: 22 -> 21; matrix products, arithmetic and copies ran while one was open for 8% -> 9% of each run, Pallas kernels for 29% -> 28%
where the time goes in v8:
time: 323 us; the launch traced here: 322 us
  waiting for transfers between devices  119 us (37%)
  Pallas kernels  108 us (33%)
  starting transfers between devices  42.6 us (13%)
  other arithmetic  25.5 us (8%)
  local copies, waits for them, and re-layouts  24.2 us (7%)
    pallas_call x6, Pallas kernels, call(): pl.pallas_call(kernel, name=name, out_shape=[jax.ShapeDtypeStruct(s, d) f...  72.6 us
    ppermute x32, waiting for transfers between devices, flip(): return lax.ppermute(value, 'dp', [(k, k ^ bits) for k in range(n)])  64.7 us
    ppermute x12, waiting for transfers between devices, cross(): return lax.ppermute(value, 'tensor', [(k, k ^ bits) for k in range(4)])  39.6 us
    pallas_call x4, Pallas kernels, call_groups(): pl.pallas_call(kernel, name=name, out_shape=[jax.ShapeDtypeStruct(s, d) f...  35 us
    ppermute x32, starting transfers between devices, flip(): return lax.ppermute(value, 'dp', [(k, k ^ bits) for k in range(n)])  24 us
    ppermute x6, waiting for transfers between devices, rotate(): return lax.ppermute(value, 'tensor', [(k, (k + 1) % 4) for k in range(4)])  15.2 us
    ppermute x12, starting transfers between devices, cross(): return lax.ppermute(value, 'tensor', [(k, k ^ bits) for k in range(4)])  15 us
    unnamed x78, local copies, waits for them, and re-layouts  8.36 us
  transfers between devices with their start and end apart: 50, of which 21 were waited for; matrix products, arithmetic and copies ran while one was open for 9% of the time, Pallas kernels for 28%

profile of v8, /device:TPU:0, one launch (start us, length us, event | category | flops | bytes accessed | tf_op | source)
XLA Modules:
  0.0 321.5 jit_solution(8646678696545479032)
XLA Ops:
  13.1 5.4 %collective-permute-done = bf16[112,768]{1,0:T(8,128)(2,1)S(1)} collective-permute-done((bf16[112,768]{1,0:T(8,128)(2,1)S(1)}, bf16[112,768]{1,0:T(8,128)(2,1)S(1)}, u32[]{:S(2)}, u32[]{:S(2)}) %collective-permute-start) | collective-permute-done | bytes 172064 | tf_op jit(solution)/shard_map/ppermute | solution.py:374
  18.5 7.6 %collective-permute-done.1 = bf16[112,768]{1,0:T(8,128)(2,1)S(1)} collective-permute-done((bf16[112,768]{1,0:T(8,128)(2,1)S(1)}, bf16[112,768]{1,0:T(8,128)(2,1)S(1)}, u32[]{:S(2)}, u32[]{:S(2)}) %collective-permute-start.1) | collective-permute-done | bytes 172064 | tf_op jit(solution)/shard_map/ppermute | solution.py:374
  35.7 6.3 %collective-permute-done.6.refs_1_ = bf16[4,112,768]{2,1,0:T(8,128)(2,1)} collective-permute-done((bf16[4,112,768]{2,1,0:T(8,128)(2,1)S(1)}, bf16[4,112,768]{2,1,0:T(8,128)(2,1)}, u32[]{:S(2)}, u32[]{:S(2)}) %collective-permute-start.6) | collective-permute-done | bytes 688160 | tf_op jit(solution)/shard_map/ppermute | solution.py:370
  49.2 3.4 %collective-permute-start.9 = (bf16[2,112,768]{2,1,0:T(8,128)(2,1)S(1)}, bf16[2,112,768]{2,1,0:T(8,128)(2,1)S(1)}, u32[]{:S(2)}, u32[]{:S(2)}) collective-permute-start(bf16[2,112,768]{2,1,0:T(8,128)(2,1)S(1)} %slice.506), channel_id=1, source_target_pairs={{0,8},{4,12},{8,0},{12,4},{16,24},{20,28},{24,16},{28,20},{1,9},{5... | collective-permute-start | bytes 1032200 | tf_op jit(solution)/shard_map/ppermute | solution.py:370
  52.7 8.6 %collective-permute-done.5 = bf16[192,768]{1,0:T(8,128)(2,1)S(1)} collective-permute-done((bf16[192,768]{1,0:T(8,128)(2,1)S(1)}, bf16[192,768]{1,0:T(8,128)(2,1)S(1)}, u32[]{:S(2)}, u32[]{:S(2)}) %collective-permute-start.5) | collective-permute-done | bytes 294944 | tf_op jit(solution)/shard_map/ppermute | solution.py:374
  70.8 15.7 %attn_fwd.1 = (bf16[4,512,768]{2,1,0:T(8,128)(2,1)}, bf16[4,512,256]{2,1,0:T(8,128)(2,1)}, f32[4,3,1,512]{3,2,1,0:T(1,128)}, bf16[4,8,112,768]{3,2,1,0:T(8,128)(...) custom-call(s32[2]{0:T(128)} %pad_add_fusion.1.where_ref, ...), custom_call_target="tpu_custom_call" | custom-call | flops 1000 | bytes 1000 | tf_op jit(solution)/shard_map/attn_fwd/pallas_call | solution.py:316
  91.3 12.7 %collective-permute-done.17.refs_3_ = bf16[2,192,768]{2,1,0:T(8,128)(2,1)S(1)} collective-permute-done((bf16[2,192,768]{2,1,0:T(8,128)(2,1)S(1)}, bf16[2,192,768]{2,1,0:T(8,128)(2,1)S(1)}, u32[]{:S(2)}, u32[]{:S(2)}) %collective-permute-start.17) | collective-permute-done | bytes 589856 | tf_op jit(solution)/shard_map/ppermute | solution.py:370
  108.5 17.7 %ffn_fwd.1 = (bf16[512,768]{1,0:T(8,128)(2,1)}, f32[512,768]{1,0:T(8,128)}, bf16[4,512,768]{2,1,0:T(8,128)(2,1)}, f32[4,512,768]{2,1,0:T(8,128)}, f32[3,768]{1,0...) custom-call(s32[2]{0:T(128)} %pad_add_fusion.1.where_ref, ...), custom_call_target="tpu_custom_call" | custom-call | flops 1000 | bytes 1000 | tf_op jit(solution)/shard_map/ffn_fwd/pallas_call | solution.py:316
  127.2 8.2 %down_weights.1 = (bf16[4,4,96,768]{3,2,1,0:T(8,128)(2,1)}, bf16[1,4,96,768]{3,2,1,0:T(8,128)(2,1)}, bf16[1,4,96,768]{3,2,1,0:T(8,128)(2,1)}, bf16[1,4,96,768]{3,2,1,0:T(8,128)(2,1)}, bf16[1,4,96,768]{3,2,1,0:T(8,128)(2,1)}) custom-call(s32[2]{0:T(128)} %pad_add_fusion.1.where_ref, f32[512,768]{1,0:T(8,128)} %get-tuple-element.100.dr2_ref, ...), custom_call_target="tpu_custom_call" | custom-call | flops 1000 | bytes 1000 | tf_op jit(solution)/shard_map/down_weights/pallas_call | solution.py:350
  136.4 9.3 %down_bwd.1 = (bf16[4,512,768]{2,1,0:T(8,128)(2,1)}, f32[4,1,768]{2,1,0:T(1,128)}) custom-call(s32[2]{0:T(128)} %pad_add_fusion.1.where_ref, f32[512,768]{1,0:T(8,128)} %get-tuple-element.100.dr2_ref, f32[4,512,768]{2,1,0:T(8,128)} %get-tuple-element.101.slope_ref, bf16[4,8,96,768]{3,2,1,0:T(8,128)(2,1)} %get-tuple-element.102.weight_ref), custom_call_target="tpu_custom_call" | custom-call | flops 1000 | bytes 1000 | tf_op jit(solution)/shard_map/down_bwd/pallas_call | solution.py:350
  153.6 12.2 %up_bwd.1 = (f32[512,768]{1,0:T(8,128)}, bf16[4,512,256]{2,1,0:T(8,128)(2,1)}, f32[3,768]{1,0:T(4,128)}) custom-call(s32[2]{0:T(128)} %pad_add_fusion.1.where_ref, f32[512,768]{1,0:T(8,128)} %get-tuple-element.100.dr2_ref, bf16[4,512,768]{2,1,0:T(8,128)(2,1)} %get-tuple-element.114.dup_ref, f32[512,768]{1,0:T(8,128)} %get-tuple-element.93.xhat_ref, ...), custom_call_target="tpu_custom_call" | custom-call | flops 1000 | bytes 1000 | tf_op jit(solution)/shard_map/up_bwd/pallas_call | solution.py:316
  165.8 7.7 %up_weights.1 = (bf16[4,4,96,768]{3,2,1,0:T(8,128)(2,1)}, bf16[4,4,96,768]{3,2,1,0:T(8,128)(2,1)}) custom-call(s32[2]{0:T(128)} %pad_add_fusion.1.where_ref, bf16[512,768]{1,0:T(8,128)(2,1)} %get-tuple-element.94.first_ref, bf16[4,512,768]{2,1,0:T(8,128)(2,1)} %get-tuple-element.114.dup_ref), custom_call_target="tpu_custom_call" | custom-call | flops 1000 | bytes 1000 | tf_op jit(solution)/shard_map/up_weights/pallas_call | solution.py:350
  175.0 19.5 %attn_bwd.1 = (bf16[512,768]{1,0:T(8,128)(2,1)}, bf16[4,512,768]{2,1,0:T(8,128)(2,1)}, f32[4,1,768]{2,1,0:T(1,128)}) custom-call(s32[2]{0:T(128)} %pad_add_fusion.1.where_ref, s32[1,512]{1,0:T(1,128)} %constant_dynamic-slice_fusion.2.seg_row_ref, s32[512,1]{1,0:T(8,128)} %copy.38.seg_col_ref, bf16[4,512,768]{2,1,0:T(8,128)(2,1)} %get-tuple-element.123.proj_ref, ...), custom_call_target="tpu_custom_call" | custom-call | flops 1000 | bytes 1000 | tf_op jit(solution)/shard_map/attn_bwd/pallas_call | solution.py:316
  198.6 9.8 %attn_weights.1 = (bf16[4,4,112,768]{3,2,1,0:T(8,128)(2,1)}, bf16[4,4,112,768]{3,2,1,0:T(8,128)(2,1)}) custom-call(s32[2]{0:T(128)} %pad_add_fusion.1.where_ref, bf16[512,768]{1,0:T(8,128)(2,1)} %dynamic-slice_bitcast_fusion.1.x_ref, bf16[4,512,768]{2,1,0:T(8,128)(2,1)} %get-tuple-element.135.dproj_ref, bf16[4,512,256]{2,1,0:T(8,128)(2,1)} %get-tuple-element.136.ctx_ref, ...), custom_call_target="tpu_custom_call" | custom-call | flops 1000 | bytes 1000 | tf_op jit(solution)/shard_map/attn_weights/pallas_call | solution.py:350
  212.7 5.0 %collective-permute-done.31.refs_1_ = bf16[512,768]{1,0:T(8,128)(2,1)} collective-permute-done((bf16[512,768]{1,0:T(8,128)(2,1)}, bf16[512,768]{1,0:T(8,128)(2,1)}, u32[]{:S(2)}, u32[]{:S(2)}) %collective-permute-start.31) | collective-permute-done | bytes 786464 | tf_op jit(solution)/shard_map/ppermute | solution.py:378
  218.2 8.2 %collective-permute-done.32 = bf16[4,4,96,768]{3,2,1,0:T(8,128)(2,1)S(1)} collective-permute-done((bf16[4,4,96,768]{3,2,1,0:T(8,128)(2,1)}, bf16[4,4,96,768]{3,2,1,0:T(8,128)(2,1)S(1)}, u32[]{:S(2)}, u32[]{:S(2)}) %collective-permute-start.32) | collective-permute-done | bytes 2359328 | tf_op jit(solution)/shard_map/ppermute | solution.py:370
  231.8 7.9 %collective-permute-done.40.refs_2_ = bf16[512,768]{1,0:T(8,128)(2,1)} collective-permute-done((bf16[512,768]{1,0:T(8,128)(2,1)}, bf16[512,768]{1,0:T(8,128)(2,1)}, u32[]{:S(2)}, u32[]{:S(2)}) %collective-permute-start.40) | collective-permute-done | bytes 786464 | tf_op jit(solution)/shard_map/ppermute | solution.py:378
  239.8 16.2 %collective-permute-done.33 = bf16[2,4,96,768]{3,2,1,0:T(8,128)(2,1)S(1)} collective-permute-done((bf16[2,4,96,768]{3,2,1,0:T(8,128)(2,1)S(1)}, bf16[2,4,96,768]{3,2,1,0:T(8,128)(2,1)S(1)}, u32[]{:S(2)}, u32[]{:S(2)}) %collective-permute-start.33) | collective-permute-done | bytes 1179680 | tf_op jit(solution)/shard_map/ppermute | solution.py:370
  258.7 11.2 %collective-permute-done.38 = bf16[2,2,112,768]{3,2,1,0:T(8,128)(2,1)S(1)} collective-permute-done((bf16[2,2,112,768]{3,2,1,0:T(8,128)(2,1)S(1)}, bf16[2,2,112,768]{3,2,1,0:T(8,128)(2,1)S(1)}, u32[]{:S(2)}, u32[]{:S(2)}) %collective-permute-start.38) | collective-permute-done | bytes 688160 | tf_op jit(solution)/shard_map/ppermute | solution.py:370
  274.3 5.3 %collective-permute-done.42 = bf16[2,112,768]{2,1,0:T(8,128)(2,1)} collective-permute-done((bf16[2,112,768]{2,1,0:T(8,128)(2,1)S(1)}, bf16[2,112,768]{2,1,0:T(8,128)(2,1)}, u32[]{:S(2)}, u32[]{:S(2)}) %collective-permute-start.42) | collective-permute-done | bytes 344096 | tf_op jit(solution)/shard_map/ppermute | solution.py:370
  284.1 3.7 %place_rows.2 = bf16[4,512,768]{2,1,0:T(8,128)(2,1)} custom-call(s32[2]{0:T(128)} %pad_add_fusion.where_ref, bf16[512,768]{1,0:T(8,128)(2,1)} %get-tuple-element.99.refs_0_, bf16[512,768]{1,0:T(8,128)(2,1)} %copy-done.10, bf16[512,768]{1,0:T(8,128)(2,1)} %collective-permute-done.25.refs_2_, bf16[512,768]{1,0:T(8,128)(2,1)} %copy-done.11), custom_call_target="tpu_custom_call" | custom-call | flops 1000 | bytes 1000 | tf_op jit(solution)/shard_map/place_rows/pallas_call | solution.py:316
  292.5 3.8 %place_rows.3 = bf16[4,512,768]{2,1,0:T(8,128)(2,1)} custom-call(s32[2]{0:T(128)} %pad_add_fusion.where_ref, bf16[512,768]{1,0:T(8,128)(2,1)} %get-tuple-element.130.refs_0_, bf16[512,768]{1,0:T(8,128)(2,1)} %collective-permute-done.31.refs_1_, bf16[512,768]{1,0:T(8,128)(2,1)} %collective-permute-done.40.refs_2_, ...), custom_call_target="tpu_custom_call" | custom-call | flops 1000 | bytes 1000 | tf_op jit(solution)/shard_map/place_rows/pallas_call | solution.py:316
  297.7 5.1 %collective-permute-done.44 = bf16[2,112,768]{2,1,0:T(8,128)(2,1)S(1)} collective-permute-done((bf16[2,112,768]{2,1,0:T(8,128)(2,1)S(1)}, bf16[2,112,768]{2,1,0:T(8,128)(2,1)S(1)}, u32[]{:S(2)}, u32[]{:S(2)}) %collective-permute-start.44) | collective-permute-done | bytes 344096 | tf_op jit(solution)/shard_map/ppermute | solution.py:374
  304.9 7.2 %collective-permute-done.47 = bf16[96,768]{1,0:T(8,128)(2,1)S(1)} collective-permute-done((bf16[96,768]{1,0:T(8,128)(2,1)S(1)}, bf16[96,768]{1,0:T(8,128)(2,1)S(1)}, u32[]{:S(2)}, u32[]{:S(2)}) %collective-permute-start.47) | collective-permute-done | bytes 147488 | tf_op jit(solution)/shard_map/ppermute | solution.py:374
  (266 shorter events, 101.8 us)
Async XLA Ops:
  10.5 15.6 %collective-permute-start.1 = (bf16[112,768]{1,0:T(8,128)(2,1)S(1)}, bf16[112,768]{1,0:T(8,128)(2,1)S(1)}, u32[]{:S(2)}, u32[]{:S(2)}) collective-permute-start(bf16[112,768]{1,0:T(8,128)(2,1)S(1)} %concatenate.62), channel_id=1, source_target_pairs={{0,2},{1,3},{2,0},{3,1},{4,6},{5,7},{6,4},{7,5},{8,10},{9,11},{10,... | collective-permute-start | bytes 516104 | tf_op jit(solution)/shard_map/ppermute | solution.py:374
  26.2 15.9 %collective-permute-start.6 = (bf16[4,112,768]{2,1,0:T(8,128)(2,1)S(1)}, bf16[4,112,768]{2,1,0:T(8,128)(2,1)}, u32[]{:S(2)}, u32[]{:S(2)}) collective-permute-start(bf16[4,112,768]{2,1,0:T(8,128)(2,1)S(1)} %pad_maximum_fusion.2.refs_0_), channel_id=1, source_target_pairs={{0,8},{4,12},{8,0},{12,4},{16,24},{20,28},{24,16},{28,20},{1,9},{5... | collective-permute-start | bytes 2064392 | tf_op jit(solution)/shard_map/ppermute | solution.py:370
  28.2 14.9 %collective-permute-start.7 = (bf16[4,112,768]{2,1,0:T(8,128)(2,1)S(1)}, bf16[4,112,768]{2,1,0:T(8,128)(2,1)}, u32[]{:S(2)}, u32[]{:S(2)}) collective-permute-start(bf16[4,112,768]{2,1,0:T(8,128)(2,1)S(1)} %pad_maximum_fusion.2.refs_0_), channel_id=1, source_target_pairs={{0,16},{4,20},{8,24},{12,28},{16,0},{20,4},{24,8},{28,12},{1,17},{... | collective-permute-start | bytes 2064392 | tf_op jit(solution)/shard_map/ppermute | solution.py:370
  31.7 14.6 %collective-permute-start.3 = (bf16[192,768]{1,0:T(8,128)(2,1)S(1)}, bf16[192,768]{1,0:T(8,128)(2,1)S(1)}, u32[]{:S(2)}, u32[]{:S(2)}) collective-permute-start(bf16[192,768]{1,0:T(8,128)(2,1)S(1)} %pad_maximum_fusion.8), channel_id=1, source_target_pairs={{0,1},{1,0},{2,3},{3,2},{4,5},{5,4},{6,7},{7,6},{8,9},{9,8},{10,11... | collective-permute-start | bytes 884744 | tf_op jit(solution)/shard_map/ppermute | solution.py:374
  63.2 23.3 %collective-permute-start.15 = (bf16[4,192,768]{2,1,0:T(8,128)(2,1)}, bf16[4,192,768]{2,1,0:T(8,128)(2,1)}, u32[]{:S(2)}, u32[]{:S(2)}) collective-permute-start(bf16[4,192,768]{2,1,0:T(8,128)(2,1)} %pad_maximum_fusion.refs_0_), channel_id=1, source_target_pairs={{0,8},{4,12},{8,0},{12,4},{16,24},{20,28},{24,16},{28,20},{1,9},{5... | collective-permute-start | bytes 3538952 | tf_op jit(solution)/shard_map/ppermute | solution.py:370
  63.2 24.4 %collective-permute-start.16 = (bf16[4,192,768]{2,1,0:T(8,128)(2,1)}, bf16[4,192,768]{2,1,0:T(8,128)(2,1)}, u32[]{:S(2)}, u32[]{:S(2)}) collective-permute-start(bf16[4,192,768]{2,1,0:T(8,128)(2,1)} %pad_maximum_fusion.refs_0_), channel_id=1, source_target_pairs={{0,16},{4,20},{8,24},{12,28},{16,0},{20,4},{24,8},{28,12},{1,17},{... | collective-permute-start | bytes 3538952 | tf_op jit(solution)/shard_map/ppermute | solution.py:370
  70.1 36.5 %collective-permute-start.19 = (bf16[4,192,768]{2,1,0:T(8,128)(2,1)}, bf16[4,192,768]{2,1,0:T(8,128)(2,1)S(1)}, u32[]{:S(2)}, u32[]{:S(2)}) collective-permute-start(bf16[4,192,768]{2,1,0:T(8,128)(2,1)} %pad_maximum_fusion.refs_0_), channel_id=1, source_target_pairs={{0,4},{4,0},{8,12},{12,8},{16,20},{20,16},{24,28},{28,24},{1,5},{5... | collective-permute-start | bytes 3538952 | tf_op jit(solution)/shard_map/ppermute | solution.py:370
  88.7 15.3 %collective-permute-start.17 = (bf16[2,192,768]{2,1,0:T(8,128)(2,1)S(1)}, bf16[2,192,768]{2,1,0:T(8,128)(2,1)S(1)}, u32[]{:S(2)}, u32[]{:S(2)}) collective-permute-start(bf16[2,192,768]{2,1,0:T(8,128)(2,1)S(1)} %slice.507), channel_id=1, source_target_pairs={{0,16},{4,20},{8,24},{12,28},{16,0},{20,4},{24,8},{28,12},{1,17},{... | collective-permute-start | bytes 1769480 | tf_op jit(solution)/shard_map/ppermute | solution.py:370
  88.8 15.5 %collective-permute-start.18 = (bf16[2,192,768]{2,1,0:T(8,128)(2,1)S(1)}, bf16[2,192,768]{2,1,0:T(8,128)(2,1)S(1)}, u32[]{:S(2)}, u32[]{:S(2)}) collective-permute-start(bf16[2,192,768]{2,1,0:T(8,128)(2,1)S(1)} %slice.508), channel_id=1, source_target_pairs={{0,8},{4,12},{8,0},{12,4},{16,24},{20,28},{24,16},{28,20},{1,9},{5... | collective-permute-start | bytes 1769480 | tf_op jit(solution)/shard_map/ppermute | solution.py:370
  90.8 16.1 %collective-permute-start.20 = (bf16[4,192,768]{2,1,0:T(8,128)(2,1)}, bf16[4,192,768]{2,1,0:T(8,128)(2,1)S(1)}, u32[]{:S(2)}, u32[]{:S(2)}) collective-permute-start(bf16[4,192,768]{2,1,0:T(8,128)(2,1)} %collective-permute-done.15.refs_1_), channel_id=1, source_target_pairs={{0,4},{4,0},{8,12},{12,8},{16,20},{20,16},{24,28},{28,24},{1,5},{5... | collective-permute-start | bytes 3538952 | tf_op jit(solution)/shard_map/ppermute | solution.py:370
  90.8 16.7 %collective-permute-start.21 = (bf16[4,192,768]{2,1,0:T(8,128)(2,1)}, bf16[4,192,768]{2,1,0:T(8,128)(2,1)}, u32[]{:S(2)}, u32[]{:S(2)}) collective-permute-start(bf16[4,192,768]{2,1,0:T(8,128)(2,1)} %collective-permute-done.16.refs_2_), channel_id=1, source_target_pairs={{0,4},{4,0},{8,12},{12,8},{16,20},{20,16},{24,28},{28,24},{1,5},{5... | collective-permute-start | bytes 3538952 | tf_op jit(solution)/shard_map/ppermute | solution.py:370
  126.2 21.8 %collective-permute-start.24 = (bf16[512,768]{1,0:T(8,128)(2,1)}, bf16[512,768]{1,0:T(8,128)(2,1)S(1)}, u32[]{:S(2)}, u32[]{:S(2)}) collective-permute-start(bf16[512,768]{1,0:T(8,128)(2,1)} %get-tuple-element.99.refs_0_), channel_id=1, source_target_pairs={{0,1},{1,2},{2,3},{3,0},{4,5},{5,6},{6,7},{7,4},{8,9},{9,10},{10,1... | collective-permute-start | bytes 2359304 | tf_op jit(solution)/shard_map/ppermute | solution.py:378
  151.1 43.4 %collective-permute-start.34 = (bf16[2,4,96,768]{3,2,1,0:T(8,128)(2,1)}, bf16[2,4,96,768]{3,2,1,0:T(8,128)(2,1)}, u32[]{:S(2)}, u32[]{:S(2)}) collective-permute-start(bf16[2,4,96,768]{3,2,1,0:T(8,128)(2,1)} %pad_maximum_fusion.1), channel_id=1, source_target_pairs={{0,8},{4,12},{8,0},{12,4},{16,24},{20,28},{24,16},{28,20},{1,9},{5... | collective-permute-start | bytes 3538952 | tf_op jit(solution)/shard_map/ppermute | solution.py:370
  153.0 20.5 %collective-permute-start.25 = (bf16[512,768]{1,0:T(8,128)(2,1)S(1)}, bf16[512,768]{1,0:T(8,128)(2,1)}, u32[]{:S(2)}, u32[]{:S(2)}) collective-permute-start(bf16[512,768]{1,0:T(8,128)(2,1)S(1)} %collective-permute-done.24.refs_1_), channel_id=1, source_target_pairs={{0,1},{1,2},{2,3},{3,0},{4,5},{5,6},{6,7},{7,4},{8,9},{9,10},{10,1... | collective-permute-start | bytes 2359304 | tf_op jit(solution)/shard_map/ppermute | solution.py:378
  173.6 25.1 %collective-permute-start.30 = (bf16[512,768]{1,0:T(8,128)(2,1)}, bf16[512,768]{1,0:T(8,128)(2,1)S(1)}, u32[]{:S(2)}, u32[]{:S(2)}) collective-permute-start(bf16[512,768]{1,0:T(8,128)(2,1)} %collective-permute-done.25.refs_2_), channel_id=1, source_target_pairs={{0,1},{1,2},{2,3},{3,0},{4,5},{5,6},{6,7},{7,4},{8,9},{9,10},{10,1... | collective-permute-start | bytes 2359304 | tf_op jit(solution)/shard_map/ppermute | solution.py:378
  197.9 19.8 %collective-permute-start.31 = (bf16[512,768]{1,0:T(8,128)(2,1)}, bf16[512,768]{1,0:T(8,128)(2,1)}, u32[]{:S(2)}, u32[]{:S(2)}) collective-permute-start(bf16[512,768]{1,0:T(8,128)(2,1)} %get-tuple-element.130.refs_0_), channel_id=1, source_target_pairs={{0,1},{1,2},{2,3},{3,0},{4,5},{5,6},{6,7},{7,4},{8,9},{9,10},{10,1... | collective-permute-start | bytes 2359304 | tf_op jit(solution)/shard_map/ppermute | solution.py:378
  218.2 21.6 %collective-permute-start.40 = (bf16[512,768]{1,0:T(8,128)(2,1)}, bf16[512,768]{1,0:T(8,128)(2,1)}, u32[]{:S(2)}, u32[]{:S(2)}) collective-permute-start(bf16[512,768]{1,0:T(8,128)(2,1)} %collective-permute-done.31.refs_1_), channel_id=1, source_target_pairs={{0,1},{1,2},{2,3},{3,0},{4,5},{5,6},{6,7},{7,4},{8,9},{9,10},{10,1... | collective-permute-start | bytes 2359304 | tf_op jit(solution)/shard_map/ppermute | solution.py:378
  227.1 28.9 %collective-permute-start.33 = (bf16[2,4,96,768]{3,2,1,0:T(8,128)(2,1)S(1)}, bf16[2,4,96,768]{3,2,1,0:T(8,128)(2,1)S(1)}, u32[]{:S(2)}, u32[]{:S(2)}) collective-permute-start(bf16[2,4,96,768]{3,2,1,0:T(8,128)(2,1)S(1)} %get-tuple-element.205), channel_id=1, source_target_pairs={{0,8},{4,12},{8,0},{12,4},{16,24},{20,28},{24,16},{28,20},{1,9},{5... | collective-permute-start | bytes 3538952 | tf_op jit(solution)/shard_map/ppermute | solution.py:370
  229.0 29.7 %collective-permute-start.39 = (bf16[2,2,112,768]{3,2,1,0:T(8,128)(2,1)S(1)}, bf16[2,2,112,768]{3,2,1,0:T(8,128)(2,1)S(1)}, u32[]{:S(2)}, u32[]{:S(2)}) collective-permute-start(bf16[2,2,112,768]{3,2,1,0:T(8,128)(2,1)S(1)} %pad_maximum_fusion.4), channel_id=1, source_target_pairs={{0,16},{4,20},{8,24},{12,28},{16,0},{20,4},{24,8},{28,12},{1,17},{... | collective-permute-start | bytes 2064392 | tf_op jit(solution)/shard_map/ppermute | solution.py:370
  230.7 39.2 %collective-permute-start.38 = (bf16[2,2,112,768]{3,2,1,0:T(8,128)(2,1)S(1)}, bf16[2,2,112,768]{3,2,1,0:T(8,128)(2,1)S(1)}, u32[]{:S(2)}, u32[]{:S(2)}) collective-permute-start(bf16[2,2,112,768]{3,2,1,0:T(8,128)(2,1)S(1)} %pad_maximum_fusion.3), channel_id=1, source_target_pairs={{0,8},{4,12},{8,0},{12,4},{16,24},{20,28},{24,16},{28,20},{1,9},{5... | collective-permute-start | bytes 2064392 | tf_op jit(solution)/shard_map/ppermute | solution.py:370
  239.8 34.5 %collective-permute-start.43 = (bf16[512,768]{1,0:T(8,128)(2,1)}, bf16[512,768]{1,0:T(8,128)(2,1)}, u32[]{:S(2)}, u32[]{:S(2)}) collective-permute-start(bf16[512,768]{1,0:T(8,128)(2,1)} %collective-permute-done.40.refs_2_), channel_id=1, source_target_pairs={{0,1},{1,2},{2,3},{3,0},{4,5},{5,6},{6,7},{7,4},{8,9},{9,10},{10,1... | collective-permute-start | bytes 2359304 | tf_op jit(solution)/shard_map/ppermute | solution.py:378
  257.1 25.1 %collective-permute-start.37 = (bf16[4,96,768]{2,1,0:T(8,128)(2,1)}, bf16[4,96,768]{2,1,0:T(8,128)(2,1)}, u32[]{:S(2)}, u32[]{:S(2)}) collective-permute-start(bf16[4,96,768]{2,1,0:T(8,128)(2,1)} %get-tuple-element.209), channel_id=1, source_target_pairs={{0,16},{4,20},{8,24},{12,28},{16,0},{20,4},{24,8},{28,12},{1,17},{... | collective-permute-start | bytes 1769480 | tf_op jit(solution)/shard_map/ppermute | solution.py:370
  287.9 15.0 %collective-permute-start.44 = (bf16[2,112,768]{2,1,0:T(8,128)(2,1)S(1)}, bf16[2,112,768]{2,1,0:T(8,128)(2,1)S(1)}, u32[]{:S(2)}, u32[]{:S(2)}) collective-permute-start(bf16[2,112,768]{2,1,0:T(8,128)(2,1)S(1)} %get-tuple-element.150), channel_id=1, source_target_pairs={{0,1},{1,0},{2,3},{3,2},{4,5},{5,4},{6,7},{7,6},{8,9},{9,8},{10,11... | collective-permute-start | bytes 1032200 | tf_op jit(solution)/shard_map/ppermute | solution.py:374
  296.4 15.7 %collective-permute-start.47 = (bf16[96,768]{1,0:T(8,128)(2,1)S(1)}, bf16[96,768]{1,0:T(8,128)(2,1)S(1)}, u32[]{:S(2)}, u32[]{:S(2)}) collective-permute-start(bf16[96,768]{1,0:T(8,128)(2,1)S(1)} %fusion.19), channel_id=1, source_target_pairs={{0,2},{1,3},{2,0},{3,1},{4,6},{5,7},{6,4},{7,5},{8,10},{9,11},{10,... | collective-permute-start | bytes 442376 | tf_op jit(solution)/shard_map/ppermute | solution.py:374
  (61 other events, 525.9 us)

commit v9 on v8

--- a/solution.py
+++ b/solution.py
@@ -556,7 +556,7 @@
     attn_whole = ((4, SLABS, DEPTH + EXTRA, 768), bf)
     down_outs = [(((n, 4, DEPTH, 768), bf), slab_block) for n in (4, 1, 1, 1, 1)]
     up_outs = [(((n, 4, DEPTH, 768), bf), slab_block) for n in (4, 4)]
-    attn_outs = [(((n, 4, DEPTH + EXTRA, 768), bf), slab_block) for n in (4, 4)]
+    attn_outs = [(((n, 4, DEPTH + EXTRA, 768), bf), slab_block) for n in (4, 1, 1, 1, 1)]
     thin = ((4, 1, 768), fl)
 
     if fast:
@@ -635,20 +635,20 @@
     wait = []
     if fast:
         down_plane = reduce_chip(down_pair, 2, [attn_near])
-        attn_far = late(attn_far, in_one, *down_plane)
-        up_half = reduce_core(up_near, late(up_far, in_one), parts=2)
-        attn_sums = reduce_core(attn_near, attn_far, parts=4)
-        up_pair = reduce_pair(up_half, 1, attn_sums)
-        attn_some = reduce_some(attn_sums, [in_two])
-        up_plane = reduce_chip(up_pair, 2, attn_some)
+        attn_far = late(attn_far, *down_plane)
+        attn_sums = reduce_core(attn_near, attn_far, [in_one, hidden_out])
+        up_half = reduce_core(up_near, late(up_far, in_one, *attn_sums), parts=2)
+        attn_some = reduce_some(attn_sums, [in_two, *up_half])
+        up_pair = reduce_pair(up_half, 1, attn_some)
         attn_plane = reduce_rest(attn_some, [in_three])
-        down_last = reduce_tensor(down_plane, [*up_pair, *attn_some])
-        attn_last = reduce_tensor([attn_plane[0]] + late(attn_plane[1:], *up_plane))
+        up_plane = reduce_chip(up_pair, 2, attn_plane)
+        down_last = reduce_tensor(down_plane, attn_some)
+        attn_last = reduce_tensor(attn_plane, up_pair)
         up_last = reduce_tensor(up_plane)
-        down_sum = reduce_last(down_last, [attn_last[1], up_last[1]])
-        attn_sum = reduce_last(attn_last)
+        down_sum = reduce_last(down_last, [attn_last[1]])
+        attn_sum = reduce_last(attn_last, up_last[1:])
         up_sum = reduce_last(up_last)
-        wait = up_plane + attn_plane
+        wait = attn_plane
     else:
         down_sum = reduce_plain(down_near, down_far, x_last=True)
         up_sum = reduce_plain(up_near, up_far, x_last=True)

time: 323 us -> 315 us (0.975)
  waiting for transfers between devices: 119 us -> 109 us
    ppermute x32 -> x35, waiting for transfers between devices: 64.7 us -> 35.5 us  [flip(): return lax.ppermute(value, 'dp', [(k, k ^ bits) for k in range(n)])]
    ppermute x6, waiting for transfers between devices: 15.2 us -> 33.5 us  [rotate(): return lax.ppermute(value, 'tensor', [(k, (k + 1) % 4) for k in range(4)])]
    unnamed x78 -> x92, local copies, waits for them, and re-layouts: 8.36 us -> 10.2 us
    ppermute x32 -> x35, starting transfers between devices: 24 us -> 22.4 us  [flip(): return lax.ppermute(value, 'dp', [(k, k ^ bits) for k in range(n)])]
  transfers between devices with their start and end apart: 50 -> 53, of which waited for: 21 -> 22; matrix products, arithmetic and copies ran while one was open for 9% -> 10% of each run, Pallas kernels for 28% -> 29%
where the time goes in v9:
time: 315 us; the launch traced here: 314 us
  waiting for transfers between devices  109 us (35%)
  Pallas kernels  108 us (34%)
  starting transfers between devices  42.9 us (14%)
  other arithmetic  26.9 us (9%)
  local copies, waits for them, and re-layouts  26 us (8%)
    pallas_call x6, Pallas kernels, call(): pl.pallas_call(kernel, name=name, out_shape=[jax.ShapeDtypeStruct(s, d) f...  72.8 us
    ppermute x12, waiting for transfers between devices, cross(): return lax.ppermute(value, 'tensor', [(k, k ^ bits) for k in range(4)])  39.8 us
    ppermute x35, waiting for transfers between devices, flip(): return lax.ppermute(value, 'dp', [(k, k ^ bits) for k in range(n)])  35.5 us
    pallas_call x4, Pallas kernels, call_groups(): pl.pallas_call(kernel, name=name, out_shape=[jax.ShapeDtypeStruct(s, d) f...  34.9 us
    ppermute x6, waiting for transfers between devices, rotate(): return lax.ppermute(value, 'tensor', [(k, (k + 1) % 4) for k in range(4)])  33.5 us
    ppermute x35, starting transfers between devices, flip(): return lax.ppermute(value, 'dp', [(k, k ^ bits) for k in range(n)])  22.4 us
    ppermute x12, starting transfers between devices, cross(): return lax.ppermute(value, 'tensor', [(k, k ^ bits) for k in range(4)])  16.6 us
    unnamed x92, local copies, waits for them, and re-layouts  10.2 us
  transfers between devices with their start and end apart: 53, of which 22 were waited for; matrix products, arithmetic and copies ran while one was open for 10% of the time, Pallas kernels for 29%

profile of v9, /device:TPU:0, one launch (start us, length us, event | category | flops | bytes accessed | tf_op | source)
XLA Modules:
  0.0 314.4 jit_solution(2603387470980611188)
XLA Ops:
  7.4 3.1 collective-permute-start
  13.1 5.4 %collective-permute-done = bf16[112,768]{1,0:T(8,128)(2,1)S(1)} collective-permute-done((bf16[112,768]{1,0:T(8,128)(2,1)S(1)}, bf16[112,768]{1,0:T(8,128)(2,1)S(1)}, u32[]{:S(2)}, u32[]{:S(2)}) %collective-permute-start) | collective-permute-done | bytes 172064 | tf_op jit(solution)/shard_map/ppermute | solution.py:374
  18.5 7.6 %collective-permute-done.1 = bf16[112,768]{1,0:T(8,128)(2,1)S(1)} collective-permute-done((bf16[112,768]{1,0:T(8,128)(2,1)S(1)}, bf16[112,768]{1,0:T(8,128)(2,1)S(1)}, u32[]{:S(2)}, u32[]{:S(2)}) %collective-permute-start.1) | collective-permute-done | bytes 172064 | tf_op jit(solution)/shard_map/ppermute | solution.py:374
  31.7 2.9 collective-permute-start.3
  35.7 6.3 %collective-permute-done.6.refs_1_ = bf16[4,112,768]{2,1,0:T(8,128)(2,1)} collective-permute-done((bf16[4,112,768]{2,1,0:T(8,128)(2,1)S(1)}, bf16[4,112,768]{2,1,0:T(8,128)(2,1)}, u32[]{:S(2)}, u32[]{:S(2)}) %collective-permute-start.6) | collective-permute-done | bytes 688160 | tf_op jit(solution)/shard_map/ppermute | solution.py:370
  49.2 3.4 %collective-permute-start.9 = (bf16[2,112,768]{2,1,0:T(8,128)(2,1)S(1)}, bf16[2,112,768]{2,1,0:T(8,128)(2,1)S(1)}, u32[]{:S(2)}, u32[]{:S(2)}) collective-permute-start(bf16[2,112,768]{2,1,0:T(8,128)(2,1)S(1)} %slice.490), channel_id=1, source_target_pairs={{0,8},{4,12},{8,0},{12,4},{16,24},{20,28},{24,16},{28,20},{1,9},{5... | collective-permute-start | bytes 1032200 | tf_op jit(solution)/shard_map/ppermute | solution.py:370
  52.7 8.6 %collective-permute-done.5 = bf16[192,768]{1,0:T(8,128)(2,1)S(1)} collective-permute-done((bf16[192,768]{1,0:T(8,128)(2,1)S(1)}, bf16[192,768]{1,0:T(8,128)(2,1)S(1)}, u32[]{:S(2)}, u32[]{:S(2)}) %collective-permute-start.5) | collective-permute-done | bytes 294944 | tf_op jit(solution)/shard_map/ppermute | solution.py:374
  70.8 15.7 %attn_fwd.1 = (bf16[4,512,768]{2,1,0:T(8,128)(2,1)}, bf16[4,512,256]{2,1,0:T(8,128)(2,1)}, f32[4,3,1,512]{3,2,1,0:T(1,128)}, bf16[4,8,112,768]{3,2,1,0:T(8,128)(...) custom-call(s32[2]{0:T(128)} %pad_add_fusion.1.where_ref, ...), custom_call_target="tpu_custom_call" | custom-call | flops 1000 | bytes 1000 | tf_op jit(solution)/shard_map/attn_fwd/pallas_call | solution.py:316
  91.3 12.7 %collective-permute-done.17.refs_3_ = bf16[2,192,768]{2,1,0:T(8,128)(2,1)S(1)} collective-permute-done((bf16[2,192,768]{2,1,0:T(8,128)(2,1)S(1)}, bf16[2,192,768]{2,1,0:T(8,128)(2,1)S(1)}, u32[]{:S(2)}, u32[]{:S(2)}) %collective-permute-start.17) | collective-permute-done | bytes 589856 | tf_op jit(solution)/shard_map/ppermute | solution.py:370
  108.9 17.7 %ffn_fwd.1 = (bf16[512,768]{1,0:T(8,128)(2,1)}, f32[512,768]{1,0:T(8,128)}, bf16[4,512,768]{2,1,0:T(8,128)(2,1)}, f32[4,512,768]{2,1,0:T(8,128)}, f32[3,768]{1,0...) custom-call(s32[2]{0:T(128)} %pad_add_fusion.1.where_ref, ...), custom_call_target="tpu_custom_call" | custom-call | flops 1000 | bytes 1000 | tf_op jit(solution)/shard_map/ffn_fwd/pallas_call | solution.py:316
  127.5 8.2 %down_weights.1 = (bf16[4,4,96,768]{3,2,1,0:T(8,128)(2,1)}, bf16[1,4,96,768]{3,2,1,0:T(8,128)(2,1)}, bf16[1,4,96,768]{3,2,1,0:T(8,128)(2,1)}, bf16[1,4,96,768]{3,2,1,0:T(8,128)(2,1)}, bf16[1,4,96,768]{3,2,1,0:T(8,128)(2,1)}) custom-call(s32[2]{0:T(128)} %pad_add_fusion.1.where_ref, f32[512,768]{1,0:T(8,128)} %get-tuple-element.111.dr2_ref, ...), custom_call_target="tpu_custom_call" | custom-call | flops 1000 | bytes 1000 | tf_op jit(solution)/shard_map/down_weights/pallas_call | solution.py:350
  136.7 9.3 %down_bwd.1 = (bf16[4,512,768]{2,1,0:T(8,128)(2,1)}, f32[4,1,768]{2,1,0:T(1,128)}) custom-call(s32[2]{0:T(128)} %pad_add_fusion.1.where_ref, f32[512,768]{1,0:T(8,128)} %get-tuple-element.111.dr2_ref, f32[4,512,768]{2,1,0:T(8,128)} %get-tuple-element.112.slope_ref, bf16[4,8,96,768]{3,2,1,0:T(8,128)(2,1)} %get-tuple-element.113.weight_ref), custom_call_target="tpu_custom_call" | custom-call | flops 1000 | bytes 1000 | tf_op jit(solution)/shard_map/down_bwd/pallas_call | solution.py:350
  152.7 12.3 %up_bwd.1 = (f32[512,768]{1,0:T(8,128)}, bf16[4,512,256]{2,1,0:T(8,128)(2,1)}, f32[3,768]{1,0:T(4,128)}) custom-call(s32[2]{0:T(128)} %pad_add_fusion.1.where_ref, f32[512,768]{1,0:T(8,128)} %get-tuple-element.111.dr2_ref, bf16[4,512,768]{2,1,0:T(8,128)(2,1)} %get-tuple-element.125.dup_ref, f32[512,768]{1,0:T(8,128)} %get-tuple-element.104.xhat_ref, ...), custom_call_target="tpu_custom_call" | custom-call | flops 1000 | bytes 1000 | tf_op jit(solution)/shard_map/up_bwd/pallas_call | solution.py:316
  165.0 7.8 %up_weights.1 = (bf16[4,4,96,768]{3,2,1,0:T(8,128)(2,1)}, bf16[4,4,96,768]{3,2,1,0:T(8,128)(2,1)}) custom-call(s32[2]{0:T(128)} %pad_add_fusion.1.where_ref, bf16[512,768]{1,0:T(8,128)(2,1)} %get-tuple-element.105.first_ref, bf16[4,512,768]{2,1,0:T(8,128)(2,1)} %get-tuple-element.125.dup_ref), custom_call_target="tpu_custom_call" | custom-call | flops 1000 | bytes 1000 | tf_op jit(solution)/shard_map/up_weights/pallas_call | solution.py:350
  174.3 19.5 %attn_bwd.1 = (bf16[512,768]{1,0:T(8,128)(2,1)}, bf16[4,512,768]{2,1,0:T(8,128)(2,1)}, f32[4,1,768]{2,1,0:T(1,128)}) custom-call(s32[2]{0:T(128)} %pad_add_fusion.1.where_ref, s32[1,512]{1,0:T(1,128)} %constant_dynamic-slice_fusion.2.seg_row_ref, s32[512,1]{1,0:T(8,128)} %copy.38.seg_col_ref, bf16[4,512,768]{2,1,0:T(8,128)(2,1)} %get-tuple-element.134.proj_ref, ...), custom_call_target="tpu_custom_call" | custom-call | flops 1000 | bytes 1000 | tf_op jit(solution)/shard_map/attn_bwd/pallas_call | solution.py:316
  197.1 9.7 %attn_weights.1 = (bf16[4,4,112,768]{3,2,1,0:T(8,128)(2,1)}, bf16[1,4,112,768]{3,2,1,0:T(8,128)(2,1)}, bf16[1,4,112,768]{3,2,1,0:T(8,128)(2,1)}, bf16[1,4,112,76...) custom-call(s32[2]{0:T(128)} %pad_add_fusion.1.where_ref, bf16[512,768]{1,0:T(8,128)(2,1)} %dynamic-slice_bitcast_fusion.1.x_ref, ...), custom_call_target="tpu_custom_call" | custom-call | flops 1000 | bytes 1000 | tf_op jit(solution)/shard_map/attn_weights/pallas_call | solution.py:350
  206.7 3.0 collective-permute-done.32
  212.2 3.9 %place_rows.2 = bf16[4,512,768]{2,1,0:T(8,128)(2,1)} custom-call(s32[2]{0:T(128)} %pad_add_fusion.where_ref, bf16[512,768]{1,0:T(8,128)(2,1)} %get-tuple-element.110.refs_0_, bf16[512,768]{1,0:T(8,128)(2,1)} %collective-permute-done.24.refs_1_, bf16[512,768]{1,0:T(8,128)(2,1)} %collective-permute-done.25.refs_2_, ...), custom_call_target="tpu_custom_call" | custom-call | flops 1000 | bytes 1000 | tf_op jit(solution)/shard_map/place_rows/pallas_call | solution.py:316
  226.1 15.4 %collective-permute-done.40.refs_2_ = bf16[512,768]{1,0:T(8,128)(2,1)S(1)} collective-permute-done((bf16[512,768]{1,0:T(8,128)(2,1)}, bf16[512,768]{1,0:T(8,128)(2,1)S(1)}, u32[]{:S(2)}, u32[]{:S(2)}) %collective-permute-start.40) | collective-permute-done | bytes 786464 | tf_op jit(solution)/shard_map/ppermute | solution.py:378
  248.4 15.4 %collective-permute-done.44.refs_3_ = bf16[512,768]{1,0:T(8,128)(2,1)} collective-permute-done((bf16[512,768]{1,0:T(8,128)(2,1)S(1)}, bf16[512,768]{1,0:T(8,128)(2,1)}, u32[]{:S(2)}, u32[]{:S(2)}) %collective-permute-start.44) | collective-permute-done | bytes 786464 | tf_op jit(solution)/shard_map/ppermute | solution.py:378
  263.8 8.0 %collective-permute-done.43 = bf16[2,112,768]{2,1,0:T(8,128)(2,1)} collective-permute-done((bf16[2,112,768]{2,1,0:T(8,128)(2,1)}, bf16[2,112,768]{2,1,0:T(8,128)(2,1)}, u32[]{:S(2)}, u32[]{:S(2)}) %collective-permute-start.43) | collective-permute-done | bytes 344096 | tf_op jit(solution)/shard_map/ppermute | solution.py:370
  281.2 3.8 %place_rows.3 = bf16[4,512,768]{2,1,0:T(8,128)(2,1)} custom-call(s32[2]{0:T(128)} %pad_add_fusion.where_ref, bf16[512,768]{1,0:T(8,128)(2,1)} %get-tuple-element.157.refs_0_, bf16[512,768]{1,0:T(8,128)(2,1)} %collective-permute-done.37.refs_1_, bf16[512,768]{1,0:T(8,128)(2,1)} %copy-done.12, bf16[512,768]{1,0:T(8,128)(2,1)} %collective-permute-done.44.refs_3_), custom_call_target="tpu_custom_call" | custom-call | flops 1000 | bytes 1000 | tf_op jit(solution)/shard_map/place_rows/pallas_call | solution.py:316
  290.4 2.9 collective-permute-done.48
  294.7 7.4 %collective-permute-done.49 = bf16[2,96,768]{2,1,0:T(8,128)(2,1)S(1)} collective-permute-done((bf16[2,96,768]{2,1,0:T(8,128)(2,1)S(1)}, bf16[2,96,768]{2,1,0:T(8,128)(2,1)S(1)}, u32[]{:S(2)}, u32[]{:S(2)}) %collective-permute-start.49) | collective-permute-done | bytes 294944 | tf_op jit(solution)/shard_map/ppermute | solution.py:374
  (286 shorter events, 102.4 us)
Async XLA Ops:
  10.5 15.6 %collective-permute-start.1 = (bf16[112,768]{1,0:T(8,128)(2,1)S(1)}, bf16[112,768]{1,0:T(8,128)(2,1)S(1)}, u32[]{:S(2)}, u32[]{:S(2)}) collective-permute-start(bf16[112,768]{1,0:T(8,128)(2,1)S(1)} %concatenate.62), channel_id=1, source_target_pairs={{0,2},{1,3},{2,0},{3,1},{4,6},{5,7},{6,4},{7,5},{8,10},{9,11},{10,... | collective-permute-start | bytes 516104 | tf_op jit(solution)/shard_map/ppermute | solution.py:374
  26.2 15.9 %collective-permute-start.6 = (bf16[4,112,768]{2,1,0:T(8,128)(2,1)S(1)}, bf16[4,112,768]{2,1,0:T(8,128)(2,1)}, u32[]{:S(2)}, u32[]{:S(2)}) collective-permute-start(bf16[4,112,768]{2,1,0:T(8,128)(2,1)S(1)} %pad_maximum_fusion.2.refs_0_), channel_id=1, source_target_pairs={{0,8},{4,12},{8,0},{12,4},{16,24},{20,28},{24,16},{28,20},{1,9},{5... | collective-permute-start | bytes 2064392 | tf_op jit(solution)/shard_map/ppermute | solution.py:370
  28.2 14.9 %collective-permute-start.7 = (bf16[4,112,768]{2,1,0:T(8,128)(2,1)S(1)}, bf16[4,112,768]{2,1,0:T(8,128)(2,1)}, u32[]{:S(2)}, u32[]{:S(2)}) collective-permute-start(bf16[4,112,768]{2,1,0:T(8,128)(2,1)S(1)} %pad_maximum_fusion.2.refs_0_), channel_id=1, source_target_pairs={{0,16},{4,20},{8,24},{12,28},{16,0},{20,4},{24,8},{28,12},{1,17},{... | collective-permute-start | bytes 2064392 | tf_op jit(solution)/shard_map/ppermute | solution.py:370
  63.2 23.3 %collective-permute-start.15 = (bf16[4,192,768]{2,1,0:T(8,128)(2,1)}, bf16[4,192,768]{2,1,0:T(8,128)(2,1)}, u32[]{:S(2)}, u32[]{:S(2)}) collective-permute-start(bf16[4,192,768]{2,1,0:T(8,128)(2,1)} %pad_maximum_fusion.refs_0_), channel_id=1, source_target_pairs={{0,8},{4,12},{8,0},{12,4},{16,24},{20,28},{24,16},{28,20},{1,9},{5... | collective-permute-start | bytes 3538952 | tf_op jit(solution)/shard_map/ppermute | solution.py:370
  63.2 24.4 %collective-permute-start.16 = (bf16[4,192,768]{2,1,0:T(8,128)(2,1)}, bf16[4,192,768]{2,1,0:T(8,128)(2,1)}, u32[]{:S(2)}, u32[]{:S(2)}) collective-permute-start(bf16[4,192,768]{2,1,0:T(8,128)(2,1)} %pad_maximum_fusion.refs_0_), channel_id=1, source_target_pairs={{0,16},{4,20},{8,24},{12,28},{16,0},{20,4},{24,8},{28,12},{1,17},{... | collective-permute-start | bytes 3538952 | tf_op jit(solution)/shard_map/ppermute | solution.py:370
  70.1 36.6 %collective-permute-start.19 = (bf16[4,192,768]{2,1,0:T(8,128)(2,1)}, bf16[4,192,768]{2,1,0:T(8,128)(2,1)S(1)}, u32[]{:S(2)}, u32[]{:S(2)}) collective-permute-start(bf16[4,192,768]{2,1,0:T(8,128)(2,1)} %pad_maximum_fusion.refs_0_), channel_id=1, source_target_pairs={{0,4},{4,0},{8,12},{12,8},{16,20},{20,16},{24,28},{28,24},{1,5},{5... | collective-permute-start | bytes 3538952 | tf_op jit(solution)/shard_map/ppermute | solution.py:370
  88.7 15.3 %collective-permute-start.17 = (bf16[2,192,768]{2,1,0:T(8,128)(2,1)S(1)}, bf16[2,192,768]{2,1,0:T(8,128)(2,1)S(1)}, u32[]{:S(2)}, u32[]{:S(2)}) collective-permute-start(bf16[2,192,768]{2,1,0:T(8,128)(2,1)S(1)} %slice.491), channel_id=1, source_target_pairs={{0,16},{4,20},{8,24},{12,28},{16,0},{20,4},{24,8},{28,12},{1,17},{... | collective-permute-start | bytes 1769480 | tf_op jit(solution)/shard_map/ppermute | solution.py:370
  88.8 15.5 %collective-permute-start.18 = (bf16[2,192,768]{2,1,0:T(8,128)(2,1)S(1)}, bf16[2,192,768]{2,1,0:T(8,128)(2,1)S(1)}, u32[]{:S(2)}, u32[]{:S(2)}) collective-permute-start(bf16[2,192,768]{2,1,0:T(8,128)(2,1)S(1)} %slice.492), channel_id=1, source_target_pairs={{0,8},{4,12},{8,0},{12,4},{16,24},{20,28},{24,16},{28,20},{1,9},{5... | collective-permute-start | bytes 1769480 | tf_op jit(solution)/shard_map/ppermute | solution.py:370
  90.8 16.1 %collective-permute-start.20 = (bf16[4,192,768]{2,1,0:T(8,128)(2,1)}, bf16[4,192,768]{2,1,0:T(8,128)(2,1)S(1)}, u32[]{:S(2)}, u32[]{:S(2)}) collective-permute-start(bf16[4,192,768]{2,1,0:T(8,128)(2,1)} %collective-permute-done.15.refs_1_), channel_id=1, source_target_pairs={{0,4},{4,0},{8,12},{12,8},{16,20},{20,16},{24,28},{28,24},{1,5},{5... | collective-permute-start | bytes 3538952 | tf_op jit(solution)/shard_map/ppermute | solution.py:370
  90.8 16.1 %collective-permute-start.21 = (bf16[4,192,768]{2,1,0:T(8,128)(2,1)}, bf16[4,192,768]{2,1,0:T(8,128)(2,1)S(1)}, u32[]{:S(2)}, u32[]{:S(2)}) collective-permute-start(bf16[4,192,768]{2,1,0:T(8,128)(2,1)} %collective-permute-done.16.refs_2_), channel_id=1, source_target_pairs={{0,4},{4,0},{8,12},{12,8},{16,20},{20,16},{24,28},{28,24},{1,5},{5... | collective-permute-start | bytes 3538952 | tf_op jit(solution)/shard_map/ppermute | solution.py:370
  126.5 21.9 %collective-permute-start.24 = (bf16[512,768]{1,0:T(8,128)(2,1)}, bf16[512,768]{1,0:T(8,128)(2,1)}, u32[]{:S(2)}, u32[]{:S(2)}) collective-permute-start(bf16[512,768]{1,0:T(8,128)(2,1)} %get-tuple-element.110.refs_0_), channel_id=1, source_target_pairs={{0,1},{1,2},{2,3},{3,0},{4,5},{5,6},{6,7},{7,4},{8,9},{9,10},{10,1... | collective-permute-start | bytes 2359304 | tf_op jit(solution)/shard_map/ppermute | solution.py:378
  150.3 43.5 %collective-permute-start.31 = (bf16[2,4,96,768]{3,2,1,0:T(8,128)(2,1)S(1)}, bf16[2,4,96,768]{3,2,1,0:T(8,128)(2,1)}, u32[]{:S(2)}, u32[]{:S(2)}) collective-permute-start(bf16[2,4,96,768]{3,2,1,0:T(8,128)(2,1)S(1)} %pad_maximum_fusion.1), channel_id=1, source_target_pairs={{0,8},{4,12},{8,0},{12,4},{16,24},{20,28},{24,16},{28,20},{1,9},{5... | collective-permute-start | bytes 3538952 | tf_op jit(solution)/shard_map/ppermute | solution.py:370
  152.3 20.6 %collective-permute-start.25 = (bf16[512,768]{1,0:T(8,128)(2,1)}, bf16[512,768]{1,0:T(8,128)(2,1)}, u32[]{:S(2)}, u32[]{:S(2)}) collective-permute-start(bf16[512,768]{1,0:T(8,128)(2,1)} %collective-permute-done.24.refs_1_), channel_id=1, source_target_pairs={{0,1},{1,2},{2,3},{3,0},{4,5},{5,6},{6,7},{7,4},{8,9},{9,10},{10,1... | collective-permute-start | bytes 2359304 | tf_op jit(solution)/shard_map/ppermute | solution.py:378
  172.9 24.1 %collective-permute-start.30 = (bf16[512,768]{1,0:T(8,128)(2,1)}, bf16[512,768]{1,0:T(8,128)(2,1)}, u32[]{:S(2)}, u32[]{:S(2)}) collective-permute-start(bf16[512,768]{1,0:T(8,128)(2,1)} %collective-permute-done.25.refs_2_), channel_id=1, source_target_pairs={{0,1},{1,2},{2,3},{3,0},{4,5},{5,6},{6,7},{7,4},{8,9},{9,10},{10,1... | collective-permute-start | bytes 2359304 | tf_op jit(solution)/shard_map/ppermute | solution.py:378
  196.4 19.8 %collective-permute-start.37 = (bf16[512,768]{1,0:T(8,128)(2,1)}, bf16[512,768]{1,0:T(8,128)(2,1)}, u32[]{:S(2)}, u32[]{:S(2)}) collective-permute-start(bf16[512,768]{1,0:T(8,128)(2,1)} %get-tuple-element.157.refs_0_), channel_id=1, source_target_pairs={{0,1},{1,2},{2,3},{3,0},{4,5},{5,6},{6,7},{7,4},{8,9},{9,10},{10,1... | collective-permute-start | bytes 2359304 | tf_op jit(solution)/shard_map/ppermute | solution.py:378
  219.5 22.0 %collective-permute-start.40 = (bf16[512,768]{1,0:T(8,128)(2,1)}, bf16[512,768]{1,0:T(8,128)(2,1)S(1)}, u32[]{:S(2)}, u32[]{:S(2)}) collective-permute-start(bf16[512,768]{1,0:T(8,128)(2,1)} %collective-permute-done.37.refs_1_), channel_id=1, source_target_pairs={{0,1},{1,2},{2,3},{3,0},{4,5},{5,6},{6,7},{7,4},{8,9},{9,10},{10,1... | collective-permute-start | bytes 2359304 | tf_op jit(solution)/shard_map/ppermute | solution.py:378
  220.3 21.2 %collective-permute-start.39 = (bf16[2,2,112,768]{3,2,1,0:T(8,128)(2,1)S(1)}, bf16[2,2,112,768]{3,2,1,0:T(8,128)(2,1)S(1)}, u32[]{:S(2)}, u32[]{:S(2)}) collective-permute-start(bf16[2,2,112,768]{3,2,1,0:T(8,128)(2,1)S(1)} %pad_maximum_fusion.4), channel_id=1, source_target_pairs={{0,16},{4,20},{8,24},{12,28},{16,0},{20,4},{24,8},{28,12},{1,17},{... | collective-permute-start | bytes 2064392 | tf_op jit(solution)/shard_map/ppermute | solution.py:370
  221.6 19.9 %collective-permute-start.38 = (bf16[2,2,112,768]{3,2,1,0:T(8,128)(2,1)S(1)}, bf16[2,2,112,768]{3,2,1,0:T(8,128)(2,1)S(1)}, u32[]{:S(2)}, u32[]{:S(2)}) collective-permute-start(bf16[2,2,112,768]{3,2,1,0:T(8,128)(2,1)S(1)} %pad_maximum_fusion.3), channel_id=1, source_target_pairs={{0,8},{4,12},{8,0},{12,4},{16,24},{20,28},{24,16},{28,20},{1,9},{5... | collective-permute-start | bytes 2064392 | tf_op jit(solution)/shard_map/ppermute | solution.py:370
  225.8 50.9 %collective-permute-start.46 = (bf16[2,4,96,768]{3,2,1,0:T(8,128)(2,1)}, bf16[2,4,96,768]{3,2,1,0:T(8,128)(2,1)}, u32[]{:S(2)}, u32[]{:S(2)}) collective-permute-start(bf16[2,4,96,768]{3,2,1,0:T(8,128)(2,1)} %get-tuple-element.223), channel_id=1, source_target_pairs={{0,8},{4,12},{8,0},{12,4},{16,24},{20,28},{24,16},{28,20},{1,9},{5... | collective-permute-start | bytes 3538952 | tf_op jit(solution)/shard_map/ppermute | solution.py:370
  241.5 22.3 %collective-permute-start.44 = (bf16[512,768]{1,0:T(8,128)(2,1)S(1)}, bf16[512,768]{1,0:T(8,128)(2,1)}, u32[]{:S(2)}, u32[]{:S(2)}) collective-permute-start(bf16[512,768]{1,0:T(8,128)(2,1)S(1)} %collective-permute-done.40.refs_2_), channel_id=1, source_target_pairs={{0,1},{1,2},{2,3},{3,0},{4,5},{5,6},{6,7},{7,4},{8,9},{9,10},{10,1... | collective-permute-start | bytes 2359304 | tf_op jit(solution)/shard_map/ppermute | solution.py:378
  242.5 29.4 %collective-permute-start.43 = (bf16[2,112,768]{2,1,0:T(8,128)(2,1)}, bf16[2,112,768]{2,1,0:T(8,128)(2,1)}, u32[]{:S(2)}, u32[]{:S(2)}) collective-permute-start(bf16[2,112,768]{2,1,0:T(8,128)(2,1)} %fusion.8), channel_id=1, source_target_pairs={{0,8},{4,12},{8,0},{12,4},{16,24},{20,28},{24,16},{28,20},{1,9},{5... | collective-permute-start | bytes 1032200 | tf_op jit(solution)/shard_map/ppermute | solution.py:370
  243.6 28.2 %collective-permute-start.42 = (bf16[2,112,768]{2,1,0:T(8,128)(2,1)}, bf16[2,112,768]{2,1,0:T(8,128)(2,1)}, u32[]{:S(2)}, u32[]{:S(2)}) collective-permute-start(bf16[2,112,768]{2,1,0:T(8,128)(2,1)} %fusion.7), channel_id=1, source_target_pairs={{0,16},{4,20},{8,24},{12,28},{16,0},{20,4},{24,8},{28,12},{1,17},{... | collective-permute-start | bytes 1032200 | tf_op jit(solution)/shard_map/ppermute | solution.py:370
  247.4 29.2 %collective-permute-start.51 = (bf16[2,96,768]{2,1,0:T(8,128)(2,1)}, bf16[2,96,768]{2,1,0:T(8,128)(2,1)S(1)}, u32[]{:S(2)}, u32[]{:S(2)}) collective-permute-start(bf16[2,96,768]{2,1,0:T(8,128)(2,1)} %get-tuple-element.239), channel_id=1, source_target_pairs={{0,1},{1,0},{2,3},{3,2},{4,5},{5,4},{6,7},{7,6},{8,9},{9,8},{10,11... | collective-permute-start | bytes 884744 | tf_op jit(solution)/shard_map/ppermute | solution.py:374
  287.3 14.9 %collective-permute-start.47 = (bf16[112,768]{1,0:T(8,128)(2,1)S(1)}, bf16[112,768]{1,0:T(8,128)(2,1)S(1)}, u32[]{:S(2)}, u32[]{:S(2)}) collective-permute-start(bf16[112,768]{1,0:T(8,128)(2,1)S(1)} %fusion.18), channel_id=1, source_target_pairs={{0,2},{1,3},{2,0},{3,1},{4,6},{5,7},{6,4},{7,5},{8,10},{9,11},{10,... | collective-permute-start | bytes 516104 | tf_op jit(solution)/shard_map/ppermute | solution.py:374
  (71 other events, 510.8 us)

commit v10 on v7

--- a/solution.py
+++ b/solution.py
@@ -437,6 +437,20 @@
     return [add(pair[0][k : k + 2], got[k : k + 2]).astype(bf) for k in (0, 2)]
 
 
+def reduce_some(sums, gates):
+    one, two, three, four = [part[0] for part in sums]
+    over_x = flip(jnp.stack([two[:2], four[:2]]), 2)
+    over_y = flip(jnp.stack([three[2:], four[2:]]), 4)
+    over_x, over_y = late([over_x, over_y], *gates)
+    pairs = ((one[:2], over_x[0]), (three[:2], over_x[1]), (one[2:], over_y[0]), (two[2:], over_y[1]))
+    return [add(*pair).astype(bf) for pair in pairs]
+
+
+def reduce_rest(some, gates):
+    over_y, over_x = late([flip(some[1], 4), flip(some[3], 2)], *gates)
+    return [add(some[0], over_y).astype(bf), add(some[2], over_x).astype(bf)]
+
+
 def reduce_tensor(plane, gates=()):
     got = cross(plane[1], 1)
     if gates:
@@ -622,13 +636,13 @@
     if fast:
         down_plane = reduce_chip(down_pair, 2)
         attn_far = late(attn_far, *down_plane)
-        attn_half = halves(reduce_core(attn_near, attn_far, [up_near, in_one]))
-        up_far = late(up_far, in_one, *attn_half)
+        attn_sums = reduce_core(attn_near, attn_far, [up_near, in_one])
+        up_far = late(up_far, in_one, *attn_sums)
         up_pair = reduce_pair(reduce_core(up_near, up_far, parts=2), 1, [in_two])
         up_plane = reduce_chip(up_pair, 2)
-        attn_pair = reduce_pair(attn_half, 2)
-        attn_plane = reduce_chip(attn_pair, 1, [in_three, *up_pair])
-        down_last = reduce_tensor(down_plane, [*up_pair, *attn_pair])
+        attn_some = reduce_some(attn_sums, [in_two])
+        attn_plane = reduce_rest(attn_some, [in_three, *up_pair])
+        down_last = reduce_tensor(down_plane, [*up_pair, *attn_some])
         attn_last = reduce_tensor([attn_plane[0]] + late(attn_plane[1:], *up_plane))
         up_last = reduce_tensor(up_plane)
         down_sum = reduce_last(down_last, [attn_last[1], up_last[1]])

time: 314 us -> 334 us (1.064)
  waiting for transfers between devices: 116 us -> 131 us
  starting transfers between devices: 39.9 us -> 44.4 us
    ppermute x33 -> x35, waiting for transfers between devices: 34.6 us -> 64.6 us  [flip(): return lax.ppermute(value, 'dp', [(k, k ^ bits) for k in range(n)])]
    ppermute x6, waiting for transfers between devices: 35.6 us -> 23.1 us  [rotate(): return lax.ppermute(value, 'tensor', [(k, (k + 1) % 4) for k in range(4)])]
    ppermute x33 -> x35, starting transfers between devices: 23.5 us -> 25.6 us  [flip(): return lax.ppermute(value, 'dp', [(k, k ^ bits) for k in range(n)])]
    unnamed x88 -> x96, local copies, waits for them, and re-layouts: 8.96 us -> 9.51 us
  transfers between devices with their start and end apart: 51 -> 53, of which waited for: 22 -> 21; matrix products, arithmetic and copies ran while one was open for 8% -> 7% of each run, Pallas kernels for 29% -> 27%
where the time goes in v10:
time: 334 us; the launch traced here: 333 us
  waiting for transfers between devices  131 us (39%)
  Pallas kernels  108 us (32%)
  starting transfers between devices  44.4 us (13%)
  local copies, waits for them, and re-layouts  25.3 us (8%)
  other arithmetic  22.6 us (7%)
    pallas_call x6, Pallas kernels, call(): pl.pallas_call(kernel, name=name, out_shape=[jax.ShapeDtypeStruct(s, d) f...  72.7 us
    ppermute x35, waiting for transfers between devices, flip(): return lax.ppermute(value, 'dp', [(k, k ^ bits) for k in range(n)])  64.6 us
    ppermute x12, waiting for transfers between devices, cross(): return lax.ppermute(value, 'tensor', [(k, k ^ bits) for k in range(4)])  42.9 us
    pallas_call x4, Pallas kernels, call_groups(): pl.pallas_call(kernel, name=name, out_shape=[jax.ShapeDtypeStruct(s, d) f...  35.1 us
    ppermute x35, starting transfers between devices, flip(): return lax.ppermute(value, 'dp', [(k, k ^ bits) for k in range(n)])  25.6 us
    ppermute x6, waiting for transfers between devices, rotate(): return lax.ppermute(value, 'tensor', [(k, (k + 1) % 4) for k in range(4)])  23.1 us
    ppermute x12, starting transfers between devices, cross(): return lax.ppermute(value, 'tensor', [(k, k ^ bits) for k in range(4)])  17.3 us
    unnamed x96, local copies, waits for them, and re-layouts  9.51 us
  transfers between devices with their start and end apart: 53, of which 21 were waited for; matrix products, arithmetic and copies ran while one was open for 7% of the time, Pallas kernels for 27%

profile of v10, /device:TPU:0, one launch (start us, length us, event | category | flops | bytes accessed | tf_op | source)
XLA Modules:
  0.0 333.0 jit_solution(1525596635258125558)
XLA Ops:
  7.4 3.1 collective-permute-start
  13.1 5.4 %collective-permute-done = bf16[112,768]{1,0:T(8,128)(2,1)S(1)} collective-permute-done((bf16[112,768]{1,0:T(8,128)(2,1)S(1)}, bf16[112,768]{1,0:T(8,128)(2,1)S(1)}, u32[]{:S(2)}, u32[]{:S(2)}) %collective-permute-start) | collective-permute-done | bytes 172064 | tf_op jit(solution)/shard_map/ppermute | solution.py:374
  18.5 7.6 %collective-permute-done.1 = bf16[112,768]{1,0:T(8,128)(2,1)S(1)} collective-permute-done((bf16[112,768]{1,0:T(8,128)(2,1)S(1)}, bf16[112,768]{1,0:T(8,128)(2,1)S(1)}, u32[]{:S(2)}, u32[]{:S(2)}) %collective-permute-start.1) | collective-permute-done | bytes 172064 | tf_op jit(solution)/shard_map/ppermute | solution.py:374
  35.7 6.3 %collective-permute-done.6.refs_1_ = bf16[4,112,768]{2,1,0:T(8,128)(2,1)} collective-permute-done((bf16[4,112,768]{2,1,0:T(8,128)(2,1)S(1)}, bf16[4,112,768]{2,1,0:T(8,128)(2,1)}, u32[]{:S(2)}, u32[]{:S(2)}) %collective-permute-start.6) | collective-permute-done | bytes 688160 | tf_op jit(solution)/shard_map/ppermute | solution.py:370
  49.2 3.4 %collective-permute-start.9 = (bf16[2,112,768]{2,1,0:T(8,128)(2,1)S(1)}, bf16[2,112,768]{2,1,0:T(8,128)(2,1)S(1)}, u32[]{:S(2)}, u32[]{:S(2)}) collective-permute-start(bf16[2,112,768]{2,1,0:T(8,128)(2,1)S(1)} %slice.490), channel_id=1, source_target_pairs={{0,8},{4,12},{8,0},{12,4},{16,24},{20,28},{24,16},{28,20},{1,9},{5... | collective-permute-start | bytes 1032200 | tf_op jit(solution)/shard_map/ppermute | solution.py:370
  52.7 8.6 %collective-permute-done.5 = bf16[192,768]{1,0:T(8,128)(2,1)S(1)} collective-permute-done((bf16[192,768]{1,0:T(8,128)(2,1)S(1)}, bf16[192,768]{1,0:T(8,128)(2,1)S(1)}, u32[]{:S(2)}, u32[]{:S(2)}) %collective-permute-start.5) | collective-permute-done | bytes 294944 | tf_op jit(solution)/shard_map/ppermute | solution.py:374
  70.8 15.7 %attn_fwd.1 = (bf16[4,512,768]{2,1,0:T(8,128)(2,1)}, bf16[4,512,256]{2,1,0:T(8,128)(2,1)}, f32[4,3,1,512]{3,2,1,0:T(1,128)}, bf16[4,8,112,768]{3,2,1,0:T(8,128)(...) custom-call(s32[2]{0:T(128)} %pad_add_fusion.1.where_ref, ...), custom_call_target="tpu_custom_call" | custom-call | flops 1000 | bytes 1000 | tf_op jit(solution)/shard_map/attn_fwd/pallas_call | solution.py:316
  91.3 12.7 %collective-permute-done.17.refs_3_ = bf16[2,192,768]{2,1,0:T(8,128)(2,1)S(1)} collective-permute-done((bf16[2,192,768]{2,1,0:T(8,128)(2,1)S(1)}, bf16[2,192,768]{2,1,0:T(8,128)(2,1)S(1)}, u32[]{:S(2)}, u32[]{:S(2)}) %collective-permute-start.17) | collective-permute-done | bytes 589856 | tf_op jit(solution)/shard_map/ppermute | solution.py:370
  108.8 17.7 %ffn_fwd.1 = (bf16[512,768]{1,0:T(8,128)(2,1)}, f32[512,768]{1,0:T(8,128)}, bf16[4,512,768]{2,1,0:T(8,128)(2,1)}, f32[4,512,768]{2,1,0:T(8,128)}, f32[3,768]{1,0...) custom-call(s32[2]{0:T(128)} %pad_add_fusion.1.where_ref, ...), custom_call_target="tpu_custom_call" | custom-call | flops 1000 | bytes 1000 | tf_op jit(solution)/shard_map/ffn_fwd/pallas_call | solution.py:316
  127.5 8.2 %down_weights.1 = (bf16[4,4,96,768]{3,2,1,0:T(8,128)(2,1)}, bf16[1,4,96,768]{3,2,1,0:T(8,128)(2,1)}, bf16[1,4,96,768]{3,2,1,0:T(8,128)(2,1)}, bf16[1,4,96,768]{3,2,1,0:T(8,128)(2,1)}, bf16[1,4,96,768]{3,2,1,0:T(8,128)(2,1)}) custom-call(s32[2]{0:T(128)} %pad_add_fusion.1.where_ref, f32[512,768]{1,0:T(8,128)} %get-tuple-element.108.dr2_ref, ...), custom_call_target="tpu_custom_call" | custom-call | flops 1000 | bytes 1000 | tf_op jit(solution)/shard_map/down_weights/pallas_call | solution.py:350
  136.7 9.3 %down_bwd.1 = (bf16[4,512,768]{2,1,0:T(8,128)(2,1)}, f32[4,1,768]{2,1,0:T(1,128)}) custom-call(s32[2]{0:T(128)} %pad_add_fusion.1.where_ref, f32[512,768]{1,0:T(8,128)} %get-tuple-element.108.dr2_ref, f32[4,512,768]{2,1,0:T(8,128)} %get-tuple-element.109.slope_ref, bf16[4,8,96,768]{3,2,1,0:T(8,128)(2,1)} %get-tuple-element.110.weight_ref), custom_call_target="tpu_custom_call" | custom-call | flops 1000 | bytes 1000 | tf_op jit(solution)/shard_map/down_bwd/pallas_call | solution.py:350
  152.7 12.3 %up_bwd.1 = (f32[512,768]{1,0:T(8,128)}, bf16[4,512,256]{2,1,0:T(8,128)(2,1)}, f32[3,768]{1,0:T(4,128)}) custom-call(s32[2]{0:T(128)} %pad_add_fusion.1.where_ref, f32[512,768]{1,0:T(8,128)} %get-tuple-element.108.dr2_ref, bf16[4,512,768]{2,1,0:T(8,128)(2,1)} %get-tuple-element.122.dup_ref, f32[512,768]{1,0:T(8,128)} %get-tuple-element.101.xhat_ref, ...), custom_call_target="tpu_custom_call" | custom-call | flops 1000 | bytes 1000 | tf_op jit(solution)/shard_map/up_bwd/pallas_call | solution.py:316
  165.0 7.9 %collective-permute-done.25.refs_2_ = bf16[512,768]{1,0:T(8,128)(2,1)} collective-permute-done((bf16[512,768]{1,0:T(8,128)(2,1)}, bf16[512,768]{1,0:T(8,128)(2,1)}, u32[]{:S(2)}, u32[]{:S(2)}) %collective-permute-start.25) | collective-permute-done | bytes 786464 | tf_op jit(solution)/shard_map/ppermute | solution.py:378
  172.9 19.5 %attn_bwd.1 = (bf16[512,768]{1,0:T(8,128)(2,1)}, bf16[4,512,768]{2,1,0:T(8,128)(2,1)}, f32[4,1,768]{2,1,0:T(1,128)}) custom-call(s32[2]{0:T(128)} %pad_add_fusion.1.where_ref, s32[1,512]{1,0:T(1,128)} %constant_dynamic-slice_fusion.2.seg_row_ref, s32[512,1]{1,0:T(8,128)} %copy.38.seg_col_ref, bf16[4,512,768]{2,1,0:T(8,128)(2,1)} %get-tuple-element.129.proj_ref, ...), custom_call_target="tpu_custom_call" | custom-call | flops 1000 | bytes 1000 | tf_op jit(solution)/shard_map/attn_bwd/pallas_call | solution.py:316
  196.1 9.7 %attn_weights.1 = (bf16[4,4,112,768]{3,2,1,0:T(8,128)(2,1)}, bf16[1,4,112,768]{3,2,1,0:T(8,128)(2,1)}, bf16[1,4,112,768]{3,2,1,0:T(8,128)(2,1)}, bf16[1,4,112,76...) custom-call(s32[2]{0:T(128)} %pad_add_fusion.1.where_ref, bf16[512,768]{1,0:T(8,128)(2,1)} %dynamic-slice_bitcast_fusion.1.x_ref, ...), custom_call_target="tpu_custom_call" | custom-call | flops 1000 | bytes 1000 | tf_op jit(solution)/shard_map/attn_weights/pallas_call | solution.py:350
  209.3 8.0 %up_weights.1 = (bf16[4,4,96,768]{3,2,1,0:T(8,128)(2,1)}, bf16[4,4,96,768]{3,2,1,0:T(8,128)(2,1)}) custom-call(s32[2]{0:T(128)} %pad_add_fusion.1.where_ref, bf16[512,768]{1,0:T(8,128)(2,1)} %get-tuple-element.102.first_ref, bf16[4,512,768]{2,1,0:T(8,128)(2,1)} %get-tuple-element.122.dup_ref), custom_call_target="tpu_custom_call" | custom-call | flops 1000 | bytes 1000 | tf_op jit(solution)/shard_map/up_weights/pallas_call | solution.py:350
  220.9 4.3 %collective-permute-done.38 = bf16[4,4,96,768]{3,2,1,0:T(8,128)(2,1)S(1)} collective-permute-done((bf16[4,4,96,768]{3,2,1,0:T(8,128)(2,1)S(1)}, bf16[4,4,96,768]{3,2,1,0:T(8,128)(2,1)S(1)}, u32[]{:S(2)}, u32[]{:S(2)}) %collective-permute-start.38) | collective-permute-done | bytes 2359328 | tf_op jit(solution)/shard_map/ppermute | solution.py:370
  229.9 12.8 %collective-permute-done.40.refs_2_ = bf16[512,768]{1,0:T(8,128)(2,1)} collective-permute-done((bf16[512,768]{1,0:T(8,128)(2,1)}, bf16[512,768]{1,0:T(8,128)(2,1)}, u32[]{:S(2)}, u32[]{:S(2)}) %collective-permute-start.40) | collective-permute-done | bytes 786464 | tf_op jit(solution)/shard_map/ppermute | solution.py:378
  243.9 24.8 %collective-permute-done.42 = bf16[2,2,112,768]{3,2,1,0:T(8,128)(2,1)S(1)} collective-permute-done((bf16[2,2,112,768]{3,2,1,0:T(8,128)(2,1)S(1)}, bf16[2,2,112,768]{3,2,1,0:T(8,128)(2,1)S(1)}, u32[]{:S(2)}, u32[]{:S(2)}) %collective-permute-start.42) | collective-permute-done | bytes 688160 | tf_op jit(solution)/shard_map/ppermute | solution.py:370
  276.9 3.7 %place_rows.2 = bf16[4,512,768]{2,1,0:T(8,128)(2,1)} custom-call(s32[2]{0:T(128)} %pad_add_fusion.where_ref, bf16[512,768]{1,0:T(8,128)(2,1)} %get-tuple-element.107.refs_0_, bf16[512,768]{1,0:T(8,128)(2,1)} %collective-permute-done.24.refs_1_, bf16[512,768]{1,0:T(8,128)(2,1)} %collective-permute-done.25.refs_2_, ...), custom_call_target="tpu_custom_call" | custom-call | flops 1000 | bytes 1000 | tf_op jit(solution)/shard_map/place_rows/pallas_call | solution.py:316
  280.7 12.6 %collective-permute-done.44 = bf16[2,112,768]{2,1,0:T(8,128)(2,1)} collective-permute-done((bf16[2,112,768]{2,1,0:T(8,128)(2,1)}, bf16[2,112,768]{2,1,0:T(8,128)(2,1)}, u32[]{:S(2)}, u32[]{:S(2)}) %collective-permute-start.44) | collective-permute-done | bytes 344096 | tf_op jit(solution)/shard_map/ppermute | solution.py:370
  299.7 3.8 %place_rows.3 = bf16[4,512,768]{2,1,0:T(8,128)(2,1)} custom-call(s32[2]{0:T(128)} %pad_add_fusion.where_ref, bf16[512,768]{1,0:T(8,128)(2,1)} %get-tuple-element.145.refs_0_, bf16[512,768]{1,0:T(8,128)(2,1)} %collective-permute-done.32.refs_1_, bf16[512,768]{1,0:T(8,128)(2,1)} %collective-permute-done.40.refs_2_, ...), custom_call_target="tpu_custom_call" | custom-call | flops 1000 | bytes 1000 | tf_op jit(solution)/shard_map/place_rows/pallas_call | solution.py:316
  303.5 5.4 %collective-permute-done.49 = bf16[2,96,768]{2,1,0:T(8,128)(2,1)S(1)} collective-permute-done((bf16[2,96,768]{2,1,0:T(8,128)(2,1)}, bf16[2,96,768]{2,1,0:T(8,128)(2,1)S(1)}, u32[]{:S(2)}, u32[]{:S(2)}) %collective-permute-start.49) | collective-permute-done | bytes 294944 | tf_op jit(solution)/shard_map/ppermute | solution.py:374
  316.2 7.3 %collective-permute-done.50 = bf16[96,768]{1,0:T(8,128)(2,1)S(1)} collective-permute-done((bf16[96,768]{1,0:T(8,128)(2,1)S(1)}, bf16[96,768]{1,0:T(8,128)(2,1)S(1)}, u32[]{:S(2)}, u32[]{:S(2)}) %collective-permute-start.50) | collective-permute-done | bytes 147488 | tf_op jit(solution)/shard_map/ppermute | solution.py:374
  (290 shorter events, 100.7 us)
Async XLA Ops:
  10.5 15.6 %collective-permute-start.1 = (bf16[112,768]{1,0:T(8,128)(2,1)S(1)}, bf16[112,768]{1,0:T(8,128)(2,1)S(1)}, u32[]{:S(2)}, u32[]{:S(2)}) collective-permute-start(bf16[112,768]{1,0:T(8,128)(2,1)S(1)} %concatenate.62), channel_id=1, source_target_pairs={{0,2},{1,3},{2,0},{3,1},{4,6},{5,7},{6,4},{7,5},{8,10},{9,11},{10,... | collective-permute-start | bytes 516104 | tf_op jit(solution)/shard_map/ppermute | solution.py:374
  26.2 15.9 %collective-permute-start.6 = (bf16[4,112,768]{2,1,0:T(8,128)(2,1)S(1)}, bf16[4,112,768]{2,1,0:T(8,128)(2,1)}, u32[]{:S(2)}, u32[]{:S(2)}) collective-permute-start(bf16[4,112,768]{2,1,0:T(8,128)(2,1)S(1)} %pad_maximum_fusion.2.refs_0_), channel_id=1, source_target_pairs={{0,8},{4,12},{8,0},{12,4},{16,24},{20,28},{24,16},{28,20},{1,9},{5... | collective-permute-start | bytes 2064392 | tf_op jit(solution)/shard_map/ppermute | solution.py:370
  28.2 14.9 %collective-permute-start.7 = (bf16[4,112,768]{2,1,0:T(8,128)(2,1)S(1)}, bf16[4,112,768]{2,1,0:T(8,128)(2,1)}, u32[]{:S(2)}, u32[]{:S(2)}) collective-permute-start(bf16[4,112,768]{2,1,0:T(8,128)(2,1)S(1)} %pad_maximum_fusion.2.refs_0_), channel_id=1, source_target_pairs={{0,16},{4,20},{8,24},{12,28},{16,0},{20,4},{24,8},{28,12},{1,17},{... | collective-permute-start | bytes 2064392 | tf_op jit(solution)/shard_map/ppermute | solution.py:370
  63.2 23.3 %collective-permute-start.15 = (bf16[4,192,768]{2,1,0:T(8,128)(2,1)}, bf16[4,192,768]{2,1,0:T(8,128)(2,1)}, u32[]{:S(2)}, u32[]{:S(2)}) collective-permute-start(bf16[4,192,768]{2,1,0:T(8,128)(2,1)} %pad_maximum_fusion.refs_0_), channel_id=1, source_target_pairs={{0,8},{4,12},{8,0},{12,4},{16,24},{20,28},{24,16},{28,20},{1,9},{5... | collective-permute-start | bytes 3538952 | tf_op jit(solution)/shard_map/ppermute | solution.py:370
  63.2 24.4 %collective-permute-start.16 = (bf16[4,192,768]{2,1,0:T(8,128)(2,1)}, bf16[4,192,768]{2,1,0:T(8,128)(2,1)}, u32[]{:S(2)}, u32[]{:S(2)}) collective-permute-start(bf16[4,192,768]{2,1,0:T(8,128)(2,1)} %pad_maximum_fusion.refs_0_), channel_id=1, source_target_pairs={{0,16},{4,20},{8,24},{12,28},{16,0},{20,4},{24,8},{28,12},{1,17},{... | collective-permute-start | bytes 3538952 | tf_op jit(solution)/shard_map/ppermute | solution.py:370
  70.0 36.6 %collective-permute-start.19 = (bf16[4,192,768]{2,1,0:T(8,128)(2,1)}, bf16[4,192,768]{2,1,0:T(8,128)(2,1)S(1)}, u32[]{:S(2)}, u32[]{:S(2)}) collective-permute-start(bf16[4,192,768]{2,1,0:T(8,128)(2,1)} %pad_maximum_fusion.refs_0_), channel_id=1, source_target_pairs={{0,4},{4,0},{8,12},{12,8},{16,20},{20,16},{24,28},{28,24},{1,5},{5... | collective-permute-start | bytes 3538952 | tf_op jit(solution)/shard_map/ppermute | solution.py:370
  88.7 15.3 %collective-permute-start.17 = (bf16[2,192,768]{2,1,0:T(8,128)(2,1)S(1)}, bf16[2,192,768]{2,1,0:T(8,128)(2,1)S(1)}, u32[]{:S(2)}, u32[]{:S(2)}) collective-permute-start(bf16[2,192,768]{2,1,0:T(8,128)(2,1)S(1)} %slice.491), channel_id=1, source_target_pairs={{0,16},{4,20},{8,24},{12,28},{16,0},{20,4},{24,8},{28,12},{1,17},{... | collective-permute-start | bytes 1769480 | tf_op jit(solution)/shard_map/ppermute | solution.py:370
  88.8 15.5 %collective-permute-start.18 = (bf16[2,192,768]{2,1,0:T(8,128)(2,1)S(1)}, bf16[2,192,768]{2,1,0:T(8,128)(2,1)S(1)}, u32[]{:S(2)}, u32[]{:S(2)}) collective-permute-start(bf16[2,192,768]{2,1,0:T(8,128)(2,1)S(1)} %slice.492), channel_id=1, source_target_pairs={{0,8},{4,12},{8,0},{12,4},{16,24},{20,28},{24,16},{28,20},{1,9},{5... | collective-permute-start | bytes 1769480 | tf_op jit(solution)/shard_map/ppermute | solution.py:370
  90.8 16.1 %collective-permute-start.20 = (bf16[4,192,768]{2,1,0:T(8,128)(2,1)}, bf16[4,192,768]{2,1,0:T(8,128)(2,1)S(1)}, u32[]{:S(2)}, u32[]{:S(2)}) collective-permute-start(bf16[4,192,768]{2,1,0:T(8,128)(2,1)} %collective-permute-done.15.refs_1_), channel_id=1, source_target_pairs={{0,4},{4,0},{8,12},{12,8},{16,20},{20,16},{24,28},{28,24},{1,5},{5... | collective-permute-start | bytes 3538952 | tf_op jit(solution)/shard_map/ppermute | solution.py:370
  90.8 16.1 %collective-permute-start.21 = (bf16[4,192,768]{2,1,0:T(8,128)(2,1)}, bf16[4,192,768]{2,1,0:T(8,128)(2,1)S(1)}, u32[]{:S(2)}, u32[]{:S(2)}) collective-permute-start(bf16[4,192,768]{2,1,0:T(8,128)(2,1)} %collective-permute-done.16.refs_2_), channel_id=1, source_target_pairs={{0,4},{4,0},{8,12},{12,8},{16,20},{20,16},{24,28},{28,24},{1,5},{5... | collective-permute-start | bytes 3538952 | tf_op jit(solution)/shard_map/ppermute | solution.py:370
  126.5 21.9 %collective-permute-start.24 = (bf16[512,768]{1,0:T(8,128)(2,1)}, bf16[512,768]{1,0:T(8,128)(2,1)}, u32[]{:S(2)}, u32[]{:S(2)}) collective-permute-start(bf16[512,768]{1,0:T(8,128)(2,1)} %get-tuple-element.107.refs_0_), channel_id=1, source_target_pairs={{0,1},{1,2},{2,3},{3,0},{4,5},{5,6},{6,7},{7,4},{8,9},{9,10},{10,1... | collective-permute-start | bytes 2359304 | tf_op jit(solution)/shard_map/ppermute | solution.py:378
  150.3 42.1 %collective-permute-start.31 = (bf16[2,4,96,768]{3,2,1,0:T(8,128)(2,1)S(1)}, bf16[2,4,96,768]{3,2,1,0:T(8,128)(2,1)}, u32[]{:S(2)}, u32[]{:S(2)}) collective-permute-start(bf16[2,4,96,768]{3,2,1,0:T(8,128)(2,1)S(1)} %pad_maximum_fusion.1), channel_id=1, source_target_pairs={{0,8},{4,12},{8,0},{12,4},{16,24},{20,28},{24,16},{28,20},{1,9},{5... | collective-permute-start | bytes 3538952 | tf_op jit(solution)/shard_map/ppermute | solution.py:370
  152.3 20.7 %collective-permute-start.25 = (bf16[512,768]{1,0:T(8,128)(2,1)}, bf16[512,768]{1,0:T(8,128)(2,1)}, u32[]{:S(2)}, u32[]{:S(2)}) collective-permute-start(bf16[512,768]{1,0:T(8,128)(2,1)} %collective-permute-done.24.refs_1_), channel_id=1, source_target_pairs={{0,1},{1,2},{2,3},{3,0},{4,5},{5,6},{6,7},{7,4},{8,9},{9,10},{10,1... | collective-permute-start | bytes 2359304 | tf_op jit(solution)/shard_map/ppermute | solution.py:378
  172.9 23.2 %collective-permute-start.30 = (bf16[512,768]{1,0:T(8,128)(2,1)}, bf16[512,768]{1,0:T(8,128)(2,1)}, u32[]{:S(2)}, u32[]{:S(2)}) collective-permute-start(bf16[512,768]{1,0:T(8,128)(2,1)} %collective-permute-done.25.refs_2_), channel_id=1, source_target_pairs={{0,1},{1,2},{2,3},{3,0},{4,5},{5,6},{6,7},{7,4},{8,9},{9,10},{10,1... | collective-permute-start | bytes 2359304 | tf_op jit(solution)/shard_map/ppermute | solution.py:378
  196.1 21.1 %collective-permute-start.32 = (bf16[512,768]{1,0:T(8,128)(2,1)}, bf16[512,768]{1,0:T(8,128)(2,1)}, u32[]{:S(2)}, u32[]{:S(2)}) collective-permute-start(bf16[512,768]{1,0:T(8,128)(2,1)} %get-tuple-element.145.refs_0_), channel_id=1, source_target_pairs={{0,1},{1,2},{2,3},{3,0},{4,5},{5,6},{6,7},{7,4},{8,9},{9,10},{10,1... | collective-permute-start | bytes 2359304 | tf_op jit(solution)/shard_map/ppermute | solution.py:378
  220.8 22.0 %collective-permute-start.40 = (bf16[512,768]{1,0:T(8,128)(2,1)}, bf16[512,768]{1,0:T(8,128)(2,1)}, u32[]{:S(2)}, u32[]{:S(2)}) collective-permute-start(bf16[512,768]{1,0:T(8,128)(2,1)} %collective-permute-done.32.refs_1_), channel_id=1, source_target_pairs={{0,1},{1,2},{2,3},{3,0},{4,5},{5,6},{6,7},{7,4},{8,9},{9,10},{10,1... | collective-permute-start | bytes 2359304 | tf_op jit(solution)/shard_map/ppermute | solution.py:378
  225.9 44.3 %collective-permute-start.39 = (bf16[2,4,96,768]{3,2,1,0:T(8,128)(2,1)S(1)}, bf16[2,4,96,768]{3,2,1,0:T(8,128)(2,1)S(1)}, u32[]{:S(2)}, u32[]{:S(2)}) collective-permute-start(bf16[2,4,96,768]{3,2,1,0:T(8,128)(2,1)S(1)} %get-tuple-element.217), channel_id=1, source_target_pairs={{0,8},{4,12},{8,0},{12,4},{16,24},{20,28},{24,16},{28,20},{1,9},{5... | collective-permute-start | bytes 3538952 | tf_op jit(solution)/shard_map/ppermute | solution.py:370
  226.7 17.3 %collective-permute-start.43 = (bf16[2,2,112,768]{3,2,1,0:T(8,128)(2,1)S(1)}, bf16[2,2,112,768]{3,2,1,0:T(8,128)(2,1)S(1)}, u32[]{:S(2)}, u32[]{:S(2)}) collective-permute-start(bf16[2,2,112,768]{3,2,1,0:T(8,128)(2,1)S(1)} %pad_maximum_fusion.4), channel_id=1, source_target_pairs={{0,16},{4,20},{8,24},{12,28},{16,0},{20,4},{24,8},{28,12},{1,17},{... | collective-permute-start | bytes 2064392 | tf_op jit(solution)/shard_map/ppermute | solution.py:370
  228.3 40.5 %collective-permute-start.42 = (bf16[2,2,112,768]{3,2,1,0:T(8,128)(2,1)S(1)}, bf16[2,2,112,768]{3,2,1,0:T(8,128)(2,1)S(1)}, u32[]{:S(2)}, u32[]{:S(2)}) collective-permute-start(bf16[2,2,112,768]{3,2,1,0:T(8,128)(2,1)S(1)} %pad_maximum_fusion.3), channel_id=1, source_target_pairs={{0,8},{4,12},{8,0},{12,4},{16,24},{20,28},{24,16},{28,20},{1,9},{5... | collective-permute-start | bytes 2064392 | tf_op jit(solution)/shard_map/ppermute | solution.py:370
  242.8 37.9 %collective-permute-start.46 = (bf16[512,768]{1,0:T(8,128)(2,1)}, bf16[512,768]{1,0:T(8,128)(2,1)}, u32[]{:S(2)}, u32[]{:S(2)}) collective-permute-start(bf16[512,768]{1,0:T(8,128)(2,1)} %collective-permute-done.40.refs_2_), channel_id=1, source_target_pairs={{0,1},{1,2},{2,3},{3,0},{4,5},{5,6},{6,7},{7,4},{8,9},{9,10},{10,1... | collective-permute-start | bytes 2359304 | tf_op jit(solution)/shard_map/ppermute | solution.py:378
  271.3 21.9 %collective-permute-start.41 = (bf16[4,96,768]{2,1,0:T(8,128)(2,1)}, bf16[4,96,768]{2,1,0:T(8,128)(2,1)S(1)}, u32[]{:S(2)}, u32[]{:S(2)}) collective-permute-start(bf16[4,96,768]{2,1,0:T(8,128)(2,1)} %get-tuple-element.226), channel_id=1, source_target_pairs={{0,16},{4,20},{8,24},{12,28},{16,0},{20,4},{24,8},{28,12},{1,17},{... | collective-permute-start | bytes 1769480 | tf_op jit(solution)/shard_map/ppermute | solution.py:370
  273.6 19.6 %collective-permute-start.44 = (bf16[2,112,768]{2,1,0:T(8,128)(2,1)}, bf16[2,112,768]{2,1,0:T(8,128)(2,1)}, u32[]{:S(2)}, u32[]{:S(2)}) collective-permute-start(bf16[2,112,768]{2,1,0:T(8,128)(2,1)} %fusion.7), channel_id=1, source_target_pairs={{0,16},{4,20},{8,24},{12,28},{16,0},{20,4},{24,8},{28,12},{1,17},{... | collective-permute-start | bytes 1032200 | tf_op jit(solution)/shard_map/ppermute | solution.py:370
  295.5 18.0 %collective-permute-start.47 = (bf16[2,112,768]{2,1,0:T(8,128)(2,1)S(1)}, bf16[2,112,768]{2,1,0:T(8,128)(2,1)S(1)}, u32[]{:S(2)}, u32[]{:S(2)}) collective-permute-start(bf16[2,112,768]{2,1,0:T(8,128)(2,1)S(1)} %get-tuple-element.166), channel_id=1, source_target_pairs={{0,1},{1,0},{2,3},{3,2},{4,5},{5,4},{6,7},{7,6},{8,9},{9,8},{10,11... | collective-permute-start | bytes 1032200 | tf_op jit(solution)/shard_map/ppermute | solution.py:374
  297.6 17.5 %collective-permute-start.52 = (bf16[96,768]{1,0:T(8,128)(2,1)S(1)}, bf16[96,768]{1,0:T(8,128)(2,1)S(1)}, u32[]{:S(2)}, u32[]{:S(2)}) collective-permute-start(bf16[96,768]{1,0:T(8,128)(2,1)S(1)} %fusion.20), channel_id=1, source_target_pairs={{0,2},{1,3},{2,0},{3,1},{4,6},{5,7},{6,4},{7,5},{8,10},{9,11},{10,... | collective-permute-start | bytes 442376 | tf_op jit(solution)/shard_map/ppermute | solution.py:374
  (73 other events, 596.0 us)
